TPU v7x, 32 devices: a whole 2x2x4 slice. The times are simulated.
32 devices in a mesh: dp: 4 (over y, x), mp: 8 (over z, core).
Axes of the slice: x: 2, y: 2, z: 4, core: 2. Of those that a mesh axis runs over, the one named last changes fastest.
Arguments:
- frames: bfloat16 [1024, 12, 1280], P('mp', 'dp'), may hold values from -6 to 6
- lengths: int32 [12], P('dp'), may hold values from 1 to 1024, 10752 in all
- key_mask: int32 [12, 1024], P('dp'), may hold values from 0 to 1, as said below
- cotangent: bfloat16 [1024, 12, 1280], P('mp', 'dp'), may hold values from -6 to 6
- gain_one: bfloat16 [1280], replicated, may hold values from 0.5 to 1.5
- shift_one: bfloat16 [1280], replicated, may hold values from -1.5 to 1.5
- query_weight: bfloat16 [1280, 1280], P(None, 'mp'), may hold values from -0.25 to 0.25
- query_bias: bfloat16 [1280], P('mp'), may hold values from -2.5 to 2.5
- key_weight: bfloat16 [1280, 1280], P(None, 'mp'), may hold values from -0.25 to 0.25
- value_weight: bfloat16 [1280, 1280], P(None, 'mp'), may hold values from -0.15625 to 0.15625
- value_bias: bfloat16 [1280], P('mp'), may hold values from -2.5 to 2.5
- out_weight: bfloat16 [1280, 1280], P('mp'), may hold values from -0.625 to 0.625
- out_bias: bfloat16 [1280], replicated, may hold values from -1.5 to 1.5
- gain_two: bfloat16 [1280], replicated, may hold values from 0.5 to 1.5
- shift_two: bfloat16 [1280], replicated, may hold values from -1.5 to 1.5
- up_weight: bfloat16 [1280, 5120], P(None, 'mp'), may hold values from -0.15625 to 0.15625
- up_bias: bfloat16 [5120], P('mp'), may hold values from -2.5 to 2.5
- down_weight: bfloat16 [5120, 1280], P('mp'), may hold values from -0.125 to 0.125
- down_bias: bfloat16 [1280], replicated, may hold values from -1.5 to 1.5
- master: float32 [8, 2459520], P('mp', 'dp'), may hold values from -0.15 to 0.15
- moment_one: float32 [8, 2459520], P('mp', 'dp'), may hold values from -60 to 60
- moment_two: float32 [8, 2459520], P('mp', 'dp'), may hold values from 1 to 100
- adam_step: int32 [1], replicated, may hold values from 1 to 999
- hyper_rates: float32 [3], replicated, may hold values from 0.001 to 5, as said below
Outputs:
- layer_out: bfloat16 [1024, 12, 1280], P('mp', 'dp')
- input_grad: float32 [1024, 12, 1280], P('mp', 'dp')
- weight_grads: float32 [8, 2459520], P('mp', 'dp')
- master_new: float32 [8, 2459520], P('mp', 'dp')
- first_moment: float32 [8, 2459520], P('mp', 'dp')
- second_moment: float32 [8, 2459520], P('mp', 'dp')
- weights_new: bfloat16 [8, 2459520], P('mp')
- norm_grads: float32 [7680], P('mp')
Inputs may be any that keep to these rules, and one draw needn't show every extreme that they name: `lengths`: valid frames of each clip; they sum to 10752 and the longest is exactly 1024. `key_mask`: the first frame of every clip is 1. `adam_step`: the AdamW step count. `hyper_rates`: learning rate, weight decay and logit cap, in this order.
All inputs are finite; a program needn't handle non-finite values. No bound on the sum of `lengths` on one device may be relied on, other than what follows from the above.
Results may differ from a plain program's by a relative error of at most 0.018.
Values may be sent and summed in bfloat16 or wider, within the bound.
A program may use at most 192 MiB of HBM per device.

v0:
```python
import math

import jax
import jax.numpy as jnp
from jax import lax
from jax.sharding import PartitionSpec as P

HD = 80


NORM_EPSILON = 1e-05
ADAM_EPSILON = 1e-08
BETA_FIRST = 0.9
BETA_SECOND = 0.999
MASK_VALUE = -1e30


def layer_norm(value, gain, shift):
    center = value - jnp.mean(value, axis=-1, keepdims=True)
    spread = jnp.mean(center * center, axis=-1, keepdims=True)
    return center * lax.rsqrt(spread + NORM_EPSILON) * gain + shift


def exact_gelu(argument):
    return jax.nn.gelu(argument, approximate=False)


def body(
    frames,
    lengths,
    key_mask,
    cotangent,
    gain_one,
    shift_one,
    query_weight,
    query_bias,
    key_weight,
    value_weight,
    value_bias,
    out_weight,
    out_bias,
    gain_two,
    shift_two,
    up_weight,
    up_bias,
    down_weight,
    down_bias,
    master,
    moment_one,
    moment_two,
    adam_step,
    hyper_rates,
):
    local_rows, clip_count, model_width = frames.shape
    total_rows = key_mask.shape[1]
    head_cols = query_weight.shape[1]
    heads_here = head_cols // HD
    block_rows = min(512, total_rows)
    blocks = total_rows // block_rows
    score_scale = 1.0 / math.sqrt(HD)
    position = jnp.arange(total_rows, dtype=jnp.int32)
    keep_query = position[None, :] < lengths[:, None]
    keep_key = jnp.logical_and(keep_query, key_mask == 1)
    gain_first = gain_one.astype(jnp.float32)
    shift_first = shift_one.astype(jnp.float32)
    gain_second = gain_two.astype(jnp.float32)
    shift_second = shift_two.astype(jnp.float32)
    inputs = frames.astype(jnp.float32)
    normed = layer_norm(inputs, gain_first, shift_first).astype(jnp.bfloat16)
    joined_weight = jnp.concatenate([query_weight, key_weight, value_weight], axis=1)
    joined_bias = jnp.concatenate(
        [
            query_bias.astype(jnp.float32),
            jnp.zeros((head_cols,), jnp.float32),
            value_bias.astype(jnp.float32),
        ]
    )
    normed_full = lax.all_gather(normed, "mp", axis=0, tiled=True)
    projected = (
        jnp.einsum("rcd,de->rce", normed_full, joined_weight, preferred_element_type=jnp.float32)
        + joined_bias
    ).astype(jnp.bfloat16)
    query = projected[:, :, :head_cols].reshape(total_rows, clip_count, heads_here, HD)
    keys = projected[:, :, head_cols : 2 * head_cols].reshape(
        total_rows, clip_count, heads_here, HD
    )
    values = projected[:, :, 2 * head_cols :].reshape(total_rows, clip_count, heads_here, HD)

    def scores_of(row_start):
        query_block = lax.dynamic_slice_in_dim(query, row_start, block_rows, 0)
        raw_scores = (
            jnp.einsum("qchd,kchd->chqk", query_block, keys, preferred_element_type=jnp.float32)
            * score_scale
        )
        return (query_block, jnp.where(keep_key[:, None, None, :], raw_scores, MASK_VALUE))

    def forward_block(block_index):
        row_start = block_index * block_rows
        _, masked = scores_of(row_start)
        row_peak = jnp.max(masked, axis=-1, keepdims=True)
        exp_scores = jnp.exp(masked - row_peak)
        row_total = jnp.sum(exp_scores, axis=-1, keepdims=True)
        probability = (exp_scores / row_total).astype(jnp.bfloat16)
        attended = jnp.einsum(
            "chqk,kchd->qchd", probability, values, preferred_element_type=jnp.float32
        ).astype(jnp.bfloat16)
        live_rows = lax.dynamic_slice_in_dim(keep_query, row_start, block_rows, 1)
        block_peak = jnp.max(
            jnp.where(live_rows[:, None, :], row_peak[..., 0], MASK_VALUE), axis=(0, 2)
        )
        return (attended, (row_peak + jnp.log(row_total))[..., 0], block_peak)

    attended_blocks, log_totals, block_peaks = lax.map(forward_block, jnp.arange(blocks))
    attended_full = attended_blocks.reshape(total_rows, clip_count, head_cols)
    head_peak = lax.pmax(jnp.max(block_peaks, axis=0), "dp")
    rows_here = attended_full
    attn_branch = lax.psum_scatter(
        jnp.einsum("rck,kd->rcd", rows_here, out_weight, preferred_element_type=jnp.float32),
        "mp",
        scatter_dimension=0,
        tiled=True,
    ) + out_bias.astype(jnp.float32)
    middle = inputs + attn_branch
    normed_two = layer_norm(middle, gain_second, shift_second).astype(jnp.bfloat16)
    upstream = cotangent.astype(jnp.float32)
    normed_two_full = lax.all_gather(normed_two, "mp", axis=0, tiled=True)
    before = jnp.einsum(
        "rcd,df->rcf", normed_two_full, up_weight, preferred_element_type=jnp.float32
    ) + up_bias.astype(jnp.float32)
    hidden = exact_gelu(before).astype(jnp.bfloat16)
    rows_here = hidden
    feed = lax.psum_scatter(
        jnp.einsum(
            "rcf,fd->rcd", rows_here, down_weight, preferred_element_type=jnp.float32
        ).astype(jnp.bfloat16),
        "mp",
        scatter_dimension=0,
        tiled=True,
    ).astype(jnp.float32) + down_bias.astype(jnp.float32)
    layer_out = (middle + feed).astype(jnp.bfloat16)
    feed_grad_full = lax.all_gather(cotangent, "mp", axis=0, tiled=True)
    down_grad = jnp.einsum(
        "rcf,rcd->fd", hidden, feed_grad_full, preferred_element_type=jnp.float32
    )
    hidden_grad = jnp.einsum(
        "rcd,fd->rcf", feed_grad_full, down_weight, preferred_element_type=jnp.float32
    )
    _, gelu_pull = jax.vjp(exact_gelu, before)
    before_grad = gelu_pull(hidden_grad)[0].astype(jnp.bfloat16)
    up_bias_grad = jnp.sum(before_grad.astype(jnp.float32), axis=(0, 1))
    up_grad = jnp.einsum(
        "rcd,rcf->df", normed_two_full, before_grad, preferred_element_type=jnp.float32
    )
    rows_here = before_grad
    normed_two_grad = lax.psum_scatter(
        jnp.einsum("rcf,df->rcd", rows_here, up_weight, preferred_element_type=jnp.float32),
        "mp",
        scatter_dimension=0,
        tiled=True,
    )
    _, norm_two_pull = jax.vjp(layer_norm, middle, gain_second, shift_second)
    middle_norm_grad, gain_two_grad, shift_two_grad = norm_two_pull(normed_two_grad)
    middle_grad = upstream + middle_norm_grad
    branch_grad = middle_grad.astype(jnp.bfloat16)
    branch_grad_full = lax.all_gather(branch_grad, "mp", axis=0, tiled=True)
    out_grad = jnp.einsum(
        "rck,rcd->kd", attended_full, branch_grad_full, preferred_element_type=jnp.float32
    )
    attended_grad = jnp.einsum(
        "rcd,kd->rck", branch_grad_full, out_weight, preferred_element_type=jnp.float32
    ).astype(jnp.bfloat16)
    attended_grad = attended_grad.reshape(total_rows, clip_count, heads_here, HD)

    def backward_block(carry, block_index):
        key_total, value_total = carry
        row_start = block_index * block_rows
        query_block, masked = scores_of(row_start)
        log_total = log_totals[block_index]
        probability = jnp.exp(masked - log_total[..., None])
        grad_block = lax.dynamic_slice_in_dim(attended_grad, row_start, block_rows, 0)
        value_total = value_total + jnp.einsum(
            "chqk,qchd->kchd",
            probability.astype(jnp.bfloat16),
            grad_block,
            preferred_element_type=jnp.float32,
        )
        prob_grad = jnp.einsum(
            "qchd,kchd->chqk", grad_block, values, preferred_element_type=jnp.float32
        )
        score_grad = (
            probability * (prob_grad - jnp.sum(probability * prob_grad, axis=-1, keepdims=True))
        ).astype(jnp.bfloat16)
        query_grad = (
            jnp.einsum("chqk,kchd->qchd", score_grad, keys, preferred_element_type=jnp.float32)
            * score_scale
        ).astype(jnp.bfloat16)
        key_total = (
            key_total
            + jnp.einsum(
                "chqk,qchd->kchd", score_grad, query_block, preferred_element_type=jnp.float32
            )
            * score_scale
        )
        return ((key_total, value_total), query_grad)

    empty_grad = jnp.zeros((total_rows, clip_count, heads_here, HD), jnp.float32)
    (key_total, value_total), query_blocks = lax.scan(
        backward_block, (empty_grad, empty_grad), jnp.arange(blocks)
    )
    joined_grad = jnp.concatenate(
        [
            query_blocks.reshape(total_rows, clip_count, head_cols),
            key_total.reshape(total_rows, clip_count, head_cols).astype(jnp.bfloat16),
            value_total.reshape(total_rows, clip_count, head_cols).astype(jnp.bfloat16),
        ],
        axis=-1,
    )
    joined_bias_grad = jnp.sum(joined_grad.astype(jnp.float32), axis=(0, 1))
    normed_back = lax.all_gather(normed, "mp", axis=0, tiled=True)
    joined_weight_grad = jnp.einsum(
        "rcd,rce->de", normed_back, joined_grad, preferred_element_type=jnp.float32
    )
    rows_here = joined_grad
    normed_grad = lax.psum_scatter(
        jnp.einsum(
            "rce,de->rcd", rows_here, joined_weight, preferred_element_type=jnp.float32
        ).astype(jnp.bfloat16),
        "mp",
        scatter_dimension=0,
        tiled=True,
    ).astype(jnp.float32)
    _, norm_one_pull = jax.vjp(layer_norm, inputs, gain_first, shift_first)
    input_norm_grad, gain_one_grad, shift_one_grad = norm_one_pull(normed_grad)
    input_grad = middle_grad + input_norm_grad
    out_bias_grad = jnp.sum(branch_grad.astype(jnp.float32), axis=(0, 1))
    down_bias_grad = jnp.sum(upstream, axis=(0, 1))
    small_terms = jnp.concatenate(
        [
            gain_one_grad,
            shift_one_grad,
            out_bias_grad,
            gain_two_grad,
            shift_two_grad,
            down_bias_grad,
        ]
    )
    small_share = lax.psum_scatter(small_terms, "mp", scatter_dimension=0, tiled=True)
    small_total = lax.psum(small_share, "dp")
    packed = jnp.concatenate(
        [
            joined_weight_grad[:, :head_cols].reshape(-1),
            joined_bias_grad[:head_cols],
            joined_weight_grad[:, head_cols : 2 * head_cols].reshape(-1),
            joined_weight_grad[:, 2 * head_cols :].reshape(-1),
            joined_bias_grad[2 * head_cols :],
            out_grad.reshape(-1),
            up_grad.reshape(-1),
            up_bias_grad,
            down_grad.reshape(-1),
            small_share,
        ]
    )
    owned_grads = lax.psum_scatter(
        packed.astype(jnp.bfloat16), "dp", scatter_dimension=0, tiled=True
    ).astype(jnp.float32)
    share_size = owned_grads.shape[0]
    learn_rate = hyper_rates[0]
    weight_decay = hyper_rates[1]
    logit_cap = hyper_rates[2]
    step_count = adam_step[0].astype(jnp.float32)
    first_new = BETA_FIRST * moment_one[0] + (1.0 - BETA_FIRST) * owned_grads
    second_new = BETA_SECOND * moment_two[0] + (1.0 - BETA_SECOND) * owned_grads * owned_grads
    first_hat = first_new / (1.0 - jnp.power(BETA_FIRST, step_count))
    second_hat = second_new / (1.0 - jnp.power(BETA_SECOND, step_count))
    entry_index = lax.axis_index("dp") * share_size + jnp.arange(share_size, dtype=jnp.int32)
    query_end = model_width * head_cols
    query_bias_end = query_end + head_cols
    key_end = query_bias_end + model_width * head_cols
    column = jnp.where(
        entry_index < query_end,
        entry_index % head_cols,
        jnp.where(
            entry_index < query_bias_end,
            entry_index - query_end,
            (entry_index - query_bias_end) % head_cols,
        ),
    )
    head_index = column // HD
    root_factor = jnp.sqrt(logit_cap / jnp.maximum(head_peak, logit_cap))
    head_factor = jnp.zeros((share_size,), jnp.float32)
    for head_number in range(heads_here):
        head_factor = head_factor + jnp.where(
            head_index == head_number, root_factor[head_number], 0.0
        )
    factor = jnp.where(entry_index < key_end, head_factor, 1.0)
    master_here = master[0]
    master_new = (
        master_here
        - learn_rate
        * (first_hat / (jnp.sqrt(second_hat) + ADAM_EPSILON) + weight_decay * master_here)
    ) * factor
    weights_full = lax.all_gather(master_new.astype(jnp.bfloat16), "dp", axis=0, tiled=True)
    return (
        layer_out,
        input_grad,
        owned_grads[None],
        master_new[None],
        first_new[None],
        second_new[None],
        weights_full[None],
        small_total,
    )


def solution(mesh):
    placed = (
        P("mp", "dp", None),
        P("dp"),
        P("dp", None),
        P("mp", "dp", None),
        P(),
        P(),
        P(None, "mp"),
        P("mp"),
        P(None, "mp"),
        P(None, "mp"),
        P("mp"),
        P("mp", None),
        P(),
        P(),
        P(),
        P(None, "mp"),
        P("mp"),
        P("mp", None),
        P(),
        P("mp", "dp"),
        P("mp", "dp"),
        P("mp", "dp"),
        P(),
        P(),
    )
    return jax.shard_map(
        body,
        mesh=mesh,
        in_specs=placed,
        out_specs=(
            P("mp", "dp", None),
            P("mp", "dp", None),
            P("mp", "dp"),
            P("mp", "dp"),
            P("mp", "dp"),
            P("mp", "dp"),
            P("mp", None),
            P("mp"),
        ),
        check_vma=False,
    )
```

profile of v0, /device:TPU:0, one launch (start us, length us, event | category | flops | bytes accessed | tf_op | source)
XLA Modules:
  0.0 1434.8 jit_solution(16479061154037491986)
XLA Ops:
  15.3 80.3 %all-gather.5.cloned.1.call-done = bf16[1024,3,1280]{2,0,1:T(8,128)(2,1)} async-done(((bf16[128,3,1280]{2,0,1:T(8,128)(2,1)}), bf16[1024,3,1280]{2,0,1:T(8,128)(2,1)}) %all-gather.5.cloned.1.call-update) | async-done | bytes 7864336 | tf_op jit(solution)/shard_map/all_gather | solution.py:78
  95.6 8.3 add_convert_fusion.1
  106.5 45.4 %while.29 = (s32[]{:T(128)}, bf16[2,512,3,2,80]{1,4,3,2,0:T(8,128)(2,1)}, f32[2,3,2,512]{3,2,1,0:T(2,128)S(1)}, f32[2,2]{1,0:T(2,128)S(1)}, pred[3,1024]{1,0:T(4...) while((s32[]{:T(128)}, ...), condition=%wide.region_6.7_spmd, body=%wide.region_2.6_spmd.sunk | while | flops 1044630528 | bytes 91154184 | solution.py:113
  107.8 7.6 fusion.138
  115.6 7.6 fusion.139
  123.9 5.4 fusion.140
  130.5 7.6 fusion.138
  138.3 7.6 fusion.139
  146.6 5.4 fusion.140
  159.1 9.0 fusion.78
  168.8 157.0 %reduce-scatter.5.cloned.1.call-done = f32[128,3,1280]{2,0,1:T(8,128)} async-done(((f32[1024,3,1280]{2,0,1:T(8,128)}), f32[128,3,1280]{2,0,1:T(8,128)}) %reduce-scatter.5.cloned.1.call-update) | async-done | bytes 1966096 | tf_op jit(solution)/shard_map/reduce_scatter | solution.py:117
  331.2 75.6 %all-gather.7.cloned.1.call-done = bf16[1024,3,1280]{2,0,1:T(8,128)(2,1)} async-done(((bf16[128,3,1280]{2,0,1:T(8,128)(2,1)}), bf16[1024,3,1280]{2,0,1:T(8,128)(2,1)}) %all-gather.7.cloned.1.call-update) | async-done | bytes 7864336 | tf_op jit(solution)/shard_map/all_gather | solution.py:126
  406.7 10.9 fusion.68
  420.6 19.2 %multiply_convert_fusion.1 = (bf16[1024,3,640]{2,0,1:T(8,128)(2,1)}, f32[1024,3,640]{2,0,1:T(8,128)}) fusion(f32[1024,3,640]{2,0,1:T(8,128)S(1)} %get-tuple-element.252, f32[640]{0:T(1024)S(1)} %convert_element_type.133, u8[1024,640]{1,0:T(8,128)(4,1)S(1)} %get-tuple-element.164, u8[1024,640]{1,0:T(8,128)(4,1)S(1)} %get-tuple-element.163), kind=kLoop, calls=%fused_computation.50 | loop fusion | flops 139591680 | bytes 20974080 | tf_op jit(solution)/shard_map/convert_element_type | solution.py:130
  439.8 44.7 %all-gather.9.cloned.1.call-done = bf16[1024,3,1280]{2,0,1:T(8,128)(2,1)} async-done(((bf16[128,3,1280]{2,0,1:T(8,128)(2,1)}), bf16[1024,3,1280]{2,0,1:T(8,128)(2,1)}) %all-gather.9.cloned.1.call-update) | async-done | bytes 7864336 | tf_op jit(solution)/shard_map/all_gather | solution.py:141
  484.5 14.2 fusion.98
  500.6 9.2 fusion.71
  511.2 11.7 convolution_convert_fusion.1
  523.6 143.8 %reduce-scatter.9.cloned.1.call-done = f32[128,3,1280]{2,0,1:T(8,128)} async-done(((f32[1024,3,1280]{2,0,1:T(8,128)}), f32[128,3,1280]{2,0,1:T(8,128)}) %reduce-scatter.9.cloned.1.call-update) | async-done | bytes 1966096 | tf_op jit(solution)/shard_map/reduce_scatter | solution.py:155
  670.9 82.3 %reduce-scatter.7.cloned.1.call-done = bf16[128,3,1280]{2,0,1:T(8,128)(2,1)} async-done(((bf16[1024,3,1280]{2,0,1:T(8,128)(2,1)}), bf16[128,3,1280]{2,0,1:T(8,128)(2,1)}) %reduce-scatter.7.cloned.1.call-update) | async-done | bytes 983056 | tf_op jit(solution)/shard_map/reduce_scatter | solution.py:132
  760.6 76.1 %all-gather.11.cloned.1.call-done = bf16[1024,3,1280]{2,0,1:T(8,128)(2,1)} async-done(((bf16[128,3,1280]{2,0,1:T(8,128)(2,1)}), bf16[1024,3,1280]{2,0,1:T(8,128)(2,1)}) %all-gather.11.cloned.1.call-update) | async-done | bytes 7864336 | tf_op jit(solution)/shard_map/all_gather | solution.py:165
  836.7 6.9 convolution_convert_fusion.2
  844.8 57.4 %while.30 = (s32[]{:T(128)}, f32[1024,3,2,80]{0,3,2,1:T(8,128)}, f32[1024,3,2,80]{0,3,2,1:T(8,128)}, bf16[2,512,3,2,80]{1,4,3,2,0:T(8,128)(2,1)}, s32[2]{0:T(128...) while((s32[]{:T(128)}, f32[1024,3,2,80]{0,3,2,1:T(8,128)}, ...), condition=%wide.region_16.17_spmd.clone, body=%wide.region_14.16_spmd.clone.sunk | while | flops 2566714368 | bytes 160430544 | solution.py:207
  854.2 5.1 multiply_reduce_fusion.7
  864.1 6.0 fusion.151
  878.0 5.4 bitcast_add_fusion.5
  883.4 5.1 multiply_reduce_fusion.7
  893.4 6.0 fusion.151
  910.3 6.7 convolution_convert_fusion
  918.8 10.4 fusion.38
  931.5 11.0 fusion.39
  952.7 7.9 fusion.44
  968.7 31.7 %reduce-scatter.11.cloned.1.call-done = bf16[128,3,1280]{2,0,1:T(8,128)(2,1)} async-done(((bf16[1024,3,1280]{2,0,1:T(8,128)(2,1)}), bf16[128,3,1280]{2,0,1:T(8,128)(2,1)}) %reduce-scatter.11.cloned.1.call-update) | async-done | bytes 983056 | tf_op jit(solution)/shard_map/reduce_scatter | solution.py:224
  1008.8 25.9 %all-reduce.1 = f32[7680]{0:T(1024)S(1)} all-reduce(f32[7680]{0:T(1024)S(1)} %constant_dynamic-update-slice_fusion), channel_id=6, replica_groups=mesh['dp'=4,'mp'=8] {'mp'}, use_global_device_ids=true, to_apply=%region_28.29.clone | all-reduce | flops 7680 | bytes 61440
  1034.8 77.1 %concatenate.20 = bf16[2459520]{0:T(1024)(128)(2,1)} concatenate(bf16[204800]{0:T(1024)(128)(2,1)} %reshape.180, bf16[160]{0:T(256)(128)(2,1)S(1)} %get-tuple-element.242, bf16[204800]{0:T(1024)(128)(2,1)S(1)} %copy-done.24, bf16[204800]{0:T(1024)(128)(2,1)S(1)} %reshape.182, bf16[160]{0:T(256)(128)(2,1)S(1)} %get-tuple-element.241, bf16[204800]{0:T(1024)(128)(2,1)S(1)} %reshape.183, ...), dimensions={0} | concatenate | bytes 9838080 | tf_op jit(solution)/shard_map/concatenate | solution.py:249
  1115.2 29.3 %multiply_reduce_fusion.1 = (f32[614880]{0:T(1024)}, f32[614880]{0:T(1024)}) fusion(f32[1,614880]{1,0:T(1,128)} %param.49, f32[1,614880]{1,0:T(1,128)} %param.48), kind=kLoop, calls=%fused_computation.110 | loop fusion | flops 1229760 | bytes 9838080 | tf_op jit(solution)/shard_map/mul | solution.py:272
  1144.5 27.9 %reduce.2 = f32[614880]{0:T(1024)} reduce(f32[1,614880]{1,0:T(1,128)} %param.47, f32[]{:T(128)} %constant.220), dimensions={0}, to_apply=%param.47.reduce_sub_computation | reduce | bytes 4919044 | tf_op args[19]
  1172.4 10.3 pmax.7
  1183.9 8.8 psum.7
  1192.6 34.0 %all-reduce.8.cloned.1.call-done = bf16[2459520]{0:T(1024)(128)(2,1)} async-done(((bf16[2459520]{0:T(1024)(128)(2,1)}), bf16[2459520]{0:T(1024)(128)(2,1)}) %all-reduce.8.cloned.1.call-update) | async-done | bytes 4919056
  1226.6 14.0 fusion.85
  1243.1 19.3 %dynamic-update-slice = bf16[2459520]{0:T(1024)(128)(2,1)} dynamic-update-slice(bf16[2459520]{0:T(1024)(128)(2,1)} %broadcast.262, bf16[614880]{0:T(1024)(128)(2,1)S(1)} %get-tuple-element.214, u32[]{:T(128)} %bitcast.26) | dynamic-update-slice | bytes 2459524
  1264.4 12.3 broadcast_in_dim.130
  1276.7 12.2 broadcast_in_dim.135
  1288.9 12.2 broadcast_in_dim.137
  1301.1 12.5 broadcast_in_dim.136
  1313.6 65.7 %all-reduce.6.cloned.1.call-done = bf16[2459520]{0:T(1024)(128)(2,1)} async-done(((bf16[2459520]{0:T(1024)(128)(2,1)}), bf16[2459520]{0:T(1024)(128)(2,1)}) %all-reduce.6.cloned.1.call-update) | async-done | bytes 4919056
  1379.3 48.2 %broadcast_in_dim.138 = bf16[1,2459520]{1,0:T(2,128)(2,1)} reshape(bf16[2459520]{0:T(1024)(128)(2,1)} %all-reduce.6.cloned.1.call-done) | data formatting | bytes 9838080 | tf_op jit(solution)/shard_map/broadcast_in_dim | solution.py:310
  (255 shorter events, 114.9 us)
Async XLA Ops:
  7.2 399.6 %copy-start = (bf16[1280,640]{1,0:T(8,128)(2,1)S(1)}, bf16[1280,640]{1,0:T(8,128)(2,1)}, u32[]{:S(2)}) copy-start(bf16[1280,640]{1,0:T(8,128)(2,1)} %param.43) | copy-start | bytes 4915204
  7.2 7.9 copy-start.58
  7.2 7.9 copy-start.59
  7.2 8.0 copy-start.39
  7.2 8.0 copy-start.50
  7.2 88.4 %copy-start.52 = (bf16[1280,160]{0,1:T(8,128)(2,1)S(1)}, bf16[1280,160]{0,1:T(8,128)(2,1)}, u32[]{:S(2)}) copy-start(bf16[1280,160]{0,1:T(8,128)(2,1)} %param.37) | copy-start | bytes 1228804
  7.2 88.4 %copy-start.54 = (bf16[1280,160]{0,1:T(8,128)(2,1)S(1)}, bf16[1280,160]{0,1:T(8,128)(2,1)}, u32[]{:S(2)}) copy-start(bf16[1280,160]{0,1:T(8,128)(2,1)} %param.36) | copy-start | bytes 1228804
  7.2 88.4 %copy-start.56 = (bf16[1280,160]{0,1:T(8,128)(2,1)S(1)}, bf16[1280,160]{0,1:T(8,128)(2,1)}, u32[]{:S(2)}) copy-start(bf16[1280,160]{0,1:T(8,128)(2,1)} %param.34) | copy-start | bytes 1228804
  7.3 88.3 %all-gather.5.cloned.1.call-start = ((), (), s32[]{:S(2)}) async-start(), calls=%async_computation.4 | async-start | bytes 8847360 | tf_op jit(solution)/shard_map/all_gather | solution.py:78
  15.0 310.7 %reduce-scatter.5.cloned.1.call-start = ((), (), s32[]{:S(2)}) async-start(), calls=%async_computation.5 | async-start | bytes 17694720 | tf_op jit(solution)/shard_map/reduce_scatter | solution.py:117
  115.6 8.3 copy-start.2
  138.3 8.3 copy-start.2
  152.0 16.1 %copy-start.48 = (f32[2,2]{1,0:T(2,128)}, f32[2,2]{1,0:T(2,128)S(1)}, u32[]{:S(2)}) copy-start(f32[2,2]{1,0:T(2,128)S(1)} %get-tuple-element.126) | copy-start | bytes 52
  152.0 7.1 copy-start.25
  168.1 238.6 %all-gather.7.cloned.1.call-start = ((), (), s32[]{:S(2)}) async-start(), calls=%async_computation.6 | async-start | bytes 8847360 | tf_op jit(solution)/shard_map/all_gather | solution.py:126
  330.5 154.0 %all-gather.9.cloned.1.call-start = ((), (), s32[]{:S(2)}) async-start(), calls=%async_computation.8 | async-start | bytes 8847360 | tf_op jit(solution)/shard_map/all_gather | solution.py:141
  331.1 336.4 %reduce-scatter.9.cloned.1.call-start = ((), (), s32[]{:S(2)}) async-start(), calls=%async_computation.9 | async-start | bytes 17694720 | tf_op jit(solution)/shard_map/reduce_scatter | solution.py:155
  509.8 243.4 %reduce-scatter.7.cloned.1.call-start = ((), (), s32[]{:S(2)}) async-start(), calls=%async_computation.7 | async-start | bytes 8847360 | tf_op jit(solution)/shard_map/reduce_scatter | solution.py:132
  523.0 313.8 %all-gather.11.cloned.1.call-start = ((), (), s32[]{:S(2)}) async-start(), calls=%async_computation.10 | async-start | bytes 8847360 | tf_op jit(solution)/shard_map/all_gather | solution.py:165
  670.9 87.7 %copy-start.16 = (bf16[128,3,1280]{2,0,1:T(8,128)(2,1)S(1)}, bf16[128,3,1280]{2,0,1:T(8,128)(2,1)}, u32[]{:S(2)}) copy-start(bf16[128,3,1280]{2,0,1:T(8,128)(2,1)} %param.31) | copy-start | bytes 2949124
  757.3 86.3 %copy-start.35 = (f32[128,3]{0,1:T(4,128)}, f32[128,3]{0,1:T(4,128)S(1)}, u32[]{:S(2)}) copy-start(f32[128,3]{0,1:T(4,128)S(1)} %negate_multiply_fusion.2) | copy-start | bytes 4612
  760.5 239.8 %reduce-scatter.11.cloned.1.call-start = ((), (), s32[]{:S(2)}) async-start(), calls=%async_computation.11 | async-start | bytes 8847360 | tf_op jit(solution)/shard_map/reduce_scatter | solution.py:224
  760.6 84.2 %copy-start.6 = (bf16[1024,3,2,80]{0,3,2,1:T(8,128)(2,1)S(1)}, bf16[1024,3,2,80]{0,3,2,1:T(8,128)(2,1)}, u32[]{:S(2)}) copy-start(bf16[1024,3,2,80]{0,3,2,1:T(8,128)(2,1)} %get-tuple-element.494) | copy-start | bytes 2949124
  864.1 6.0 copy-start.3
  864.1 6.0 copy-start.7
  893.4 6.0 copy-start.3
  893.4 6.0 copy-start.7
  905.1 47.6 %copy-start.21 = (bf16[1024,3,160]{0,2,1:T(8,128)(2,1)}, bf16[1024,3,160]{0,2,1:T(8,128)(2,1)S(1)}, u32[]{:S(2)}) copy-start(bf16[1024,3,160]{0,2,1:T(8,128)(2,1)S(1)} %reshape.179) | copy-start | bytes 2949124
  907.2 9.7 copy-start.22
  917.0 309.6 %all-reduce.8.cloned.1.call-start = ((), (), s32[]{:S(2)}) async-start(), calls=%async_computation.13 | async-start | bytes 9838592
  962.3 38.1 %copy-start.10 = (bf16[128,3,1280]{2,0,1:T(8,128)(2,1)S(1)}, bf16[128,3,1280]{2,0,1:T(8,128)(2,1)}, u32[]{:S(2)}) copy-start(bf16[128,3,1280]{2,0,1:T(8,128)(2,1)} %param.28) | copy-start | bytes 2949124
  962.3 38.0 %copy-start.27 = (f32[1280]{0:T(1024)S(1)}, f32[1280]{0:T(1024)}, u32[]{:S(2)}) copy-start(f32[1280]{0:T(1024)} %copy-done.26) | copy-start | bytes 15364
  962.3 38.0 %copy-start.29 = (f32[128,3]{0,1:T(4,128)S(1)}, f32[128,3]{0,1:T(4,128)}, u32[]{:S(2)}) copy-start(f32[128,3]{0,1:T(4,128)} %copy-done.28) | copy-start | bytes 4612
  964.4 37.9 %copy-start.38 = (f32[128,3]{0,1:T(4,128)S(1)}, f32[128,3]{0,1:T(4,128)}, u32[]{:S(2)}) copy-start(f32[128,3]{0,1:T(4,128)} %copy-done.37) | copy-start | bytes 4612
  964.4 37.9 %copy-start.31 = (f32[128,3]{0,1:T(4,128)S(1)}, f32[128,3]{0,1:T(4,128)}, u32[]{:S(2)}) copy-start(f32[128,3]{0,1:T(4,128)} %copy-done.30) | copy-start | bytes 4612
  966.2 38.4 %copy-start.34 = (f32[1280]{0:T(1024)S(1)}, f32[1280]{0:T(1024)}, u32[]{:S(2)}) copy-start(f32[1280]{0:T(1024)} %get-tuple-element.220) | copy-start | bytes 15364
  966.2 38.4 %copy-start.33 = (f32[1280]{0:T(1024)S(1)}, f32[1280]{0:T(1024)}, u32[]{:S(2)}) copy-start(f32[1280]{0:T(1024)} %get-tuple-element.165) | copy-start | bytes 15364
  966.2 38.4 %copy-start.32 = (f32[1280]{0:T(1024)S(1)}, f32[1280]{0:T(1024)}, u32[]{:S(2)}) copy-start(f32[1280]{0:T(1024)} %get-tuple-element.169) | copy-start | bytes 15364
  966.2 38.4 %copy-start.17 = (bf16[128,3,1280]{2,0,1:T(8,128)(2,1)S(1)}, bf16[128,3,1280]{2,0,1:T(8,128)(2,1)}, u32[]{:S(2)}) copy-start(bf16[128,3,1280]{2,0,1:T(8,128)(2,1)} %param.31) | copy-start | bytes 2949124
  966.2 38.4 %copy-start.36 = (f32[128,3]{0,1:T(4,128)S(1)}, f32[128,3]{0,1:T(4,128)}, u32[]{:S(2)}) copy-start(f32[128,3]{0,1:T(4,128)} %copy-done.35) | copy-start | bytes 4612
  1004.7 30.1 %copy-start.24 = (bf16[204800]{0:T(1024)(128)(2,1)S(1)}, bf16[204800]{0:T(1024)(128)(2,1)}, u32[]{:S(2)}) copy-start(bf16[204800]{0:T(1024)(128)(2,1)} %reshape.181) | copy-start | bytes 1228804
  1004.7 30.1 %copy-start.45 = (bf16[640]{0:T(1024)(128)(2,1)S(1)}, bf16[640]{0:T(1024)(128)(2,1)}, u32[]{:S(2)}) copy-start(bf16[640]{0:T(1024)(128)(2,1)} %get-tuple-element.253) | copy-start | bytes 3844
  1112.0 267.3 %all-reduce.6.cloned.1.call-start = ((), (), s32[]{:S(2)}) async-start(), calls=%async_computation.12 | async-start | bytes 9838592
  1115.2 29.3 %copy-start.49 = (f32[2,2]{1,0:T(2,128)S(1)}, f32[2,2]{1,0:T(2,128)}, u32[]{:S(2)}) copy-start(f32[2,2]{1,0:T(2,128)} %copy-done.48) | copy-start | bytes 52
  1264.4 12.3 copy-start.15
  1276.7 12.2 copy-start.14
  1288.9 12.2 copy-start.13
  1379.3 48.2 %copy-start.1 = (bf16[1280,640]{1,0:T(8,128)(2,1)S(1)}, bf16[1280,640]{1,0:T(8,128)(2,1)}, u32[]{:S(2)}) copy-start(bf16[1280,640]{1,0:T(8,128)(2,1)} %param.43) | copy-start | bytes 4915204
  (31 other events, 73.0 us)
Sparse Core Ops, SparseCore 0:
  15.2 80.4 all-gather.4
  168.2 157.4 reduce-scatter.4
  330.6 76.0 all-gather.6
  408.2 76.2 all-gather.8
  510.0 157.4 reduce-scatter.8
  670.2 82.9 reduce-scatter.6
  760.6 76.0 all-gather.10
  917.1 83.2 reduce-scatter.10
  1112.1 114.4 all-reduce.7
  1262.6 116.6 all-reduce.5
where the time goes:
time: 1450 us; the launch traced here: 1430 us
  waiting for transfers between devices  792 us (55%)
  local copies, waits for them, and re-layouts  244 us (17%)
  matrix products  175 us (12%)
  other arithmetic  153 us (11%)
  blocking collectives  44.9 us (3%)
  between operations  18 us (1%)
    reduce_scatter x1, waiting for transfers between devices, body(): lax.psum_scatter(jnp.einsum('rck,kd->rcd', rows_here, out_weight, preferr...  157 us
    reduce_scatter x1, waiting for transfers between devices, body(): lax.psum_scatter(jnp.einsum('rcf,df->rcd', rows_here, up_weight, preferre...  144 us
    unnamed x12, waiting for transfers between devices  100 us
    reduce_scatter x1, waiting for transfers between devices, body(): lax.psum_scatter(jnp.einsum('rcf,fd->rcd', rows_here, down_weight, prefer...  82.3 us
    all_gather x1, waiting for transfers between devices, body(): normed_full = lax.all_gather(normed, 'mp', axis=0, tiled=True)  80.3 us
    concatenate x1, local copies, waits for them, and re-layouts, body(): jnp.concatenate([joined_weight_grad[:, :head_cols].reshape(-1), joined_bi...  77.1 us
    all_gather x1, waiting for transfers between devices, body(): branch_grad_full = lax.all_gather(branch_grad, 'mp', axis=0, tiled=True)  76.1 us
    all_gather x1, waiting for transfers between devices, body(): normed_two_full = lax.all_gather(normed_two, 'mp', axis=0, tiled=True)  75.6 us
  transfers between devices with their start and end apart: 10, of which 10 were waited for; matrix products, arithmetic and copies ran while one was open for 14% of the time, Pallas kernels for 0%

commit v1 on v0

--- a/solution.py
+++ b/solution.py
@@ -1,8 +1,11 @@
+import functools
 import math
 
 import jax
 import jax.numpy as jnp
 from jax import lax
+from jax.experimental import pallas as pl
+from jax.experimental.pallas import tpu as pltpu
 from jax.sharding import PartitionSpec as P
 
 HD = 80
@@ -23,6 +26,1069 @@
 
 def exact_gelu(argument):
     return jax.nn.gelu(argument, approximate=False)
+
+
+MESH = pl.DeviceIdType.MESH
+ANY = pl.BlockSpec(memory_space=pl.ANY)
+VMEM = pl.BlockSpec(memory_space=pltpu.VMEM)
+LINE = 4
+ROWS = 384
+BF = jnp.bfloat16
+F32 = jnp.float32
+
+
+class Place:
+    def __init__(self):
+        self.dp = lax.axis_index("dp")
+        self.mp = lax.axis_index("mp")
+        self.z = self.mp // 2
+        self.c = self.mp % 2
+        self.pair = self.z * 2 + 1 - self.c
+        self.dpx = self.dp + 1 - 2 * (self.dp % 2)
+        self.dpy = (self.dp + 2) % 4
+        self.dpd = 3 - self.dp
+
+    def zorder(self, event):
+        if event == 0:
+            return self.z
+        if event == 1:
+            return self.z + 1 - 2 * (self.z % 2)
+        if event == 2:
+            return 2 - self.z // 2
+        return 3 - 3 * (self.z // 2)
+
+
+def greet(place, mp_all=False, line=False, plane=False, pair=True):
+    barrier = pltpu.get_barrier_semaphore()
+    count = 0
+
+    def signal(dp, mp):
+        pl.semaphore_signal(barrier, inc=1, device_id=(dp, mp), device_id_type=MESH)
+
+    if mp_all:
+        for hop in range(1, 8):
+            signal(place.dp, (place.mp + hop) % 8)
+        count += 7
+    else:
+        if pair:
+            signal(place.dp, place.pair)
+            count += 1
+        if line:
+
+            @pl.when(place.z > 0)
+            def _():
+                signal(place.dp, place.mp - 2)
+
+            @pl.when(place.z < LINE - 1)
+            def _():
+                signal(place.dp, place.mp + 2)
+
+    if plane:
+        for other in (place.dpx, place.dpy, place.dpd):
+            signal(other, place.mp)
+        count += 3
+    if line and not mp_all:
+        pl.semaphore_wait(barrier, count + 1 + (place.z + 1) // 2 % 2)
+    else:
+        pl.semaphore_wait(barrier, count)
+
+
+def remote(src, dst, send, recv, dp, mp):
+    return pltpu.make_async_remote_copy(
+        src_ref=src,
+        dst_ref=dst,
+        send_sem=send,
+        recv_sem=recv,
+        device_id=(dp, mp),
+        device_id_type=MESH,
+    )
+
+
+def line_gather(place, src, out, local, send, recv, paired, ready=None):
+    dp, z, c, mp, pair = place.dp, place.z, place.c, place.mp, place.pair
+
+    def slot_of(level, core):
+        return level * 2 + core if paired else level
+
+    def hop(event, slot, source, direction, target):
+        return remote(source, out.at[slot], send.at[event, direction], recv.at[slot], dp, target)
+
+    own = slot_of(z, c)
+    keep = pltpu.make_async_copy(src, out.at[own], local)
+    keep.start()
+
+    def ways(event, level, slot, source, act):
+        up = z < LINE - 1
+        down = z > 0
+        if event > 0:
+            up = jnp.logical_and(up, level < z)
+            down = jnp.logical_and(down, level > z)
+
+        @pl.when(up)
+        def _():
+            act(hop(event, slot, source, 1, mp + 2))
+
+        @pl.when(down)
+        def _():
+            act(hop(event, slot, source, 2, mp - 2))
+
+        if paired:
+            act(hop(event, slot, source, 0, pair))
+
+    ways(0, z, own, src, lambda copy: copy.start())
+    yield
+    if ready is not None:
+        keep.wait()
+        ready(own)
+        if paired:
+            other = slot_of(z, 1 - c)
+            hop(0, other, out.at[other], 0, pair).wait_recv()
+            ready(other)
+    for event in range(1, LINE):
+        level = place.zorder(event)
+        slot = slot_of(level, c)
+        hop(event, slot, out.at[slot], 0, pair).wait_recv()
+        ways(event, level, slot, out.at[slot], lambda copy: copy.start())
+        if ready is not None:
+            ready(slot)
+            if paired:
+                other = slot_of(level, 1 - c)
+                hop(event, other, out.at[other], 0, pair).wait_recv()
+                ready(other)
+        yield
+    if ready is None:
+        if paired:
+            for level in range(LINE):
+                other = slot_of(level, 1 - c)
+                hop(0, other, out.at[other], 0, pair).wait_recv()
+        keep.wait()
+    for event in range(LINE):
+        level = place.zorder(event)
+        slot = slot_of(level, c)
+        ways(event, level, slot, out.at[slot], lambda copy: copy.wait_send())
+    yield
+
+
+def plane_gather(place, src, out, local, send, recv):
+    dp, c, mp, pair = place.dp, place.c, place.mp, place.pair
+    dpx, dpy, dpd = place.dpx, place.dpy, place.dpd
+    half = src.shape[0] // 2
+    part_a, part_b = pl.ds(0, half), pl.ds(half, half)
+
+    def at(group, core):
+        return out.at[group * 2 + core]
+
+    keep = pltpu.make_async_copy(src, at(dp, c), local)
+    keep.start()
+    here = at(dp, c)
+    sends = [
+        remote(src, here, send.at[0], recv.at[0], dp, pair),
+        remote(src, here, send.at[1], recv.at[1], dpx, mp),
+        remote(src, here, send.at[2], recv.at[2], dpy, mp),
+    ]
+    for copy in sends:
+        copy.start()
+    yield
+    from_x, from_y = at(dpx, c), at(dpy, c)
+    remote(from_x, from_x, send.at[1], recv.at[1], dpx, mp).wait_recv()
+    sends.append(
+        remote(from_x.at[part_a], from_x.at[part_a], send.at[3], recv.at[3], dpy, mp)
+    )
+    sends[-1].start()
+    remote(from_y, from_y, send.at[2], recv.at[2], dpy, mp).wait_recv()
+    sends.append(
+        remote(from_y.at[part_b], from_y.at[part_b], send.at[4], recv.at[4], dpx, mp)
+    )
+    sends[-1].start()
+    for index, block in ((5, from_x), (6, from_y)):
+        sends.append(remote(block, block, send.at[index], recv.at[index], dp, pair))
+        sends[-1].start()
+    yield
+    from_d = at(dpd, c)
+    remote(from_d.at[part_a], from_d.at[part_a], send.at[3], recv.at[3], dpy, mp).wait_recv()
+    sends.append(
+        remote(from_d.at[part_a], from_d.at[part_a], send.at[7], recv.at[7], dp, pair)
+    )
+    sends[-1].start()
+    remote(from_d.at[part_b], from_d.at[part_b], send.at[4], recv.at[4], dpx, mp).wait_recv()
+    sends.append(
+        remote(from_d.at[part_b], from_d.at[part_b], send.at[8], recv.at[8], dp, pair)
+    )
+    sends[-1].start()
+    yield
+    for index, group in ((0, dp), (5, dpx), (6, dpy)):
+        block = at(group, 1 - c)
+        remote(block, block, send.at[index], recv.at[index], dp, pair).wait_recv()
+    other = at(dpd, 1 - c)
+    for index, rows in ((7, part_a), (8, part_b)):
+        remote(other.at[rows], other.at[rows], send.at[index], recv.at[index], dp, pair).wait_recv()
+    for copy in sends:
+        copy.wait_send()
+    keep.wait()
+    yield
+
+
+def drive(*programs):
+    live = list(programs)
+    while live:
+        for program in list(live):
+            try:
+                next(program)
+            except StopIteration:
+                live.remove(program)
+
+
+def dma(*shape):
+    return pltpu.SemaphoreType.DMA(shape)
+
+
+def params(cid, vmem=40):
+    return pltpu.CompilerParams(
+        collective_id=cid, has_side_effects=True, vmem_limit_bytes=vmem << 20
+    )
+
+
+def exchange(place, src, out, local, send, recv):
+    dp, mp = place.dp, place.mp
+    keep = pltpu.make_async_copy(src.at[mp], out.at[mp], local)
+    keep.start()
+    sends = []
+    for hop in range(1, 8):
+        target = (mp + hop) % 8
+        sends.append(
+            remote(src.at[target], out.at[mp], send.at[hop], recv.at[hop], dp, target)
+        )
+        sends[-1].start()
+    yield
+    keep.wait()
+    for hop in range(1, 8):
+        origin = (mp + 8 - hop) % 8
+        remote(out.at[origin], out.at[origin], send.at[hop], recv.at[hop], dp, origin).wait_recv()
+    for copy in sends:
+        copy.wait_send()
+    yield
+
+
+def line_reduce(place, produce, tiles, result, bufs, sems, paired):
+    dp, z, c, mp, pair = place.dp, place.z, place.c, place.mp, place.pair
+    from_above, from_below, out_block = bufs["above"], bufs["below"], bufs["out"]
+    order = [place.zorder(event) for event in (3, 2, 1, 0)]
+
+    @pl.when(z == LINE - 1)
+    def _():
+        from_above[...] = jnp.zeros(from_above.shape, BF)
+
+    @pl.when(z == 0)
+    def _():
+        from_below[...] = jnp.zeros(from_below.shape, BF)
+
+    def across(step, level):
+        return remote(
+            bufs["pair_out"].at[step],
+            bufs["pair_in"].at[level],
+            sems["pair_send"].at[step],
+            sems["pair_recv"].at[level],
+            dp,
+            pair,
+        )
+
+    if paired:
+        for step, level in enumerate(order):
+            for rows in tiles:
+                bufs["pair_out"][step, rows] = produce(level, 1 - c, rows).astype(BF)
+            across(step, level).start()
+    yield
+
+    def toward(step, level, act):
+        @pl.when(level < z)
+        def _():
+            act(
+                remote(
+                    out_block.at[step],
+                    from_above.at[level],
+                    sems["line_send"].at[step],
+                    sems["above"].at[level],
+                    dp,
+                    mp - 2,
+                )
+            )
+
+        @pl.when(level > z)
+        def _():
+            act(
+                remote(
+                    out_block.at[step],
+                    from_below.at[level],
+                    sems["line_send"].at[step],
+                    sems["below"].at[level],
+                    dp,
+                    mp + 2,
+                )
+            )
+
+    def arrive(level, above):
+        if above:
+            remote(
+                from_above.at[level],
+                from_above.at[level],
+                sems["line_send"].at[0],
+                sems["above"].at[level],
+                dp,
+                mp,
+            ).wait_recv()
+        else:
+            remote(
+                from_below.at[level],
+                from_below.at[level],
+                sems["line_send"].at[0],
+                sems["below"].at[level],
+                dp,
+                mp,
+            ).wait_recv()
+
+    for step, level in enumerate(order[:3]):
+        if paired:
+            across(step, level).wait_recv()
+
+        @pl.when(jnp.logical_and(level < z, z < LINE - 1))
+        def _():
+            arrive(level, True)
+
+        @pl.when(jnp.logical_and(level > z, z > 0))
+        def _():
+            arrive(level, False)
+
+        for rows in tiles:
+            total = produce(level, c, rows)
+            if paired:
+                total = total + bufs["pair_in"][level, rows].astype(F32)
+
+            @pl.when(level < z)
+            def _():
+                out_block[step, rows] = (total + from_above[level, rows].astype(F32)).astype(BF)
+
+            @pl.when(level > z)
+            def _():
+                out_block[step, rows] = (total + from_below[level, rows].astype(F32)).astype(BF)
+
+        toward(step, level, lambda copy: copy.start())
+        yield
+
+    if paired:
+        across(3, z).wait_recv()
+
+    @pl.when(z < LINE - 1)
+    def _():
+        arrive(z, True)
+
+    @pl.when(z > 0)
+    def _():
+        arrive(z, False)
+
+    for rows in tiles:
+        total = produce(z, c, rows)
+        if paired:
+            total = total + bufs["pair_in"][z, rows].astype(F32)
+        total = total + from_above[z, rows].astype(F32) + from_below[z, rows].astype(F32)
+        result(rows, total)
+    for step, level in enumerate(order):
+        if paired:
+            across(step, level).wait_send()
+        if step < 3:
+            toward(step, level, lambda copy: copy.wait_send())
+    yield
+
+
+def line_reduce_scratch(rows, cols, paired):
+    block = lambda n: pltpu.VMEM((n, rows, cols), BF)
+    scratch = {"above": block(4), "below": block(4), "out": block(3)}
+    sems = {"line_send": dma(3), "above": dma(4), "below": dma(4)}
+    if paired:
+        scratch.update({"pair_out": block(4), "pair_in": block(4)})
+        sems.update({"pair_send": dma(4), "pair_recv": dma(4)})
+    return scratch, sems
+
+
+def plane_reduce(place, produce, tile, half, result, bufs, sems, paired=True):
+    dp, c, mp, pair = place.dp, place.c, place.mp, place.pair
+    dpx, dpy, dpd = place.dpx, place.dpy, place.dpd
+    order = [dpd, dpx, dpy, dp]
+    tiles_a = [pl.ds(start, tile) for start in range(0, half, tile)]
+    send, recv = sems["send"], sems["recv"]
+    out_block, landed = bufs["out"], bufs["in"]
+
+    def across(step):
+        return remote(
+            bufs["pair_out"].at[step],
+            bufs["pair_in"].at[step],
+            sems["pair_send"].at[step],
+            sems["pair_recv"].at[step],
+            dp,
+            pair,
+        )
+
+    if paired:
+        for step, group in enumerate(order):
+            for start in range(0, 2 * half, tile):
+                bufs["pair_out"][step, pl.ds(start, tile)] = produce(
+                    group, 1 - c, start
+                ).astype(BF)
+            across(step).start()
+    yield
+
+    def share(step, start):
+        total = produce(order[step], c, start)
+        if paired:
+            total = total + bufs["pair_in"][step, pl.ds(start, tile)].astype(F32)
+        return total
+
+    def hop(index, target):
+        return remote(
+            out_block.at[index], landed.at[index], send.at[index], recv.at[index], target, mp
+        )
+
+    def fill(index, step, base, extra=None):
+        for rows in tiles_a:
+            total = share(step, base + rows.start)
+            if extra is not None:
+                total = total + landed[extra, rows].astype(F32)
+            out_block[index, rows] = total.astype(BF)
+
+    targets = [dpx, dpy, dpx, dpx, dpy, dpy]
+    if paired:
+        across(0).wait_recv()
+    fill(0, 0, 0)
+    hop(0, dpx).start()
+    fill(1, 0, half)
+    hop(1, dpy).start()
+    yield
+    if paired:
+        across(1).wait_recv()
+        across(2).wait_recv()
+    fill(2, 1, 0)
+    hop(2, dpx).start()
+    fill(4, 2, half)
+    hop(4, dpy).start()
+    yield
+    hop(1, dpy).wait_recv()
+    fill(3, 1, half, extra=1)
+    hop(3, dpx).start()
+    hop(0, dpx).wait_recv()
+    fill(5, 2, 0, extra=0)
+    hop(5, dpy).start()
+    yield
+    if paired:
+        across(3).wait_recv()
+    for index in (2, 3, 4, 5):
+        hop(index, targets[index]).wait_recv()
+    for base, pieces in ((0, (2, 5)), (half, (3, 4))):
+        for rows in tiles_a:
+            total = share(3, base + rows.start)
+            for piece in pieces:
+                total = total + landed[piece, rows].astype(F32)
+            result(pl.ds(base + rows.start, tile), total)
+    for index in range(6):
+        hop(index, targets[index]).wait_send()
+    if paired:
+        for step in range(4):
+            across(step).wait_send()
+    yield
+
+
+def plane_reduce_scratch(half, cols, paired=True):
+    block = lambda n, rows: pltpu.VMEM((n, rows, cols), BF)
+    scratch = {"out": block(6, half), "in": block(6, half)}
+    sems = {"send": dma(6), "recv": dma(6)}
+    if paired:
+        scratch.update({"pair_out": block(4, 2 * half), "pair_in": block(4, 2 * half)})
+        sems.update({"pair_send": dma(4), "pair_recv": dma(4)})
+    return scratch, sems
+
+
+def project_kernel(
+    normed_ref, cot_ref, weight_ref, bias_ref, nfull_ref, qkv_ref, cfull_ref,
+    local, line_send, line_recv, plane_send, plane_recv,
+):
+    place = Place()
+    greet(place, line=True, plane=True)
+
+    def ready(slot):
+        @pl.loop(0, 3)
+        def _(step):
+            rows = pl.ds(step * 128, 128)
+            product = lax.dot_general(
+                nfull_ref[slot, rows],
+                weight_ref[...],
+                (((1,), (1,)), ((), ())),
+                preferred_element_type=F32,
+            )
+            qkv_ref[slot, rows] = (product + bias_ref[...]).astype(BF)
+
+    drive(
+        line_gather(
+            place, normed_ref, nfull_ref, local.at[0], line_send, line_recv, True, ready
+        ),
+        plane_gather(place, cot_ref, cfull_ref, local.at[1], plane_send, plane_recv),
+    )
+
+
+def project(normed, cotangent, weight, bias):
+    return pl.pallas_call(
+        project_kernel,
+        out_shape=(
+            jax.ShapeDtypeStruct((8,) + normed.shape, BF),
+            jax.ShapeDtypeStruct((8, ROWS, weight.shape[0]), BF),
+            jax.ShapeDtypeStruct((8,) + cotangent.shape, BF),
+        ),
+        in_specs=[ANY, ANY, VMEM, VMEM],
+        out_specs=(VMEM, VMEM, ANY),
+        scratch_shapes=[dma(2), dma(4, 3), dma(8), dma(9), dma(9)],
+        compiler_params=params(0),
+        name="project",
+    )(normed, cotangent, weight, bias)
+
+
+def attend_kernel(
+    qkv_ref, mask_ref, live_ref, weights_ref, att_ref, logs_ref, peak_ref, wfull_ref,
+    out_ref, vt_ref, local, send, recv, line_send, line_recv,
+):
+    place = Place()
+    greet(place, mp_all=True)
+    gather = line_gather(
+        place, weights_ref, wfull_ref, local.at[1], line_send, line_recv, True
+    )
+    next(gather)
+    factor = math.log2(math.e) / math.sqrt(HD)
+    peak_ref[...] = jnp.full(peak_ref.shape, MASK_VALUE, F32)
+
+    @pl.loop(0, 6)
+    def _(turn):
+        clip = turn // 2
+        head = turn % 2
+        lane = pl.multiple_of(head * 128, 128)
+        row = pl.multiple_of(head * HD, 16)
+        keys = qkv_ref[:, clip, :, pl.ds(256 + lane, 128)].reshape(1024, 128)
+        vt_ref[...] = qkv_ref[:, clip, :, pl.ds(512 + lane, 128)].reshape(1024, 128).T
+
+        @pl.loop(0, 4)
+        def _(block):
+            query = qkv_ref[pl.ds(block * 2, 2), clip, :, pl.ds(lane, 128)].reshape(256, 128)
+            columns = pl.ds(pl.multiple_of(block * 256, 256), 256)
+            scores = lax.dot_general(
+                keys, query, (((1,), (1,)), ((), ())), preferred_element_type=F32
+            )
+            scores = scores + mask_ref[clip]
+            peak = jnp.max(scores, axis=0, keepdims=True)
+            powers = jnp.exp2((scores - peak) * factor)
+            total = jnp.sum(powers, axis=0, keepdims=True)
+            mixed = lax.dot_general(
+                vt_ref[...],
+                powers.astype(BF),
+                (((1,), (0,)), ((), ())),
+                preferred_element_type=F32,
+            )
+            mixed = (mixed / total).astype(BF)
+            for part in range(2):
+                out_ref[block * 2 + part, clip, pl.ds(row, HD)] = mixed[
+                    :HD, part * 128 : part * 128 + 128
+                ]
+            logs_ref[turn, :, columns] = peak * factor + jnp.log2(total)
+            peak_ref[head] = jnp.maximum(
+                peak_ref[head], jnp.where(live_ref[clip, :, columns] > 0, peak, MASK_VALUE)
+            )
+
+    drive(exchange(place, out_ref, att_ref, local.at[0], send, recv), gather)
+
+
+def attend(qkv, mask, live, weights):
+    return pl.pallas_call(
+        attend_kernel,
+        out_shape=(
+            jax.ShapeDtypeStruct((8, 3, 160, 128), BF),
+            jax.ShapeDtypeStruct((6, 1, 1024), F32),
+            jax.ShapeDtypeStruct((2, 1, 256), F32),
+            jax.ShapeDtypeStruct((8,) + weights.shape, BF),
+        ),
+        in_specs=[VMEM, VMEM, VMEM, ANY],
+        out_specs=(VMEM, VMEM, VMEM, ANY),
+        scratch_shapes=[
+            pltpu.VMEM((8, 3, 160, 128), BF),
+            pltpu.VMEM((128, 1024), BF),
+            dma(2),
+            dma(8),
+            dma(8),
+            dma(4, 3),
+            dma(8),
+        ],
+        compiler_params=params(1),
+        name="attend",
+    )(qkv, mask, live, weights)
+
+
+def attend_back_kernel(
+    qkv_ref, mask_ref, logs_ref, grads_ref, dqkv_ref,
+    grad_ref, kt_ref, dk_ref, dv_ref, block_ref, local, send, recv,
+):
+    place = Place()
+    greet(place, mp_all=True)
+    drive(exchange(place, grads_ref, grad_ref, local, send, recv))
+    scale = 1.0 / math.sqrt(HD)
+    factor = math.log2(math.e) * scale
+    block_ref[...] = jnp.zeros(block_ref.shape, BF)
+
+    @pl.loop(0, 6)
+    def _(turn):
+        clip = turn // 2
+        head = turn % 2
+        lane = pl.multiple_of(head * 128, 128)
+        row = pl.multiple_of(head * HD, 16)
+        keys = qkv_ref[:, clip, :, pl.ds(256 + lane, 128)].reshape(1024, 128)
+        kt_ref[...] = keys.T
+        dk_ref[...] = jnp.zeros(dk_ref.shape, F32)
+        dv_ref[...] = jnp.zeros(dv_ref.shape, F32)
+
+        @pl.loop(0, 4)
+        def _(block):
+            query = qkv_ref[pl.ds(block * 2, 2), clip, :, pl.ds(lane, 128)].reshape(256, 128)
+            values = qkv_ref[:, clip, :, pl.ds(512 + lane, 128)].reshape(1024, 128)
+            keys = qkv_ref[:, clip, :, pl.ds(256 + lane, 128)].reshape(1024, 128)
+            columns = pl.ds(pl.multiple_of(block * 256, 256), 256)
+            for part in range(2):
+                block_ref[:HD, part * 128 : part * 128 + 128] = grad_ref[
+                    block * 2 + part, clip, pl.ds(row, HD)
+                ]
+            scores = lax.dot_general(
+                keys, query, (((1,), (1,)), ((), ())), preferred_element_type=F32
+            )
+            chance = jnp.exp2((scores + mask_ref[clip]) * factor - logs_ref[turn, :, columns])
+            dv_ref[...] += lax.dot_general(
+                chance.astype(BF),
+                block_ref[...],
+                (((1,), (1,)), ((), ())),
+                preferred_element_type=F32,
+            )
+            slope = lax.dot_general(
+                values, block_ref[...], (((1,), (0,)), ((), ())), preferred_element_type=F32
+            )
+            center = jnp.sum(chance * slope, axis=0, keepdims=True)
+            change = (chance * (slope - center)).astype(BF)
+            dk_ref[...] += lax.dot_general(
+                change, query, (((1,), (0,)), ((), ())), preferred_element_type=F32
+            )
+            dq = lax.dot_general(
+                kt_ref[...], change, (((1,), (0,)), ((), ())), preferred_element_type=F32
+            )
+            dqkv_ref[pl.ds(block * 2, 2), clip, :, pl.ds(lane, 128)] = (
+                (dq.T * scale).astype(BF).reshape(2, 128, 128)
+            )
+
+        dqkv_ref[:, clip, :, pl.ds(256 + lane, 128)] = (
+            (dk_ref[...] * scale).astype(BF).reshape(8, 128, 128)
+        )
+        dqkv_ref[:, clip, :, pl.ds(512 + lane, 128)] = (
+            dv_ref[...].astype(BF).reshape(8, 128, 128)
+        )
+
+
+def attend_back(qkv, mask, logs, grads):
+    return pl.pallas_call(
+        attend_back_kernel,
+        out_shape=jax.ShapeDtypeStruct(qkv.shape, BF),
+        in_specs=[VMEM, VMEM, VMEM, ANY],
+        out_specs=VMEM,
+        scratch_shapes=[
+            pltpu.VMEM((8, 3, 160, 128), BF),
+            pltpu.VMEM((128, 1024), BF),
+            pltpu.VMEM((1024, 128), F32),
+            pltpu.VMEM((1024, 128), F32),
+            pltpu.VMEM((128, 256), BF),
+            pltpu.SemaphoreType.DMA(()),
+            dma(8),
+            dma(8),
+        ],
+        compiler_params=params(2),
+        name="attend_back",
+    )(qkv, mask, logs, grads)
+
+
+def plane_share_kernel(block_ref, full_ref, local, send, recv):
+    place = Place()
+    greet(place, plane=True)
+    drive(plane_gather(place, block_ref, full_ref, local, send, recv))
+
+
+def plane_share(block):
+    return pl.pallas_call(
+        plane_share_kernel,
+        out_shape=jax.ShapeDtypeStruct((8,) + block.shape, BF),
+        in_specs=[ANY],
+        out_specs=ANY,
+        scratch_shapes=[pltpu.SemaphoreType.DMA(()), dma(9), dma(9)],
+        compiler_params=params(3),
+        name="plane_share",
+    )(block)
+
+
+def flatten(*pairs):
+    names, shapes = [], []
+    for number, group in enumerate(pairs):
+        for name, shape in group.items():
+            names.append((number, name))
+            shapes.append(shape)
+
+    def split(refs):
+        groups = [{} for _ in pairs]
+        for (number, name), ref in zip(names, refs):
+            groups[number][name] = ref
+        return groups
+
+    return shapes, split
+
+
+def plane_sums_kernel(split, first_ref, second_ref, first_out, second_out, *scratch):
+    place = Place()
+    bufs_one, sems_one, bufs_two, sems_two = split(scratch)
+    greet(place, plane=True)
+
+    def reader(ref):
+        return lambda group, core, start: ref[group * 2 + core, pl.ds(start, 96)].astype(F32)
+
+    def writer(ref):
+        def write(rows, total):
+            ref[rows] = total
+
+        return write
+
+    drive(
+        plane_reduce(place, reader(first_ref), 96, 192, writer(first_out), bufs_one, sems_one),
+        plane_reduce(place, reader(second_ref), 96, 192, writer(second_out), bufs_two, sems_two),
+    )
+
+
+def plane_sums(first, second):
+    shapes, split = flatten(*plane_reduce_scratch(192, 1280), *plane_reduce_scratch(192, 1280))
+    out = jax.ShapeDtypeStruct(first.shape[1:], F32)
+    return pl.pallas_call(
+        functools.partial(plane_sums_kernel, split),
+        out_shape=(out, out),
+        in_specs=[VMEM, VMEM],
+        out_specs=(VMEM, VMEM),
+        scratch_shapes=shapes,
+        compiler_params=params(4, 60),
+        name="plane_sums",
+    )(first, second)
+
+
+def line_product_kernel(split, grad_ref, weight_ref, out_ref, *scratch):
+    place = Place()
+    bufs, sems = split(scratch)
+    greet(place, line=True)
+
+    def produce(level, core, rows):
+        return jnp.dot(
+            grad_ref[level * 2 + core, rows], weight_ref[...], preferred_element_type=F32
+        )
+
+    def result(rows, total):
+        out_ref[rows] = total
+
+    tiles = [pl.ds(start, 128) for start in range(0, ROWS, 128)]
+    drive(line_reduce(place, produce, tiles, result, bufs, sems, True))
+
+
+def line_product(grads, weight):
+    shapes, split = flatten(*line_reduce_scratch(ROWS, 1280, True))
+    return pl.pallas_call(
+        functools.partial(line_product_kernel, split),
+        out_shape=jax.ShapeDtypeStruct((ROWS, 1280), F32),
+        in_specs=[VMEM, VMEM],
+        out_specs=VMEM,
+        scratch_shapes=shapes,
+        compiler_params=params(5, 60),
+        name="line_product",
+    )(grads, weight)
+
+
+def line_sums_kernel(split, feed_ref, out_grad_ref, feed_out, out_out, *scratch):
+    place = Place()
+    bufs_one, sems_one, bufs_two, sems_two = split(scratch)
+    greet(place, line=True)
+
+    def write_feed(rows, total):
+        feed_out[rows] = total
+
+    def write_out(rows, total):
+        out_out[rows] = total
+
+    tiles = lambda rows, tile: [pl.ds(start, tile) for start in range(0, rows, tile)]
+    drive(
+        line_reduce(
+            place,
+            lambda level, core, rows: feed_ref[level, rows].astype(F32),
+            tiles(feed_ref.shape[1], 112),
+            write_feed,
+            bufs_one,
+            sems_one,
+            False,
+        ),
+        line_reduce(
+            place,
+            lambda level, core, rows: out_grad_ref[level * 2 + core, rows].astype(F32),
+            tiles(160, 80),
+            write_out,
+            bufs_two,
+            sems_two,
+            True,
+        ),
+    )
+
+
+def line_sums(feed, out_grad):
+    rows = feed.shape[1]
+    shapes, split = flatten(
+        *line_reduce_scratch(rows, 1280, False), *line_reduce_scratch(160, 1280, True)
+    )
+    return pl.pallas_call(
+        functools.partial(line_sums_kernel, split),
+        out_shape=(
+            jax.ShapeDtypeStruct((rows, 1280), F32),
+            jax.ShapeDtypeStruct((160, 1280), F32),
+        ),
+        in_specs=[VMEM, VMEM],
+        out_specs=(VMEM, VMEM),
+        scratch_shapes=shapes,
+        compiler_params=params(6, 60),
+        name="line_sums",
+    )(feed, out_grad)
+
+
+def fast_body(
+    frames,
+    lengths,
+    key_mask,
+    cotangent,
+    gain_one,
+    shift_one,
+    query_weight,
+    query_bias,
+    key_weight,
+    value_weight,
+    value_bias,
+    out_weight,
+    out_bias,
+    gain_two,
+    shift_two,
+    up_weight,
+    up_bias,
+    down_weight,
+    down_bias,
+    master,
+    moment_one,
+    moment_two,
+    adam_step,
+    hyper_rates,
+):
+    group = lax.axis_index("dp")
+    position = jnp.arange(1024, dtype=jnp.int32)
+    keep_query = position[None, :] < lengths[:, None]
+    keep_key = jnp.logical_and(keep_query, key_mask == 1)
+    mask = jnp.where(keep_key, 0.0, MASK_VALUE)[:, :, None]
+    live = keep_query.astype(F32)[:, None, :]
+    gain_first = gain_one.astype(F32)
+    shift_first = shift_one.astype(F32)
+    gain_second = gain_two.astype(F32)
+    shift_second = shift_two.astype(F32)
+    inputs = frames.transpose(1, 0, 2).reshape(ROWS, 1280).astype(F32)
+    upstream_low = cotangent.transpose(1, 0, 2).reshape(ROWS, 1280)
+    upstream = upstream_low.astype(F32)
+    normed = layer_norm(inputs, gain_first, shift_first).astype(BF)
+
+    def head_rows(weight):
+        rows = weight.T.reshape(2, HD, 1280)
+        return jnp.pad(rows, ((0, 0), (0, 128 - HD), (0, 0))).reshape(256, 1280)
+
+    def head_lanes(bias):
+        lanes = bias.astype(F32).reshape(2, HD)
+        return jnp.pad(lanes, ((0, 0), (0, 128 - HD))).reshape(256)
+
+    joined_weight = jnp.concatenate(
+        [head_rows(query_weight), head_rows(key_weight), head_rows(value_weight)]
+    )
+    joined_bias = jnp.concatenate(
+        [head_lanes(query_bias), jnp.zeros((256,), F32), head_lanes(value_bias)]
+    )[None]
+    normed_full, qkv, upstream_full = project(normed, upstream_low, joined_weight, joined_bias)
+    qkv = qkv.reshape(8, 3, 128, 768)
+
+    quarter = group * 160
+    up_share = lax.dynamic_slice_in_dim(up_weight, quarter, 160, 1).T
+    down_share = lax.dynamic_slice_in_dim(down_weight, quarter, 160, 0)
+    bias_share = lax.dynamic_slice_in_dim(up_bias, quarter, 160, 0)
+    bias_rows = jnp.pad(bias_share[None], ((0, 15), (0, 1280 - 160)))
+    message = jnp.concatenate([up_share, down_share, bias_rows, out_weight])
+    attended, logs, peaks, gathered = attend(qkv, mask, live, message)
+    core = lax.axis_index("mp") % 2
+    own_core = lax.dynamic_slice_in_dim(gathered.reshape(4, 2, 496, 1280), core, 1, 1)[:, 0]
+    up_rows = own_core[:, :160].reshape(640, 1280)
+    down_rows = own_core[:, 160:320].reshape(640, 1280)
+    up_lanes = own_core[:, 320, :160].reshape(640).astype(F32)
+    out_rows = gathered[:, 336:]
+    head_peak = lax.pmax(jnp.max(peaks, axis=(1, 2)) / math.sqrt(HD), "dp")
+
+    branch = jnp.einsum("schr,shd->crd", attended, out_rows, preferred_element_type=F32)
+    middle = inputs + branch.reshape(ROWS, 1280) + out_bias.astype(F32)
+    normed_two = layer_norm(middle, gain_second, shift_second).astype(BF)
+    normed_two_full = plane_share(normed_two)
+    before = (
+        jnp.einsum("prd,ud->pru", normed_two_full, up_rows, preferred_element_type=F32)
+        + up_lanes
+    )
+    hidden = exact_gelu(before).astype(BF)
+    hidden_grad = jnp.einsum("prd,ud->pru", upstream_full, down_rows, preferred_element_type=F32)
+    _, gelu_pull = jax.vjp(exact_gelu, before)
+    before_grad = gelu_pull(hidden_grad)[0].astype(BF)
+    feed_part = jnp.einsum("pru,ud->prd", hidden, down_rows, preferred_element_type=F32).astype(BF)
+    normed_part = jnp.einsum(
+        "pru,ud->prd", before_grad, up_rows, preferred_element_type=F32
+    ).astype(BF)
+    normed_two_grad, feed = plane_sums(normed_part, feed_part)
+    layer_out = (middle + feed + down_bias.astype(F32)).astype(BF)
+    up_grad = jnp.einsum("pru,prd->ud", before_grad, normed_two_full, preferred_element_type=F32)
+    down_grad = jnp.einsum("pru,prd->ud", hidden, upstream_full, preferred_element_type=F32)
+    up_bias_grad = jnp.sum(before_grad.astype(F32), axis=(0, 1))
+
+    _, norm_two_pull = jax.vjp(layer_norm, middle, gain_second, shift_second)
+    middle_norm_grad, gain_two_grad, shift_two_grad = norm_two_pull(normed_two_grad)
+    middle_grad = upstream + middle_norm_grad
+    branch_grad = middle_grad.astype(BF)
+    branch_clips = branch_grad.reshape(3, 128, 1280)
+    out_grad = jnp.einsum("schr,crd->shd", attended, branch_clips, preferred_element_type=F32)
+    attended_grad = jnp.einsum(
+        "shd,crd->schr", out_rows, branch_clips, preferred_element_type=F32
+    ).astype(BF)
+    joined_grad = attend_back(qkv, mask, logs, attended_grad).reshape(8, ROWS, 768)
+    normed_grad = line_product(joined_grad, joined_weight)
+    joined_weight_grad = jnp.einsum(
+        "prd,pre->de", normed_full, joined_grad, preferred_element_type=F32
+    )
+    joined_bias_grad = jnp.sum(joined_grad.astype(F32), axis=(0, 1))
+
+    _, norm_one_pull = jax.vjp(layer_norm, inputs, gain_first, shift_first)
+    input_norm_grad, gain_one_grad, shift_one_grad = norm_one_pull(normed_grad)
+    input_grad = middle_grad + input_norm_grad
+
+    feed_grads = jnp.concatenate(
+        [
+            up_grad.astype(BF).reshape(4, 160, 1280),
+            down_grad.astype(BF).reshape(4, 160, 1280),
+            jnp.pad(up_bias_grad.astype(BF).reshape(4, 1, 160), ((0, 0), (0, 15), (0, 1120))),
+        ],
+        axis=1,
+    )
+    feed_sum, out_sum = line_sums(feed_grads, out_grad.astype(BF))
+
+    def spread(rows):
+        return lax.dynamic_update_slice(
+            jnp.zeros((640,) + rows.shape[1:], F32), rows, (quarter,) + (0,) * (rows.ndim - 1)
+        )
+
+    up_whole = spread(feed_sum[:160]).T
+    down_whole = spread(feed_sum[160:320])
+    up_bias_whole = spread(feed_sum[320, :160])
+
+    out_bias_grad = jnp.sum(branch_grad.astype(F32), axis=0)
+    down_bias_grad = jnp.sum(upstream, axis=0)
+    small_terms = jnp.concatenate(
+        [
+            gain_one_grad,
+            shift_one_grad,
+            out_bias_grad,
+            gain_two_grad,
+            shift_two_grad,
+            down_bias_grad,
+        ]
+    )
+    small_share = lax.psum_scatter(small_terms, "mp", scatter_dimension=0, tiled=True)
+    small_total = lax.psum(small_share, "dp")
+
+    def head_columns(first):
+        return jnp.concatenate(
+            [
+                joined_weight_grad[:, first : first + HD],
+                joined_weight_grad[:, first + 128 : first + 128 + HD],
+            ],
+            axis=1,
+        ).reshape(-1)
+
+    def head_entries(first):
+        return jnp.concatenate(
+            [joined_bias_grad[first : first + HD], joined_bias_grad[first + 128 : first + 128 + HD]]
+        )
+
+    packed = jnp.concatenate(
+        [
+            head_columns(0),
+            head_entries(0),
+            head_columns(256),
+            head_columns(512),
+            head_entries(512),
+            out_sum.reshape(-1),
+            up_whole.reshape(-1),
+            up_bias_whole,
+            down_whole.reshape(-1),
+            small_share,
+        ]
+    )
+    owned_grads = lax.psum_scatter(
+        packed.astype(jnp.bfloat16), "dp", scatter_dimension=0, tiled=True
+    ).astype(jnp.float32)
+    share_size = owned_grads.shape[0]
+    learn_rate = hyper_rates[0]
+    weight_decay = hyper_rates[1]
+    logit_cap = hyper_rates[2]
+    step_count = adam_step[0].astype(jnp.float32)
+    first_new = BETA_FIRST * moment_one[0] + (1.0 - BETA_FIRST) * owned_grads
+    second_new = BETA_SECOND * moment_two[0] + (1.0 - BETA_SECOND) * owned_grads * owned_grads
+    first_hat = first_new / (1.0 - jnp.power(BETA_FIRST, step_count))
+    second_hat = second_new / (1.0 - jnp.power(BETA_SECOND, step_count))
+    entry_index = lax.axis_index("dp") * share_size + jnp.arange(share_size, dtype=jnp.int32)
+    query_end = 1280 * 160
+    query_bias_end = query_end + 160
+    key_end = query_bias_end + 1280 * 160
+    column = jnp.where(
+        entry_index < query_end,
+        entry_index % 160,
+        jnp.where(
+            entry_index < query_bias_end,
+            entry_index - query_end,
+            (entry_index - query_bias_end) % 160,
+        ),
+    )
+    head_index = column // HD
+    root_factor = jnp.sqrt(logit_cap / jnp.maximum(head_peak, logit_cap))
+    head_factor = jnp.zeros((share_size,), jnp.float32)
+    for head_number in range(2):
+        head_factor = head_factor + jnp.where(
+            head_index == head_number, root_factor[head_number], 0.0
+        )
+    factor = jnp.where(entry_index < key_end, head_factor, 1.0)
+    master_here = master[0]
+    master_new = (
+        master_here
+        - learn_rate
+        * (first_hat / (jnp.sqrt(second_hat) + ADAM_EPSILON) + weight_decay * master_here)
+    ) * factor
+    weights_full = lax.all_gather(master_new.astype(jnp.bfloat16), "dp", axis=0, tiled=True)
+    return (
+        layer_out.reshape(3, 128, 1280).transpose(1, 0, 2),
+        input_grad.reshape(3, 128, 1280).transpose(1, 0, 2),
+        owned_grads[None],
+        master_new[None],
+        first_new[None],
+        second_new[None],
+        weights_full[None],
+        small_total,
+    )
 
 
 def body(
@@ -313,6 +1379,7 @@
 
 
 def solution(mesh):
+    chosen = fast_body if dict(mesh.shape) == {"dp": 4, "mp": 8} else body
     placed = (
         P("mp", "dp", None),
         P("dp"),
@@ -340,7 +1407,7 @@
         P(),
     )
     return jax.shard_map(
-        body,
+        chosen,
         mesh=mesh,
         in_specs=placed,
         out_specs=(

time: 1450 us -> 1170 us (0.81)
  waiting for transfers between devices: 792 us -> 96.3 us
  Pallas kernels: 0 us -> 543 us
  matrix products: 175 us -> 78.4 us
  other arithmetic: 153 us -> 121 us
    pallas_call x0 -> x7, Pallas kernels: none -> 543 us  [the longest x1 113 us: attend(): pl.pallas_call(attend_kernel, out_shape=(jax.ShapeDtypeStruct((8, 3, 160,...]
    reduce_scatter x4 -> x0, waiting for transfers between devices: 415 us -> none  [the longest x1 157 us: body(): lax.psum_scatter(jnp.einsum('rck,kd->rcd', rows_here, out_weight, preferr...]
    all_gather x4 -> x0, waiting for transfers between devices: 277 us -> none  [the longest x1 80.3 us: body(): normed_full = lax.all_gather(normed, 'mp', axis=0, tiled=True)]
    dot_general x26 -> x10, matrix products: 175 us -> 78.4 us  [the longest x1 13.7 us: fast_body(): jnp.einsum('prd,ud->pru', upstream_full, down_rows, preferred_element_typ...]
    reduce_sum x5 -> x3, other arithmetic: 23.4 us -> 3.6 us  [the longest x1 3.08 us: fast_body(): joined_bias_grad = jnp.sum(joined_grad.astype(F32), axis=(0, 1))]
    convert_element_type x18 -> x13, other arithmetic: 54.2 us -> 37.2 us  [the longest x1 18.7 us: fast_body(): hidden = exact_gelu(before).astype(BF)]
    unnamed x119 -> x114, local copies, waits for them, and re-layouts: 35.1 us -> 30.3 us
    unnamed x12 -> x4, waiting for transfers between devices: 100 us -> 96.3 us
  transfers between devices with their start and end apart: 10 -> 2, of which waited for: 10 -> 2; matrix products, arithmetic and copies ran while one was open for 14% -> 10% of each run, Pallas kernels for 0% -> 0%
where the time goes in v1:
time: 1170 us; the launch traced here: 1150 us
  Pallas kernels  543 us (46%)
  local copies, waits for them, and re-layouts  248 us (21%)
  other arithmetic  121 us (10%)
  waiting for transfers between devices  96.3 us (8%)
  matrix products  78.4 us (7%)
  blocking collectives  47.3 us (4%)
  between operations  17.7 us (2%)
    pallas_call x1, Pallas kernels, attend(): pl.pallas_call(attend_kernel, out_shape=(jax.ShapeDtypeStruct((8, 3, 160,...  113 us
    unnamed x4, waiting for transfers between devices  96.3 us
    pallas_call x1, Pallas kernels, line_sums(): pl.pallas_call(functools.partial(line_sums_kernel, split), out_shape=(jax...  92 us
    pallas_call x1, Pallas kernels, line_product(): pl.pallas_call(functools.partial(line_product_kernel, split), out_shape=j...  88.9 us
    pallas_call x1, Pallas kernels, project(): pl.pallas_call(project_kernel, out_shape=(jax.ShapeDtypeStruct((8,) + nor...  83.7 us
    concatenate x1, local copies, waits for them, and re-layouts, fast_body(): jnp.concatenate([head_columns(0), head_entries(0), head_columns(256), hea...  78.3 us
    pallas_call x1, Pallas kernels, plane_sums(): pl.pallas_call(functools.partial(plane_sums_kernel, split), out_shape=(ou...  77.2 us
    broadcast_in_dim x1, local copies, waits for them, and re-layouts, fast_body(): weights_full[None]  48.2 us
  transfers between devices with their start and end apart: 2, of which 2 were waited for; matrix products, arithmetic and copies ran while one was open for 10% of the time, Pallas kernels for 0%

profile of v1, /device:TPU:0, one launch (start us, length us, event | category | flops | bytes accessed | tf_op | source)
XLA Modules:
  0.0 1150.7 jit_solution(10135748830946526609)
XLA Ops:
  22.7 83.7 %project.1 = (bf16[8,384,1280]{2,1,0:T(8,128)(2,1)}, bf16[8,384,768]{2,1,0:T(8,128)(2,1)S(1)}, bf16[8,384,1280]{2,1,0:T(8,128)(2,1)}) custom-call(bf16[384,1280]{1,0:T(8,128)(2,1)S(1)} %fusion.42.normed_ref, bf16[384,1280]{1,0:T(8,128)(2,1)S(1)} %bitcast.191, bf16[768,1280]{1,0:T(8,128)(2,1)S(1)} %pad_maximum_fusion.weight_ref, ...), custom_call_target="tpu_custom_call" | custom-call | tf_op jit(solution)/shard_map/project/pallas_call | solution.py:536
  106.5 113.1 %attend.1 = (bf16[8,3,160,128]{3,2,1,0:T(8,128)(2,1)S(1)}, f32[6,1,1024]{2,1,0:T(1,128)S(1)}, f32[2,1,256]{2,1,0:T(1,128)S(1)}, bf16[8,496,1280]{2,1,0:T(8,128)(2,1)}) custom-call(bf16[8,3,128,768]{3,2,1,0:T(8,128)(2,1)S(1)} %bitcast.189, f32[3,1024,1]{2,1,0:T(8,128)S(1)} %copy-done.8, f32[3,1,1024]{2,1,0:T(1,128)S(1)} %compare_convert_fusion.live_ref, ...), custom_call_target="tpu_custom_call" | custom-call | tf_op jit(solution)/shard_map/attend/pallas_call | solution.py:604
  219.6 3.1 dynamic-slice_bitcast_fusion
  224.9 3.9 fusion.58
  229.9 39.6 %plane_share.1 = bf16[8,384,1280]{2,1,0:T(8,128)(2,1)S(1)} custom-call(bf16[384,1280]{1,0:T(8,128)(2,1)S(1)} %get-tuple-element.51.block_ref), custom_call_target="tpu_custom_call" | custom-call | tf_op jit(solution)/shard_map/plane_share/pallas_call | solution.py:721
  269.6 8.4 fusion.48
  278.0 18.7 %multiply_convert_fusion = (bf16[8,384,640]{2,1,0:T(8,128)(2,1)S(1)}, f32[8,384,640]{2,1,0:T(8,128)}) fusion(f32[8,384,640]{2,1,0:T(8,128)S(1)} %get-tuple-element.79, f32[640]{0:T(1024)S(1)} %reshape.317, u8[384,640]{1,0:T(8,128)(4,1)S(1)} %get-tuple-element.31, u8[384,640]{1,0:T(8,128)(4,1)S(1)} %get-tuple-element.30), kind=kLoop, calls=%fused_computation.7 | loop fusion | flops 139591680 | bytes 20154880 | tf_op jit(solution)/shard_map/convert_element_type | solution.py:946
  296.7 8.6 convolution_convert_fusion.second_ref
  305.3 9.8 fusion.13
  315.1 13.7 %fusion.78 = (bf16[640]{0:T(1024)(128)(2,1)}, bf16[8,384,640]{2,1,0:T(8,128)(2,1)S(1)}) fusion(f32[8,384,640]{2,1,0:T(8,128)} %get-tuple-element.50, bf16[8,384,1280]{2,1,0:T(8,128)(2,1)} %get-tuple-element.22, bf16[640,1280,1]{1,0,2:T(8,128)(2,1)S(1)} %bitcast.203, f32[8,384,640]{2,1,0:T(8,128)} %copy-done.23, f32[640]{0:T(1024)S(1)} %reshape.317), kind=kOutput, calls=%fused_computation.159 | convolution fusion | flops 5064621568 | bytes 29167360 | tf_op jit(solution)/shard_map/prd,ud->pru/dot_general | solution.py:947
  328.8 8.8 convolution_convert_fusion.1.first_ref
  337.6 6.8 fusion.12
  344.4 77.2 %plane_sums.1 = (f32[384,1280]{1,0:T(8,128)}, f32[384,1280]{1,0:T(8,128)}) custom-call(bf16[8,384,1280]{2,1,0:T(8,128)(2,1)} %convolution_convert_fusion.1.first_ref, bf16[8,384,1280]{2,1,0:T(8,128)(2,1)} %convolution_convert_fusion.second_ref), custom_call_target="tpu_custom_call" | custom-call | tf_op jit(solution)/shard_map/plane_sums/pallas_call | solution.py:771
  421.7 2.4 multiply_reduce_fusion.2
  426.5 5.1 fusion.52.grads_ref
  431.6 3.4 bitcast_convert_fusion.out_grad_ref
  435.2 2.3 copy-done.5
  438.7 48.2 %attend_back.1 = bf16[8,3,128,768]{3,2,1,0:T(8,128)(2,1)S(1)} custom-call(bf16[8,3,128,768]{3,2,1,0:T(8,128)(2,1)S(1)} %bitcast.190, f32[3,1024,1]{2,1,0:T(8,128)S(1)} %copy-done.9, f32[6,1,1024]{2,1,0:T(1,128)S(1)} %get-tuple-element.25.logs_ref, bf16[8,3,160,128]{3,2,1,0:T(8,128)(2,1)S(1)} %copy-done.10), custom_call_target="tpu_custom_call" | custom-call | tf_op jit(solution)/shard_map/attend_back/pallas_call | solution.py:694
  486.9 2.2 copy-done.2
  489.0 3.1 reduce.7
  492.1 88.9 %line_product.1 = f32[384,1280]{1,0:T(8,128)} custom-call(bf16[8,384,768]{2,1,0:T(8,128)(2,1)} %bitcast.187, bf16[768,1280]{1,0:T(8,128)(2,1)} %copy-done.6), custom_call_target="tpu_custom_call" | custom-call | tf_op jit(solution)/shard_map/line_product/pallas_call | solution.py:801
  581.0 2.2 fusion.64
  583.3 3.0 fusion.43
  586.3 9.8 bitcast_convert_fusion.1
  603.0 2.0 reshape.305
  605.1 3.3 fusion.7.feed_ref
  608.4 92.0 %line_sums.1 = (f32[336,1280]{1,0:T(8,128)}, f32[160,1280]{1,0:T(8,128)}) custom-call(bf16[4,336,1280]{2,1,0:T(8,128)(2,1)} %fusion.7.feed_ref, bf16[8,160,1280]{2,1,0:T(8,128)(2,1)} %bitcast_convert_fusion.out_grad_ref), custom_call_target="tpu_custom_call" | custom-call | tf_op jit(solution)/shard_map/line_sums/pallas_call | solution.py:851
  706.0 3.5 copy.75
  709.5 3.9 reshape.310
  714.7 2.0 slice_dynamic-update-slice_fusion
  716.7 4.4 reshape.311
  721.1 28.3 %all-reduce.8 = f32[7680]{0:T(1024)S(1)} all-reduce(f32[7680]{0:T(1024)S(1)} %constant_dynamic-update-slice_fusion), channel_id=2, replica_groups=mesh['dp'=4,'mp'=8] {'mp'}, use_global_device_ids=true, to_apply=%region_16.17.clone | all-reduce | flops 7680 | bytes 61440
  751.0 78.3 %concatenate.39 = bf16[2459520]{0:T(1024)(128)(2,1)} concatenate(bf16[204800]{0:T(1024)(128)(2,1)S(1)} %copy-done.30, bf16[80]{0:T(256)(128)(2,1)S(1)} %copy-done.46, bf16[80]{0:T(256)(128)(2,1)S(1)} %copy-done.45, bf16[204800]{0:T(1024)(128)(2,1)S(1)} %copy-done.31, bf16[204800]{0:T(1024)(128)(2,1)} %reshape.305, bf16[80]{0:T(256)(128)(2,1)S(1)} %copy-done.44, ...), dimensions={0} | concatenate | bytes 9838080 | tf_op jit(solution)/shard_map/concatenate | solution.py:1028
  829.5 9.1 pmax.7
  840.6 27.9 %reduce.9 = f32[614880]{0:T(1024)} reduce(f32[1,614880]{1,0:T(1,128)} %param.43, f32[]{:T(128)} %constant.210), dimensions={0}, to_apply=%param.43.reduce_sub_computation | reduce | bytes 4919044 | tf_op args[19]
  869.1 9.9 psum.7
  880.9 29.2 %multiply_reduce_fusion = (f32[614880]{0:T(1024)}, f32[614880]{0:T(1024)}) fusion(f32[1,614880]{1,0:T(1,128)} %param.45, f32[1,614880]{1,0:T(1,128)} %param.44), kind=kLoop, calls=%fused_computation.69 | loop fusion | flops 1229760 | bytes 9838080 | tf_op jit(solution)/shard_map/mul | solution.py:1051
  910.2 2.1 add_add_fusion.2
  912.3 30.5 %all-reduce.15.cloned.1.call-done = bf16[2459520]{0:T(1024)(128)(2,1)} async-done(((bf16[2459520]{0:T(1024)(128)(2,1)}), bf16[2459520]{0:T(1024)(128)(2,1)}) %all-reduce.15.cloned.1.call-update) | async-done | bytes 4919056
  942.8 14.0 %fusion.65 = (bf16[614880]{0:T(1024)(128)(2,1)S(1)}, f32[614880]{0:T(1024)}, f32[614880]{0:T(1024)}, f32[614880]{0:T(1024)}) fusion(f32[]{:T(128)} %bitcast.60, f32[]{:T(128)} %bitcast.59, s32[]{:T(128)S(6)} %mul.254, f32[614880]{0:T(1024)} %reduce.9, f32[]{:T(128)} %bitcast.57, f32[]{:T(128)} %bitcast.56, f32[]{:T(128)} %bitcast.55, f32[]{:T(128)} %bitcast.54, ...), kind=kLoop, calls=%fused_computation.150 | loop fusion | flops 30744000 | bytes 17216672 | tf_op jit(solution)/shard_map/convert_element_type | solution.py:1081
  956.8 2.5 broadcast.298
  959.3 19.3 %dynamic-update-slice = bf16[2459520]{0:T(1024)(128)(2,1)} dynamic-update-slice(bf16[2459520]{0:T(1024)(128)(2,1)} %broadcast.298, bf16[614880]{0:T(1024)(128)(2,1)S(1)} %get-tuple-element.39, u32[]{:T(128)} %bitcast.61) | dynamic-update-slice | bytes 2459524
  980.6 12.3 %broadcast_in_dim.97 = f32[1,614880]{1,0:T(1,128)} reshape(f32[614880]{0:T(1024)S(1)} %dynamic-slice_convert_fusion) | data formatting | bytes 4919040 | tf_op jit(solution)/shard_map/broadcast_in_dim | solution.py:1085
  992.8 12.4 %broadcast_in_dim.102 = f32[1,614880]{1,0:T(1,128)} reshape(f32[614880]{0:T(1024)S(1)} %copy-done.21) | data formatting | bytes 4919040 | tf_op jit(solution)/shard_map/broadcast_in_dim | solution.py:1086
  1005.2 12.2 %broadcast_in_dim.103 = f32[1,614880]{1,0:T(1,128)} reshape(f32[614880]{0:T(1024)S(1)} %copy-done.20) | data formatting | bytes 4919040 | tf_op jit(solution)/shard_map/broadcast_in_dim | solution.py:1087
  1017.5 12.2 %broadcast_in_dim.104 = f32[1,614880]{1,0:T(1,128)} reshape(f32[614880]{0:T(1024)S(1)} %copy-done.19) | data formatting | bytes 4919040 | tf_op jit(solution)/shard_map/broadcast_in_dim | solution.py:1088
  1029.7 65.7 %all-reduce.13.cloned.1.call-done = bf16[2459520]{0:T(1024)(128)(2,1)} async-done(((bf16[2459520]{0:T(1024)(128)(2,1)}), bf16[2459520]{0:T(1024)(128)(2,1)}) %all-reduce.13.cloned.1.call-update) | async-done | bytes 4919056
  1095.4 48.2 %broadcast_in_dim.105 = bf16[1,2459520]{1,0:T(2,128)(2,1)} reshape(bf16[2459520]{0:T(1024)(128)(2,1)} %all-reduce.13.cloned.1.call-done) | data formatting | bytes 9838080 | tf_op jit(solution)/shard_map/broadcast_in_dim | solution.py:1089
  (185 shorter events, 41.7 us)
Async XLA Ops:
  7.2 10.3 copy-start
  7.2 5.8 copy-start.33
  7.2 6.6 copy-start.34
  7.2 935.6 %all-reduce.15.cloned.1.call-start = ((), (), s32[]{:S(2)}) async-start(), calls=%async_computation.1 | async-start | bytes 9838592
  8.8 5.9 copy-start.49
  8.8 6.0 copy-start.50
  8.8 6.1 copy-start.42
  8.8 6.2 copy-start.35
  18.3 2.5 copy-start.24
  19.8 2.3 copy-start.13
  22.1 84.2 %copy-start.6 = (bf16[768,1280]{1,0:T(8,128)(2,1)}, bf16[768,1280]{1,0:T(8,128)(2,1)S(1)}, u32[]{:S(2)}) copy-start(bf16[768,1280]{1,0:T(8,128)(2,1)S(1)} %pad_maximum_fusion.weight_ref) | copy-start | bytes 5898244
  22.6 83.8 %copy-start.26 = (bf16[160,1280]{1,0:T(8,128)(2,1)S(1)}, bf16[160,1280]{1,0:T(8,128)(2,1)}, u32[]{:S(2)}) copy-start(bf16[160,1280]{1,0:T(8,128)(2,1)} %constant_dynamic-slice_fusion) | copy-start | bytes 1228804
  22.6 83.8 %copy-start.27 = (bf16[1280,160]{0,1:T(8,128)(2,1)S(1)}, bf16[1280,160]{0,1:T(8,128)(2,1)}, u32[]{:S(2)}) copy-start(bf16[1280,160]{0,1:T(8,128)(2,1)} %copy.82) | copy-start | bytes 1228804
  22.6 83.8 %copy-start.32 = (bf16[160,1280]{1,0:T(8,128)(2,1)S(1)}, bf16[160,1280]{1,0:T(8,128)(2,1)}, u32[]{:S(2)}) copy-start(bf16[160,1280]{1,0:T(8,128)(2,1)} %param.35) | copy-start | bytes 1228804
  22.7 83.8 %copy-start.8 = (f32[3,1024,1]{2,1,0:T(8,128)S(1)}, f32[3,1024,1]{2,1,0:T(8,128)}, u32[]{:S(2)}) copy-start(f32[3,1024,1]{2,1,0:T(8,128)} %copy.65.mask_ref) | copy-start | bytes 36868
  106.4 113.3 %copy-start.4 = (bf16[8,384,768]{2,1,0:T(8,128)(2,1)}, bf16[8,384,768]{2,1,0:T(8,128)(2,1)S(1)}, u32[]{:S(2)}) copy-start(bf16[8,384,768]{2,1,0:T(8,128)(2,1)S(1)} %get-tuple-element.19) | copy-start | bytes 14155780
  219.6 5.3 copy-start.11
  224.9 4.0 copy-start.14
  229.9 39.7 %copy-start.28 = (bf16[4,160,1280]{2,1,0:T(8,128)(2,1)S(1)}, bf16[4,160,1280]{2,1,0:T(8,128)(2,1)}, u32[]{:S(2)}) copy-start(bf16[4,160,1280]{2,1,0:T(8,128)(2,1)} %get-tuple-element.54) | copy-start | bytes 4915204
  278.0 18.7 %copy-start.23 = (f32[8,384,640]{2,1,0:T(8,128)}, f32[8,384,640]{2,1,0:T(8,128)S(1)}, u32[]{:S(2)}) copy-start(f32[8,384,640]{2,1,0:T(8,128)S(1)} %get-tuple-element.79) | copy-start | bytes 23592964
  278.0 18.7 %copy-start.29 = (bf16[4,160,1280]{2,1,0:T(8,128)(2,1)S(1)}, bf16[4,160,1280]{2,1,0:T(8,128)(2,1)}, u32[]{:S(2)}) copy-start(bf16[4,160,1280]{2,1,0:T(8,128)(2,1)} %get-tuple-element.53) | copy-start | bytes 4915204
  421.7 2.4 copy-start.41
  421.7 2.4 copy-start.22
  421.7 2.7 copy-start.25
  426.1 5.5 copy-start.17
  426.5 5.1 copy-start.12
  431.6 3.6 copy-start.9
  435.1 2.3 copy-start.5
  492.1 88.9 %copy-start.15 = (bf16[128,3,1280]{2,0,1:T(8,128)(2,1)S(1)}, bf16[128,3,1280]{2,0,1:T(8,128)(2,1)}, u32[]{:S(2)}) copy-start(bf16[128,3,1280]{2,0,1:T(8,128)(2,1)} %param.24) | copy-start | bytes 2949124
  581.0 5.2 copy-start.3
  600.7 4.4 copy-start.47
  714.6 35.0 %copy-start.51 = (u32[32]{0:T(128)S(1)}, u32[32]{0:T(128)}, u32[]{:S(2)}) copy-start(u32[32]{0:T(128)} %constant.204) | copy-start | bytes 388
  714.6 36.3 %copy-start.30 = (bf16[204800]{0:T(1024)(128)(2,1)S(1)}, bf16[204800]{0:T(1024)(128)(2,1)}, u32[]{:S(2)}) copy-start(bf16[204800]{0:T(1024)(128)(2,1)} %reshape.303) | copy-start | bytes 1228804
  714.6 36.3 %copy-start.31 = (bf16[204800]{0:T(1024)(128)(2,1)S(1)}, bf16[204800]{0:T(1024)(128)(2,1)}, u32[]{:S(2)}) copy-start(bf16[204800]{0:T(1024)(128)(2,1)} %reshape.304) | copy-start | bytes 1228804
  714.6 36.3 %copy-start.43 = (bf16[80]{0:T(256)(128)(2,1)S(1)}, bf16[80]{0:T(256)(128)(2,1)}, u32[]{:S(2)}) copy-start(bf16[80]{0:T(256)(128)(2,1)} %get-tuple-element.62) | copy-start | bytes 484
  714.7 36.3 %copy-start.44 = (bf16[80]{0:T(256)(128)(2,1)S(1)}, bf16[80]{0:T(256)(128)(2,1)}, u32[]{:S(2)}) copy-start(bf16[80]{0:T(256)(128)(2,1)} %get-tuple-element.63) | copy-start | bytes 484
  714.7 36.3 %copy-start.45 = (bf16[80]{0:T(256)(128)(2,1)S(1)}, bf16[80]{0:T(256)(128)(2,1)}, u32[]{:S(2)}) copy-start(bf16[80]{0:T(256)(128)(2,1)} %get-tuple-element.64) | copy-start | bytes 484
  714.7 36.3 %copy-start.46 = (bf16[80]{0:T(256)(128)(2,1)S(1)}, bf16[80]{0:T(256)(128)(2,1)}, u32[]{:S(2)}) copy-start(bf16[80]{0:T(256)(128)(2,1)} %get-tuple-element.65) | copy-start | bytes 484
  829.3 10.0 copy-start.48
  829.3 266.1 %all-reduce.13.cloned.1.call-start = ((), (), s32[]{:S(2)}) async-start(), calls=%async_computation | async-start | bytes 9838592
  840.6 38.5 %copy-start.37 = (f32[3]{0:T(128)S(1)}, f32[3]{0:T(128)}, u32[]{:S(2)}) copy-start(f32[3]{0:T(128)} %param.47) | copy-start | bytes 40
  840.6 40.3 %copy-start.36 = (f32[384]{0:T(512)S(1)}, f32[384]{0:T(512)}, u32[]{:S(2)}) copy-start(f32[384]{0:T(512)} %get-tuple-element.35) | copy-start | bytes 4612
  880.9 29.3 %copy-start.16 = (f32[384,1280]{1,0:T(8,128)S(1)}, f32[384,1280]{1,0:T(8,128)}, u32[]{:S(2)}) copy-start(f32[384,1280]{1,0:T(8,128)} %line_product.1) | copy-start | bytes 5898244
  880.9 29.3 %copy-start.18 = (f32[384,1280]{1,0:T(8,128)S(1)}, f32[384,1280]{1,0:T(8,128)}, u32[]{:S(2)}) copy-start(f32[384,1280]{1,0:T(8,128)} %copy-done.17) | copy-start | bytes 5898244
  980.6 12.3 %copy-start.21 = (f32[614880]{0:T(1024)S(1)}, f32[614880]{0:T(1024)}, u32[]{:S(2)}) copy-start(f32[614880]{0:T(1024)} %get-tuple-element.40) | copy-start | bytes 7378564
  992.8 12.4 %copy-start.20 = (f32[614880]{0:T(1024)S(1)}, f32[614880]{0:T(1024)}, u32[]{:S(2)}) copy-start(f32[614880]{0:T(1024)} %get-tuple-element.42) | copy-start | bytes 7378564
  1005.2 12.2 %copy-start.19 = (f32[614880]{0:T(1024)S(1)}, f32[614880]{0:T(1024)}, u32[]{:S(2)}) copy-start(f32[614880]{0:T(1024)} %get-tuple-element.41) | copy-start | bytes 7378564
  1095.4 48.2 %copy-start.1 = (bf16[640,1280]{1,0:T(8,128)(2,1)S(1)}, bf16[640,1280]{1,0:T(8,128)(2,1)}, u32[]{:S(2)}) copy-start(bf16[640,1280]{1,0:T(8,128)(2,1)} %param.41) | copy-start | bytes 4915204
  (6 other events, 11.3 us)
Sparse Core Ops, SparseCore 0:
  829.5 113.2 all-reduce.14
  978.8 116.6 all-reduce.12

commit v2 on v1

--- a/solution.py
+++ b/solution.py
@@ -606,7 +606,7 @@
         out_shape=(
             jax.ShapeDtypeStruct((8, 3, 160, 128), BF),
             jax.ShapeDtypeStruct((6, 1, 1024), F32),
-            jax.ShapeDtypeStruct((2, 1, 256), F32),
+            jax.ShapeDtypeStruct((2, 8, 256), F32),
             jax.ShapeDtypeStruct((8,) + weights.shape, BF),
         ),
         in_specs=[VMEM, VMEM, VMEM, ANY],
@@ -860,6 +860,282 @@
         compiler_params=params(6, 60),
         name="line_sums",
     )(feed, out_grad)
+
+
+GROUP_ROWS = 4832
+GROUP_STEP = 4800
+PACK_ROWS = GROUP_STEP * 3 + GROUP_ROWS
+SEGMENTS = (
+    ("query", 0, 1600),
+    ("query_bias", 204800, 2),
+    ("key", 204960, 1600),
+    ("value", 409760, 1600),
+    ("value_bias", 614560, 2),
+    ("out", 614720, 1600),
+    ("up", 819520, 6400),
+    ("up_bias", 1638720, 5),
+    ("down", 1639360, 6400),
+    ("small", 2458560, 8),
+)
+PACK_END = 19216
+
+
+def segment_table():
+    table, cursor = {}, 0
+    for name, start, rows in SEGMENTS:
+        row = start // 128
+        cursor += 32
+        cursor += (row - cursor) % 8
+        table[name] = (cursor, row, rows, start % 128)
+        cursor += rows
+    return table, (cursor + 32 + 7) // 8 * 8
+
+
+TABLE, STAGE_ROWS = segment_table()
+
+
+def lane_of(rows):
+    return lax.broadcasted_iota(jnp.int32, (rows, 128), 1)
+
+
+def pack_rows(stage, packed):
+    def piece(name, first, rows):
+        base, row, _, shift = TABLE[name]
+        at = base - row + first
+        here = stage[pl.ds(at, rows)]
+        if shift == 0:
+            return here
+        above = stage[pl.ds(at - 1, rows)]
+        return jnp.where(
+            lane_of(rows) >= shift, pltpu.roll(here, shift, 1), pltpu.roll(above, shift, 1)
+        )
+
+    done = set()
+    for name, _, _ in SEGMENTS:
+        _, row, rows, shift = TABLE[name]
+        low = -(-(row + (1 if shift else 0)) // 16) * 16
+        high = (row + rows) // 16 * 16
+        if high <= low:
+            continue
+        done.update(range(low, high, 16))
+        turns = (high - low) // 128
+
+        @pl.loop(0, turns)
+        def _(turn):
+            first = pl.multiple_of(low + turn * 128, 16)
+            packed[pl.ds(first, 128)] = piece(name, first, 128).astype(BF)
+
+        for first in range(low + turns * 128, high, 16):
+            packed[pl.ds(first, 16)] = piece(name, first, 16).astype(BF)
+    for first in range(0, PACK_ROWS, 16):
+        if first in done:
+            continue
+        total = jnp.zeros((16, 128), F32)
+        for name, _, _ in SEGMENTS:
+            _, row, rows, shift = TABLE[name]
+            if row < first + 16 and row + rows + (1 if shift else 0) > first:
+                total = total + piece(name, first, 16)
+        packed[pl.ds(first, 16)] = total.astype(BF)
+
+
+def stage_wide(stage, name, ref, step):
+    base = TABLE[name][0]
+    rows, wide = ref.shape[0], ref.shape[1] // 128
+
+    @pl.loop(0, rows // step)
+    def _(turn):
+        first = pl.multiple_of(turn * step, step)
+        for block in range(wide):
+            stage[pl.ds(base + first * wide + block, step, stride=wide), :] = ref[
+                pl.ds(first, step), pl.ds(block * 128, 128)
+            ].astype(F32)
+
+
+def stage_heads(stage, name, ref, lanes, column):
+    base = TABLE[name][0]
+    for head in range(2):
+        column[head] = ref[:, pl.ds(lanes + head * 128, 128)]
+
+    @pl.loop(0, 5)
+    def _(turn):
+        lane = lane_of(64)
+        rows = [jnp.zeros((64, 128), F32) for _ in range(5)]
+        for block in range(8):
+            item, head = block // 2, block % 2
+            value = column[head, pl.ds(turn * 256 + item, 64, stride=4)]
+            offset = block * HD
+            first, shift = offset // 128, offset % 128
+            if shift:
+                value = pltpu.roll(value, shift, 1)
+            if shift + HD > 128:
+                rows[first] = rows[first] + jnp.where(lane >= shift, value, 0.0)
+                rows[first + 1] = rows[first + 1] + jnp.where(
+                    lane < shift + HD - 128, value, 0.0
+                )
+            else:
+                rows[first] = rows[first] + value
+        for index in range(5):
+            stage[pl.ds(base + turn * 320 + index, 64, stride=5), :] = rows[index]
+
+
+def stage_head_bias(stage, name, ref, lanes):
+    base = TABLE[name][0]
+    lane = lane_of(1)
+    first = ref[0:1, pl.ds(lanes, 128)]
+    second = pltpu.roll(ref[0:1, pl.ds(lanes + 128, 128)], HD, 1)
+    stage[pl.ds(base, 1)] = first + jnp.where(lane >= HD, second, 0.0)
+    stage[pl.ds(base + 1, 1)] = jnp.where(lane < 2 * HD - 128, second, 0.0)
+
+
+def pack_reduce_kernel(
+    split, joined_ref, bias_ref, out_ref, up_ref, up_bias_ref, down_ref, small_ref, peak_ref,
+    grads_ref, small_out, peak_out,
+    stage, packed, column, small_in, small_all, peak_all,
+    local, small_send, small_recv, plane_send, plane_recv, *scratch,
+):
+    place = Place()
+    bufs, sems = split(scratch)
+    greet(place, mp_all=True, plane=True)
+    peers = (place.dpx, place.dpy, place.dpd)
+    mixing = exchange(place, small_ref, small_in, local, small_send, small_recv)
+    next(mixing)
+
+    def tell(index, source, target, group, act):
+        act(
+            remote(
+                source,
+                target.at[place.dp],
+                plane_send.at[index],
+                plane_recv.at[index],
+                group,
+                place.mp,
+            )
+        )
+
+    def heard(index, target, group):
+        block = target.at[group]
+        remote(
+            block, block, plane_send.at[index], plane_recv.at[index], group, place.mp
+        ).wait_recv()
+
+    for index, group in enumerate(peers):
+        tell(index, peak_ref, peak_all, group, lambda copy: copy.start())
+    stage[...] = jnp.zeros(stage.shape, F32)
+    for name, lanes in (("query", 0), ("key", 256), ("value", 512)):
+        stage_heads(stage, name, joined_ref, lanes, column)
+    stage_head_bias(stage, "query_bias", bias_ref, 0)
+    stage_head_bias(stage, "value_bias", bias_ref, 512)
+    stage_wide(stage, "out", out_ref, 160)
+    stage_wide(stage, "up", up_ref, 256)
+    stage_wide(stage, "down", down_ref, 128)
+    stage[pl.ds(TABLE["up_bias"][0], 5)] = up_bias_ref[...]
+    for _ in mixing:
+        pass
+    share = jnp.sum(small_in[...], axis=0)
+    small_all[place.dp] = share
+    stage[pl.ds(TABLE["small"][0], 8)] = share
+    for index, group in enumerate(peers):
+        tell(3 + index, small_all.at[place.dp], small_all, group, lambda copy: copy.start())
+    pack_rows(stage, packed)
+
+    def produce(group, core, start):
+        first = pl.multiple_of(group * GROUP_STEP + start, 16)
+        return packed[pl.ds(first, GROUP_ROWS // 2)].astype(F32)
+
+    def result(rows, total):
+        grads_ref[rows] = total
+
+    half = GROUP_ROWS // 2
+    drive(plane_reduce(place, produce, half, half, result, bufs, sems, False))
+    for index, group in enumerate(peers):
+        heard(index, peak_all, group)
+        heard(3 + index, small_all, group)
+    top = peak_ref[...]
+    for group in peers:
+        top = jnp.maximum(top, peak_all[group])
+    peak_out[...] = top
+    small_out[...] = jnp.sum(small_all[...], axis=0)
+    for index, group in enumerate(peers):
+        tell(index, peak_ref, peak_all, group, lambda copy: copy.wait_send())
+        tell(3 + index, small_all.at[place.dp], small_all, group, lambda copy: copy.wait_send())
+
+
+def pack_reduce(joined, bias, out, up, up_bias, down, small, peaks):
+    shapes, split = flatten(*plane_reduce_scratch(GROUP_ROWS // 2, 128, False))
+    return pl.pallas_call(
+        functools.partial(pack_reduce_kernel, split),
+        out_shape=(
+            jax.ShapeDtypeStruct((GROUP_ROWS, 128), F32),
+            jax.ShapeDtypeStruct((8, 128), F32),
+            jax.ShapeDtypeStruct(peaks.shape, F32),
+        ),
+        in_specs=[VMEM] * 8,
+        out_specs=(VMEM,) * 3,
+        scratch_shapes=[
+            pltpu.VMEM((STAGE_ROWS, 128), F32),
+            pltpu.VMEM((PACK_ROWS, 128), BF),
+            pltpu.VMEM((2, 1280, 128), F32),
+            pltpu.VMEM((8, 8, 128), F32),
+            pltpu.VMEM((4, 8, 128), F32),
+            pltpu.VMEM((4,) + peaks.shape, F32),
+            pltpu.SemaphoreType.DMA(()),
+            dma(8),
+            dma(8),
+            dma(6),
+            dma(6),
+            *shapes,
+        ],
+        compiler_params=params(7, 60),
+        name="pack_reduce",
+    )(joined, bias, out, up, up_bias, down, small, peaks)
+
+
+def share_master_kernel(rows_ref, whole_ref, parts, send, recv):
+    place = Place()
+    greet(place, plane=True, pair=False)
+    dp, mp, dpx, dpy, dpd = place.dp, place.mp, place.dpx, place.dpy, place.dpd
+    half = GROUP_ROWS // 2
+    part_a, part_b = pl.ds(0, half), pl.ds(half, half)
+    parts[dp] = rows_ref[...].astype(BF)
+
+    def hop(index, block, target):
+        return remote(block, block, send.at[index], recv.at[index], target, mp)
+
+    own = parts.at[dp]
+    sends = [hop(0, own, dpx), hop(1, own, dpy)]
+    for copy in sends:
+        copy.start()
+    hop(0, parts.at[dpx], dpx).wait_recv()
+    sends.append(hop(2, parts.at[dpx, part_a], dpy))
+    sends[-1].start()
+    hop(1, parts.at[dpy], dpy).wait_recv()
+    sends.append(hop(3, parts.at[dpy, part_b], dpx))
+    sends[-1].start()
+    hop(2, parts.at[dpd, part_a], dpy).wait_recv()
+    hop(3, parts.at[dpd, part_b], dpx).wait_recv()
+    for group in range(4):
+        base = group * GROUP_STEP
+        first = parts[group, pl.ds(0, 32)].astype(F32)
+        if group > 0:
+            first = first + parts[group - 1, pl.ds(GROUP_STEP, 32)].astype(F32)
+        whole_ref[pl.ds(base, 32)] = first
+        for start in range(32, GROUP_STEP, 1192):
+            whole_ref[pl.ds(base + start, 1192)] = parts[group, pl.ds(start, 1192)].astype(F32)
+    whole_ref[pl.ds(4 * GROUP_STEP, 16)] = parts[3, pl.ds(GROUP_STEP, 16)].astype(F32)
+    for copy in sends:
+        copy.wait_send()
+
+
+def share_master(rows):
+    return pl.pallas_call(
+        share_master_kernel,
+        out_shape=jax.ShapeDtypeStruct((PACK_END, 128), F32),
+        in_specs=[VMEM],
+        out_specs=VMEM,
+        scratch_shapes=[pltpu.VMEM((4, GROUP_ROWS, 128), BF), dma(4), dma(4)],
+        compiler_params=params(8, 60),
+        name="share_master",
+    )(rows)
 
 
 def fast_body(
@@ -933,7 +1209,6 @@
     down_rows = own_core[:, 160:320].reshape(640, 1280)
     up_lanes = own_core[:, 320, :160].reshape(640).astype(F32)
     out_rows = gathered[:, 336:]
-    head_peak = lax.pmax(jnp.max(peaks, axis=(1, 2)) / math.sqrt(HD), "dp")
 
     branch = jnp.einsum("schr,shd->crd", attended, out_rows, preferred_element_type=F32)
     middle = inputs + branch.reshape(ROWS, 1280) + out_bias.astype(F32)
@@ -1008,85 +1283,62 @@
             down_bias_grad,
         ]
     )
-    small_share = lax.psum_scatter(small_terms, "mp", scatter_dimension=0, tiled=True)
-    small_total = lax.psum(small_share, "dp")
-
-    def head_columns(first):
-        return jnp.concatenate(
-            [
-                joined_weight_grad[:, first : first + HD],
-                joined_weight_grad[:, first + 128 : first + 128 + HD],
-            ],
-            axis=1,
-        ).reshape(-1)
-
-    def head_entries(first):
-        return jnp.concatenate(
-            [joined_bias_grad[first : first + HD], joined_bias_grad[first + 128 : first + 128 + HD]]
-        )
-
-    packed = jnp.concatenate(
-        [
-            head_columns(0),
-            head_entries(0),
-            head_columns(256),
-            head_columns(512),
-            head_entries(512),
-            out_sum.reshape(-1),
-            up_whole.reshape(-1),
-            up_bias_whole,
-            down_whole.reshape(-1),
-            small_share,
-        ]
-    )
-    owned_grads = lax.psum_scatter(
-        packed.astype(jnp.bfloat16), "dp", scatter_dimension=0, tiled=True
-    ).astype(jnp.float32)
-    share_size = owned_grads.shape[0]
+    small_tiles = jnp.pad(small_terms.reshape(8, 960), ((0, 0), (0, 64))).reshape(8, 8, 128)
+    grad_rows, small_sum, peak_sum = pack_reduce(
+        joined_weight_grad,
+        joined_bias_grad[None],
+        out_sum,
+        up_whole,
+        up_bias_whole.reshape(5, 128),
+        down_whole,
+        small_tiles,
+        peaks,
+    )
+    small_total = small_sum.reshape(1024)[:960]
+    head_peak = jnp.max(peak_sum, axis=(1, 2)) / math.sqrt(HD)
+    share_size = master.shape[1]
+    owned_grads = lax.dynamic_slice(
+        grad_rows.reshape(1, GROUP_ROWS * 128), (0, 480 * group), (1, share_size)
+    )
     learn_rate = hyper_rates[0]
     weight_decay = hyper_rates[1]
     logit_cap = hyper_rates[2]
-    step_count = adam_step[0].astype(jnp.float32)
-    first_new = BETA_FIRST * moment_one[0] + (1.0 - BETA_FIRST) * owned_grads
-    second_new = BETA_SECOND * moment_two[0] + (1.0 - BETA_SECOND) * owned_grads * owned_grads
+    step_count = adam_step[0].astype(F32)
+    first_new = BETA_FIRST * moment_one + (1.0 - BETA_FIRST) * owned_grads
+    second_new = BETA_SECOND * moment_two + (1.0 - BETA_SECOND) * owned_grads * owned_grads
     first_hat = first_new / (1.0 - jnp.power(BETA_FIRST, step_count))
     second_hat = second_new / (1.0 - jnp.power(BETA_SECOND, step_count))
-    entry_index = lax.axis_index("dp") * share_size + jnp.arange(share_size, dtype=jnp.int32)
+    entry_index = group * share_size + lax.broadcasted_iota(jnp.int32, (1, share_size), 1)
     query_end = 1280 * 160
     query_bias_end = query_end + 160
     key_end = query_bias_end + 1280 * 160
     column = jnp.where(
-        entry_index < query_end,
-        entry_index % 160,
-        jnp.where(
-            entry_index < query_bias_end,
-            entry_index - query_end,
-            (entry_index - query_bias_end) % 160,
-        ),
-    )
-    head_index = column // HD
+        entry_index < query_bias_end, entry_index, entry_index - query_bias_end
+    ) % 160
     root_factor = jnp.sqrt(logit_cap / jnp.maximum(head_peak, logit_cap))
-    head_factor = jnp.zeros((share_size,), jnp.float32)
-    for head_number in range(2):
-        head_factor = head_factor + jnp.where(
-            head_index == head_number, root_factor[head_number], 0.0
-        )
+    head_factor = jnp.where(column < HD, root_factor[0], root_factor[1])
     factor = jnp.where(entry_index < key_end, head_factor, 1.0)
-    master_here = master[0]
     master_new = (
-        master_here
-        - learn_rate
-        * (first_hat / (jnp.sqrt(second_hat) + ADAM_EPSILON) + weight_decay * master_here)
+        master
+        - learn_rate * (first_hat / (jnp.sqrt(second_hat) + ADAM_EPSILON) + weight_decay * master)
     ) * factor
-    weights_full = lax.all_gather(master_new.astype(jnp.bfloat16), "dp", axis=0, tiled=True)
+
+    def placed_rows(offset):
+        room = GROUP_ROWS * 128 - share_size - offset
+        return lambda value: jnp.pad(value, ((0, 0), (offset, room))).reshape(GROUP_ROWS, 128)
+
+    master_rows = lax.switch(group, [placed_rows(480 * part) for part in range(4)], master_new)
+    whole = share_master(master_rows).reshape(1, PACK_END * 128)
+    whole = lax.optimization_barrier(whole)
+    weights_new = whole[:, : 4 * share_size].astype(BF)
     return (
         layer_out.reshape(3, 128, 1280).transpose(1, 0, 2),
         input_grad.reshape(3, 128, 1280).transpose(1, 0, 2),
-        owned_grads[None],
-        master_new[None],
-        first_new[None],
-        second_new[None],
-        weights_full[None],
+        owned_grads,
+        master_new,
+        first_new,
+        second_new,
+        weights_new,
         small_total,
     )
 

time: 1170 us -> 892 us (0.76); the launches traced: 1150 us -> 884 us
  local copies, waits for them, and re-layouts: 248 us -> 56.7 us
  Pallas kernels: 543 us -> 660 us
  waiting for transfers between devices: 96.3 us -> 0 us
  blocking collectives: 47.3 us -> 0 us
  other arithmetic: 121 us -> 83 us
  between operations: 17.7 us -> 2.28 us
    pallas_call x0 -> x2, Pallas kernels: none -> 118 us  [the longest x1 68.3 us: pack_reduce(): pl.pallas_call(functools.partial(pack_reduce_kernel, split), out_shape=(j...]
    broadcast_in_dim x5 -> x1, local copies, waits for them, and re-layouts: 97.3 us -> 0.58 us  [fast_body(): joined_bias_grad[None]]
    unnamed x4 -> x0, waiting for transfers between devices: 96.3 us -> none
    concatenate x4 -> x0, local copies, waits for them, and re-layouts: 79 us -> none  [the longest x1 78.3 us: fast_body(): jnp.concatenate([head_columns(0), head_entries(0), head_columns(256), hea...]
    unnamed x1 -> x0, blocking collectives: 28.3 us -> none
    unnamed x2 -> x4, other arithmetic: 27.9 us -> 0.01 us
    convert_element_type x2 -> x0, other arithmetic: 15.9 us -> none  [the longest x1 14 us: fast_body(): master_new.astype(jnp.bfloat16)]
    reshape x6 -> x1, local copies, waits for them, and re-layouts: 14.4 us -> 0.08 us  [fast_body(): small_terms.reshape(8, 960)]
  transfers between devices with their start and end apart: 2 -> 0, of which waited for: 2 -> 0; matrix products, arithmetic and copies ran while one was open for 10% -> 0% of each run, Pallas kernels for 0% -> 0%
where the time goes in v2:
time: 892 us; the launch traced here: 884 us
  Pallas kernels  660 us (74%)
  other arithmetic  83 us (9%)
  matrix products  82.8 us (9%)
  local copies, waits for them, and re-layouts  56.7 us (6%)
    pallas_call x1, Pallas kernels, attend(): pl.pallas_call(attend_kernel, out_shape=(jax.ShapeDtypeStruct((8, 3, 160,...  113 us
    pallas_call x1, Pallas kernels, line_sums(): pl.pallas_call(functools.partial(line_sums_kernel, split), out_shape=(jax...  91.9 us
    pallas_call x1, Pallas kernels, line_product(): pl.pallas_call(functools.partial(line_product_kernel, split), out_shape=j...  88.6 us
    pallas_call x1, Pallas kernels, project(): pl.pallas_call(project_kernel, out_shape=(jax.ShapeDtypeStruct((8,) + nor...  83.8 us
    pallas_call x1, Pallas kernels, plane_sums(): pl.pallas_call(functools.partial(plane_sums_kernel, split), out_shape=(ou...  77.1 us
    pallas_call x1, Pallas kernels, pack_reduce(): pl.pallas_call(functools.partial(pack_reduce_kernel, split), out_shape=(j...  68.3 us
    pallas_call x1, Pallas kernels, share_master(): pl.pallas_call(share_master_kernel, out_shape=jax.ShapeDtypeStruct((PACK_...  49.2 us
    pallas_call x1, Pallas kernels, attend_back(): pl.pallas_call(attend_back_kernel, out_shape=jax.ShapeDtypeStruct(qkv.sha...  48.2 us

profile of v2, /device:TPU:0, one launch (start us, length us, event | category | flops | bytes accessed | tf_op | source)
XLA Modules:
  0.0 884.4 jit_solution(17863699809006786479)
XLA Ops:
  2.3 1.4 fusion.24
  3.7 1.6 fusion.35
  5.4 1.4 fusion.31.normed_ref
  7.0 1.4 pad_maximum_fusion.weight_ref
  8.6 1.5 copy-done.5
  11.3 83.8 %project.1 = (bf16[8,384,1280]{2,1,0:T(8,128)(2,1)}, bf16[8,384,768]{2,1,0:T(8,128)(2,1)S(1)}, bf16[8,384,1280]{2,1,0:T(8,128)(2,1)}) custom-call(bf16[384,1280]{1,0:T(8,128)(2,1)S(1)} %copy-done.9, bf16[384,1280]{1,0:T(8,128)(2,1)S(1)} %bitcast.201, bf16[768,1280]{1,0:T(8,128)(2,1)S(1)} %copy-done.5, f32[1,768]{1,0:T(1,128)S(1)} %broadcast_in_dim.71.bias_ref), custom_call_target="tpu_custom_call" | custom-call | tf_op jit(solution)/shard_map/project/pallas_call | solution.py:536
  95.2 2.1 copy-done.3
  97.3 1.7 copy.40.mask_ref
  100.6 1.6 constant_dynamic-slice_fusion.2
  104.6 2.3 copy-done.4
  106.9 113.0 %attend.1 = (bf16[8,3,160,128]{3,2,1,0:T(8,128)(2,1)S(1)}, f32[6,1,1024]{2,1,0:T(1,128)S(1)}, f32[2,8,256]{2,1,0:T(8,128)S(1)}, bf16[8,496,1280]{2,1,0:T(8,128)(2,1)}) custom-call(bf16[8,3,128,768]{3,2,1,0:T(8,128)(2,1)S(1)} %bitcast.197, f32[3,1024,1]{2,1,0:T(8,128)S(1)} %copy-done.7, f32[3,1,1024]{2,1,0:T(1,128)S(1)} %compare_convert_fusion.live_ref, ...), custom_call_target="tpu_custom_call" | custom-call | tf_op jit(solution)/shard_map/attend/pallas_call | solution.py:604
  220.8 2.8 dynamic-slice_bitcast_fusion
  223.7 2.3 copy-done.19
  226.1 4.2 fusion.47
  230.8 1.8 add_convert_fusion.2
  232.6 39.3 %plane_share.1 = bf16[8,384,1280]{2,1,0:T(8,128)(2,1)S(1)} custom-call(bf16[384,1280]{1,0:T(8,128)(2,1)S(1)} %get-tuple-element.65.block_ref), custom_call_target="tpu_custom_call" | custom-call | tf_op jit(solution)/shard_map/plane_share/pallas_call | solution.py:721
  272.0 1.6 fusion.59
  273.6 8.1 fusion.37
  281.7 18.7 %multiply_convert_fusion = (bf16[8,384,640]{2,1,0:T(8,128)(2,1)S(1)}, f32[8,384,640]{2,1,0:T(8,128)}) fusion(f32[8,384,640]{2,1,0:T(8,128)S(1)} %get-tuple-element.81, f32[640]{0:T(1024)S(1)} %reshape.375, u8[384,640]{1,0:T(8,128)(4,1)S(1)} %get-tuple-element.47, u8[384,640]{1,0:T(8,128)(4,1)S(1)} %get-tuple-element.46), kind=kLoop, calls=%fused_computation.13 | loop fusion | flops 139591680 | bytes 20154880 | tf_op jit(solution)/shard_map/convert_element_type | solution.py:1221
  300.4 14.7 %fusion.62 = (bf16[640]{0:T(1024)(128)(2,1)S(1)}, bf16[8,384,640]{2,1,0:T(8,128)(2,1)}) fusion(f32[8,384,640]{2,1,0:T(8,128)} %get-tuple-element.64, bf16[8,384,1280]{2,1,0:T(8,128)(2,1)} %get-tuple-element.35, bf16[640,1280,1]{1,0,2:T(8,128)(2,1)S(1)} %bitcast.213, f32[8,384,640]{2,1,0:T(8,128)S(1)} %get-tuple-element.81, f32[640]{0:T(1024)S(1)} %reshape.375), kind=kOutput, calls=%fused_computation.136 | convolution fusion | flops 5064621568 | bytes 29167360 | tf_op jit(solution)/shard_map/prd,ud->pru/dot_general | solution.py:1222
  315.1 10.4 %convolution_convert_fusion.1.first_ref = bf16[8,384,1280]{2,1,0:T(8,128)(2,1)} fusion(bf16[8,384,640]{2,1,0:T(8,128)(2,1)} %get-tuple-element.83, bf16[640,1280,1]{1,0,2:T(8,128)(2,1)} %bitcast.216), kind=kOutput, calls=%fused_computation.28 | convolution fusion | flops 5037096960 | bytes 13434880 | tf_op jit(solution)/shard_map/pru,ud->prd/dot_general | solution.py:1226
  325.5 8.5 convolution_convert_fusion.second_ref
  334.0 77.1 %plane_sums.1 = (f32[384,1280]{1,0:T(8,128)}, f32[384,1280]{1,0:T(8,128)}) custom-call(bf16[8,384,1280]{2,1,0:T(8,128)(2,1)} %convolution_convert_fusion.1.first_ref, bf16[8,384,1280]{2,1,0:T(8,128)(2,1)} %convolution_convert_fusion.second_ref), custom_call_target="tpu_custom_call" | custom-call | tf_op jit(solution)/shard_map/plane_sums/pallas_call | solution.py:771
  411.2 3.0 multiply_reduce_fusion
  414.5 3.2 fusion.56
  419.3 4.5 fusion.41.grads_ref
  423.9 48.2 %attend_back.1 = bf16[8,3,128,768]{3,2,1,0:T(8,128)(2,1)S(1)} custom-call(bf16[8,3,128,768]{3,2,1,0:T(8,128)(2,1)S(1)} %bitcast.200, f32[3,1024,1]{2,1,0:T(8,128)S(1)} %copy-done.7, f32[6,1,1024]{2,1,0:T(1,128)S(1)} %get-tuple-element.38.logs_ref, bf16[8,3,160,128]{3,2,1,0:T(8,128)(2,1)S(1)} %fusion.41.grads_ref), custom_call_target="tpu_custom_call" | custom-call | tf_op jit(solution)/shard_map/attend_back/pallas_call | solution.py:694
  472.1 2.2 copy-done.2
  474.3 88.6 %line_product.1 = f32[384,1280]{1,0:T(8,128)} custom-call(bf16[8,384,768]{2,1,0:T(8,128)(2,1)} %bitcast.193, bf16[768,1280]{1,0:T(8,128)(2,1)} %pad_maximum_fusion.weight_ref), custom_call_target="tpu_custom_call" | custom-call | tf_op jit(solution)/shard_map/line_product/pallas_call | solution.py:801
  562.9 2.2 fusion.53
  566.0 2.1 add_add_fusion.2
  568.2 10.5 %convolution_bitcast_fusion.joined_ref = f32[1280,768]{1,0:T(8,128)} fusion(bf16[8,384,1280]{2,1,0:T(8,128)(2,1)} %get-tuple-element.39, bf16[8,384,768]{2,1,0:T(8,128)(2,1)S(1)} %bitcast.196), kind=kOutput, calls=%fused_computation.35 | convolution fusion | flops 6039797760 | bytes 16515072 | tf_op jit(solution)/shard_map/prd,pre->de/dot_general | solution.py:1246
  580.0 9.9 %fusion.13 = bf16[640,1280]{1,0:T(8,128)(2,1)S(1)} fusion(bf16[8,384,640]{2,1,0:T(8,128)(2,1)} %copy-done.21, bf16[8,384,1280]{2,1,0:T(8,128)(2,1)} %get-tuple-element.35), kind=kOutput, calls=%fused_computation.45 | convolution fusion | flops 5033984000 | bytes 13434880 | tf_op jit(solution)/shard_map/pru,prd->ud/dot_general | solution.py:1232
  589.9 8.7 fusion.12
  598.6 1.9 fusion.7.feed_ref
  601.2 3.4 bitcast_convert_fusion.out_grad_ref
  604.6 91.9 %line_sums.1 = (f32[336,1280]{1,0:T(8,128)}, f32[160,1280]{1,0:T(8,128)}) custom-call(bf16[4,336,1280]{2,1,0:T(8,128)(2,1)} %fusion.7.feed_ref, bf16[8,160,1280]{2,1,0:T(8,128)(2,1)} %bitcast_convert_fusion.out_grad_ref), custom_call_target="tpu_custom_call" | custom-call | tf_op jit(solution)/shard_map/line_sums/pallas_call | solution.py:851
  696.5 1.9 broadcast.383.clone
  698.5 2.1 slice_dynamic-update-slice_fusion.1
  700.6 4.6 copy.48.up_ref
  706.0 1.9 broadcast.383.clone.1
  708.0 2.1 slice_dynamic-update-slice_fusion.down_ref
  711.0 68.3 %pack_reduce.1 = (f32[4832,128]{1,0:T(8,128)}, f32[8,128]{1,0:T(8,128)}, f32[2,8,256]{2,1,0:T(8,128)}) custom-call(f32[1280,768]{1,0:T(8,128)} %convolution_bitcast_fusion.joined_ref, f32[1,768]{1,0:T(1,128)} %broadcast_in_dim.80.bias_ref, f32[160,1280]{1,0:T(8,128)} %get-tuple-element.40.out_ref, f32[1280,640]{1,0:T(8,128)} %copy.48.up_ref, ...), custom_call_target="tpu_custom_call" | custom-call | tf_op jit(solution)/shard_map/pack_reduce/pallas_call | solution.py:1065
  782.8 37.1 %fusion.19 = (f32[1,614880]{1,0:T(1,128)}, f32[1,614880]{1,0:T(1,128)}, f32[1,614880]{1,0:T(1,128)}, f32[1,614880]{1,0:T(1,128)}) fusion(f32[1,614880]{1,0:T(1,128)S(1)} %copy-done.22, f32[]{:T(128)} %bitcast.62, f32[]{:T(128)} %bitcast.61, s32[]{:T(128)S(6)} %mul.258, f32[]{:T(128)} %bitcast.59, f32[]{:T(128)} %bitcast.58, f32[]{:T(128)} %bitcast.57, ...), kind=kLoop, calls=%fused_computation.53 | loop fusion | flops 18446400 | bytes 19676192 | tf_op jit(solution)/shard_map/mul | solution.py:1321
  819.9 5.1 conditional.1
  819.9 5.1 pad.35
  825.0 49.2 %share_master.1 = f32[19216,128]{1,0:T(8,128)} custom-call(f32[4832,128]{1,0:T(8,128)S(1)} %bitcast.205), custom_call_target="tpu_custom_call" | custom-call | tf_op jit(solution)/shard_map/share_master/pallas_call | solution.py:1130
  874.3 9.3 %slice.79 = bf16[1,2459520]{1,0:T(2,128)(2,1)} slice(f32[1,2459648]{1,0:T(1,128)} %bitcast.202), slice={[0:1], [0:2459520]} | slice | bytes 9838080 | tf_op jit(solution)/shard_map/slice | solution.py:1333
  (151 shorter events, 18.7 us)
Async XLA Ops:
  0.6 99.2 %copy-start = (bf16[640,1280]{1,0:T(8,128)(2,1)S(1)}, bf16[640,1280]{1,0:T(8,128)(2,1)}, u32[]{:S(2)}) copy-start(bf16[640,1280]{1,0:T(8,128)(2,1)} %param.45) | copy-start | bytes 4915204
  0.7 4.7 copy-start.13
  0.7 6.1 copy-start.27
  0.7 6.1 copy-start.28
  3.7 3.2 copy-start.29
  6.9 1.5 copy-start.39
  6.9 1.6 copy-start.40
  6.9 1.7 copy-start.6
  8.4 88.9 %copy-start.31 = (s32[3,1024]{1,0:T(4,128)S(1)}, s32[3,1024]{1,0:T(4,128)}, u32[]{:S(2)}) copy-start(s32[3,1024]{1,0:T(4,128)} %param.30) | copy-start | bytes 36868
  8.4 88.9 %copy-start.38 = (s32[3]{0:T(128)S(1)}, s32[3]{0:T(128)}, u32[]{:S(2)}) copy-start(s32[3]{0:T(128)} %param.29) | copy-start | bytes 40
  8.6 1.5 copy-start.5
  10.1 1.2 copy-start.9
  95.2 2.1 copy-start.3
  100.6 3.9 copy-start.7
  104.5 2.3 copy-start.4
  219.9 0.9 copy-start.11
  220.8 2.8 copy-start.10
  220.8 5.2 copy-start.33
  220.8 5.3 copy-start.34
  220.8 5.3 copy-start.35
  223.7 2.3 copy-start.19
  226.1 4.2 copy-start.14
  230.8 41.2 %slice-start.4 = ((s8[5079040]{0:T(1024)(128)(4,1)}), s8[4194304]{0:T(1024)(128)(4,1)S(1)}, s32[]{:S(2)}) async-start(s8[5079040]{0:T(1024)(128)(4,1)} %bitcast.203), calls=%async_computation.4 | async-start | bytes 8388608
  232.6 39.4 %slice-start.5 = ((s8[5079040]{0:T(1024)(128)(4,1)}), s8[884736]{0:T(1024)(128)(4,1)S(1)}, s32[]{:S(2)}) async-start(s8[5079040]{0:T(1024)(128)(4,1)} %bitcast.203), calls=%async_computation.5 | async-start | bytes 1769472
  272.0 9.7 %copy-start.8 = (bf16[8,384,1280]{2,1,0:T(8,128)(2,1)}, bf16[8,384,1280]{2,1,0:T(8,128)(2,1)S(1)}, u32[]{:S(2)}) copy-start(bf16[8,384,1280]{2,1,0:T(8,128)(2,1)S(1)} %plane_share.1) | copy-start | bytes 23592964
  273.6 8.1 copy-start.24
  281.7 18.7 %copy-start.23 = (bf16[4,160,1280]{2,1,0:T(8,128)(2,1)S(1)}, bf16[4,160,1280]{2,1,0:T(8,128)(2,1)}, u32[]{:S(2)}) copy-start(bf16[4,160,1280]{2,1,0:T(8,128)(2,1)} %get-tuple-element.67) | copy-start | bytes 4915204
  300.4 25.1 %copy-start.21 = (bf16[8,384,640]{2,1,0:T(8,128)(2,1)}, bf16[8,384,640]{2,1,0:T(8,128)(2,1)S(1)}, u32[]{:S(2)}) copy-start(bf16[8,384,640]{2,1,0:T(8,128)(2,1)S(1)} %get-tuple-element.63) | copy-start | bytes 11796484
  411.1 3.0 copy-start.36
  411.2 3.0 copy-start.16
  411.2 3.3 copy-start.20
  417.7 1.3 copy-start.17
  418.1 1.2 copy-start.25
  418.1 5.7 slice-start.2
  419.3 4.6 slice-start.3
  472.1 2.2 copy-start.2
  562.9 2.2 copy-start.15
  562.9 3.1 copy-start.18
  565.1 3.0 slice-start
  566.0 2.2 slice-start.1
  580.0 9.9 %copy-start.41 = (bf16[8,384,640]{2,1,0:T(8,128)(2,1)S(1)}, bf16[8,384,640]{2,1,0:T(8,128)(2,1)}, u32[]{:S(2)}) copy-start(bf16[8,384,640]{2,1,0:T(8,128)(2,1)} %get-tuple-element.83) | copy-start | bytes 11796484
  598.6 1.9 copy-start.12
  598.6 2.5 copy-start.26
  706.0 4.3 copy-start.30
  711.0 69.2 %copy-start.32 = (f32[3]{0:T(128)S(1)}, f32[3]{0:T(128)}, u32[]{:S(2)}) copy-start(f32[3]{0:T(128)} %param.51) | copy-start | bytes 40
  711.0 71.7 %copy-start.22 = (f32[1,614880]{1,0:T(1,128)S(1)}, f32[1,614880]{1,0:T(1,128)}, u32[]{:S(2)}) copy-start(f32[1,614880]{1,0:T(1,128)} %param.47) | copy-start | bytes 7378564
  874.3 9.4 %copy-start.37 = (f32[8,128]{1,0:T(8,128)S(1)}, f32[8,128]{1,0:T(8,128)}, u32[]{:S(2)}) copy-start(f32[8,128]{1,0:T(8,128)} %get-tuple-element.45) | copy-start | bytes 12292
  874.3 10.0 %copy-start.1 = (bf16[640,1280]{1,0:T(8,128)(2,1)S(1)}, bf16[640,1280]{1,0:T(8,128)(2,1)}, u32[]{:S(2)}) copy-start(bf16[640,1280]{1,0:T(8,128)(2,1)} %param.45) | copy-start | bytes 4915204

commit v3 on v2

--- a/solution.py
+++ b/solution.py
@@ -144,17 +144,24 @@
             other = slot_of(z, 1 - c)
             hop(0, other, out.at[other], 0, pair).wait_recv()
             ready(other)
+
+    def settle(event):
+        level = place.zorder(event)
+        ready(slot_of(level, c))
+        if paired:
+            other = slot_of(level, 1 - c)
+            hop(event, other, out.at[other], 0, pair).wait_recv()
+            ready(other)
+
     for event in range(1, LINE):
         level = place.zorder(event)
         slot = slot_of(level, c)
         hop(event, slot, out.at[slot], 0, pair).wait_recv()
         ways(event, level, slot, out.at[slot], lambda copy: copy.start())
-        if ready is not None:
-            ready(slot)
-            if paired:
-                other = slot_of(level, 1 - c)
-                hop(event, other, out.at[other], 0, pair).wait_recv()
-                ready(other)
+        if ready is not None and event > 1:
+            if event == 2:
+                settle(1)
+            settle(event)
         yield
     if ready is None:
         if paired:
@@ -169,7 +176,7 @@
     yield
 
 
-def plane_gather(place, src, out, local, send, recv):
+def plane_gather(place, src, out, local, send, recv, ready=None):
     dp, c, mp, pair = place.dp, place.c, place.mp, place.pair
     dpx, dpy, dpd = place.dpx, place.dpy, place.dpd
     half = src.shape[0] // 2
@@ -178,53 +185,67 @@
     def at(group, core):
         return out.at[group * 2 + core]
 
+    def hop(index, block, group, target):
+        return remote(block, block, send.at[index], recv.at[index], group, target)
+
+    def done(group, core):
+        if ready is not None:
+            ready(group * 2 + core)
+
     keep = pltpu.make_async_copy(src, at(dp, c), local)
     keep.start()
     here = at(dp, c)
-    sends = [
+    from_x, from_y, from_d = at(dpx, c), at(dpy, c), at(dpd, c)
+    firsts = [
         remote(src, here, send.at[0], recv.at[0], dp, pair),
         remote(src, here, send.at[1], recv.at[1], dpx, mp),
         remote(src, here, send.at[2], recv.at[2], dpy, mp),
     ]
-    for copy in sends:
+    seconds = [
+        hop(3, from_x.at[part_a], dpy, mp),
+        hop(4, from_y.at[part_b], dpx, mp),
+        hop(5, from_x, dp, pair),
+        hop(6, from_y, dp, pair),
+        hop(7, from_d.at[part_a], dp, pair),
+        hop(8, from_d.at[part_b], dp, pair),
+    ]
+    for copy in firsts:
         copy.start()
     yield
-    from_x, from_y = at(dpx, c), at(dpy, c)
-    remote(from_x, from_x, send.at[1], recv.at[1], dpx, mp).wait_recv()
-    sends.append(
-        remote(from_x.at[part_a], from_x.at[part_a], send.at[3], recv.at[3], dpy, mp)
-    )
-    sends[-1].start()
-    remote(from_y, from_y, send.at[2], recv.at[2], dpy, mp).wait_recv()
-    sends.append(
-        remote(from_y.at[part_b], from_y.at[part_b], send.at[4], recv.at[4], dpx, mp)
-    )
-    sends[-1].start()
-    for index, block in ((5, from_x), (6, from_y)):
-        sends.append(remote(block, block, send.at[index], recv.at[index], dp, pair))
-        sends[-1].start()
+    if ready is not None:
+        keep.wait()
+        done(dp, c)
+        hop(0, at(dp, 1 - c), dp, pair).wait_recv()
+        done(dp, 1 - c)
+    hop(1, from_x, dpx, mp).wait_recv()
+    seconds[0].start()
+    hop(2, from_y, dpy, mp).wait_recv()
+    seconds[1].start()
+    seconds[2].start()
+    seconds[3].start()
+    done(dpx, c)
+    hop(5, at(dpx, 1 - c), dp, pair).wait_recv()
+    done(dpx, 1 - c)
     yield
-    from_d = at(dpd, c)
-    remote(from_d.at[part_a], from_d.at[part_a], send.at[3], recv.at[3], dpy, mp).wait_recv()
-    sends.append(
-        remote(from_d.at[part_a], from_d.at[part_a], send.at[7], recv.at[7], dp, pair)
-    )
-    sends[-1].start()
-    remote(from_d.at[part_b], from_d.at[part_b], send.at[4], recv.at[4], dpx, mp).wait_recv()
-    sends.append(
-        remote(from_d.at[part_b], from_d.at[part_b], send.at[8], recv.at[8], dp, pair)
-    )
-    sends[-1].start()
+    done(dpy, c)
+    hop(6, at(dpy, 1 - c), dp, pair).wait_recv()
+    done(dpy, 1 - c)
     yield
-    for index, group in ((0, dp), (5, dpx), (6, dpy)):
-        block = at(group, 1 - c)
-        remote(block, block, send.at[index], recv.at[index], dp, pair).wait_recv()
+    hop(3, from_d.at[part_a], dpy, mp).wait_recv()
+    seconds[4].start()
+    hop(4, from_d.at[part_b], dpx, mp).wait_recv()
+    seconds[5].start()
+    done(dpd, c)
     other = at(dpd, 1 - c)
-    for index, rows in ((7, part_a), (8, part_b)):
-        remote(other.at[rows], other.at[rows], send.at[index], recv.at[index], dp, pair).wait_recv()
-    for copy in sends:
+    hop(7, other.at[part_a], dp, pair).wait_recv()
+    hop(8, other.at[part_b], dp, pair).wait_recv()
+    done(dpd, 1 - c)
+    yield
+    if ready is None:
+        hop(0, at(dp, 1 - c), dp, pair).wait_recv()
+        keep.wait()
+    for copy in firsts + seconds:
         copy.wait_send()
-    keep.wait()
     yield
 
 
@@ -409,89 +430,110 @@
     return scratch, sems
 
 
-def plane_reduce(place, produce, tile, half, result, bufs, sems, paired=True):
+def plane_reduce(place, produce, tile, half, result, bufs, sems, paired=True, early=False):
     dp, c, mp, pair = place.dp, place.c, place.mp, place.pair
     dpx, dpy, dpd = place.dpx, place.dpy, place.dpd
-    order = [dpd, dpx, dpy, dp]
-    tiles_a = [pl.ds(start, tile) for start in range(0, half, tile)]
+    starts = range(0, half, tile)
     send, recv = sems["send"], sems["recv"]
     out_block, landed = bufs["out"], bufs["in"]
-
-    def across(step):
+    groups = {"far": dpd, "x": dpx, "y": dpy, "own": dp}
+    steps = ["x", "y", "far", "own"] if early else ["far", "x", "y", "own"]
+
+    def across(name):
+        step = steps.index(name)
         return remote(
-            bufs["pair_out"].at[step],
+            bufs["pair_out"].at[step % 2],
             bufs["pair_in"].at[step],
-            sems["pair_send"].at[step],
+            sems["pair_send"].at[step % 2],
             sems["pair_recv"].at[step],
             dp,
             pair,
         )
 
-    if paired:
-        for step, group in enumerate(order):
-            for start in range(0, 2 * half, tile):
-                bufs["pair_out"][step, pl.ds(start, tile)] = produce(
-                    group, 1 - c, start
-                ).astype(BF)
-            across(step).start()
-    yield
-
-    def share(step, start):
-        total = produce(order[step], c, start)
+    def cross(name):
+        if not paired:
+            return
+        step = steps.index(name)
+        if step > 1:
+            across(steps[step - 2]).wait_send()
+        for start in range(0, 2 * half, tile):
+            bufs["pair_out"][step % 2, pl.ds(start, tile)] = produce(
+                groups[name], 1 - c, start
+            ).astype(BF)
+        across(name).start()
+
+    def crossed(name):
         if paired:
-            total = total + bufs["pair_in"][step, pl.ds(start, tile)].astype(F32)
+            across(name).wait_recv()
+
+    def share(name, start):
+        total = produce(groups[name], c, start)
+        if paired:
+            total = total + bufs["pair_in"][steps.index(name), pl.ds(start, tile)].astype(F32)
         return total
 
-    def hop(index, target):
+    def hop(index):
+        target = (dpx, dpy, dpx, dpx, dpy, dpy)[index]
         return remote(
             out_block.at[index], landed.at[index], send.at[index], recv.at[index], target, mp
         )
 
-    def fill(index, step, base, extra=None):
-        for rows in tiles_a:
-            total = share(step, base + rows.start)
+    def fill(index, name, base, extra=None):
+        for start in starts:
+            total = share(name, base + start)
             if extra is not None:
-                total = total + landed[extra, rows].astype(F32)
-            out_block[index, rows] = total.astype(BF)
-
-    targets = [dpx, dpy, dpx, dpx, dpy, dpy]
+                total = total + landed[extra, pl.ds(start, tile)].astype(F32)
+            out_block[index, pl.ds(start, tile)] = total.astype(BF)
+        hop(index).start()
+
+    def far():
+        crossed("far")
+        fill(0, "far", 0)
+        fill(1, "far", half)
+
+    def near():
+        crossed("x")
+        fill(2, "x", 0)
+        crossed("y")
+        fill(4, "y", half)
+
+    if early:
+        cross("x")
+        yield
+        cross("y")
+        near()
+        yield
+        cross("far")
+        far()
+        cross("own")
+    else:
+        cross("far")
+        cross("x")
+        yield
+        far()
+        cross("y")
+        near()
+        cross("own")
+    yield
+    hop(1).wait_recv()
+    fill(3, "x", half, extra=1)
+    hop(0).wait_recv()
+    fill(5, "y", 0, extra=0)
+    yield
+    crossed("own")
+    for index in (2, 3, 4, 5):
+        hop(index).wait_recv()
+    for base, pieces in ((0, (2, 5)), (half, (3, 4))):
+        for start in starts:
+            total = share("own", base + start)
+            for piece in pieces:
+                total = total + landed[piece, pl.ds(start, tile)].astype(F32)
+            result(pl.ds(base + start, tile), total)
+    for index in range(6):
+        hop(index).wait_send()
     if paired:
-        across(0).wait_recv()
-    fill(0, 0, 0)
-    hop(0, dpx).start()
-    fill(1, 0, half)
-    hop(1, dpy).start()
-    yield
-    if paired:
-        across(1).wait_recv()
-        across(2).wait_recv()
-    fill(2, 1, 0)
-    hop(2, dpx).start()
-    fill(4, 2, half)
-    hop(4, dpy).start()
-    yield
-    hop(1, dpy).wait_recv()
-    fill(3, 1, half, extra=1)
-    hop(3, dpx).start()
-    hop(0, dpx).wait_recv()
-    fill(5, 2, 0, extra=0)
-    hop(5, dpy).start()
-    yield
-    if paired:
-        across(3).wait_recv()
-    for index in (2, 3, 4, 5):
-        hop(index, targets[index]).wait_recv()
-    for base, pieces in ((0, (2, 5)), (half, (3, 4))):
-        for rows in tiles_a:
-            total = share(3, base + rows.start)
-            for piece in pieces:
-                total = total + landed[piece, rows].astype(F32)
-            result(pl.ds(base + rows.start, tile), total)
-    for index in range(6):
-        hop(index, targets[index]).wait_send()
-    if paired:
-        for step in range(4):
-            across(step).wait_send()
+        for name in steps[2:]:
+            across(name).wait_send()
     yield
 
 
@@ -500,8 +542,8 @@
     scratch = {"out": block(6, half), "in": block(6, half)}
     sems = {"send": dma(6), "recv": dma(6)}
     if paired:
-        scratch.update({"pair_out": block(4, 2 * half), "pair_in": block(4, 2 * half)})
-        sems.update({"pair_send": dma(4), "pair_recv": dma(4)})
+        scratch.update({"pair_out": block(2, 2 * half), "pair_in": block(4, 2 * half)})
+        sems.update({"pair_send": dma(2), "pair_recv": dma(4)})
     return scratch, sems
 
 
@@ -625,15 +667,192 @@
     )(qkv, mask, live, weights)
 
 
-def attend_back_kernel(
-    qkv_ref, mask_ref, logs_ref, grads_ref, dqkv_ref,
-    grad_ref, kt_ref, dk_ref, dv_ref, block_ref, local, send, recv,
+def flatten(*pairs):
+    names, shapes = [], []
+    for number, group in enumerate(pairs):
+        for name, shape in group.items():
+            names.append((number, name))
+            shapes.append(shape)
+
+    def split(refs):
+        groups = [{} for _ in pairs]
+        for (number, name), ref in zip(names, refs):
+            groups[number][name] = ref
+        return groups
+
+    return shapes, split
+
+
+def feed_forward_kernel(
+    split, normed_ref, upstream_ref, up_ref, down_ref, bias_ref,
+    total_ref, hidden_ref, grads_ref, bias_out,
+    normed_all, upstream_all, slope_all, sum_ref, load, local, gather_send, gather_recv, *scratch,
 ):
     place = Place()
-    greet(place, mp_all=True)
-    drive(exchange(place, grads_ref, grad_ref, local, send, recv))
+    bufs, sems = split(scratch)
+    loads = []
+    for slot in range(8):
+        loads.append(
+            pltpu.make_async_copy(upstream_ref.at[slot], upstream_all.at[slot], load.at[slot])
+        )
+        loads[-1].start()
+    greet(place, plane=True)
+    bias_out[...] = jnp.zeros(bias_out.shape, F32)
+
+    def ready(slot):
+        @pl.loop(0, 3)
+        def _(step):
+            rows = pl.ds(step * 128, 128)
+            before = (
+                lax.dot_general(
+                    normed_all[slot, rows],
+                    up_ref[...],
+                    (((1,), (1,)), ((), ())),
+                    preferred_element_type=F32,
+                )
+                + bias_ref[...]
+            )
+            pull = lax.dot_general(
+                upstream_all[slot, rows],
+                down_ref[...],
+                (((1,), (1,)), ((), ())),
+                preferred_element_type=F32,
+            )
+            share = 0.5 + 0.5 * lax.erf(before * math.sqrt(0.5))
+            hidden_ref[slot, rows] = (before * share).astype(BF)
+            density = jnp.exp(before * before * -0.5) * (1.0 / math.sqrt(2.0 * math.pi))
+            slope = (pull * (share + before * density)).astype(BF)
+            slope_all[slot, rows] = slope
+            bias_out[...] += jnp.sum(slope.astype(F32), axis=0, keepdims=True)
+
+    gather = plane_gather(
+        place, normed_ref, normed_all, local, gather_send, gather_recv, ready
+    )
+
+    def produce(group, core, start):
+        return jnp.dot(
+            slope_all[group * 2 + core, pl.ds(start, 192)],
+            up_ref[...],
+            preferred_element_type=F32,
+        )
+
+    def result(rows, total):
+        total_ref[rows] = total
+
+    reduce = plane_reduce(place, produce, 192, 192, result, bufs, sems, True, True)
+    next(gather)
+    for copy in loads:
+        copy.wait()
+    next(gather)
+    next(reduce)
+    next(gather)
+    next(reduce)
+    next(gather)
+    next(reduce)
+
+    def weight_grads(left_all, right_all, base):
+        for block in range(5):
+            lanes = pl.ds(block * 128, 128)
+
+            @pl.loop(0, 8)
+            def _(slot):
+                product = lax.dot_general(
+                    left_all[slot, :, lanes],
+                    right_all[slot],
+                    (((0,), (0,)), ((), ())),
+                    preferred_element_type=F32,
+                )
+                sum_ref[...] = jnp.where(slot == 0, product, sum_ref[...] + product)
+
+            for part in range(4):
+                unit = block * 128 + part * 32
+                grads_ref[unit // 160, pl.ds(base + unit % 160, 32)] = sum_ref[
+                    pl.ds(part * 32, 32)
+                ].astype(BF)
+
+    weight_grads(slope_all, normed_all, 0)
+    next(reduce)
+    weight_grads(hidden_ref, upstream_all, 160)
+    for level in range(4):
+        grads_ref[level, pl.ds(320, 16)] = jnp.zeros((16, 1280), BF)
+        grads_ref[level, pl.ds(320, 16), pl.ds(0, 640)] = jnp.broadcast_to(
+            bias_out[...], (16, 640)
+        ).astype(BF)
+    drive(reduce, gather)
+
+
+def feed_forward(normed, upstream, up, down, bias):
+    shapes, split = flatten(*plane_reduce_scratch(192, 1280))
+    return pl.pallas_call(
+        functools.partial(feed_forward_kernel, split),
+        out_shape=(
+            jax.ShapeDtypeStruct((ROWS, 1280), F32),
+            jax.ShapeDtypeStruct((8, ROWS, 640), BF),
+            jax.ShapeDtypeStruct((4, 336, 1280), BF),
+            jax.ShapeDtypeStruct((1, 640), F32),
+        ),
+        in_specs=[ANY, ANY, VMEM, VMEM, VMEM],
+        out_specs=(VMEM,) * 4,
+        scratch_shapes=[
+            pltpu.VMEM((8, ROWS, 1280), BF),
+            pltpu.VMEM((8, ROWS, 1280), BF),
+            pltpu.VMEM((8, ROWS, 640), BF),
+            pltpu.VMEM((128, 1280), F32),
+            dma(8),
+            pltpu.SemaphoreType.DMA(()),
+            dma(9),
+            dma(9),
+            *shapes,
+        ],
+        compiler_params=params(3, 60),
+        name="feed_forward",
+    )(normed, upstream, up, down, bias)
+
+
+def attend_back_kernel(
+    split, qkv_ref, mask_ref, logs_ref, pull_ref, hidden_ref, down_ref, feed_grads_ref,
+    dqkv_ref, feed_ref, feed_sum_ref,
+    grad_ref, kt_ref, dk_ref, dv_ref, block_ref, local, send, recv, *scratch,
+):
+    place = Place()
+    line_bufs, line_sems, plane_bufs, plane_sems = split(scratch)
+    greet(place, mp_all=True, plane=True)
     scale = 1.0 / math.sqrt(HD)
     factor = math.log2(math.e) * scale
+    arriving = exchange(place, pull_ref, grad_ref, local, send, recv)
+    next(arriving)
+
+    def feed_block(group, core, start):
+        return jnp.dot(
+            hidden_ref[group * 2 + core, pl.ds(start, 192)],
+            down_ref[...],
+            preferred_element_type=F32,
+        )
+
+    def feed_result(rows, total):
+        feed_ref[rows] = total
+
+    def sum_result(rows, total):
+        feed_sum_ref[rows] = total
+
+    plane = plane_reduce(
+        place, feed_block, 192, 192, feed_result, plane_bufs, plane_sems, True
+    )
+    line = line_reduce(
+        place,
+        lambda level, core, rows: feed_grads_ref[level, rows].astype(F32),
+        [pl.ds(start, 112) for start in range(0, 336, 112)],
+        sum_result,
+        line_bufs,
+        line_sems,
+        False,
+    )
+    next(plane)
+    next(line)
+    next(plane)
+    for _ in arriving:
+        pass
+    next(line)
     block_ref[...] = jnp.zeros(block_ref.shape, BF)
 
     @pl.loop(0, 6)
@@ -642,8 +861,7 @@
         head = turn % 2
         lane = pl.multiple_of(head * 128, 128)
         row = pl.multiple_of(head * HD, 16)
-        keys = qkv_ref[:, clip, :, pl.ds(256 + lane, 128)].reshape(1024, 128)
-        kt_ref[...] = keys.T
+        kt_ref[...] = qkv_ref[:, clip, :, pl.ds(256 + lane, 128)].reshape(1024, 128).T
         dk_ref[...] = jnp.zeros(dk_ref.shape, F32)
         dv_ref[...] = jnp.zeros(dv_ref.shape, F32)
 
@@ -689,13 +907,30 @@
             dv_ref[...].astype(BF).reshape(8, 128, 128)
         )
 
-
-def attend_back(qkv, mask, logs, grads):
+        @pl.when(turn == 2)
+        def _():
+            next(plane)
+
+        @pl.when(turn == 4)
+        def _():
+            next(line)
+
+    drive(line, plane)
+
+
+def attend_back(qkv, mask, logs, pull, hidden, down, feed_grads):
+    shapes, split = flatten(
+        *line_reduce_scratch(336, 1280, False), *plane_reduce_scratch(192, 1280)
+    )
     return pl.pallas_call(
-        attend_back_kernel,
-        out_shape=jax.ShapeDtypeStruct(qkv.shape, BF),
-        in_specs=[VMEM, VMEM, VMEM, ANY],
-        out_specs=VMEM,
+        functools.partial(attend_back_kernel, split),
+        out_shape=(
+            jax.ShapeDtypeStruct(qkv.shape, BF),
+            jax.ShapeDtypeStruct((ROWS, 1280), F32),
+            jax.ShapeDtypeStruct((336, 1280), F32),
+        ),
+        in_specs=[VMEM, VMEM, VMEM, ANY, VMEM, VMEM, VMEM],
+        out_specs=(VMEM,) * 3,
         scratch_shapes=[
             pltpu.VMEM((8, 3, 160, 128), BF),
             pltpu.VMEM((128, 1024), BF),
@@ -705,84 +940,19 @@
             pltpu.SemaphoreType.DMA(()),
             dma(8),
             dma(8),
+            *shapes,
         ],
-        compiler_params=params(2),
+        compiler_params=params(2, 61),
         name="attend_back",
-    )(qkv, mask, logs, grads)
-
-
-def plane_share_kernel(block_ref, full_ref, local, send, recv):
+    )(qkv, mask, logs, pull, hidden, down, feed_grads)
+
+
+def line_product_kernel(
+    split, grad_ref, weight_ref, out_grad_ref, total_ref, out_ref, middle_ref, *scratch
+):
     place = Place()
-    greet(place, plane=True)
-    drive(plane_gather(place, block_ref, full_ref, local, send, recv))
-
-
-def plane_share(block):
-    return pl.pallas_call(
-        plane_share_kernel,
-        out_shape=jax.ShapeDtypeStruct((8,) + block.shape, BF),
-        in_specs=[ANY],
-        out_specs=ANY,
-        scratch_shapes=[pltpu.SemaphoreType.DMA(()), dma(9), dma(9)],
-        compiler_params=params(3),
-        name="plane_share",
-    )(block)
-
-
-def flatten(*pairs):
-    names, shapes = [], []
-    for number, group in enumerate(pairs):
-        for name, shape in group.items():
-            names.append((number, name))
-            shapes.append(shape)
-
-    def split(refs):
-        groups = [{} for _ in pairs]
-        for (number, name), ref in zip(names, refs):
-            groups[number][name] = ref
-        return groups
-
-    return shapes, split
-
-
-def plane_sums_kernel(split, first_ref, second_ref, first_out, second_out, *scratch):
-    place = Place()
-    bufs_one, sems_one, bufs_two, sems_two = split(scratch)
-    greet(place, plane=True)
-
-    def reader(ref):
-        return lambda group, core, start: ref[group * 2 + core, pl.ds(start, 96)].astype(F32)
-
-    def writer(ref):
-        def write(rows, total):
-            ref[rows] = total
-
-        return write
-
-    drive(
-        plane_reduce(place, reader(first_ref), 96, 192, writer(first_out), bufs_one, sems_one),
-        plane_reduce(place, reader(second_ref), 96, 192, writer(second_out), bufs_two, sems_two),
-    )
-
-
-def plane_sums(first, second):
-    shapes, split = flatten(*plane_reduce_scratch(192, 1280), *plane_reduce_scratch(192, 1280))
-    out = jax.ShapeDtypeStruct(first.shape[1:], F32)
-    return pl.pallas_call(
-        functools.partial(plane_sums_kernel, split),
-        out_shape=(out, out),
-        in_specs=[VMEM, VMEM],
-        out_specs=(VMEM, VMEM),
-        scratch_shapes=shapes,
-        compiler_params=params(4, 60),
-        name="plane_sums",
-    )(first, second)
-
-
-def line_product_kernel(split, grad_ref, weight_ref, out_ref, *scratch):
-    place = Place()
-    bufs, sems = split(scratch)
-    greet(place, line=True)
+    bufs, sems, plane_bufs, plane_sems, out_bufs, out_sems = split(scratch)
+    greet(place, line=True, plane=True)
 
     def produce(level, core, rows):
         return jnp.dot(
@@ -790,76 +960,65 @@
         )
 
     def result(rows, total):
+        total_ref[rows] = total
+
+    def middle(rows, total):
+        middle_ref[rows] = total
+
+    def out_result(rows, total):
         out_ref[rows] = total
 
-    tiles = [pl.ds(start, 128) for start in range(0, ROWS, 128)]
-    drive(line_reduce(place, produce, tiles, result, bufs, sems, True))
-
-
-def line_product(grads, weight):
-    shapes, split = flatten(*line_reduce_scratch(ROWS, 1280, True))
+    line = line_reduce(
+        place,
+        produce,
+        [pl.ds(start, 128) for start in range(0, ROWS, 128)],
+        result,
+        bufs,
+        sems,
+        True,
+    )
+    plane = plane_reduce(
+        place,
+        lambda group, core, start: out_grad_ref[group, core, pl.ds(start, 96)].astype(F32),
+        96,
+        96,
+        middle,
+        plane_bufs,
+        plane_sems,
+    )
+    outer = line_reduce(
+        place,
+        lambda level, core, rows: middle_ref[
+            pl.ds(pl.multiple_of(level * 48 + rows.start, 16), rows.size)
+        ],
+        [pl.ds(0, 48)],
+        out_result,
+        out_bufs,
+        out_sems,
+        False,
+    )
+    drive(plane, line)
+    drive(outer)
+
+
+def line_product(grads, weight, out_grad):
+    shapes, split = flatten(
+        *line_reduce_scratch(ROWS, 1280, True),
+        *plane_reduce_scratch(96, 1280),
+        *line_reduce_scratch(48, 1280, False),
+    )
     return pl.pallas_call(
         functools.partial(line_product_kernel, split),
-        out_shape=jax.ShapeDtypeStruct((ROWS, 1280), F32),
-        in_specs=[VMEM, VMEM],
-        out_specs=VMEM,
-        scratch_shapes=shapes,
+        out_shape=(
+            jax.ShapeDtypeStruct((ROWS, 1280), F32),
+            jax.ShapeDtypeStruct((48, 1280), F32),
+        ),
+        in_specs=[VMEM, VMEM, VMEM],
+        out_specs=(VMEM, VMEM),
+        scratch_shapes=[pltpu.VMEM((192, 1280), F32), *shapes],
         compiler_params=params(5, 60),
         name="line_product",
-    )(grads, weight)
-
-
-def line_sums_kernel(split, feed_ref, out_grad_ref, feed_out, out_out, *scratch):
-    place = Place()
-    bufs_one, sems_one, bufs_two, sems_two = split(scratch)
-    greet(place, line=True)
-
-    def write_feed(rows, total):
-        feed_out[rows] = total
-
-    def write_out(rows, total):
-        out_out[rows] = total
-
-    tiles = lambda rows, tile: [pl.ds(start, tile) for start in range(0, rows, tile)]
-    drive(
-        line_reduce(
-            place,
-            lambda level, core, rows: feed_ref[level, rows].astype(F32),
-            tiles(feed_ref.shape[1], 112),
-            write_feed,
-            bufs_one,
-            sems_one,
-            False,
-        ),
-        line_reduce(
-            place,
-            lambda level, core, rows: out_grad_ref[level * 2 + core, rows].astype(F32),
-            tiles(160, 80),
-            write_out,
-            bufs_two,
-            sems_two,
-            True,
-        ),
-    )
-
-
-def line_sums(feed, out_grad):
-    rows = feed.shape[1]
-    shapes, split = flatten(
-        *line_reduce_scratch(rows, 1280, False), *line_reduce_scratch(160, 1280, True)
-    )
-    return pl.pallas_call(
-        functools.partial(line_sums_kernel, split),
-        out_shape=(
-            jax.ShapeDtypeStruct((rows, 1280), F32),
-            jax.ShapeDtypeStruct((160, 1280), F32),
-        ),
-        in_specs=[VMEM, VMEM],
-        out_specs=(VMEM, VMEM),
-        scratch_shapes=shapes,
-        compiler_params=params(6, 60),
-        name="line_sums",
-    )(feed, out_grad)
+    )(grads, weight, out_grad)
 
 
 GROUP_ROWS = 4832
@@ -1213,24 +1372,9 @@
     branch = jnp.einsum("schr,shd->crd", attended, out_rows, preferred_element_type=F32)
     middle = inputs + branch.reshape(ROWS, 1280) + out_bias.astype(F32)
     normed_two = layer_norm(middle, gain_second, shift_second).astype(BF)
-    normed_two_full = plane_share(normed_two)
-    before = (
-        jnp.einsum("prd,ud->pru", normed_two_full, up_rows, preferred_element_type=F32)
-        + up_lanes
-    )
-    hidden = exact_gelu(before).astype(BF)
-    hidden_grad = jnp.einsum("prd,ud->pru", upstream_full, down_rows, preferred_element_type=F32)
-    _, gelu_pull = jax.vjp(exact_gelu, before)
-    before_grad = gelu_pull(hidden_grad)[0].astype(BF)
-    feed_part = jnp.einsum("pru,ud->prd", hidden, down_rows, preferred_element_type=F32).astype(BF)
-    normed_part = jnp.einsum(
-        "pru,ud->prd", before_grad, up_rows, preferred_element_type=F32
-    ).astype(BF)
-    normed_two_grad, feed = plane_sums(normed_part, feed_part)
-    layer_out = (middle + feed + down_bias.astype(F32)).astype(BF)
-    up_grad = jnp.einsum("pru,prd->ud", before_grad, normed_two_full, preferred_element_type=F32)
-    down_grad = jnp.einsum("pru,prd->ud", hidden, upstream_full, preferred_element_type=F32)
-    up_bias_grad = jnp.sum(before_grad.astype(F32), axis=(0, 1))
+    normed_two_grad, hidden, feed_grads, _ = feed_forward(
+        normed_two, upstream_full, up_rows, down_rows, up_lanes[None]
+    )
 
     _, norm_two_pull = jax.vjp(layer_norm, middle, gain_second, shift_second)
     middle_norm_grad, gain_two_grad, shift_two_grad = norm_two_pull(normed_two_grad)
@@ -1241,8 +1385,16 @@
     attended_grad = jnp.einsum(
         "shd,crd->schr", out_rows, branch_clips, preferred_element_type=F32
     ).astype(BF)
-    joined_grad = attend_back(qkv, mask, logs, attended_grad).reshape(8, ROWS, 768)
-    normed_grad = line_product(joined_grad, joined_weight)
+    out_quarters = jnp.pad(
+        out_grad.astype(BF).reshape(4, 2, 4, 40, 1280), ((0, 0),) * 3 + ((0, 8), (0, 0))
+    )
+    out_quarters = out_quarters.transpose(2, 1, 0, 3, 4).reshape(4, 2, 192, 1280)
+    joined_grad, feed, feed_sum = attend_back(
+        qkv, mask, logs, attended_grad, hidden, down_rows, feed_grads
+    )
+    layer_out = (middle + feed + down_bias.astype(F32)).astype(BF)
+    joined_grad = joined_grad.reshape(8, ROWS, 768)
+    normed_grad, out_sum = line_product(joined_grad, joined_weight, out_quarters)
     joined_weight_grad = jnp.einsum(
         "prd,pre->de", normed_full, joined_grad, preferred_element_type=F32
     )
@@ -1252,24 +1404,19 @@
     input_norm_grad, gain_one_grad, shift_one_grad = norm_one_pull(normed_grad)
     input_grad = middle_grad + input_norm_grad
 
-    feed_grads = jnp.concatenate(
-        [
-            up_grad.astype(BF).reshape(4, 160, 1280),
-            down_grad.astype(BF).reshape(4, 160, 1280),
-            jnp.pad(up_bias_grad.astype(BF).reshape(4, 1, 160), ((0, 0), (0, 15), (0, 1120))),
-        ],
-        axis=1,
-    )
-    feed_sum, out_sum = line_sums(feed_grads, out_grad.astype(BF))
-
     def spread(rows):
+        size = rows.shape[0]
         return lax.dynamic_update_slice(
-            jnp.zeros((640,) + rows.shape[1:], F32), rows, (quarter,) + (0,) * (rows.ndim - 1)
+            jnp.zeros((4 * size,) + rows.shape[1:], F32),
+            rows,
+            (size * group,) + (0,) * (rows.ndim - 1),
         )
 
     up_whole = spread(feed_sum[:160]).T
     down_whole = spread(feed_sum[160:320])
-    up_bias_whole = spread(feed_sum[320, :160])
+    level = lax.axis_index("mp") // 2
+    up_bias_whole = spread(lax.dynamic_slice_in_dim(feed_sum[320], level * 160, 160, 0))
+    out_whole = spread(out_sum[:40])
 
     out_bias_grad = jnp.sum(branch_grad.astype(F32), axis=0)
     down_bias_grad = jnp.sum(upstream, axis=0)
@@ -1287,7 +1434,7 @@
     grad_rows, small_sum, peak_sum = pack_reduce(
         joined_weight_grad,
         joined_bias_grad[None],
-        out_sum,
+        out_whole,
         up_whole,
         up_bias_whole.reshape(5, 128),
         down_whole,
@@ -1312,11 +1459,10 @@
     query_end = 1280 * 160
     query_bias_end = query_end + 160
     key_end = query_bias_end + 1280 * 160
-    column = jnp.where(
-        entry_index < query_bias_end, entry_index, entry_index - query_bias_end
-    ) % 160
+    block = jnp.floor((entry_index.astype(F32) + 0.5) * (1.0 / HD))
+    odd = block - 2.0 * jnp.floor(block * 0.5) > 0.5
     root_factor = jnp.sqrt(logit_cap / jnp.maximum(head_peak, logit_cap))
-    head_factor = jnp.where(column < HD, root_factor[0], root_factor[1])
+    head_factor = jnp.where(odd, root_factor[1], root_factor[0])
     factor = jnp.where(entry_index < key_end, head_factor, 1.0)
     master_new = (
         master

time: 892 us -> 758 us (0.85)
  matrix products: 82.8 us -> 20.9 us
  Pallas kernels: 660 us -> 611 us
  other arithmetic: 83 us -> 57.4 us
    dot_general x6 -> x0, matrix products: 60.3 us -> none  [the longest x1 14.7 us: fast_body(): jnp.einsum('prd,ud->pru', upstream_full, down_rows, preferred_element_typ...]
    pallas_call x5 -> x3, Pallas kernels: 345 us -> 297 us  [the longest x1 104 us: line_product(): pl.pallas_call(functools.partial(line_product_kernel, split), out_shape=(...]
    convert_element_type x1 -> x0, other arithmetic: 18.7 us -> none  [fast_body(): hidden = exact_gelu(before).astype(BF)]
where the time goes in v3:
time: 758 us; the launch traced here: 747 us
  Pallas kernels  611 us (81%)
  other arithmetic  57.4 us (8%)
  local copies, waits for them, and re-layouts  55.3 us (7%)
  matrix products  20.9 us (3%)
    pallas_call x1, Pallas kernels, attend(): pl.pallas_call(attend_kernel, out_shape=(jax.ShapeDtypeStruct((8, 3, 160,...  113 us
    pallas_call x1, Pallas kernels, line_product(): pl.pallas_call(functools.partial(line_product_kernel, split), out_shape=(...  104 us
    pallas_call x1, Pallas kernels, attend_back(): pl.pallas_call(functools.partial(attend_back_kernel, split), out_shape=(j...  99.6 us
    pallas_call x1, Pallas kernels, feed_forward(): pl.pallas_call(functools.partial(feed_forward_kernel, split), out_shape=(...  93.5 us
    pallas_call x1, Pallas kernels, project(): pl.pallas_call(project_kernel, out_shape=(jax.ShapeDtypeStruct((8,) + nor...  84.9 us
    pallas_call x1, Pallas kernels, pack_reduce(): pl.pallas_call(functools.partial(pack_reduce_kernel, split), out_shape=(j...  66.8 us
    pallas_call x1, Pallas kernels, share_master(): pl.pallas_call(share_master_kernel, out_shape=jax.ShapeDtypeStruct((PACK_...  49.1 us
    mul x1, other arithmetic, fast_body(): (master - learn_rate * (first_hat / (jnp.sqrt(second_hat) + ADAM_EPSILON)...  30.3 us

profile of v3, /device:TPU:0, one launch (start us, length us, event | category | flops | bytes accessed | tf_op | source)
XLA Modules:
  0.0 747.2 jit_solution(2468549432523411936)
XLA Ops:
  0.7 0.8 convert_element_type.140
  1.5 0.7 convert_element_type.139
  4.3 1.5 fusion.13
  5.7 1.6 fusion.24
  7.4 1.4 fusion.20.normed_ref
  9.0 1.4 pad_maximum_fusion.weight_ref
  10.6 1.5 copy-done.4
  12.2 1.2 copy-done.7
  13.4 84.9 %project.1 = (bf16[8,384,1280]{2,1,0:T(8,128)(2,1)}, bf16[8,384,768]{2,1,0:T(8,128)(2,1)S(1)}, bf16[8,384,1280]{2,1,0:T(8,128)(2,1)}) custom-call(bf16[384,1280]{1,0:T(8,128)(2,1)S(1)} %copy-done.7, bf16[384,1280]{1,0:T(8,128)(2,1)S(1)} %bitcast.173, bf16[768,1280]{1,0:T(8,128)(2,1)S(1)} %copy-done.4, f32[1,768]{1,0:T(1,128)S(1)} %broadcast_in_dim.74.bias_ref), custom_call_target="tpu_custom_call" | custom-call | tf_op jit(solution)/shard_map/project/pallas_call | solution.py:578
  98.3 2.2 copy-done.2
  100.5 1.7 copy.39.mask_ref
  102.3 0.8 dynamic_slice.22
  103.0 2.3 constant_dynamic-slice_fusion.3
  105.4 1.4 copy.51
  106.8 1.1 fusion.32.weights_ref
  107.9 2.3 copy-done.3
  110.2 112.8 %attend.1 = (bf16[8,3,160,128]{3,2,1,0:T(8,128)(2,1)S(1)}, f32[6,1,1024]{2,1,0:T(1,128)S(1)}, f32[2,8,256]{2,1,0:T(8,128)S(1)}, bf16[8,496,1280]{2,1,0:T(8,128)(2,1)}) custom-call(bf16[8,3,128,768]{3,2,1,0:T(8,128)(2,1)S(1)} %bitcast.172, f32[3,1024,1]{2,1,0:T(8,128)S(1)} %copy-done.6, f32[3,1,1024]{2,1,0:T(1,128)S(1)} %compare_convert_fusion.live_ref, ...), custom_call_target="tpu_custom_call" | custom-call | tf_op jit(solution)/shard_map/attend/pallas_call | solution.py:646
  223.1 3.9 fusion.34
  227.6 1.5 add_convert_fusion.1
  229.1 3.5 dynamic-slice_bitcast_fusion
  232.6 1.9 fusion.45
  235.2 93.5 %feed_forward.1 = (f32[384,1280]{1,0:T(8,128)}, bf16[8,384,640]{2,1,0:T(8,128)(2,1)}, bf16[4,336,1280]{2,1,0:T(8,128)(2,1)}, f32[1,640]{1,0:T(1,128)}) custom-call(bf16[384,1280]{1,0:T(8,128)(2,1)} %get-tuple-element.69.normed_ref, bf16[8,384,1280]{2,1,0:T(8,128)(2,1)} %get-tuple-element.40.upstream_ref, bf16[640,1280]{1,0:T(8,128)(2,1)} %bitcast.183, ...), custom_call_target="tpu_custom_call" | custom-call | tf_op jit(solution)/shard_map/feed_forward/pallas_call | solution.py:786
  328.7 2.3 multiply_reduce_fusion
  332.1 0.9 copy-done.16
  333.0 4.8 fusion.28.pull_ref
  337.7 99.6 %attend_back.1 = (bf16[8,3,128,768]{3,2,1,0:T(8,128)(2,1)}, f32[384,1280]{1,0:T(8,128)}, f32[336,1280]{1,0:T(8,128)}) custom-call(bf16[8,3,128,768]{3,2,1,0:T(8,128)(2,1)} %bitcast.171, f32[3,1024,1]{2,1,0:T(8,128)} %copy.39.mask_ref, f32[6,1,1024]{2,1,0:T(1,128)} %copy-done.8, bf16[8,3,160,128]{3,2,1,0:T(8,128)(2,1)} %fusion.28.pull_ref, ...), custom_call_target="tpu_custom_call" | custom-call | tf_op jit(solution)/shard_map/attend_back/pallas_call | solution.py:925
  437.4 3.4 add_convert_fusion
  440.8 2.0 bitcast_convert_fusion
  443.1 2.3 pad.53
  445.3 104.2 %line_product.1 = (f32[384,1280]{1,0:T(8,128)}, f32[48,1280]{1,0:T(8,128)}) custom-call(bf16[8,384,768]{2,1,0:T(8,128)(2,1)} %bitcast.175, bf16[768,1280]{1,0:T(8,128)(2,1)} %pad_maximum_fusion.weight_ref, bf16[4,2,192,1280]{3,2,1,0:T(8,128)(2,1)} %bitcast.179), custom_call_target="tpu_custom_call" | custom-call | tf_op jit(solution)/shard_map/line_product/pallas_call | solution.py:1010
  549.6 2.2 fusion.40
  551.8 0.9 fusion.21
  553.3 2.1 add_add_fusion.2
  555.4 10.2 %convolution_bitcast_fusion.joined_ref = f32[1280,768]{1,0:T(8,128)} fusion(bf16[8,384,1280]{2,1,0:T(8,128)(2,1)} %get-tuple-element.47, bf16[8,384,768]{2,1,0:T(8,128)(2,1)S(1)} %bitcast.178), kind=kOutput, calls=%fused_computation.8 | convolution fusion | flops 6039797760 | bytes 16515072 | tf_op jit(solution)/shard_map/prd,pre->de/dot_general | solution.py:1398
  565.6 0.7 convert_reduce_fusion
  567.1 2.0 broadcast.243.clone
  569.0 2.1 slice_dynamic-update-slice_fusion.1
  571.1 4.6 copy.45.up_ref
  575.7 0.8 slice.52
  576.8 1.9 broadcast.243.clone.1
  578.7 2.1 slice_dynamic-update-slice_fusion.down_ref
  581.8 66.8 %pack_reduce.1 = (f32[4832,128]{1,0:T(8,128)}, f32[8,128]{1,0:T(8,128)}, f32[2,8,256]{2,1,0:T(8,128)}) custom-call(f32[1280,768]{1,0:T(8,128)} %convolution_bitcast_fusion.joined_ref, f32[1,768]{1,0:T(1,128)} %broadcast_in_dim.83.bias_ref, f32[160,1280]{1,0:T(8,128)} %copy-done.20, f32[1280,640]{1,0:T(8,128)} %copy.45.up_ref, f32[5,128]{1,0:T(8,128)} %bitcast.199, ...), custom_call_target="tpu_custom_call" | custom-call | tf_op jit(solution)/shard_map/pack_reduce/pallas_call | solution.py:1224
  648.6 0.8 reduce_max.9
  652.0 30.3 %fusion.9 = (f32[1,614880]{1,0:T(1,128)}, f32[1,614880]{1,0:T(1,128)}, f32[1,614880]{1,0:T(1,128)}, f32[1,614880]{1,0:T(1,128)}) fusion(f32[1,614880]{1,0:T(1,128)S(1)} %copy-done.21, f32[]{:T(128)} %bitcast.58, f32[]{:T(128)} %bitcast.57, s32[]{:T(128)S(6)} %mul.262, f32[]{:T(128)} %bitcast.55, f32[]{:T(128)} %bitcast.54, f32[]{:T(128)} %bitcast.53, ...), kind=kLoop, calls=%fused_computation.21 | loop fusion | flops 17831520 | bytes 19676192 | tf_op jit(solution)/shard_map/mul | solution.py:1467
  682.2 5.4 conditional.1
  682.2 5.1 pad.35
  687.7 49.1 %share_master.1 = f32[19216,128]{1,0:T(8,128)} custom-call(f32[4832,128]{1,0:T(8,128)S(1)} %bitcast.182), custom_call_target="tpu_custom_call" | custom-call | tf_op jit(solution)/shard_map/share_master/pallas_call | solution.py:1289
  736.7 9.3 %slice.84 = bf16[1,2459520]{1,0:T(2,128)(2,1)} slice(f32[1,2459648]{1,0:T(1,128)} %bitcast.174), slice={[0:1], [0:2459520]} | slice | bytes 9838080 | tf_op jit(solution)/shard_map/slice | solution.py:1479
  (120 shorter events, 10.1 us)
Async XLA Ops:
  0.6 102.4 %copy-start = (bf16[640,1280]{1,0:T(8,128)(2,1)S(1)}, bf16[640,1280]{1,0:T(8,128)(2,1)}, u32[]{:S(2)}) copy-start(bf16[640,1280]{1,0:T(8,128)(2,1)} %param.45) | copy-start | bytes 4915204
  0.6 6.7 copy-start.12
  4.3 4.5 copy-start.22
  5.7 3.1 copy-start.23
  7.4 1.5 copy-start.24
  9.0 1.4 copy-start.32
  9.0 1.5 copy-start.33
  9.0 1.6 copy-start.5
  10.6 1.5 copy-start.4
  12.2 1.2 copy-start.7
  13.4 87.1 %copy-start.27 = (s32[3,1024]{1,0:T(4,128)S(1)}, s32[3,1024]{1,0:T(4,128)}, u32[]{:S(2)}) copy-start(s32[3,1024]{1,0:T(4,128)} %param.30) | copy-start | bytes 36868
  13.4 87.1 %copy-start.31 = (s32[3]{0:T(128)S(1)}, s32[3]{0:T(128)}, u32[]{:S(2)}) copy-start(s32[3]{0:T(128)} %param.29) | copy-start | bytes 40
  98.2 2.2 copy-start.2
  105.4 2.5 copy-start.6
  107.9 2.3 copy-start.3
  110.2 112.8 %copy-start.13 = (bf16[128,3,1280]{2,0,1:T(8,128)(2,1)S(1)}, bf16[128,3,1280]{2,0,1:T(8,128)(2,1)}, u32[]{:S(2)}) copy-start(bf16[128,3,1280]{2,0,1:T(8,128)(2,1)} %param.28) | copy-start | bytes 2949124
  223.0 4.0 copy-start.8
  223.0 4.0 copy-start.9
  223.1 4.0 copy-start.10
  229.1 102.0 %copy-start.15 = (f32[384,1280]{1,0:T(8,128)}, f32[384,1280]{1,0:T(8,128)S(1)}, u32[]{:S(2)}) copy-start(f32[384,1280]{1,0:T(8,128)S(1)} %get-tuple-element.70) | copy-start | bytes 5898244
  328.7 2.4 copy-start.19
  331.7 1.3 copy-start.16
  337.7 99.6 %copy-start.29 = (bf16[1280]{0:T(1024)(128)(2,1)S(1)}, bf16[1280]{0:T(1024)(128)(2,1)}, u32[]{:S(2)}) copy-start(bf16[1280]{0:T(1024)(128)(2,1)} %param.46) | copy-start | bytes 7684
  437.4 3.4 copy-start.11
  445.3 104.2 %copy-start.14 = (bf16[128,3,1280]{2,0,1:T(8,128)(2,1)S(1)}, bf16[128,3,1280]{2,0,1:T(8,128)(2,1)}, u32[]{:S(2)}) copy-start(bf16[128,3,1280]{2,0,1:T(8,128)(2,1)} %param.28) | copy-start | bytes 2949124
  549.5 2.2 copy-start.18
  551.7 1.5 copy-start.17
  551.8 3.6 slice-start
  553.3 2.1 slice-start.1
  565.6 1.4 copy-start.25
  567.0 4.1 copy-start.20
  576.8 4.0 copy-start.26
  581.8 67.6 %copy-start.28 = (f32[3]{0:T(128)S(1)}, f32[3]{0:T(128)}, u32[]{:S(2)}) copy-start(f32[3]{0:T(128)} %param.51) | copy-start | bytes 40
  581.8 70.2 %copy-start.21 = (f32[1,614880]{1,0:T(1,128)S(1)}, f32[1,614880]{1,0:T(1,128)}, u32[]{:S(2)}) copy-start(f32[1,614880]{1,0:T(1,128)} %param.47) | copy-start | bytes 7378564
  736.7 9.4 %copy-start.30 = (f32[8,128]{1,0:T(8,128)S(1)}, f32[8,128]{1,0:T(8,128)}, u32[]{:S(2)}) copy-start(f32[8,128]{1,0:T(8,128)} %get-tuple-element.53) | copy-start | bytes 12292
  736.7 10.0 %copy-start.1 = (bf16[640,1280]{1,0:T(8,128)(2,1)S(1)}, bf16[640,1280]{1,0:T(8,128)(2,1)}, u32[]{:S(2)}) copy-start(bf16[640,1280]{1,0:T(8,128)(2,1)} %param.45) | copy-start | bytes 4915204

commit v4 on v3

--- a/solution.py
+++ b/solution.py
@@ -104,17 +104,22 @@
     )
 
 
-def line_gather(place, src, out, local, send, recv, paired, ready=None):
+def line_gather(place, src, out, local, send, recv, paired, ready=None, rows=None):
     dp, z, c, mp, pair = place.dp, place.z, place.c, place.mp, place.pair
+
+    def at(slot):
+        if rows is None:
+            return out.at[slot]
+        return out.at[pl.ds(pl.multiple_of(slot * rows, 16), rows)]
 
     def slot_of(level, core):
         return level * 2 + core if paired else level
 
     def hop(event, slot, source, direction, target):
-        return remote(source, out.at[slot], send.at[event, direction], recv.at[slot], dp, target)
+        return remote(source, at(slot), send.at[event, direction], recv.at[slot], dp, target)
 
     own = slot_of(z, c)
-    keep = pltpu.make_async_copy(src, out.at[own], local)
+    keep = pltpu.make_async_copy(src, at(own), local)
     keep.start()
 
     def ways(event, level, slot, source, act):
@@ -142,7 +147,7 @@
         ready(own)
         if paired:
             other = slot_of(z, 1 - c)
-            hop(0, other, out.at[other], 0, pair).wait_recv()
+            hop(0, other, at(other), 0, pair).wait_recv()
             ready(other)
 
     def settle(event):
@@ -150,14 +155,14 @@
         ready(slot_of(level, c))
         if paired:
             other = slot_of(level, 1 - c)
-            hop(event, other, out.at[other], 0, pair).wait_recv()
+            hop(event, other, at(other), 0, pair).wait_recv()
             ready(other)
 
     for event in range(1, LINE):
         level = place.zorder(event)
         slot = slot_of(level, c)
-        hop(event, slot, out.at[slot], 0, pair).wait_recv()
-        ways(event, level, slot, out.at[slot], lambda copy: copy.start())
+        hop(event, slot, at(slot), 0, pair).wait_recv()
+        ways(event, level, slot, at(slot), lambda copy: copy.start())
         if ready is not None and event > 1:
             if event == 2:
                 settle(1)
@@ -167,16 +172,16 @@
         if paired:
             for level in range(LINE):
                 other = slot_of(level, 1 - c)
-                hop(0, other, out.at[other], 0, pair).wait_recv()
+                hop(0, other, at(other), 0, pair).wait_recv()
         keep.wait()
     for event in range(LINE):
         level = place.zorder(event)
         slot = slot_of(level, c)
-        ways(event, level, slot, out.at[slot], lambda copy: copy.wait_send())
+        ways(event, level, slot, at(slot), lambda copy: copy.wait_send())
     yield
 
 
-def plane_gather(place, src, out, local, send, recv, ready=None):
+def plane_gather(place, src, out, local, send, recv, ready=None, primed=False):
     dp, c, mp, pair = place.dp, place.c, place.mp, place.pair
     dpx, dpy, dpd = place.dpx, place.dpy, place.dpd
     half = src.shape[0] // 2
@@ -193,7 +198,6 @@
             ready(group * 2 + core)
 
     keep = pltpu.make_async_copy(src, at(dp, c), local)
-    keep.start()
     here = at(dp, c)
     from_x, from_y, from_d = at(dpx, c), at(dpy, c), at(dpd, c)
     firsts = [
@@ -209,6 +213,9 @@
         hop(7, from_d.at[part_a], dp, pair),
         hop(8, from_d.at[part_b], dp, pair),
     ]
+    if primed:
+        yield
+    keep.start()
     for copy in firsts:
         copy.start()
     yield
@@ -223,18 +230,21 @@
     seconds[1].start()
     seconds[2].start()
     seconds[3].start()
+    if ready is None:
+        yield
     done(dpx, c)
     hop(5, at(dpx, 1 - c), dp, pair).wait_recv()
     done(dpx, 1 - c)
-    yield
+    if ready is not None:
+        yield
+    hop(3, from_d.at[part_a], dpy, mp).wait_recv()
+    seconds[4].start()
+    hop(4, from_d.at[part_b], dpx, mp).wait_recv()
+    seconds[5].start()
     done(dpy, c)
     hop(6, at(dpy, 1 - c), dp, pair).wait_recv()
     done(dpy, 1 - c)
     yield
-    hop(3, from_d.at[part_a], dpy, mp).wait_recv()
-    seconds[4].start()
-    hop(4, from_d.at[part_b], dpx, mp).wait_recv()
-    seconds[5].start()
     done(dpd, c)
     other = at(dpd, 1 - c)
     hop(7, other.at[part_a], dp, pair).wait_recv()
@@ -292,22 +302,28 @@
 
 def line_reduce(place, produce, tiles, result, bufs, sems, paired):
     dp, z, c, mp, pair = place.dp, place.z, place.c, place.mp, place.pair
-    from_above, from_below, out_block = bufs["above"], bufs["below"], bufs["out"]
+    above_block, below_block, out_block = bufs["above"], bufs["below"], bufs["out"]
     order = [place.zorder(event) for event in (3, 2, 1, 0)]
 
     @pl.when(z == LINE - 1)
     def _():
-        from_above[...] = jnp.zeros(from_above.shape, BF)
+        above_block[...] = jnp.zeros(above_block.shape, BF)
 
     @pl.when(z == 0)
     def _():
-        from_below[...] = jnp.zeros(from_below.shape, BF)
+        below_block[...] = jnp.zeros(below_block.shape, BF)
+
+    def from_above(level):
+        return above_block.at[jnp.minimum(level, LINE - 2)]
+
+    def from_below(level):
+        return below_block.at[jnp.maximum(level - 1, 0)]
 
     def across(step, level):
         return remote(
-            bufs["pair_out"].at[step],
+            bufs["pair_out"].at[step % 2],
             bufs["pair_in"].at[level],
-            sems["pair_send"].at[step],
+            sems["pair_send"].at[step % 2],
             sems["pair_recv"].at[level],
             dp,
             pair,
@@ -315,8 +331,10 @@
 
     if paired:
         for step, level in enumerate(order):
+            if step > 1:
+                across(step - 2, order[step - 2]).wait_send()
             for rows in tiles:
-                bufs["pair_out"][step, rows] = produce(level, 1 - c, rows).astype(BF)
+                bufs["pair_out"][step % 2, rows] = produce(level, 1 - c, rows).astype(BF)
             across(step, level).start()
     yield
 
@@ -326,7 +344,7 @@
             act(
                 remote(
                     out_block.at[step],
-                    from_above.at[level],
+                    from_above(level),
                     sems["line_send"].at[step],
                     sems["above"].at[level],
                     dp,
@@ -339,7 +357,7 @@
             act(
                 remote(
                     out_block.at[step],
-                    from_below.at[level],
+                    from_below(level),
                     sems["line_send"].at[step],
                     sems["below"].at[level],
                     dp,
@@ -350,8 +368,8 @@
     def arrive(level, above):
         if above:
             remote(
-                from_above.at[level],
-                from_above.at[level],
+                from_above(level),
+                from_above(level),
                 sems["line_send"].at[0],
                 sems["above"].at[level],
                 dp,
@@ -359,8 +377,8 @@
             ).wait_recv()
         else:
             remote(
-                from_below.at[level],
-                from_below.at[level],
+                from_below(level),
+                from_below(level),
                 sems["line_send"].at[0],
                 sems["below"].at[level],
                 dp,
@@ -386,11 +404,11 @@
 
             @pl.when(level < z)
             def _():
-                out_block[step, rows] = (total + from_above[level, rows].astype(F32)).astype(BF)
+                out_block[step, rows] = (total + from_above(level)[rows].astype(F32)).astype(BF)
 
             @pl.when(level > z)
             def _():
-                out_block[step, rows] = (total + from_below[level, rows].astype(F32)).astype(BF)
+                out_block[step, rows] = (total + from_below(level)[rows].astype(F32)).astype(BF)
 
         toward(step, level, lambda copy: copy.start())
         yield
@@ -410,10 +428,10 @@
         total = produce(z, c, rows)
         if paired:
             total = total + bufs["pair_in"][z, rows].astype(F32)
-        total = total + from_above[z, rows].astype(F32) + from_below[z, rows].astype(F32)
+        total = total + from_above(z)[rows].astype(F32) + from_below(z)[rows].astype(F32)
         result(rows, total)
     for step, level in enumerate(order):
-        if paired:
+        if paired and step > 1:
             across(step, level).wait_send()
         if step < 3:
             toward(step, level, lambda copy: copy.wait_send())
@@ -422,11 +440,11 @@
 
 def line_reduce_scratch(rows, cols, paired):
     block = lambda n: pltpu.VMEM((n, rows, cols), BF)
-    scratch = {"above": block(4), "below": block(4), "out": block(3)}
+    scratch = {"above": block(3), "below": block(3), "out": block(3)}
     sems = {"line_send": dma(3), "above": dma(4), "below": dma(4)}
     if paired:
-        scratch.update({"pair_out": block(4), "pair_in": block(4)})
-        sems.update({"pair_send": dma(4), "pair_recv": dma(4)})
+        scratch.update({"pair_out": block(2), "pair_in": block(4)})
+        sems.update({"pair_send": dma(2), "pair_recv": dma(4)})
     return scratch, sems
 
 
@@ -591,13 +609,19 @@
 
 
 def attend_kernel(
-    qkv_ref, mask_ref, live_ref, weights_ref, att_ref, logs_ref, peak_ref, wfull_ref,
-    out_ref, vt_ref, local, send, recv, line_send, line_recv,
+    qkv_ref, mask_ref, live_ref, weights_ref, outer_ref,
+    att_ref, logs_ref, peak_ref, wfull_ref, ofull_ref,
+    out_ref, vt_ref, outer_all, local, send, recv, line_send, line_recv,
+    outer_send, outer_recv, plane_send, plane_recv,
 ):
     place = Place()
-    greet(place, mp_all=True)
+    greet(place, mp_all=True, plane=True)
+    outer = line_gather(
+        place, outer_ref, outer_all, local.at[2], outer_send, outer_recv, False, None, 48
+    )
+    next(outer)
     gather = line_gather(
-        place, weights_ref, wfull_ref, local.at[1], line_send, line_recv, True
+        place, weights_ref, wfull_ref, local.at[1], line_send, line_recv, False
     )
     next(gather)
     factor = math.log2(math.e) / math.sqrt(HD)
@@ -639,32 +663,52 @@
                 peak_ref[head], jnp.where(live_ref[clip, :, columns] > 0, peak, MASK_VALUE)
             )
 
-    drive(exchange(place, out_ref, att_ref, local.at[0], send, recv), gather)
-
-
-def attend(qkv, mask, live, weights):
+        @pl.when(turn == 2)
+        def _():
+            next(outer)
+
+        @pl.when(turn == 4)
+        def _():
+            next(outer)
+            next(gather)
+
+    mixing = exchange(place, out_ref, att_ref, local.at[0], send, recv)
+    next(mixing)
+    for _ in outer:
+        pass
+    spread = plane_gather(place, outer_all, ofull_ref, local.at[3], plane_send, plane_recv)
+    drive(spread, gather, mixing)
+
+
+def attend(qkv, mask, live, weights, outer):
     return pl.pallas_call(
         attend_kernel,
         out_shape=(
             jax.ShapeDtypeStruct((8, 3, 160, 128), BF),
             jax.ShapeDtypeStruct((6, 1, 1024), F32),
             jax.ShapeDtypeStruct((2, 8, 256), F32),
-            jax.ShapeDtypeStruct((8,) + weights.shape, BF),
+            jax.ShapeDtypeStruct((4,) + weights.shape, BF),
+            jax.ShapeDtypeStruct((8, 192, 1280), BF),
         ),
-        in_specs=[VMEM, VMEM, VMEM, ANY],
-        out_specs=(VMEM, VMEM, VMEM, ANY),
+        in_specs=[VMEM, VMEM, VMEM, ANY, ANY],
+        out_specs=(VMEM, VMEM, VMEM, ANY, ANY),
         scratch_shapes=[
             pltpu.VMEM((8, 3, 160, 128), BF),
             pltpu.VMEM((128, 1024), BF),
-            dma(2),
+            pltpu.VMEM((192, 1280), BF),
+            dma(4),
             dma(8),
             dma(8),
             dma(4, 3),
-            dma(8),
+            dma(4),
+            dma(4, 3),
+            dma(4),
+            dma(9),
+            dma(9),
         ],
         compiler_params=params(1),
         name="attend",
-    )(qkv, mask, live, weights)
+    )(qkv, mask, live, weights, outer)
 
 
 def flatten(*pairs):
@@ -684,7 +728,7 @@
 
 
 def feed_forward_kernel(
-    split, normed_ref, upstream_ref, up_ref, down_ref, bias_ref,
+    split, normed_ref, upstream_ref, weights_ref, bias_ref,
     total_ref, hidden_ref, grads_ref, bias_out,
     normed_all, upstream_all, slope_all, sum_ref, load, local, gather_send, gather_recv, *scratch,
 ):
@@ -699,6 +743,12 @@
     greet(place, plane=True)
     bias_out[...] = jnp.zeros(bias_out.shape, F32)
 
+    def up_rows():
+        return weights_ref[:, pl.ds(0, 160)].reshape(640, 1280)
+
+    def down_rows():
+        return weights_ref[:, pl.ds(160, 160)].reshape(640, 1280)
+
     def ready(slot):
         @pl.loop(0, 3)
         def _(step):
@@ -706,7 +756,7 @@
             before = (
                 lax.dot_general(
                     normed_all[slot, rows],
-                    up_ref[...],
+                    up_rows(),
                     (((1,), (1,)), ((), ())),
                     preferred_element_type=F32,
                 )
@@ -714,7 +764,7 @@
             )
             pull = lax.dot_general(
                 upstream_all[slot, rows],
-                down_ref[...],
+                down_rows(),
                 (((1,), (1,)), ((), ())),
                 preferred_element_type=F32,
             )
@@ -732,7 +782,7 @@
     def produce(group, core, start):
         return jnp.dot(
             slope_all[group * 2 + core, pl.ds(start, 192)],
-            up_ref[...],
+            up_rows(),
             preferred_element_type=F32,
         )
 
@@ -781,7 +831,7 @@
     drive(reduce, gather)
 
 
-def feed_forward(normed, upstream, up, down, bias):
+def feed_forward(normed, upstream, weights, bias):
     shapes, split = flatten(*plane_reduce_scratch(192, 1280))
     return pl.pallas_call(
         functools.partial(feed_forward_kernel, split),
@@ -791,7 +841,7 @@
             jax.ShapeDtypeStruct((4, 336, 1280), BF),
             jax.ShapeDtypeStruct((1, 640), F32),
         ),
-        in_specs=[ANY, ANY, VMEM, VMEM, VMEM],
+        in_specs=[ANY, ANY, VMEM, VMEM],
         out_specs=(VMEM,) * 4,
         scratch_shapes=[
             pltpu.VMEM((8, ROWS, 1280), BF),
@@ -806,16 +856,19 @@
         ],
         compiler_params=params(3, 60),
         name="feed_forward",
-    )(normed, upstream, up, down, bias)
+    )(normed, upstream, weights, bias)
 
 
 def attend_back_kernel(
-    split, qkv_ref, mask_ref, logs_ref, pull_ref, hidden_ref, down_ref, feed_grads_ref,
-    dqkv_ref, feed_ref, feed_sum_ref,
-    grad_ref, kt_ref, dk_ref, dv_ref, block_ref, local, send, recv, *scratch,
+    split, qkv_ref, mask_ref, logs_ref, pull_ref, hidden_ref, weights_ref, feed_grads_ref,
+    out_grad_ref, dqkv_ref, feed_ref, feed_sum_ref, out_sum_ref,
+    grad_ref, kt_ref, dk_ref, dv_ref, block_ref, middle_ref, local, send, recv, *scratch,
 ):
     place = Place()
-    line_bufs, line_sems, plane_bufs, plane_sems = split(scratch)
+    (
+        line_bufs, line_sems, plane_bufs, plane_sems,
+        out_plane_bufs, out_plane_sems, out_line_bufs, out_line_sems,
+    ) = split(scratch)
     greet(place, mp_all=True, plane=True)
     scale = 1.0 / math.sqrt(HD)
     factor = math.log2(math.e) * scale
@@ -825,7 +878,7 @@
     def feed_block(group, core, start):
         return jnp.dot(
             hidden_ref[group * 2 + core, pl.ds(start, 192)],
-            down_ref[...],
+            weights_ref[:, pl.ds(160, 160)].reshape(640, 1280),
             preferred_element_type=F32,
         )
 
@@ -847,12 +900,39 @@
         line_sems,
         False,
     )
-    next(plane)
+    def middle(rows, total):
+        middle_ref[rows] = total
+
+    def out_result(rows, total):
+        out_sum_ref[rows] = total
+
+    out_plane = plane_reduce(
+        place,
+        lambda group, core, start: out_grad_ref[group, core, pl.ds(start, 96)].astype(F32),
+        96,
+        96,
+        middle,
+        out_plane_bufs,
+        out_plane_sems,
+    )
+    out_line = line_reduce(
+        place,
+        lambda level, core, rows: middle_ref[
+            pl.ds(pl.multiple_of(level * 48 + rows.start, 16), rows.size)
+        ],
+        [pl.ds(0, 48)],
+        out_result,
+        out_line_bufs,
+        out_line_sems,
+        False,
+    )
+    next(line)
     next(line)
     next(plane)
+    next(plane)
+    next(out_plane)
     for _ in arriving:
         pass
-    next(line)
     block_ref[...] = jnp.zeros(block_ref.shape, BF)
 
     @pl.loop(0, 6)
@@ -907,20 +987,32 @@
             dv_ref[...].astype(BF).reshape(8, 128, 128)
         )
 
+        @pl.when(turn == 1)
+        def _():
+            next(out_plane)
+
         @pl.when(turn == 2)
         def _():
             next(plane)
 
+        @pl.when(turn == 3)
+        def _():
+            next(line)
+
         @pl.when(turn == 4)
         def _():
-            next(line)
-
-    drive(line, plane)
-
-
-def attend_back(qkv, mask, logs, pull, hidden, down, feed_grads):
+            next(out_plane)
+
+    drive(out_plane)
+    drive(out_line, line, plane)
+
+
+def attend_back(qkv, mask, logs, pull, hidden, weights, feed_grads, out_grad):
     shapes, split = flatten(
-        *line_reduce_scratch(336, 1280, False), *plane_reduce_scratch(192, 1280)
+        *line_reduce_scratch(336, 1280, False),
+        *plane_reduce_scratch(192, 1280),
+        *plane_reduce_scratch(96, 1280),
+        *line_reduce_scratch(48, 1280, False),
     )
     return pl.pallas_call(
         functools.partial(attend_back_kernel, split),
@@ -928,97 +1020,25 @@
             jax.ShapeDtypeStruct(qkv.shape, BF),
             jax.ShapeDtypeStruct((ROWS, 1280), F32),
             jax.ShapeDtypeStruct((336, 1280), F32),
+            jax.ShapeDtypeStruct((48, 1280), F32),
         ),
-        in_specs=[VMEM, VMEM, VMEM, ANY, VMEM, VMEM, VMEM],
-        out_specs=(VMEM,) * 3,
+        in_specs=[VMEM, VMEM, VMEM, ANY, VMEM, VMEM, VMEM, VMEM],
+        out_specs=(VMEM,) * 4,
         scratch_shapes=[
             pltpu.VMEM((8, 3, 160, 128), BF),
             pltpu.VMEM((128, 1024), BF),
             pltpu.VMEM((1024, 128), F32),
             pltpu.VMEM((1024, 128), F32),
             pltpu.VMEM((128, 256), BF),
+            pltpu.VMEM((192, 1280), F32),
             pltpu.SemaphoreType.DMA(()),
             dma(8),
             dma(8),
             *shapes,
         ],
-        compiler_params=params(2, 61),
+        compiler_params=params(2, 62),
         name="attend_back",
-    )(qkv, mask, logs, pull, hidden, down, feed_grads)
-
-
-def line_product_kernel(
-    split, grad_ref, weight_ref, out_grad_ref, total_ref, out_ref, middle_ref, *scratch
-):
-    place = Place()
-    bufs, sems, plane_bufs, plane_sems, out_bufs, out_sems = split(scratch)
-    greet(place, line=True, plane=True)
-
-    def produce(level, core, rows):
-        return jnp.dot(
-            grad_ref[level * 2 + core, rows], weight_ref[...], preferred_element_type=F32
-        )
-
-    def result(rows, total):
-        total_ref[rows] = total
-
-    def middle(rows, total):
-        middle_ref[rows] = total
-
-    def out_result(rows, total):
-        out_ref[rows] = total
-
-    line = line_reduce(
-        place,
-        produce,
-        [pl.ds(start, 128) for start in range(0, ROWS, 128)],
-        result,
-        bufs,
-        sems,
-        True,
-    )
-    plane = plane_reduce(
-        place,
-        lambda group, core, start: out_grad_ref[group, core, pl.ds(start, 96)].astype(F32),
-        96,
-        96,
-        middle,
-        plane_bufs,
-        plane_sems,
-    )
-    outer = line_reduce(
-        place,
-        lambda level, core, rows: middle_ref[
-            pl.ds(pl.multiple_of(level * 48 + rows.start, 16), rows.size)
-        ],
-        [pl.ds(0, 48)],
-        out_result,
-        out_bufs,
-        out_sems,
-        False,
-    )
-    drive(plane, line)
-    drive(outer)
-
-
-def line_product(grads, weight, out_grad):
-    shapes, split = flatten(
-        *line_reduce_scratch(ROWS, 1280, True),
-        *plane_reduce_scratch(96, 1280),
-        *line_reduce_scratch(48, 1280, False),
-    )
-    return pl.pallas_call(
-        functools.partial(line_product_kernel, split),
-        out_shape=(
-            jax.ShapeDtypeStruct((ROWS, 1280), F32),
-            jax.ShapeDtypeStruct((48, 1280), F32),
-        ),
-        in_specs=[VMEM, VMEM, VMEM],
-        out_specs=(VMEM, VMEM),
-        scratch_shapes=[pltpu.VMEM((192, 1280), F32), *shapes],
-        compiler_params=params(5, 60),
-        name="line_product",
-    )(grads, weight, out_grad)
+    )(qkv, mask, logs, pull, hidden, weights, feed_grads, out_grad)
 
 
 GROUP_ROWS = 4832
@@ -1034,7 +1054,6 @@
     ("up", 819520, 6400),
     ("up_bias", 1638720, 5),
     ("down", 1639360, 6400),
-    ("small", 2458560, 8),
 )
 PACK_END = 19216
 
@@ -1146,18 +1165,47 @@
     stage[pl.ds(base + 1, 1)] = jnp.where(lane < 2 * HD - 128, second, 0.0)
 
 
-def pack_reduce_kernel(
-    split, joined_ref, bias_ref, out_ref, up_ref, up_bias_ref, down_ref, small_ref, peak_ref,
-    grads_ref, small_out, peak_out,
-    stage, packed, column, small_in, small_all, peak_all,
+def stage_share(stage, name, ref, first, count, place):
+    base = TABLE[name][0] + place.dp * count * 10
+    for block in range(10):
+        stage[pl.ds(base + block, count, stride=10), :] = ref[
+            pl.ds(first, count), pl.ds(block * 128, 128)
+        ]
+
+
+def stage_up(stage, ref, place):
+    base = TABLE["up"][0]
+    lane = lane_of(128)
+    for quarter in range(4):
+
+        @pl.when(place.dp == quarter)
+        def _():
+            for block in range(10):
+                columns = pl.ds(block * 128, 128)
+                first = ref[pl.ds(0, 128), columns].T
+                second = jnp.where(lane < 32, ref[pl.ds(128, 128), columns].T, 0.0)
+                shift = 32 * quarter
+                if shift:
+                    first = pltpu.roll(first, shift, 1)
+                    second = pltpu.roll(second, shift, 1)
+                    second = second + jnp.where(lane < shift, first, 0.0)
+                    first = jnp.where(lane >= shift, first, 0.0)
+                at = base + block * 640 + quarter
+                stage[pl.ds(at, 128, stride=5), :] = first
+                stage[pl.ds(at + 1, 128, stride=5), :] = second
+
+
+def finish_kernel(
+    split, grad_ref, weight_ref, joined_ref, bias_ref, sum_ref, out_ref, up_bias_ref,
+    small_ref, peak_ref, frames_ref, middle_ref, gain_ref,
+    input_grad_ref, grads_ref, small_out, peak_out,
+    stage, packed, column, gains, tiles, small_in, small_all, peak_all, edge,
     local, small_send, small_recv, plane_send, plane_recv, *scratch,
 ):
     place = Place()
-    bufs, sems = split(scratch)
+    line_bufs, line_sems, bufs, sems = split(scratch)
     greet(place, mp_all=True, plane=True)
     peers = (place.dpx, place.dpy, place.dpd)
-    mixing = exchange(place, small_ref, small_in, local, small_send, small_recv)
-    next(mixing)
 
     def tell(index, source, target, group, act):
         act(
@@ -1177,24 +1225,48 @@
             block, block, plane_send.at[index], plane_recv.at[index], group, place.mp
         ).wait_recv()
 
+    def produce_rows(level, core, rows):
+        return jnp.dot(
+            grad_ref[level * 2 + core, rows], weight_ref[...], preferred_element_type=F32
+        )
+
+    def norm_back(rows, total):
+        value = frames_ref[rows].astype(F32)
+        center = value - jnp.mean(value, axis=-1, keepdims=True)
+        spread = jnp.mean(center * center, axis=-1, keepdims=True)
+        root = lax.rsqrt(spread + NORM_EPSILON)
+        scaled = center * root
+        gains[pl.ds(0, 1)] += jnp.sum(total * scaled, axis=0, keepdims=True)
+        gains[pl.ds(8, 1)] += jnp.sum(total, axis=0, keepdims=True)
+        pull = total * gain_ref[...]
+        along = jnp.mean(pull * scaled, axis=-1, keepdims=True)
+        input_grad_ref[rows] = middle_ref[rows] + root * (
+            pull - jnp.mean(pull, axis=-1, keepdims=True) - scaled * along
+        )
+
+    gains[...] = jnp.zeros(gains.shape, F32)
+    line = line_reduce(
+        place,
+        produce_rows,
+        [pl.ds(start, 128) for start in range(0, ROWS, 128)],
+        norm_back,
+        line_bufs,
+        line_sems,
+        True,
+    )
+    next(line)
     for index, group in enumerate(peers):
         tell(index, peak_ref, peak_all, group, lambda copy: copy.start())
+    next(line)
     stage[...] = jnp.zeros(stage.shape, F32)
     for name, lanes in (("query", 0), ("key", 256), ("value", 512)):
         stage_heads(stage, name, joined_ref, lanes, column)
     stage_head_bias(stage, "query_bias", bias_ref, 0)
     stage_head_bias(stage, "value_bias", bias_ref, 512)
-    stage_wide(stage, "out", out_ref, 160)
-    stage_wide(stage, "up", up_ref, 256)
-    stage_wide(stage, "down", down_ref, 128)
+    stage_share(stage, "out", out_ref, 0, 40, place)
+    stage_share(stage, "down", sum_ref, 160, 160, place)
+    stage_up(stage, sum_ref, place)
     stage[pl.ds(TABLE["up_bias"][0], 5)] = up_bias_ref[...]
-    for _ in mixing:
-        pass
-    share = jnp.sum(small_in[...], axis=0)
-    small_all[place.dp] = share
-    stage[pl.ds(TABLE["small"][0], 8)] = share
-    for index, group in enumerate(peers):
-        tell(3 + index, small_all.at[place.dp], small_all, group, lambda copy: copy.start())
     pack_rows(stage, packed)
 
     def produce(group, core, start):
@@ -1205,7 +1277,27 @@
         grads_ref[rows] = total
 
     half = GROUP_ROWS // 2
-    drive(plane_reduce(place, produce, half, half, result, bufs, sems, False))
+    plane = plane_reduce(place, produce, half, half, result, bufs, sems, False)
+    next(plane)
+    next(plane)
+    next(line)
+    next(plane)
+    next(line)
+    next(plane)
+    drive(line, plane)
+
+    for row in range(10):
+        tiles[pl.ds(row, 1)] = gains[pl.ds(0, 1), pl.ds(row * 128, 128)]
+        tiles[pl.ds(10 + row, 1)] = gains[pl.ds(8, 1), pl.ds(row * 128, 128)]
+    tiles[pl.ds(20, 44)] = small_ref[...]
+    for run in range(8):
+        edge[run] = tiles[pl.ds(run * 15 // 2, 8)]
+    mixing = exchange(place, edge, small_in, local, small_send, small_recv)
+    for _ in mixing:
+        pass
+    small_all[place.dp] = jnp.sum(small_in[...], axis=0)
+    for index, group in enumerate(peers):
+        tell(3 + index, small_all.at[place.dp], small_all, group, lambda copy: copy.start())
     for index, group in enumerate(peers):
         heard(index, peak_all, group)
         heard(3 + index, small_all, group)
@@ -1213,30 +1305,57 @@
     for group in peers:
         top = jnp.maximum(top, peak_all[group])
     peak_out[...] = top
-    small_out[...] = jnp.sum(small_all[...], axis=0)
+    whole = jnp.sum(small_all[...], axis=0)
+    lane = lane_of(8)
+    row = lax.broadcasted_iota(jnp.int32, (8, 128), 0)
+    tiles[pl.ds(0, 64)] = jnp.zeros((64, 128), F32)
+    tiles[pl.ds(8, 8)] = whole
+    ahead = pltpu.roll(tiles[pl.ds(9, 8)], 64, 1)
+    here = pltpu.roll(whole, 64, 1)
+    odd = jnp.where(lane < 64, here, ahead)
+    run_of = jnp.where(place.c == 1, odd, whole)
+    run_of = jnp.where(jnp.logical_and(row == 7, lane >= 64), 0.0, run_of)
+    small_out[...] = run_of
+    tiles[pl.ds(8, 8)] = run_of
+    wide = lane_of(16)
+    entry = jnp.where(
+        wide >= 64, pltpu.roll(tiles[pl.ds(1, 16)], 64, 1), pltpu.roll(tiles[pl.ds(0, 16)], 64, 1)
+    )
+
+    @pl.when(place.dp == 3)
+    def _():
+        grads_ref[pl.ds(GROUP_STEP, 16)] += entry
+
     for index, group in enumerate(peers):
         tell(index, peak_ref, peak_all, group, lambda copy: copy.wait_send())
         tell(3 + index, small_all.at[place.dp], small_all, group, lambda copy: copy.wait_send())
 
 
-def pack_reduce(joined, bias, out, up, up_bias, down, small, peaks):
-    shapes, split = flatten(*plane_reduce_scratch(GROUP_ROWS // 2, 128, False))
+def finish(grads, weight, joined, bias, sums, out, up_bias, small, peaks, frames, middle, gain):
+    shapes, split = flatten(
+        *line_reduce_scratch(ROWS, 1280, True),
+        *plane_reduce_scratch(GROUP_ROWS // 2, 128, False),
+    )
     return pl.pallas_call(
-        functools.partial(pack_reduce_kernel, split),
+        functools.partial(finish_kernel, split),
         out_shape=(
+            jax.ShapeDtypeStruct((ROWS, 1280), F32),
             jax.ShapeDtypeStruct((GROUP_ROWS, 128), F32),
             jax.ShapeDtypeStruct((8, 128), F32),
             jax.ShapeDtypeStruct(peaks.shape, F32),
         ),
-        in_specs=[VMEM] * 8,
-        out_specs=(VMEM,) * 3,
+        in_specs=[VMEM] * 12,
+        out_specs=(VMEM,) * 4,
         scratch_shapes=[
             pltpu.VMEM((STAGE_ROWS, 128), F32),
             pltpu.VMEM((PACK_ROWS, 128), BF),
             pltpu.VMEM((2, 1280, 128), F32),
+            pltpu.VMEM((16, 1280), F32),
+            pltpu.VMEM((64, 128), F32),
             pltpu.VMEM((8, 8, 128), F32),
             pltpu.VMEM((4, 8, 128), F32),
             pltpu.VMEM((4,) + peaks.shape, F32),
+            pltpu.VMEM((8, 8, 128), F32),
             pltpu.SemaphoreType.DMA(()),
             dma(8),
             dma(8),
@@ -1244,9 +1363,9 @@
             dma(6),
             *shapes,
         ],
-        compiler_params=params(7, 60),
-        name="pack_reduce",
-    )(joined, bias, out, up, up_bias, down, small, peaks)
+        compiler_params=params(7, 62),
+        name="finish",
+    )(grads, weight, joined, bias, sums, out, up_bias, small, peaks, frames, middle, gain)
 
 
 def share_master_kernel(rows_ref, whole_ref, parts, send, recv):
@@ -1360,20 +1479,18 @@
     down_share = lax.dynamic_slice_in_dim(down_weight, quarter, 160, 0)
     bias_share = lax.dynamic_slice_in_dim(up_bias, quarter, 160, 0)
     bias_rows = jnp.pad(bias_share[None], ((0, 15), (0, 1280 - 160)))
-    message = jnp.concatenate([up_share, down_share, bias_rows, out_weight])
-    attended, logs, peaks, gathered = attend(qkv, mask, live, message)
-    core = lax.axis_index("mp") % 2
-    own_core = lax.dynamic_slice_in_dim(gathered.reshape(4, 2, 496, 1280), core, 1, 1)[:, 0]
-    up_rows = own_core[:, :160].reshape(640, 1280)
-    down_rows = own_core[:, 160:320].reshape(640, 1280)
-    up_lanes = own_core[:, 320, :160].reshape(640).astype(F32)
-    out_rows = gathered[:, 336:]
+    message = jnp.concatenate([up_share, down_share, bias_rows])
+    outer = jnp.pad(lax.dynamic_slice_in_dim(out_weight, group * 40, 40, 0), ((0, 8), (0, 0)))
+    attended, logs, peaks, gathered, outer_all = attend(qkv, mask, live, message, outer)
+    up_lanes = gathered[:, 320, :160].reshape(1, 640).astype(F32)
+    out_rows = outer_all.reshape(4, 2, 4, 48, 1280)[:, :, :, :40]
+    out_rows = out_rows.transpose(2, 1, 0, 3, 4).reshape(8, 160, 1280)
 
     branch = jnp.einsum("schr,shd->crd", attended, out_rows, preferred_element_type=F32)
     middle = inputs + branch.reshape(ROWS, 1280) + out_bias.astype(F32)
     normed_two = layer_norm(middle, gain_second, shift_second).astype(BF)
     normed_two_grad, hidden, feed_grads, _ = feed_forward(
-        normed_two, upstream_full, up_rows, down_rows, up_lanes[None]
+        normed_two, upstream_full, gathered, up_lanes
     )
 
     _, norm_two_pull = jax.vjp(layer_norm, middle, gain_second, shift_second)
@@ -1389,57 +1506,43 @@
         out_grad.astype(BF).reshape(4, 2, 4, 40, 1280), ((0, 0),) * 3 + ((0, 8), (0, 0))
     )
     out_quarters = out_quarters.transpose(2, 1, 0, 3, 4).reshape(4, 2, 192, 1280)
-    joined_grad, feed, feed_sum = attend_back(
-        qkv, mask, logs, attended_grad, hidden, down_rows, feed_grads
+    joined_grad, feed, feed_sum, out_sum = attend_back(
+        qkv, mask, logs, attended_grad, hidden, gathered, feed_grads, out_quarters
     )
     layer_out = (middle + feed + down_bias.astype(F32)).astype(BF)
     joined_grad = joined_grad.reshape(8, ROWS, 768)
-    normed_grad, out_sum = line_product(joined_grad, joined_weight, out_quarters)
     joined_weight_grad = jnp.einsum(
         "prd,pre->de", normed_full, joined_grad, preferred_element_type=F32
     )
     joined_bias_grad = jnp.sum(joined_grad.astype(F32), axis=(0, 1))
 
-    _, norm_one_pull = jax.vjp(layer_norm, inputs, gain_first, shift_first)
-    input_norm_grad, gain_one_grad, shift_one_grad = norm_one_pull(normed_grad)
-    input_grad = middle_grad + input_norm_grad
-
-    def spread(rows):
-        size = rows.shape[0]
-        return lax.dynamic_update_slice(
-            jnp.zeros((4 * size,) + rows.shape[1:], F32),
-            rows,
-            (size * group,) + (0,) * (rows.ndim - 1),
-        )
-
-    up_whole = spread(feed_sum[:160]).T
-    down_whole = spread(feed_sum[160:320])
     level = lax.axis_index("mp") // 2
-    up_bias_whole = spread(lax.dynamic_slice_in_dim(feed_sum[320], level * 160, 160, 0))
-    out_whole = spread(out_sum[:40])
-
-    out_bias_grad = jnp.sum(branch_grad.astype(F32), axis=0)
-    down_bias_grad = jnp.sum(upstream, axis=0)
-    small_terms = jnp.concatenate(
+    up_bias_share = lax.dynamic_slice_in_dim(feed_sum[320], level * 160, 160, 0)
+    up_bias_rows = lax.dynamic_update_slice(
+        jnp.zeros((640,), F32), up_bias_share, (quarter,)
+    ).reshape(5, 128)
+    small_rows = jnp.concatenate(
         [
-            gain_one_grad,
-            shift_one_grad,
-            out_bias_grad,
+            jnp.sum(branch_grad.astype(F32), axis=0),
             gain_two_grad,
             shift_two_grad,
-            down_bias_grad,
+            jnp.sum(upstream, axis=0),
+            jnp.zeros((512,), F32),
         ]
-    )
-    small_tiles = jnp.pad(small_terms.reshape(8, 960), ((0, 0), (0, 64))).reshape(8, 8, 128)
-    grad_rows, small_sum, peak_sum = pack_reduce(
+    ).reshape(44, 128)
+    input_grad, grad_rows, small_sum, peak_sum = finish(
+        joined_grad,
+        joined_weight,
         joined_weight_grad,
         joined_bias_grad[None],
-        out_whole,
-        up_whole,
-        up_bias_whole.reshape(5, 128),
-        down_whole,
-        small_tiles,
+        feed_sum,
+        out_sum,
+        up_bias_rows,
+        small_rows,
         peaks,
+        frames.transpose(1, 0, 2).reshape(ROWS, 1280),
+        middle_grad,
+        gain_first[None],
     )
     small_total = small_sum.reshape(1024)[:960]
     head_peak = jnp.max(peak_sum, axis=(1, 2)) / math.sqrt(HD)
@@ -1453,8 +1556,8 @@
     step_count = adam_step[0].astype(F32)
     first_new = BETA_FIRST * moment_one + (1.0 - BETA_FIRST) * owned_grads
     second_new = BETA_SECOND * moment_two + (1.0 - BETA_SECOND) * owned_grads * owned_grads
-    first_hat = first_new / (1.0 - jnp.power(BETA_FIRST, step_count))
-    second_hat = second_new / (1.0 - jnp.power(BETA_SECOND, step_count))
+    first_hat = first_new * (learn_rate / (1.0 - jnp.power(BETA_FIRST, step_count)))
+    second_hat = second_new * (1.0 / (1.0 - jnp.power(BETA_SECOND, step_count)))
     entry_index = group * share_size + lax.broadcasted_iota(jnp.int32, (1, share_size), 1)
     query_end = 1280 * 160
     query_bias_end = query_end + 160
@@ -1465,8 +1568,8 @@
     head_factor = jnp.where(odd, root_factor[1], root_factor[0])
     factor = jnp.where(entry_index < key_end, head_factor, 1.0)
     master_new = (
-        master
-        - learn_rate * (first_hat / (jnp.sqrt(second_hat) + ADAM_EPSILON) + weight_decay * master)
+        master * (1.0 - learn_rate * weight_decay)
+        - first_hat / (jnp.sqrt(second_hat) + ADAM_EPSILON)
     ) * factor
 
     def placed_rows(offset):

time: 758 us -> 690 us (0.910)
  Pallas kernels: 611 us -> 559 us
  other arithmetic: 57.4 us -> 42.3 us
    pallas_call x2 -> x1, Pallas kernels: 171 us -> 110 us  [finish(): pl.pallas_call(functools.partial(finish_kernel, split), out_shape=(jax.Sh...]
    pallas_call x1, Pallas kernels: 99.6 us -> 134 us  [attend_back(): pl.pallas_call(functools.partial(attend_back_kernel, split), out_shape=(j...]
    pallas_call x1, Pallas kernels: 113 us -> 90.2 us  [attend(): pl.pallas_call(attend_kernel, out_shape=(jax.ShapeDtypeStruct((8, 3, 160,...]
where the time goes in v4:
time: 690 us; the launch traced here: 678 us
  Pallas kernels  559 us (81%)
  local copies, waits for them, and re-layouts  50.4 us (7%)
  other arithmetic  42.3 us (6%)
  matrix products  21.3 us (3%)
    pallas_call x1, Pallas kernels, attend_back(): pl.pallas_call(functools.partial(attend_back_kernel, split), out_shape=(j...  134 us
    pallas_call x1, Pallas kernels, finish(): pl.pallas_call(functools.partial(finish_kernel, split), out_shape=(jax.Sh...  110 us
    pallas_call x1, Pallas kernels, feed_forward(): pl.pallas_call(functools.partial(feed_forward_kernel, split), out_shape=(...  97.8 us
    pallas_call x1, Pallas kernels, attend(): pl.pallas_call(attend_kernel, out_shape=(jax.ShapeDtypeStruct((8, 3, 160,...  90.2 us
    pallas_call x1, Pallas kernels, project(): pl.pallas_call(project_kernel, out_shape=(jax.ShapeDtypeStruct((8,) + nor...  79.8 us
    pallas_call x1, Pallas kernels, share_master(): pl.pallas_call(share_master_kernel, out_shape=jax.ShapeDtypeStruct((PACK_...  48.3 us
    mul x1, other arithmetic, fast_body(): (master * (1.0 - learn_rate * weight_decay) - first_hat / (jnp.sqrt(secon...  27.8 us
    unnamed x87, local copies, waits for them, and re-layouts  14.2 us

profile of v4, /device:TPU:0, one launch (start us, length us, event | category | flops | bytes accessed | tf_op | source)
XLA Modules:
  0.0 677.6 jit_solution(10651158535818180814)
XLA Ops:
  0.7 1.4 copy-done
  2.1 1.1 constant_dynamic-slice_fusion.4
  3.2 1.3 copy.53
  4.5 1.1 constant_dynamic-slice_fusion.3
  5.6 0.8 dynamic_slice.22
  6.4 1.0 fusion.21.weights_ref
  7.4 1.0 constant_dynamic-slice_fusion.2
  8.3 0.7 pad.53.outer_ref
  10.7 1.2 copy-done.6
  11.9 79.8 %project.1 = (bf16[8,384,1280]{2,1,0:T(8,128)(2,1)}, bf16[8,384,768]{2,1,0:T(8,128)(2,1)S(1)}, bf16[8,384,1280]{2,1,0:T(8,128)(2,1)}) custom-call(bf16[384,1280]{1,0:T(8,128)(2,1)S(1)} %fusion.16.normed_ref, bf16[384,1280]{1,0:T(8,128)(2,1)S(1)} %bitcast.99, bf16[768,1280]{1,0:T(8,128)(2,1)S(1)} %pad_maximum_fusion.weight_ref, ...), custom_call_target="tpu_custom_call" | custom-call | tf_op jit(solution)/shard_map/project/pallas_call | solution.py:596
  91.7 2.2 copy-done.2
  93.9 1.7 copy.38.mask_ref
  95.7 1.4 copy-done.4
  97.1 1.2 copy-done.8
  98.2 0.9 copy-done.11
  99.1 90.2 %attend.1 = (bf16[8,3,160,128]{3,2,1,0:T(8,128)(2,1)S(1)}, f32[6,1,1024]{2,1,0:T(1,128)S(1)}, f32[2,8,256]{2,1,0:T(8,128)S(1)}, bf16[4,336,1280]{2,1,0:T(8,128)(2,1)S(1)}, bf16[8,192,1280]{2,1,0:T(8,128)(2,1)S(1)}) custom-call(bf16[8,3,128,768]{3,2,1,0:T(8,128)(2,1)} %bitcast.97, f32[3,1024,1]{2,1,0:T(8,128)S(1)} %copy-done.4, ...), custom_call_target="tpu_custom_call" | custom-call | tf_op jit(solution)/shard_map/attend/pallas_call | solution.py:684
  190.0 2.4 copy.40
  192.4 1.7 copy.39
  194.1 3.7 reshape.335
  197.8 5.0 fusion.29
  203.3 1.3 add_convert_fusion.1.normed_ref
  204.6 0.7 reshape.326.bias_ref
  205.3 97.8 %feed_forward.1 = (f32[384,1280]{1,0:T(8,128)}, bf16[8,384,640]{2,1,0:T(8,128)(2,1)}, bf16[4,336,1280]{2,1,0:T(8,128)(2,1)}, f32[1,640]{1,0:T(1,128)}) custom-call(bf16[384,1280]{1,0:T(8,128)(2,1)} %add_convert_fusion.1.normed_ref, bf16[8,384,1280]{2,1,0:T(8,128)(2,1)} %get-tuple-element.41.upstream_ref, bf16[4,336,1280]{2,1,0:T(8,128)(2,1)} %copy-done.5, ...), custom_call_target="tpu_custom_call" | custom-call | tf_op jit(solution)/shard_map/feed_forward/pallas_call | solution.py:836
  303.1 2.3 multiply_reduce_fusion
  305.5 0.6 fusion.26
  306.7 1.7 convert_reduce_fusion.3
  308.6 2.0 bitcast_convert_fusion
  310.9 2.3 pad.54
  313.2 1.0 copy-done.20
  314.2 2.8 fusion.20.pull_ref
  317.1 133.9 %attend_back.1 = (bf16[8,3,128,768]{3,2,1,0:T(8,128)(2,1)}, f32[384,1280]{1,0:T(8,128)}, f32[336,1280]{1,0:T(8,128)}, f32[48,1280]{1,0:T(8,128)}) custom-call(bf16[8,3,128,768]{3,2,1,0:T(8,128)(2,1)} %bitcast.98, f32[3,1024,1]{2,1,0:T(8,128)} %copy.38.mask_ref, f32[6,1,1024]{2,1,0:T(1,128)} %copy-done.12, bf16[8,3,160,128]{3,2,1,0:T(8,128)(2,1)} %fusion.20.pull_ref, ...), custom_call_target="tpu_custom_call" | custom-call | tf_op jit(solution)/shard_map/attend_back/pallas_call | solution.py:1017
  451.0 11.4 %convolution_bitcast_fusion.joined_ref = f32[1280,768]{1,0:T(8,128)} fusion(bf16[8,384,1280]{2,1,0:T(8,128)(2,1)} %get-tuple-element.48, bf16[8,384,768]{2,1,0:T(8,128)(2,1)} %bitcast.103), kind=kOutput, calls=%fused_computation.5 | convolution fusion | flops 6039797760 | bytes 16515072 | tf_op jit(solution)/shard_map/prd,pre->de/dot_general | solution.py:1514
  462.4 0.8 slice.33
  463.4 3.1 convert_reduce_fusion
  467.1 0.6 broadcast_in_dim.77.gain_ref
  467.7 109.5 %finish.1 = (f32[384,1280]{1,0:T(8,128)}, f32[4832,128]{1,0:T(8,128)}, f32[8,128]{1,0:T(8,128)}, f32[2,8,256]{2,1,0:T(8,128)}) custom-call(bf16[8,384,768]{2,1,0:T(8,128)(2,1)} %bitcast.104, bf16[768,1280]{1,0:T(8,128)(2,1)} %copy-done.3, f32[1280,768]{1,0:T(8,128)} %convolution_bitcast_fusion.joined_ref, f32[1,768]{1,0:T(1,128)} %broadcast_in_dim.74.bias_ref, ...), custom_call_target="tpu_custom_call" | custom-call | tf_op jit(solution)/shard_map/finish/pallas_call | solution.py:1339
  577.2 0.8 reduce_max.9
  578.6 0.7 divide_sqrt_fusion
  579.3 0.6 fusion.28
  582.6 27.8 %fusion.12 = (f32[1,614880]{1,0:T(1,128)}, f32[1,614880]{1,0:T(1,128)}, f32[1,614880]{1,0:T(1,128)}, f32[1,614880]{1,0:T(1,128)}) fusion(f32[1,614880]{1,0:T(1,128)} %param.47, f32[]{:T(128)} %bitcast.53, f32[]{:T(128)} %bitcast.52, s32[]{:T(128)S(6)} %mul.236, f32[]{:T(128)} %bitcast.50, f32[]{:T(128)} %bitcast.49, f32[]{:T(128)} %bitcast.48, ...), kind=kLoop, calls=%fused_computation.15 | loop fusion | flops 16601760 | bytes 19676188 | tf_op jit(solution)/shard_map/mul | solution.py:1570
  610.4 5.1 conditional.1
  610.4 5.1 pad.35
  615.5 48.3 %share_master.1 = f32[19216,128]{1,0:T(8,128)} custom-call(f32[4832,128]{1,0:T(8,128)S(1)} %bitcast.108), custom_call_target="tpu_custom_call" | custom-call | tf_op jit(solution)/shard_map/share_master/pallas_call | solution.py:1408
  663.9 9.8 %slice.46 = bf16[1,2459520]{1,0:T(2,128)(2,1)} slice(f32[1,2459648]{1,0:T(1,128)} %bitcast.102), slice={[0:1], [0:2459520]} | slice | bytes 9838080 | tf_op jit(solution)/shard_map/slice | solution.py:1582
  673.7 1.2 add_convert_fusion
  674.9 0.7 copy-done.22
  675.6 1.3 copy.77
  676.9 0.6 copy.78
  (116 shorter events, 5.3 us)
Async XLA Ops:
  0.6 1.4 copy-start
  2.1 6.9 %copy-start.17 = (bf16[128,3,1280]{2,0,1:T(8,128)(2,1)S(1)}, bf16[128,3,1280]{2,0,1:T(8,128)(2,1)}, u32[]{:S(2)}) copy-start(bf16[128,3,1280]{2,0,1:T(8,128)(2,1)} %param.28) | copy-start | bytes 2949124
  4.5 5.1 copy-start.28
  4.5 5.2 copy-start.31
  4.5 5.2 copy-start.18
  7.4 2.8 copy-start.38
  7.4 2.8 copy-start.39
  7.4 3.0 copy-start.23
  9.0 1.4 copy-start.24
  9.2 1.3 copy-start.25
  10.5 1.4 copy-start.6
  10.7 84.9 %copy-start.3 = (bf16[768,1280]{1,0:T(8,128)(2,1)}, bf16[768,1280]{1,0:T(8,128)(2,1)S(1)}, u32[]{:S(2)}) copy-start(bf16[768,1280]{1,0:T(8,128)(2,1)S(1)} %pad_maximum_fusion.weight_ref) | copy-start | bytes 5898244
  10.7 83.2 %copy-start.29 = (s32[3,1024]{1,0:T(4,128)S(1)}, s32[3,1024]{1,0:T(4,128)}, u32[]{:S(2)}) copy-start(s32[3,1024]{1,0:T(4,128)} %param.30) | copy-start | bytes 36868
  10.7 83.1 %copy-start.37 = (s32[3]{0:T(128)S(1)}, s32[3]{0:T(128)}, u32[]{:S(2)}) copy-start(s32[3]{0:T(128)} %param.29) | copy-start | bytes 40
  91.7 2.2 copy-start.2
  95.7 1.4 copy-start.4
  97.1 1.2 copy-start.8
  98.2 0.9 copy-start.11
  189.3 0.6 copy-start.12
  189.4 0.6 copy-start.13
  189.4 3.0 copy-start.9
  189.4 15.2 %copy-start.5 = (bf16[4,336,1280]{2,1,0:T(8,128)(2,1)}, bf16[4,336,1280]{2,1,0:T(8,128)(2,1)S(1)}, u32[]{:S(2)}) copy-start(bf16[4,336,1280]{2,1,0:T(8,128)(2,1)S(1)} %get-tuple-element.42.weights_ref) | copy-start | bytes 10321924
  192.4 5.4 copy-start.32
  197.8 5.4 copy-start.33
  197.8 5.4 copy-start.34
  202.9 1.7 copy-start.14
  205.3 97.8 %copy-start.15 = (f32[384,1280]{1,0:T(8,128)S(1)}, f32[384,1280]{1,0:T(8,128)}, u32[]{:S(2)}) copy-start(f32[384,1280]{1,0:T(8,128)} %copy-done.14) | copy-start | bytes 5898244
  303.1 2.4 copy-start.19
  305.5 1.2 copy-start.7
  306.7 1.9 copy-start.10
  308.6 2.1 copy-start.26
  310.9 3.3 copy-start.20
  463.4 4.3 copy-start.27
  467.7 110.4 %copy-start.30 = (f32[3]{0:T(128)S(1)}, f32[3]{0:T(128)}, u32[]{:S(2)}) copy-start(f32[3]{0:T(128)} %param.51) | copy-start | bytes 40
  663.8 9.8 %copy-start.35 = (bf16[1280]{0:T(1024)(128)(2,1)S(1)}, bf16[1280]{0:T(1024)(128)(2,1)}, u32[]{:S(2)}) copy-start(bf16[1280]{0:T(1024)(128)(2,1)} %param.46) | copy-start | bytes 7684
  663.8 9.8 %copy-start.16 = (f32[384,1280]{1,0:T(8,128)S(1)}, f32[384,1280]{1,0:T(8,128)}, u32[]{:S(2)}) copy-start(f32[384,1280]{1,0:T(8,128)} %copy-done.14) | copy-start | bytes 5898244
  663.8 9.8 %copy-start.21 = (f32[384,1280]{1,0:T(8,128)S(1)}, f32[384,1280]{1,0:T(8,128)}, u32[]{:S(2)}) copy-start(f32[384,1280]{1,0:T(8,128)} %get-tuple-element.46) | copy-start | bytes 5898244
  673.7 1.9 copy-start.22
  673.7 3.8 copy-start.1
  674.9 2.0 copy-start.36

commit v5 on v4

--- a/solution.py
+++ b/solution.py
@@ -237,14 +237,15 @@
     done(dpx, 1 - c)
     if ready is not None:
         yield
+    done(dpy, c)
+    hop(6, at(dpy, 1 - c), dp, pair).wait_recv()
+    done(dpy, 1 - c)
+    if ready is not None:
+        yield
     hop(3, from_d.at[part_a], dpy, mp).wait_recv()
     seconds[4].start()
     hop(4, from_d.at[part_b], dpx, mp).wait_recv()
     seconds[5].start()
-    done(dpy, c)
-    hop(6, at(dpy, 1 - c), dp, pair).wait_recv()
-    done(dpy, 1 - c)
-    yield
     done(dpd, c)
     other = at(dpd, 1 - c)
     hop(7, other.at[part_a], dp, pair).wait_recv()
@@ -304,6 +305,8 @@
     dp, z, c, mp, pair = place.dp, place.z, place.c, place.mp, place.pair
     above_block, below_block, out_block = bufs["above"], bufs["below"], bufs["out"]
     order = [place.zorder(event) for event in (3, 2, 1, 0)]
+    inner = jnp.logical_and(z > 0, z < LINE - 1)
+    outer = jnp.logical_or(z == 0, z == LINE - 1)
 
     @pl.when(z == LINE - 1)
     def _():
@@ -385,7 +388,8 @@
                 mp,
             ).wait_recv()
 
-    for step, level in enumerate(order[:3]):
+    def advance(step):
+        level = order[step]
         if paired:
             across(step, level).wait_recv()
 
@@ -411,6 +415,21 @@
                 out_block[step, rows] = (total + from_below(level)[rows].astype(F32)).astype(BF)
 
         toward(step, level, lambda copy: copy.start())
+
+    advance(0)
+    for step in (1, 2):
+
+        @pl.when(outer)
+        def _():
+            advance(step)
+
+    yield
+    for step in (1, 2):
+
+        @pl.when(inner)
+        def _():
+            advance(step)
+
         yield
 
     if paired:
@@ -860,8 +879,9 @@
 
 
 def attend_back_kernel(
-    split, qkv_ref, mask_ref, logs_ref, pull_ref, hidden_ref, weights_ref, feed_grads_ref,
-    out_grad_ref, dqkv_ref, feed_ref, feed_sum_ref, out_sum_ref,
+    split, qkv_in, mask_ref, logs_ref, pull_ref, hidden_in, weights_ref, feed_grads_in,
+    out_grad_in, dqkv_ref, feed_ref, feed_sum_ref, out_sum_ref,
+    qkv_ref, hidden_ref, feed_grads_ref, out_grad_ref, load,
     grad_ref, kt_ref, dk_ref, dv_ref, block_ref, middle_ref, local, send, recv, *scratch,
 ):
     place = Place()
@@ -869,6 +889,19 @@
         line_bufs, line_sems, plane_bufs, plane_sems,
         out_plane_bufs, out_plane_sems, out_line_bufs, out_line_sems,
     ) = split(scratch)
+    loads = [
+        pltpu.make_async_copy(source, target, load.at[index])
+        for index, (source, target) in enumerate(
+            (
+                (out_grad_in, out_grad_ref),
+                (feed_grads_in, feed_grads_ref),
+                (hidden_in, hidden_ref),
+                (qkv_in, qkv_ref),
+            )
+        )
+    ]
+    for copy in loads:
+        copy.start()
     greet(place, mp_all=True, plane=True)
     scale = 1.0 / math.sqrt(HD)
     factor = math.log2(math.e) * scale
@@ -926,11 +959,18 @@
         out_line_sems,
         False,
     )
+    loads[0].wait()
+    next(out_plane)
     next(line)
+    next(out_line)
+    loads[1].wait()
     next(line)
+    next(out_plane)
+    loads[2].wait()
     next(plane)
     next(plane)
     next(out_plane)
+    loads[3].wait()
     for _ in arriving:
         pass
     block_ref[...] = jnp.zeros(block_ref.shape, BF)
@@ -987,24 +1027,21 @@
             dv_ref[...].astype(BF).reshape(8, 128, 128)
         )
 
-        @pl.when(turn == 1)
-        def _():
-            next(out_plane)
-
-        @pl.when(turn == 2)
-        def _():
-            next(plane)
-
-        @pl.when(turn == 3)
-        def _():
-            next(line)
-
-        @pl.when(turn == 4)
-        def _():
-            next(out_plane)
-
-    drive(out_plane)
-    drive(out_line, line, plane)
+        for when, programs in (
+            (0, (out_plane, out_line)),
+            (1, (line,)),
+            (2, (plane,)),
+            (3, (out_line,)),
+            (4, (line,)),
+            (5, (out_line,)),
+        ):
+
+            @pl.when(turn == when)
+            def _():
+                for program in programs:
+                    next(program)
+
+    drive(line, out_line, plane, out_plane)
 
 
 def attend_back(qkv, mask, logs, pull, hidden, weights, feed_grads, out_grad):
@@ -1022,9 +1059,11 @@
             jax.ShapeDtypeStruct((336, 1280), F32),
             jax.ShapeDtypeStruct((48, 1280), F32),
         ),
-        in_specs=[VMEM, VMEM, VMEM, ANY, VMEM, VMEM, VMEM, VMEM],
+        in_specs=[ANY, VMEM, VMEM, ANY, ANY, VMEM, ANY, ANY],
         out_specs=(VMEM,) * 4,
         scratch_shapes=[
+            *(pltpu.VMEM(ref.shape, BF) for ref in (qkv, hidden, feed_grads, out_grad)),
+            dma(4),
             pltpu.VMEM((8, 3, 160, 128), BF),
             pltpu.VMEM((128, 1024), BF),
             pltpu.VMEM((1024, 128), F32),
@@ -1195,11 +1234,43 @@
                 stage[pl.ds(at + 1, 128, stride=5), :] = second
 
 
+def norm_back(place, frames_ref, middle_ref, gain_ref, grad_ref, offset):
+    def write(rows, total):
+        rows_in = pl.ds(offset + rows.start, rows.size)
+        value = frames_ref[rows_in].astype(F32)
+        center = value - jnp.mean(value, axis=-1, keepdims=True)
+        spread = jnp.mean(center * center, axis=-1, keepdims=True)
+        root = lax.rsqrt(spread + NORM_EPSILON)
+        scaled = center * root
+        pull = total * gain_ref[...]
+        along = jnp.mean(pull * scaled, axis=-1, keepdims=True)
+        grad_ref[rows] = middle_ref[rows_in] + root * (
+            pull - jnp.mean(pull, axis=-1, keepdims=True) - scaled * along
+        )
+
+    return write
+
+
+def line_product(place, grad_ref, weight_ref, offset, rows, result, bufs, sems):
+    def produce(level, core, tile):
+        return jnp.dot(
+            grad_ref[level * 2 + core, pl.ds(offset + tile.start, tile.size)],
+            weight_ref[...],
+            preferred_element_type=F32,
+        )
+
+    tiles = [pl.ds(start, 128) for start in range(0, rows, 128)]
+    return line_reduce(place, produce, tiles, result, bufs, sems, True)
+
+
+FIRST_ROWS = 256
+
+
 def finish_kernel(
-    split, grad_ref, weight_ref, joined_ref, bias_ref, sum_ref, out_ref, up_bias_ref,
-    small_ref, peak_ref, frames_ref, middle_ref, gain_ref,
+    split, grad_ref, weight_ref, joined_ref, bias_ref, bias_column_ref, sum_ref, out_ref,
+    up_bias_ref, small_ref, peak_ref, frames_ref, middle_ref, gain_ref, shift_ref,
     input_grad_ref, grads_ref, small_out, peak_out,
-    stage, packed, column, gains, tiles, small_in, small_all, peak_all, edge,
+    stage, packed, column, tiles, small_in, small_all, peak_all, edge,
     local, small_send, small_recv, plane_send, plane_recv, *scratch,
 ):
     place = Place()
@@ -1225,39 +1296,35 @@
             block, block, plane_send.at[index], plane_recv.at[index], group, place.mp
         ).wait_recv()
 
-    def produce_rows(level, core, rows):
-        return jnp.dot(
-            grad_ref[level * 2 + core, rows], weight_ref[...], preferred_element_type=F32
-        )
-
-    def norm_back(rows, total):
-        value = frames_ref[rows].astype(F32)
-        center = value - jnp.mean(value, axis=-1, keepdims=True)
-        spread = jnp.mean(center * center, axis=-1, keepdims=True)
-        root = lax.rsqrt(spread + NORM_EPSILON)
-        scaled = center * root
-        gains[pl.ds(0, 1)] += jnp.sum(total * scaled, axis=0, keepdims=True)
-        gains[pl.ds(8, 1)] += jnp.sum(total, axis=0, keepdims=True)
-        pull = total * gain_ref[...]
-        along = jnp.mean(pull * scaled, axis=-1, keepdims=True)
-        input_grad_ref[rows] = middle_ref[rows] + root * (
-            pull - jnp.mean(pull, axis=-1, keepdims=True) - scaled * along
-        )
-
-    gains[...] = jnp.zeros(gains.shape, F32)
-    line = line_reduce(
+    line = line_product(
         place,
-        produce_rows,
-        [pl.ds(start, 128) for start in range(0, ROWS, 128)],
-        norm_back,
+        grad_ref,
+        weight_ref,
+        0,
+        FIRST_ROWS,
+        norm_back(place, frames_ref, middle_ref, gain_ref, input_grad_ref, 0),
         line_bufs,
         line_sems,
-        True,
-    )
-    next(line)
+    )
     for index, group in enumerate(peers):
         tell(index, peak_ref, peak_all, group, lambda copy: copy.start())
     next(line)
+    next(line)
+
+    for block in range(10):
+        lanes = pl.ds(block * 128, 128)
+        weight = weight_ref[:, lanes].astype(F32)
+        turned = joined_ref[lanes].T
+        whole = jnp.sum(weight * bias_column_ref[...], axis=0, keepdims=True)
+        along = jnp.sum(weight * turned, axis=0, keepdims=True)
+        tiles[pl.ds(block, 1)] = (along - shift_ref[:, lanes] * whole) / gain_ref[:, lanes]
+        tiles[pl.ds(10 + block, 1)] = whole
+    tiles[pl.ds(20, 44)] = small_ref[...]
+    for run in range(8):
+        edge[run] = tiles[pl.ds(run * 15 // 2, 8)]
+    mixing = exchange(place, edge, small_in, local, small_send, small_recv)
+    next(mixing)
+
     stage[...] = jnp.zeros(stage.shape, F32)
     for name, lanes in (("query", 0), ("key", 256), ("value", 512)):
         stage_heads(stage, name, joined_ref, lanes, column)
@@ -1280,24 +1347,16 @@
     plane = plane_reduce(place, produce, half, half, result, bufs, sems, False)
     next(plane)
     next(plane)
+    for _ in mixing:
+        pass
+    small_all[place.dp] = jnp.sum(small_in[...], axis=0)
+    for index, group in enumerate(peers):
+        tell(3 + index, small_all.at[place.dp], small_all, group, lambda copy: copy.start())
     next(line)
     next(plane)
     next(line)
     next(plane)
     drive(line, plane)
-
-    for row in range(10):
-        tiles[pl.ds(row, 1)] = gains[pl.ds(0, 1), pl.ds(row * 128, 128)]
-        tiles[pl.ds(10 + row, 1)] = gains[pl.ds(8, 1), pl.ds(row * 128, 128)]
-    tiles[pl.ds(20, 44)] = small_ref[...]
-    for run in range(8):
-        edge[run] = tiles[pl.ds(run * 15 // 2, 8)]
-    mixing = exchange(place, edge, small_in, local, small_send, small_recv)
-    for _ in mixing:
-        pass
-    small_all[place.dp] = jnp.sum(small_in[...], axis=0)
-    for index, group in enumerate(peers):
-        tell(3 + index, small_all.at[place.dp], small_all, group, lambda copy: copy.start())
     for index, group in enumerate(peers):
         heard(index, peak_all, group)
         heard(3 + index, small_all, group)
@@ -1308,7 +1367,7 @@
     whole = jnp.sum(small_all[...], axis=0)
     lane = lane_of(8)
     row = lax.broadcasted_iota(jnp.int32, (8, 128), 0)
-    tiles[pl.ds(0, 64)] = jnp.zeros((64, 128), F32)
+    tiles[...] = jnp.zeros((64, 128), F32)
     tiles[pl.ds(8, 8)] = whole
     ahead = pltpu.roll(tiles[pl.ds(9, 8)], 64, 1)
     here = pltpu.roll(whole, 64, 1)
@@ -1331,26 +1390,25 @@
         tell(3 + index, small_all.at[place.dp], small_all, group, lambda copy: copy.wait_send())
 
 
-def finish(grads, weight, joined, bias, sums, out, up_bias, small, peaks, frames, middle, gain):
+def finish(grads, weight, joined, bias, sums, out, up_bias, small, peaks, frames, middle, gain, shift):
     shapes, split = flatten(
-        *line_reduce_scratch(ROWS, 1280, True),
+        *line_reduce_scratch(FIRST_ROWS, 1280, True),
         *plane_reduce_scratch(GROUP_ROWS // 2, 128, False),
     )
     return pl.pallas_call(
         functools.partial(finish_kernel, split),
         out_shape=(
-            jax.ShapeDtypeStruct((ROWS, 1280), F32),
+            jax.ShapeDtypeStruct((FIRST_ROWS, 1280), F32),
             jax.ShapeDtypeStruct((GROUP_ROWS, 128), F32),
             jax.ShapeDtypeStruct((8, 128), F32),
             jax.ShapeDtypeStruct(peaks.shape, F32),
         ),
-        in_specs=[VMEM] * 12,
+        in_specs=[VMEM] * 14,
         out_specs=(VMEM,) * 4,
         scratch_shapes=[
             pltpu.VMEM((STAGE_ROWS, 128), F32),
             pltpu.VMEM((PACK_ROWS, 128), BF),
             pltpu.VMEM((2, 1280, 128), F32),
-            pltpu.VMEM((16, 1280), F32),
             pltpu.VMEM((64, 128), F32),
             pltpu.VMEM((8, 8, 128), F32),
             pltpu.VMEM((4, 8, 128), F32),
@@ -1365,12 +1423,29 @@
         ],
         compiler_params=params(7, 62),
         name="finish",
-    )(grads, weight, joined, bias, sums, out, up_bias, small, peaks, frames, middle, gain)
-
-
-def share_master_kernel(rows_ref, whole_ref, parts, send, recv):
+    )(
+        grads, weight, joined, bias[None], bias[:, None], sums, out, up_bias, small, peaks,
+        frames, middle, gain, shift,
+    )
+
+
+def share_master_kernel(
+    split, rows_ref, grad_ref, weight_ref, frames_ref, middle_ref, gain_ref,
+    whole_ref, input_grad_ref, parts, send, recv, *scratch,
+):
     place = Place()
-    greet(place, plane=True, pair=False)
+    line_bufs, line_sems = split(scratch)
+    greet(place, line=True, plane=True)
+    line = line_product(
+        place,
+        grad_ref,
+        weight_ref,
+        FIRST_ROWS,
+        ROWS - FIRST_ROWS,
+        norm_back(place, frames_ref, middle_ref, gain_ref, input_grad_ref, FIRST_ROWS),
+        line_bufs,
+        line_sems,
+    )
     dp, mp, dpx, dpy, dpd = place.dp, place.mp, place.dpx, place.dpy, place.dpd
     half = GROUP_ROWS // 2
     part_a, part_b = pl.ds(0, half), pl.ds(half, half)
@@ -1383,12 +1458,16 @@
     sends = [hop(0, own, dpx), hop(1, own, dpy)]
     for copy in sends:
         copy.start()
+    next(line)
+    next(line)
     hop(0, parts.at[dpx], dpx).wait_recv()
     sends.append(hop(2, parts.at[dpx, part_a], dpy))
     sends[-1].start()
     hop(1, parts.at[dpy], dpy).wait_recv()
     sends.append(hop(3, parts.at[dpy, part_b], dpx))
     sends[-1].start()
+    next(line)
+    next(line)
     hop(2, parts.at[dpd, part_a], dpy).wait_recv()
     hop(3, parts.at[dpd, part_b], dpx).wait_recv()
     for group in range(4):
@@ -1402,18 +1481,23 @@
     whole_ref[pl.ds(4 * GROUP_STEP, 16)] = parts[3, pl.ds(GROUP_STEP, 16)].astype(F32)
     for copy in sends:
         copy.wait_send()
-
-
-def share_master(rows):
+    drive(line)
+
+
+def share_master(rows, grads, weight, frames, middle, gain):
+    shapes, split = flatten(*line_reduce_scratch(ROWS - FIRST_ROWS, 1280, True))
     return pl.pallas_call(
-        share_master_kernel,
-        out_shape=jax.ShapeDtypeStruct((PACK_END, 128), F32),
-        in_specs=[VMEM],
-        out_specs=VMEM,
-        scratch_shapes=[pltpu.VMEM((4, GROUP_ROWS, 128), BF), dma(4), dma(4)],
+        functools.partial(share_master_kernel, split),
+        out_shape=(
+            jax.ShapeDtypeStruct((PACK_END, 128), F32),
+            jax.ShapeDtypeStruct((ROWS - FIRST_ROWS, 1280), F32),
+        ),
+        in_specs=[VMEM] * 6,
+        out_specs=(VMEM, VMEM),
+        scratch_shapes=[pltpu.VMEM((4, GROUP_ROWS, 128), BF), dma(4), dma(4), *shapes],
         compiler_params=params(8, 60),
         name="share_master",
-    )(rows)
+    )(rows, grads, weight, frames, middle, gain)
 
 
 def fast_body(
@@ -1530,19 +1614,21 @@
             jnp.zeros((512,), F32),
         ]
     ).reshape(44, 128)
-    input_grad, grad_rows, small_sum, peak_sum = finish(
+    frame_rows = frames.transpose(1, 0, 2).reshape(ROWS, 1280)
+    first_grad, grad_rows, small_sum, peak_sum = finish(
         joined_grad,
         joined_weight,
         joined_weight_grad,
-        joined_bias_grad[None],
+        joined_bias_grad,
         feed_sum,
         out_sum,
         up_bias_rows,
         small_rows,
         peaks,
-        frames.transpose(1, 0, 2).reshape(ROWS, 1280),
+        frame_rows,
         middle_grad,
         gain_first[None],
+        shift_first[None],
     )
     small_total = small_sum.reshape(1024)[:960]
     head_peak = jnp.max(peak_sum, axis=(1, 2)) / math.sqrt(HD)
@@ -1577,8 +1663,11 @@
         return lambda value: jnp.pad(value, ((0, 0), (offset, room))).reshape(GROUP_ROWS, 128)
 
     master_rows = lax.switch(group, [placed_rows(480 * part) for part in range(4)], master_new)
-    whole = share_master(master_rows).reshape(1, PACK_END * 128)
-    whole = lax.optimization_barrier(whole)
+    whole, second_grad = share_master(
+        master_rows, joined_grad, joined_weight, frame_rows, middle_grad, gain_first[None]
+    )
+    input_grad = jnp.concatenate([first_grad, second_grad])
+    whole = lax.optimization_barrier(whole.reshape(1, PACK_END * 128))
     weights_new = whole[:, : 4 * share_size].astype(BF)
     return (
         layer_out.reshape(3, 128, 1280).transpose(1, 0, 2),

time: 690 us -> 663 us (0.961)
  Pallas kernels: 559 us -> 540 us
  local copies, waits for them, and re-layouts: 50.4 us -> 43.3 us
    pallas_call x1, Pallas kernels: 110 us -> 83.9 us  [finish(): pl.pallas_call(functools.partial(finish_kernel, split), out_shape=(jax.Sh...]
    pallas_call x1, Pallas kernels: 48.3 us -> 62.5 us  [share_master(): pl.pallas_call(functools.partial(share_master_kernel, split), out_shape=(...]
    unnamed x87 -> x84, local copies, waits for them, and re-layouts: 14.2 us -> 12.3 us
where the time goes in v5:
time: 663 us; the launch traced here: 652 us
  Pallas kernels  540 us (81%)
  local copies, waits for them, and re-layouts  43.3 us (7%)
  other arithmetic  43.1 us (7%)
  matrix products  21.5 us (3%)
    pallas_call x1, Pallas kernels, attend_back(): pl.pallas_call(functools.partial(attend_back_kernel, split), out_shape=(j...  130 us
    pallas_call x1, Pallas kernels, feed_forward(): pl.pallas_call(functools.partial(feed_forward_kernel, split), out_shape=(...  93.4 us
    pallas_call x1, Pallas kernels, attend(): pl.pallas_call(attend_kernel, out_shape=(jax.ShapeDtypeStruct((8, 3, 160,...  90.2 us
    pallas_call x1, Pallas kernels, finish(): pl.pallas_call(functools.partial(finish_kernel, split), out_shape=(jax.Sh...  83.9 us
    pallas_call x1, Pallas kernels, project(): pl.pallas_call(project_kernel, out_shape=(jax.ShapeDtypeStruct((8,) + nor...  79.8 us
    pallas_call x1, Pallas kernels, share_master(): pl.pallas_call(functools.partial(share_master_kernel, split), out_shape=(...  62.5 us
    mul x1, other arithmetic, fast_body(): (master * (1.0 - learn_rate * weight_decay) - first_hat / (jnp.sqrt(secon...  27.8 us

profile of v5, /device:TPU:0, one launch (start us, length us, event | category | flops | bytes accessed | tf_op | source)
XLA Modules:
  0.0 651.8 jit_solution(9854401185255102107)
XLA Ops:
  0.7 1.4 copy-done
  2.6 1.1 constant_dynamic-slice_fusion.3
  3.7 0.8 dynamic_slice.22
  4.4 1.0 fusion.21.weights_ref
  5.4 0.9 constant_dynamic-slice_fusion.2
  6.7 1.0 copy-done.16
  8.3 1.4 fusion.16.normed_ref
  10.0 1.2 copy-done.7
  11.2 79.8 %project.1 = (bf16[8,384,1280]{2,1,0:T(8,128)(2,1)}, bf16[8,384,768]{2,1,0:T(8,128)(2,1)S(1)}, bf16[8,384,1280]{2,1,0:T(8,128)(2,1)}) custom-call(bf16[384,1280]{1,0:T(8,128)(2,1)S(1)} %copy-done.7, bf16[384,1280]{1,0:T(8,128)(2,1)S(1)} %bitcast.102, bf16[768,1280]{1,0:T(8,128)(2,1)S(1)} %pad_maximum_fusion.weight_ref, f32[1,768]{1,0:T(1,128)S(1)} %broadcast_in_dim.74.bias_ref), custom_call_target="tpu_custom_call" | custom-call | tf_op jit(solution)/shard_map/project/pallas_call | solution.py:615
  91.0 2.2 copy-done.3
  93.9 1.7 copy-done.8
  95.5 90.2 %attend.1 = (bf16[8,3,160,128]{3,2,1,0:T(8,128)(2,1)S(1)}, f32[6,1,1024]{2,1,0:T(1,128)S(1)}, f32[2,8,256]{2,1,0:T(8,128)S(1)}, bf16[4,336,1280]{2,1,0:T(8,128)(2,1)S(1)}, bf16[8,192,1280]{2,1,0:T(8,128)(2,1)S(1)}) custom-call(bf16[8,3,128,768]{3,2,1,0:T(8,128)(2,1)} %bitcast.100, f32[3,1024,1]{2,1,0:T(8,128)S(1)} %copy.38.mask_ref, ...), custom_call_target="tpu_custom_call" | custom-call | tf_op jit(solution)/shard_map/attend/pallas_call | solution.py:703
  186.0 1.5 copy-done.5
  187.5 1.9 copy.40
  189.5 0.7 copy.39
  190.2 1.6 reshape.339
  191.8 5.0 fusion.29
  197.3 1.3 add_convert_fusion.1.normed_ref
  198.6 0.7 convert_reduce_fusion.4
  199.3 0.7 reshape.330.bias_ref
  200.0 93.4 %feed_forward.1 = (f32[384,1280]{1,0:T(8,128)}, bf16[8,384,640]{2,1,0:T(8,128)(2,1)}, bf16[4,336,1280]{2,1,0:T(8,128)(2,1)}, f32[1,640]{1,0:T(1,128)}) custom-call(bf16[384,1280]{1,0:T(8,128)(2,1)} %add_convert_fusion.1.normed_ref, bf16[8,384,1280]{2,1,0:T(8,128)(2,1)} %get-tuple-element.42.upstream_ref, bf16[4,336,1280]{2,1,0:T(8,128)(2,1)} %copy-done.5, ...), custom_call_target="tpu_custom_call" | custom-call | tf_op jit(solution)/shard_map/feed_forward/pallas_call | solution.py:855
  293.4 2.3 multiply_reduce_fusion
  295.8 0.6 fusion.26
  296.4 1.7 convert_reduce_fusion.3
  298.3 2.0 bitcast_convert_fusion
  300.6 2.3 pad.54
  303.0 1.0 copy-done.18
  304.0 2.8 fusion.20.pull_ref
  306.8 130.0 %attend_back.1 = (bf16[8,3,128,768]{3,2,1,0:T(8,128)(2,1)}, f32[384,1280]{1,0:T(8,128)}, f32[336,1280]{1,0:T(8,128)}, f32[48,1280]{1,0:T(8,128)}) custom-call(bf16[8,3,128,768]{3,2,1,0:T(8,128)(2,1)} %bitcast.101, f32[3,1024,1]{2,1,0:T(8,128)} %copy-done.4, f32[6,1,1024]{2,1,0:T(1,128)} %copy-done.11, bf16[8,3,160,128]{3,2,1,0:T(8,128)(2,1)} %fusion.20.pull_ref, ...), custom_call_target="tpu_custom_call" | custom-call | tf_op jit(solution)/shard_map/attend_back/pallas_call | solution.py:1054
  436.8 11.5 %convolution_bitcast_fusion.joined_ref = f32[1280,768]{1,0:T(8,128)} fusion(bf16[8,384,1280]{2,1,0:T(8,128)(2,1)} %get-tuple-element.49, bf16[8,384,768]{2,1,0:T(8,128)(2,1)} %bitcast.105), kind=kOutput, calls=%fused_computation.5 | convolution fusion | flops 6039797760 | bytes 16515072 | tf_op jit(solution)/shard_map/prd,pre->de/dot_general | solution.py:1598
  448.4 0.7 convert_reduce_fusion
  449.1 0.9 broadcast_in_dim.90.bias_column_ref
  450.0 0.8 slice.33
  451.6 0.6 broadcast_in_dim.85.gain_ref
  452.2 0.6 broadcast_in_dim.86.shift_ref
  452.8 83.9 %finish.1 = (f32[256,1280]{1,0:T(8,128)}, f32[4832,128]{1,0:T(8,128)}, f32[8,128]{1,0:T(8,128)}, f32[2,8,256]{2,1,0:T(8,128)}) custom-call(bf16[8,384,768]{2,1,0:T(8,128)(2,1)} %bitcast.106, bf16[768,1280]{1,0:T(8,128)(2,1)} %copy-done.2, f32[1280,768]{1,0:T(8,128)} %convolution_bitcast_fusion.joined_ref, f32[1,768]{1,0:T(1,128)} %broadcast_in_dim.81.bias_ref, ...), custom_call_target="tpu_custom_call" | custom-call | tf_op jit(solution)/shard_map/finish/pallas_call | solution.py:1398
  536.7 0.8 reduce_max.9
  538.1 0.7 divide_sqrt_fusion
  538.8 0.6 fusion.28
  542.1 27.8 %fusion.12 = (f32[1,614880]{1,0:T(1,128)}, f32[1,614880]{1,0:T(1,128)}, f32[1,614880]{1,0:T(1,128)}, f32[1,614880]{1,0:T(1,128)}) fusion(f32[1,614880]{1,0:T(1,128)} %param.47, f32[]{:T(128)} %bitcast.55, f32[]{:T(128)} %bitcast.54, s32[]{:T(128)S(6)} %mul.236, f32[]{:T(128)} %bitcast.52, f32[]{:T(128)} %bitcast.51, f32[]{:T(128)} %bitcast.49, ...), kind=kLoop, calls=%fused_computation.15 | loop fusion | flops 16601760 | bytes 19676188 | tf_op jit(solution)/shard_map/mul | solution.py:1656
  569.9 5.1 conditional.1
  569.9 5.1 pad.35
  575.0 62.5 %share_master.1 = (f32[19216,128]{1,0:T(8,128)}, f32[128,1280]{1,0:T(8,128)}) custom-call(f32[4832,128]{1,0:T(8,128)S(1)} %get-tuple-element.98.rows_ref, bf16[8,384,768]{2,1,0:T(8,128)(2,1)} %bitcast.107, bf16[768,1280]{1,0:T(8,128)(2,1)} %copy-done.2, bf16[384,1280]{1,0:T(8,128)(2,1)} %bitcast.110, f32[384,1280]{1,0:T(8,128)} %get-tuple-element.68.middle_ref, ...), custom_call_target="tpu_custom_call" | custom-call | tf_op jit(solution)/shard_map/share_master/pallas_call | solution.py:1489
  637.6 9.4 %slice.46 = bf16[1,2459520]{1,0:T(2,128)(2,1)} slice(f32[1,2459648]{1,0:T(1,128)} %bitcast.116), slice={[0:1], [0:2459520]} | slice | bytes 9838080 | tf_op jit(solution)/shard_map/slice | solution.py:1671
  647.0 1.4 pad_maximum_fusion.1
  648.4 0.8 copy-done.14
  649.8 1.2 add_convert_fusion
  651.0 0.6 copy.77
  (116 shorter events, 5.5 us)
Async XLA Ops:
  0.6 1.4 copy-start
  2.1 4.3 copy-start.22
  2.4 4.0 copy-start.23
  2.6 3.9 copy-start.24
  6.5 1.2 copy-start.16
  6.5 1.8 copy-start.27
  6.5 1.8 copy-start.28
  7.7 83.3 %copy-start.2 = (bf16[768,1280]{1,0:T(8,128)(2,1)}, bf16[768,1280]{1,0:T(8,128)(2,1)S(1)}, u32[]{:S(2)}) copy-start(bf16[768,1280]{1,0:T(8,128)(2,1)S(1)} %pad_maximum_fusion.weight_ref) | copy-start | bytes 5898244
  7.7 2.1 copy-start.37
  7.7 2.2 copy-start.38
  7.7 2.3 copy-start.6
  9.7 83.4 %copy-start.29 = (s32[3,1024]{1,0:T(4,128)S(1)}, s32[3,1024]{1,0:T(4,128)}, u32[]{:S(2)}) copy-start(s32[3,1024]{1,0:T(4,128)} %param.30) | copy-start | bytes 36868
  9.7 83.4 %copy-start.36 = (s32[3]{0:T(128)S(1)}, s32[3]{0:T(128)}, u32[]{:S(2)}) copy-start(s32[3]{0:T(128)} %param.29) | copy-start | bytes 40
  10.0 1.2 copy-start.7
  91.0 2.2 copy-start.3
  93.8 92.0 %copy-start.4 = (f32[3,1024,1]{2,1,0:T(8,128)}, f32[3,1024,1]{2,1,0:T(8,128)S(1)}, u32[]{:S(2)}) copy-start(f32[3,1024,1]{2,1,0:T(8,128)S(1)} %copy.38.mask_ref) | copy-start | bytes 36868
  93.9 1.7 copy-start.8
  185.7 1.8 copy-start.5
  185.8 1.8 copy-start.11
  185.8 1.8 copy-start.12
  185.8 3.7 copy-start.9
  189.5 2.3 copy-start.31
  191.8 5.4 copy-start.32
  191.8 5.4 copy-start.33
  196.9 98.9 %copy-start.13 = (f32[384,1280]{1,0:T(8,128)}, f32[384,1280]{1,0:T(8,128)S(1)}, u32[]{:S(2)}) copy-start(f32[384,1280]{1,0:T(8,128)S(1)} %get-tuple-element.79) | copy-start | bytes 5898244
  293.4 2.4 copy-start.17
  296.4 1.9 copy-start.10
  298.3 2.1 copy-start.25
  300.6 3.3 copy-start.18
  436.8 11.5 %copy-start.15 = (bf16[8,3,128,768]{3,2,1,0:T(8,128)(2,1)S(1)}, bf16[8,3,128,768]{3,2,1,0:T(8,128)(2,1)}, u32[]{:S(2)}) copy-start(bf16[8,3,128,768]{3,2,1,0:T(8,128)(2,1)} %get-tuple-element.48) | copy-start | bytes 14155780
  451.1 1.8 copy-start.26
  452.8 84.7 %copy-start.30 = (f32[3]{0:T(128)S(1)}, f32[3]{0:T(128)}, u32[]{:S(2)}) copy-start(f32[3]{0:T(128)} %param.51) | copy-start | bytes 40
  637.6 9.4 %copy-start.20 = (f32[256,1280]{1,0:T(8,128)S(1)}, f32[256,1280]{1,0:T(8,128)}, u32[]{:S(2)}) copy-start(f32[256,1280]{1,0:T(8,128)} %get-tuple-element.53) | copy-start | bytes 3932164
  637.6 9.4 %copy-start.21 = (f32[128,1280]{1,0:T(8,128)S(1)}, f32[128,1280]{1,0:T(8,128)}, u32[]{:S(2)}) copy-start(f32[128,1280]{1,0:T(8,128)} %get-tuple-element.56) | copy-start | bytes 1966084
  647.0 1.4 copy-start.34
  647.0 2.3 copy-start.14
  647.0 2.9 copy-start.19
  648.4 3.2 copy-start.1
  649.8 1.2 copy-start.35

commit v6 on v5

--- a/solution.py
+++ b/solution.py
@@ -230,8 +230,7 @@
     seconds[1].start()
     seconds[2].start()
     seconds[3].start()
-    if ready is None:
-        yield
+    yield
     done(dpx, c)
     hop(5, at(dpx, 1 - c), dp, pair).wait_recv()
     done(dpx, 1 - c)
@@ -542,6 +541,7 @@
         yield
         cross("far")
         far()
+        yield
         cross("own")
     else:
         cross("far")
@@ -585,10 +585,20 @@
 
 
 def project_kernel(
-    normed_ref, cot_ref, weight_ref, bias_ref, nfull_ref, qkv_ref, cfull_ref,
-    local, line_send, line_recv, plane_send, plane_recv,
+    frames_ref, gain_ref, shift_ref, cot_ref, query_ref, key_ref, value_ref, bias_ref,
+    nfull_ref, qkv_ref, cfull_ref, weight_ref,
+    normed_ref, local, line_send, line_recv, plane_send, plane_recv,
 ):
     place = Place()
+    weight_ref[...] = jnp.zeros(weight_ref.shape, BF)
+    for index, ref in enumerate((query_ref, key_ref, value_ref)):
+        for head in range(2):
+            weight_ref[pl.ds(index * 256 + head * 128, HD)] = ref[pl.ds(head * HD, HD)]
+    for start in range(0, ROWS, 128):
+        rows = pl.ds(start, 128)
+        normed_ref[rows] = layer_norm(
+            frames_ref[rows].astype(F32), gain_ref[...], shift_ref[...]
+        ).astype(BF)
     greet(place, line=True, plane=True)
 
     def ready(slot):
@@ -611,20 +621,21 @@
     )
 
 
-def project(normed, cotangent, weight, bias):
+def project(frames, gain, shift, cotangent, query, key, value, bias):
     return pl.pallas_call(
         project_kernel,
         out_shape=(
-            jax.ShapeDtypeStruct((8,) + normed.shape, BF),
-            jax.ShapeDtypeStruct((8, ROWS, weight.shape[0]), BF),
+            jax.ShapeDtypeStruct((8,) + frames.shape, BF),
+            jax.ShapeDtypeStruct((8, ROWS, 768), BF),
             jax.ShapeDtypeStruct((8,) + cotangent.shape, BF),
+            jax.ShapeDtypeStruct((768, 1280), BF),
         ),
-        in_specs=[ANY, ANY, VMEM, VMEM],
-        out_specs=(VMEM, VMEM, ANY),
-        scratch_shapes=[dma(2), dma(4, 3), dma(8), dma(9), dma(9)],
+        in_specs=[VMEM, VMEM, VMEM, ANY, VMEM, VMEM, VMEM, VMEM],
+        out_specs=(VMEM, VMEM, ANY, VMEM),
+        scratch_shapes=[pltpu.VMEM((ROWS, 1280), BF), dma(2), dma(4, 3), dma(8), dma(9), dma(9)],
         compiler_params=params(0),
         name="project",
-    )(normed, cotangent, weight, bias)
+    )(frames, gain, shift, cotangent, query, key, value, bias)
 
 
 def attend_kernel(
@@ -747,9 +758,10 @@
 
 
 def feed_forward_kernel(
-    split, normed_ref, upstream_ref, weights_ref, bias_ref,
-    total_ref, hidden_ref, grads_ref, bias_out,
-    normed_all, upstream_all, slope_all, sum_ref, load, local, gather_send, gather_recv, *scratch,
+    split, normed_ref, upstream_ref, weights_ref, down_ref, bias_ref,
+    total_ref, hidden_ref, grads_ref, bias_out, down_all,
+    normed_all, upstream_all, slope_all, rate_ref, sum_ref,
+    load, local, line_local, gather_send, gather_recv, line_send, line_recv, *scratch,
 ):
     place = Place()
     bufs, sems = split(scratch)
@@ -759,41 +771,71 @@
             pltpu.make_async_copy(upstream_ref.at[slot], upstream_all.at[slot], load.at[slot])
         )
         loads[-1].start()
-    greet(place, plane=True)
+    greet(place, line=True, plane=True)
     bias_out[...] = jnp.zeros(bias_out.shape, F32)
 
     def up_rows():
         return weights_ref[:, pl.ds(0, 160)].reshape(640, 1280)
 
     def down_rows():
-        return weights_ref[:, pl.ds(160, 160)].reshape(640, 1280)
-
-    def ready(slot):
-        @pl.loop(0, 3)
-        def _(step):
-            rows = pl.ds(step * 128, 128)
-            before = (
-                lax.dot_general(
-                    normed_all[slot, rows],
-                    up_rows(),
-                    (((1,), (1,)), ((), ())),
-                    preferred_element_type=F32,
-                )
-                + bias_ref[...]
-            )
-            pull = lax.dot_general(
-                upstream_all[slot, rows],
-                down_rows(),
+        return down_all[...].reshape(640, 1280)
+
+    def activate(slot, rows):
+        before = (
+            lax.dot_general(
+                normed_all[slot, rows],
+                up_rows(),
                 (((1,), (1,)), ((), ())),
                 preferred_element_type=F32,
             )
-            share = 0.5 + 0.5 * lax.erf(before * math.sqrt(0.5))
-            hidden_ref[slot, rows] = (before * share).astype(BF)
-            density = jnp.exp(before * before * -0.5) * (1.0 / math.sqrt(2.0 * math.pi))
-            slope = (pull * (share + before * density)).astype(BF)
-            slope_all[slot, rows] = slope
-            bias_out[...] += jnp.sum(slope.astype(F32), axis=0, keepdims=True)
-
+            + bias_ref[...]
+        )
+        share = 0.5 + 0.5 * lax.erf(before * math.sqrt(0.5))
+        hidden_ref[slot, rows] = (before * share).astype(BF)
+        density = jnp.exp(before * before * -0.5) * (1.0 / math.sqrt(2.0 * math.pi))
+        return share + before * density
+
+    def pull_back(slot, rows, rate):
+        pull = lax.dot_general(
+            upstream_all[slot, rows],
+            down_rows(),
+            (((1,), (1,)), ((), ())),
+            preferred_element_type=F32,
+        )
+        slope = (pull * rate).astype(BF)
+        slope_all[slot, rows] = slope
+        bias_out[...] += jnp.sum(slope.astype(F32), axis=0, keepdims=True)
+
+    here = [place.dp * 2 + place.c, place.dp * 2 + 1 - place.c]
+    seen = []
+
+    def ready(slot):
+        index = len(seen)
+        seen.append(slot)
+
+        @pl.loop(0, 3)
+        def _(step):
+            rows = pl.ds(pl.multiple_of(step * 128, 128), 128)
+            rate = activate(slot, rows)
+            if index < 2:
+                rate_ref[index, rows] = rate
+            else:
+                pull_back(slot, rows, rate)
+
+        if index < 2:
+            next(down)
+
+    def finish_here():
+        for index in range(2):
+
+            @pl.loop(0, 3)
+            def _(step):
+                rows = pl.ds(pl.multiple_of(step * 128, 128), 128)
+                pull_back(here[index], rows, rate_ref[index, rows])
+
+    down = line_gather(
+        place, down_ref, down_all, line_local, line_send, line_recv, False
+    )
     gather = plane_gather(
         place, normed_ref, normed_all, local, gather_send, gather_recv, ready
     )
@@ -809,14 +851,20 @@
         total_ref[rows] = total
 
     reduce = plane_reduce(place, produce, 192, 192, result, bufs, sems, True, True)
+    next(down)
     next(gather)
     for copy in loads:
         copy.wait()
+    next(gather)
+    for _ in down:
+        pass
     next(gather)
     next(reduce)
     next(gather)
     next(reduce)
     next(gather)
+    next(reduce)
+    finish_here()
     next(reduce)
 
     def weight_grads(left_all, right_all, base):
@@ -850,7 +898,7 @@
     drive(reduce, gather)
 
 
-def feed_forward(normed, upstream, weights, bias):
+def feed_forward(normed, upstream, weights, down, bias):
     shapes, split = flatten(*plane_reduce_scratch(192, 1280))
     return pl.pallas_call(
         functools.partial(feed_forward_kernel, split),
@@ -859,23 +907,28 @@
             jax.ShapeDtypeStruct((8, ROWS, 640), BF),
             jax.ShapeDtypeStruct((4, 336, 1280), BF),
             jax.ShapeDtypeStruct((1, 640), F32),
+            jax.ShapeDtypeStruct((4, 160, 1280), BF),
         ),
-        in_specs=[ANY, ANY, VMEM, VMEM],
-        out_specs=(VMEM,) * 4,
+        in_specs=[ANY, ANY, VMEM, ANY, VMEM],
+        out_specs=(VMEM,) * 5,
         scratch_shapes=[
             pltpu.VMEM((8, ROWS, 1280), BF),
             pltpu.VMEM((8, ROWS, 1280), BF),
             pltpu.VMEM((8, ROWS, 640), BF),
+            pltpu.VMEM((2, ROWS, 640), F32),
             pltpu.VMEM((128, 1280), F32),
             dma(8),
             pltpu.SemaphoreType.DMA(()),
+            pltpu.SemaphoreType.DMA(()),
             dma(9),
             dma(9),
+            dma(4, 3),
+            dma(4),
             *shapes,
         ],
         compiler_params=params(3, 60),
         name="feed_forward",
-    )(normed, upstream, weights, bias)
+    )(normed, upstream, weights, down, bias)
 
 
 def attend_back_kernel(
@@ -911,7 +964,7 @@
     def feed_block(group, core, start):
         return jnp.dot(
             hidden_ref[group * 2 + core, pl.ds(start, 192)],
-            weights_ref[:, pl.ds(160, 160)].reshape(640, 1280),
+            weights_ref[...].reshape(640, 1280),
             preferred_element_type=F32,
         )
 
@@ -961,15 +1014,14 @@
     )
     loads[0].wait()
     next(out_plane)
-    next(line)
-    next(out_line)
-    loads[1].wait()
-    next(line)
     next(out_plane)
     loads[2].wait()
     next(plane)
     next(plane)
-    next(out_plane)
+    loads[1].wait()
+    next(line)
+    next(line)
+    next(out_line)
     loads[3].wait()
     for _ in arriving:
         pass
@@ -1027,19 +1079,14 @@
             dv_ref[...].astype(BF).reshape(8, 128, 128)
         )
 
-        for when, programs in (
-            (0, (out_plane, out_line)),
-            (1, (line,)),
-            (2, (plane,)),
-            (3, (out_line,)),
-            (4, (line,)),
-            (5, (out_line,)),
-        ):
-
-            @pl.when(turn == when)
-            def _():
-                for program in programs:
-                    next(program)
+        @pl.when(turn == 2)
+        def _():
+            next(out_plane)
+            next(plane)
+
+        @pl.when(turn == 5)
+        def _():
+            next(out_plane)
 
     drive(line, out_line, plane, out_plane)
 
@@ -1095,6 +1142,7 @@
     ("down", 1639360, 6400),
 )
 PACK_END = 19216
+SHARE_ROWS = 4808
 
 
 def segment_table():
@@ -1270,7 +1318,7 @@
     split, grad_ref, weight_ref, joined_ref, bias_ref, bias_column_ref, sum_ref, out_ref,
     up_bias_ref, small_ref, peak_ref, frames_ref, middle_ref, gain_ref, shift_ref,
     input_grad_ref, grads_ref, small_out, peak_out,
-    stage, packed, column, tiles, small_in, small_all, peak_all, edge,
+    stage, packed, sum_rows, column, tiles, small_in, small_all, peak_all, edge,
     local, small_send, small_recv, plane_send, plane_recv, *scratch,
 ):
     place = Place()
@@ -1341,7 +1389,7 @@
         return packed[pl.ds(first, GROUP_ROWS // 2)].astype(F32)
 
     def result(rows, total):
-        grads_ref[rows] = total
+        sum_rows[rows] = total
 
     half = GROUP_ROWS // 2
     plane = plane_reduce(place, produce, half, half, result, bufs, sems, False)
@@ -1383,7 +1431,23 @@
 
     @pl.when(place.dp == 3)
     def _():
-        grads_ref[pl.ds(GROUP_STEP, 16)] += entry
+        sum_rows[pl.ds(GROUP_STEP, 16)] += entry
+
+    for group in range(4):
+
+        @pl.when(place.dp == group)
+        def _():
+            down, shift = 480 * group // 128, 480 * group % 128
+            if shift == 0:
+                grads_ref[...] = sum_rows[pl.ds(0, SHARE_ROWS)]
+            else:
+                for first in range(0, SHARE_ROWS, 1208):
+                    size = min(1208, SHARE_ROWS - first)
+                    grads_ref[pl.ds(first, size)] = jnp.where(
+                        lane_of(size) < 128 - shift,
+                        pltpu.roll(sum_rows[pl.ds(first + down, size)], 128 - shift, 1),
+                        pltpu.roll(sum_rows[pl.ds(first + down + 1, size)], 128 - shift, 1),
+                    )
 
     for index, group in enumerate(peers):
         tell(index, peak_ref, peak_all, group, lambda copy: copy.wait_send())
@@ -1399,7 +1463,7 @@
         functools.partial(finish_kernel, split),
         out_shape=(
             jax.ShapeDtypeStruct((FIRST_ROWS, 1280), F32),
-            jax.ShapeDtypeStruct((GROUP_ROWS, 128), F32),
+            jax.ShapeDtypeStruct((SHARE_ROWS, 128), F32),
             jax.ShapeDtypeStruct((8, 128), F32),
             jax.ShapeDtypeStruct(peaks.shape, F32),
         ),
@@ -1408,6 +1472,7 @@
         scratch_shapes=[
             pltpu.VMEM((STAGE_ROWS, 128), F32),
             pltpu.VMEM((PACK_ROWS, 128), BF),
+            pltpu.VMEM((GROUP_ROWS, 128), F32),
             pltpu.VMEM((2, 1280, 128), F32),
             pltpu.VMEM((64, 128), F32),
             pltpu.VMEM((8, 8, 128), F32),
@@ -1431,7 +1496,7 @@
 
 def share_master_kernel(
     split, rows_ref, grad_ref, weight_ref, frames_ref, middle_ref, gain_ref,
-    whole_ref, input_grad_ref, parts, send, recv, *scratch,
+    whole_ref, input_grad_ref, parts, turned, send, recv, *scratch,
 ):
     place = Place()
     line_bufs, line_sems = split(scratch)
@@ -1449,7 +1514,24 @@
     dp, mp, dpx, dpy, dpd = place.dp, place.mp, place.dpx, place.dpy, place.dpd
     half = GROUP_ROWS // 2
     part_a, part_b = pl.ds(0, half), pl.ds(half, half)
-    parts[dp] = rows_ref[...].astype(BF)
+    for group in range(4):
+
+        @pl.when(dp == group)
+        def _():
+            down, shift = 480 * group // 128, 480 * group % 128
+            turned[pl.ds(0, 16)] = jnp.zeros((16, 128), F32)
+            turned[pl.ds(16, SHARE_ROWS)] = rows_ref[...]
+            turned[pl.ds(16 + SHARE_ROWS, 24)] = jnp.zeros((24, 128), F32)
+            for first in range(0, GROUP_ROWS, 1208):
+                here = turned[pl.ds(16 + first - down, 1208)]
+                if shift:
+                    here = jnp.where(
+                        lane_of(1208) >= shift,
+                        pltpu.roll(here, shift, 1),
+                        pltpu.roll(turned[pl.ds(15 + first - down, 1208)], shift, 1),
+                    )
+                parts[dp, pl.ds(first, 1208)] = here.astype(BF)
+
 
     def hop(index, block, target):
         return remote(block, block, send.at[index], recv.at[index], target, mp)
@@ -1494,10 +1576,60 @@
         ),
         in_specs=[VMEM] * 6,
         out_specs=(VMEM, VMEM),
-        scratch_shapes=[pltpu.VMEM((4, GROUP_ROWS, 128), BF), dma(4), dma(4), *shapes],
+        scratch_shapes=[
+            pltpu.VMEM((4, GROUP_ROWS, 128), BF),
+            pltpu.VMEM((SHARE_ROWS + 40, 128), F32),
+            dma(4),
+            dma(4),
+            *shapes,
+        ],
         compiler_params=params(8, 60),
         name="share_master",
     )(rows, grads, weight, frames, middle, gain)
+
+
+STEP_ENTRIES = 1024 * 76
+
+
+def optimize_kernel(
+    rates_ref, grads_ref, master_ref, first_ref, second_ref,
+    owned_out, master_out, first_out, second_out, padded_out,
+):
+    entry = lax.broadcasted_iota(jnp.int32, (1, STEP_ENTRIES), 1)
+    entry = entry + pl.program_id(0) * STEP_ENTRIES
+    grads = grads_ref[...]
+    first = BETA_FIRST * first_ref[...] + (1.0 - BETA_FIRST) * grads
+    second = BETA_SECOND * second_ref[...] + (1.0 - BETA_SECOND) * grads * grads
+    change = first * rates_ref[0] / (jnp.sqrt(second * rates_ref[1]) + ADAM_EPSILON)
+    block = jnp.floor((entry.astype(F32) + 0.5) * (1.0 / HD))
+    odd = block - 2.0 * jnp.floor(block * 0.5) > 0.5
+    factor = jnp.where(
+        entry < KEY_END, jnp.where(odd, rates_ref[4], rates_ref[3]), 1.0
+    )
+    master = (master_ref[...] * rates_ref[2] - change) * factor
+    owned_out[...] = grads
+    master_out[...] = master
+    first_out[...] = first
+    second_out[...] = second
+    padded_out[...] = jnp.where(entry < SHARE_ENTRIES, master, 0.0)
+
+
+KEY_END = 409760
+SHARE_ENTRIES = 614880
+
+
+def optimize(rates, grads, master, first, second):
+    block = pl.BlockSpec((1, STEP_ENTRIES), lambda step: (0, step))
+    share = jax.ShapeDtypeStruct((1, SHARE_ENTRIES), F32)
+    return pl.pallas_call(
+        optimize_kernel,
+        grid=(pl.cdiv(SHARE_ENTRIES, STEP_ENTRIES),),
+        out_shape=(share,) * 4 + (jax.ShapeDtypeStruct((1, SHARE_ROWS * 128), F32),),
+        in_specs=[pl.BlockSpec(memory_space=pltpu.SMEM)] + [block] * 4,
+        out_specs=(block,) * 5,
+        compiler_params=pltpu.CompilerParams(vmem_limit_bytes=32 << 20),
+        name="optimize",
+    )(rates, grads, master, first, second)
 
 
 def fast_body(
@@ -1539,23 +1671,24 @@
     inputs = frames.transpose(1, 0, 2).reshape(ROWS, 1280).astype(F32)
     upstream_low = cotangent.transpose(1, 0, 2).reshape(ROWS, 1280)
     upstream = upstream_low.astype(F32)
-    normed = layer_norm(inputs, gain_first, shift_first).astype(BF)
-
-    def head_rows(weight):
-        rows = weight.T.reshape(2, HD, 1280)
-        return jnp.pad(rows, ((0, 0), (0, 128 - HD), (0, 0))).reshape(256, 1280)
-
     def head_lanes(bias):
         lanes = bias.astype(F32).reshape(2, HD)
         return jnp.pad(lanes, ((0, 0), (0, 128 - HD))).reshape(256)
 
-    joined_weight = jnp.concatenate(
-        [head_rows(query_weight), head_rows(key_weight), head_rows(value_weight)]
-    )
     joined_bias = jnp.concatenate(
         [head_lanes(query_bias), jnp.zeros((256,), F32), head_lanes(value_bias)]
     )[None]
-    normed_full, qkv, upstream_full = project(normed, upstream_low, joined_weight, joined_bias)
+    frame_rows = frames.transpose(1, 0, 2).reshape(ROWS, 1280)
+    normed_full, qkv, upstream_full, joined_weight = project(
+        frame_rows,
+        gain_first[None],
+        shift_first[None],
+        upstream_low,
+        query_weight.T,
+        key_weight.T,
+        value_weight.T,
+        joined_bias,
+    )
     qkv = qkv.reshape(8, 3, 128, 768)
 
     quarter = group * 160
@@ -1563,18 +1696,18 @@
     down_share = lax.dynamic_slice_in_dim(down_weight, quarter, 160, 0)
     bias_share = lax.dynamic_slice_in_dim(up_bias, quarter, 160, 0)
     bias_rows = jnp.pad(bias_share[None], ((0, 15), (0, 1280 - 160)))
-    message = jnp.concatenate([up_share, down_share, bias_rows])
+    message = jnp.concatenate([up_share, bias_rows])
     outer = jnp.pad(lax.dynamic_slice_in_dim(out_weight, group * 40, 40, 0), ((0, 8), (0, 0)))
     attended, logs, peaks, gathered, outer_all = attend(qkv, mask, live, message, outer)
-    up_lanes = gathered[:, 320, :160].reshape(1, 640).astype(F32)
+    up_lanes = gathered[:, 160, :160].reshape(1, 640).astype(F32)
     out_rows = outer_all.reshape(4, 2, 4, 48, 1280)[:, :, :, :40]
     out_rows = out_rows.transpose(2, 1, 0, 3, 4).reshape(8, 160, 1280)
 
     branch = jnp.einsum("schr,shd->crd", attended, out_rows, preferred_element_type=F32)
     middle = inputs + branch.reshape(ROWS, 1280) + out_bias.astype(F32)
     normed_two = layer_norm(middle, gain_second, shift_second).astype(BF)
-    normed_two_grad, hidden, feed_grads, _ = feed_forward(
-        normed_two, upstream_full, gathered, up_lanes
+    normed_two_grad, hidden, feed_grads, _, down_all = feed_forward(
+        normed_two, upstream_full, gathered, down_share, up_lanes
     )
 
     _, norm_two_pull = jax.vjp(layer_norm, middle, gain_second, shift_second)
@@ -1591,7 +1724,7 @@
     )
     out_quarters = out_quarters.transpose(2, 1, 0, 3, 4).reshape(4, 2, 192, 1280)
     joined_grad, feed, feed_sum, out_sum = attend_back(
-        qkv, mask, logs, attended_grad, hidden, gathered, feed_grads, out_quarters
+        qkv, mask, logs, attended_grad, hidden, down_all, feed_grads, out_quarters
     )
     layer_out = (middle + feed + down_bias.astype(F32)).astype(BF)
     joined_grad = joined_grad.reshape(8, ROWS, 768)
@@ -1614,7 +1747,6 @@
             jnp.zeros((512,), F32),
         ]
     ).reshape(44, 128)
-    frame_rows = frames.transpose(1, 0, 2).reshape(ROWS, 1280)
     first_grad, grad_rows, small_sum, peak_sum = finish(
         joined_grad,
         joined_weight,
@@ -1632,43 +1764,35 @@
     )
     small_total = small_sum.reshape(1024)[:960]
     head_peak = jnp.max(peak_sum, axis=(1, 2)) / math.sqrt(HD)
-    share_size = master.shape[1]
-    owned_grads = lax.dynamic_slice(
-        grad_rows.reshape(1, GROUP_ROWS * 128), (0, 480 * group), (1, share_size)
-    )
     learn_rate = hyper_rates[0]
     weight_decay = hyper_rates[1]
     logit_cap = hyper_rates[2]
     step_count = adam_step[0].astype(F32)
-    first_new = BETA_FIRST * moment_one + (1.0 - BETA_FIRST) * owned_grads
-    second_new = BETA_SECOND * moment_two + (1.0 - BETA_SECOND) * owned_grads * owned_grads
-    first_hat = first_new * (learn_rate / (1.0 - jnp.power(BETA_FIRST, step_count)))
-    second_hat = second_new * (1.0 / (1.0 - jnp.power(BETA_SECOND, step_count)))
-    entry_index = group * share_size + lax.broadcasted_iota(jnp.int32, (1, share_size), 1)
-    query_end = 1280 * 160
-    query_bias_end = query_end + 160
-    key_end = query_bias_end + 1280 * 160
-    block = jnp.floor((entry_index.astype(F32) + 0.5) * (1.0 / HD))
-    odd = block - 2.0 * jnp.floor(block * 0.5) > 0.5
     root_factor = jnp.sqrt(logit_cap / jnp.maximum(head_peak, logit_cap))
-    head_factor = jnp.where(odd, root_factor[1], root_factor[0])
-    factor = jnp.where(entry_index < key_end, head_factor, 1.0)
-    master_new = (
-        master * (1.0 - learn_rate * weight_decay)
-        - first_hat / (jnp.sqrt(second_hat) + ADAM_EPSILON)
-    ) * factor
-
-    def placed_rows(offset):
-        room = GROUP_ROWS * 128 - share_size - offset
-        return lambda value: jnp.pad(value, ((0, 0), (offset, room))).reshape(GROUP_ROWS, 128)
-
-    master_rows = lax.switch(group, [placed_rows(480 * part) for part in range(4)], master_new)
+    root_factor = jnp.where(group == 0, root_factor, 1.0)
+    rates = jnp.stack(
+        [
+            learn_rate / (1.0 - jnp.power(BETA_FIRST, step_count)),
+            1.0 / (1.0 - jnp.power(BETA_SECOND, step_count)),
+            1.0 - learn_rate * weight_decay,
+            root_factor[0],
+            root_factor[1],
+        ]
+    )
+    owned_grads, master_new, first_new, second_new, padded = optimize(
+        rates, grad_rows.reshape(1, SHARE_ROWS * 128), master, moment_one, moment_two
+    )
     whole, second_grad = share_master(
-        master_rows, joined_grad, joined_weight, frame_rows, middle_grad, gain_first[None]
+        padded.reshape(SHARE_ROWS, 128),
+        joined_grad,
+        joined_weight,
+        frame_rows,
+        middle_grad,
+        gain_first[None],
     )
     input_grad = jnp.concatenate([first_grad, second_grad])
     whole = lax.optimization_barrier(whole.reshape(1, PACK_END * 128))
-    weights_new = whole[:, : 4 * share_size].astype(BF)
+    weights_new = whole[:, : 4 * SHARE_ENTRIES].astype(BF)
     return (
         layer_out.reshape(3, 128, 1280).transpose(1, 0, 2),
         input_grad.reshape(3, 128, 1280).transpose(1, 0, 2),

time: 663 us -> 638 us (0.962)
  other arithmetic: 43.1 us -> 14 us
  local copies, waits for them, and re-layouts: 43.3 us -> 52.3 us
    mul x1 -> x0, other arithmetic: 27.8 us -> none  [fast_body(): (master * (1.0 - learn_rate * weight_decay) - first_hat / (jnp.sqrt(secon...]
    pallas_call x1, Pallas kernels: 90.2 us -> 63.1 us  [attend(): pl.pallas_call(attend_kernel, out_shape=(jax.ShapeDtypeStruct((8, 3, 160,...]
    pallas_call x1, Pallas kernels: 93.4 us -> 118 us  [feed_forward(): pl.pallas_call(functools.partial(feed_forward_kernel, split), out_shape=(...]
    pallas_call x1, Pallas kernels: 130 us -> 110 us  [attend_back(): pl.pallas_call(functools.partial(attend_back_kernel, split), out_shape=(j...]
    pallas_call x1 -> x2, Pallas kernels: 79.8 us -> 98.4 us  [the longest x1 80.6 us: project(): pl.pallas_call(project_kernel, out_shape=(jax.ShapeDtypeStruct((8,) + fra...]
    unnamed x84 -> x102, local copies, waits for them, and re-layouts: 12.3 us -> 24 us
where the time goes in v6:
time: 638 us; the launch traced here: 626 us
  Pallas kernels  535 us (84%)
  local copies, waits for them, and re-layouts  52.3 us (8%)
  matrix products  21.3 us (3%)
  other arithmetic  14 us (2%)
    pallas_call x1, Pallas kernels, feed_forward(): pl.pallas_call(functools.partial(feed_forward_kernel, split), out_shape=(...  118 us
    pallas_call x1, Pallas kernels, attend_back(): pl.pallas_call(functools.partial(attend_back_kernel, split), out_shape=(j...  110 us
    pallas_call x1, Pallas kernels, finish(): pl.pallas_call(functools.partial(finish_kernel, split), out_shape=(jax.Sh...  81 us
    pallas_call x1, Pallas kernels, project(): pl.pallas_call(project_kernel, out_shape=(jax.ShapeDtypeStruct((8,) + fra...  80.6 us
    pallas_call x1, Pallas kernels, share_master(): pl.pallas_call(functools.partial(share_master_kernel, split), out_shape=(...  63.8 us
    pallas_call x1, Pallas kernels, attend(): pl.pallas_call(attend_kernel, out_shape=(jax.ShapeDtypeStruct((8, 3, 160,...  63.1 us
    unnamed x102, local copies, waits for them, and re-layouts  24 us
    pallas_call x1, Pallas kernels, optimize(): pl.pallas_call(optimize_kernel, grid=(pl.cdiv(SHARE_ENTRIES, STEP_ENTRIES...  17.7 us

profile of v6, /device:TPU:0, one launch (start us, length us, event | category | flops | bytes accessed | tf_op | source)
XLA Modules:
  0.0 626.4 jit_solution(3809512784918981208)
XLA Ops:
  0.7 1.4 copy-done
  2.1 1.1 constant_dynamic-slice_fusion.3
  3.2 2.2 copy.54
  5.4 0.8 dynamic_slice.18
  6.2 1.0 fusion.13.weights_ref
  7.2 0.9 constant_dynamic-slice_fusion.2
  9.1 1.0 copy-done.20
  10.1 80.6 %project.1 = (bf16[8,384,1280]{2,1,0:T(8,128)(2,1)}, bf16[8,384,768]{2,1,0:T(8,128)(2,1)S(1)}, bf16[8,384,1280]{2,1,0:T(8,128)(2,1)}, bf16[768,1280]{1,0:T(8,128)(2,1)S(1)}) custom-call(bf16[384,1280]{1,0:T(8,128)(2,1)S(1)} %bitcast.81, f32[1,1280]{1,0:T(1,128)S(1)} %reshape.206.gain_ref, f32[1,1280]{1,0:T(1,128)S(1)} %reshape.207.shift_ref, ...), custom_call_target="tpu_custom_call" | custom-call | tf_op jit(solution)/shard_map/project/pallas_call | solution.py:625
  90.8 2.2 copy-done.2
  93.0 1.2 copy-done.8
  94.8 0.8 compare_convert_fusion.live_ref
  95.6 2.3 copy-done.3
  97.9 0.9 copy-done.17
  98.8 63.1 %attend.1 = (bf16[8,3,160,128]{3,2,1,0:T(8,128)(2,1)S(1)}, f32[6,1,1024]{2,1,0:T(1,128)S(1)}, f32[2,8,256]{2,1,0:T(8,128)S(1)}, bf16[4,176,1280]{2,1,0:T(8,128)(2,1)S(1)}, bf16[8,192,1280]{2,1,0:T(8,128)(2,1)S(1)}) custom-call(bf16[8,3,128,768]{3,2,1,0:T(8,128)(2,1)S(1)} %bitcast.77, f32[3,1024,1]{2,1,0:T(8,128)S(1)} %copy.38.mask_ref, ...), custom_call_target="tpu_custom_call" | custom-call | tf_op jit(solution)/shard_map/attend/pallas_call | solution.py:714
  162.2 0.9 copy-done.14
  163.1 2.1 copy.40
  165.2 1.7 copy.39
  166.9 2.7 reshape.222
  169.6 4.5 fusion.18
  174.9 1.3 add_convert_fusion.1.normed_ref
  176.2 0.7 convert_reduce_fusion.3
  176.9 0.7 reshape.212.bias_ref
  177.6 1.8 constant_dynamic-slice_fusion.1.down_ref
  179.4 118.5 %feed_forward.1 = (f32[384,1280]{1,0:T(8,128)}, bf16[8,384,640]{2,1,0:T(8,128)(2,1)}, bf16[4,336,1280]{2,1,0:T(8,128)(2,1)}, f32[1,640]{1,0:T(1,128)}, bf16[4,160,1280]{2,1,0:T(8,128)(2,1)}) custom-call(bf16[384,1280]{1,0:T(8,128)(2,1)} %add_convert_fusion.1.normed_ref, bf16[8,384,1280]{2,1,0:T(8,128)(2,1)} %get-tuple-element.40.upstream_ref, ...), custom_call_target="tpu_custom_call" | custom-call | tf_op jit(solution)/shard_map/feed_forward/pallas_call | solution.py:903
  297.9 2.3 multiply_reduce_fusion
  300.9 1.7 convert_reduce_fusion.2
  302.8 2.4 bitcast_convert_fusion
  305.5 2.3 pad.25
  307.8 1.0 copy-done.30
  308.8 2.8 fusion.11.pull_ref
  311.7 110.1 %attend_back.1 = (bf16[8,3,128,768]{3,2,1,0:T(8,128)(2,1)}, f32[384,1280]{1,0:T(8,128)}, f32[336,1280]{1,0:T(8,128)}, f32[48,1280]{1,0:T(8,128)}) custom-call(bf16[8,3,128,768]{3,2,1,0:T(8,128)(2,1)} %bitcast.76, f32[3,1024,1]{2,1,0:T(8,128)} %copy-done.4, f32[6,1,1024]{2,1,0:T(1,128)} %copy-done.23, bf16[8,3,160,128]{3,2,1,0:T(8,128)(2,1)} %fusion.11.pull_ref, ...), custom_call_target="tpu_custom_call" | custom-call | tf_op jit(solution)/shard_map/attend_back/pallas_call | solution.py:1101
  421.8 11.5 %convolution_bitcast_fusion.joined_ref = f32[1280,768]{1,0:T(8,128)} fusion(bf16[8,384,1280]{2,1,0:T(8,128)(2,1)} %get-tuple-element.49, bf16[8,384,768]{2,1,0:T(8,128)(2,1)} %bitcast.90), kind=kOutput, calls=%fused_computation.3 | convolution fusion | flops 6039797760 | bytes 16515072 | tf_op jit(solution)/shard_map/prd,pre->de/dot_general | solution.py:1731
  433.3 0.7 convert_reduce_fusion
  434.1 0.9 broadcast_in_dim.86.bias_column_ref
  435.0 0.8 slice.30
  436.6 81.0 %finish.1 = (f32[256,1280]{1,0:T(8,128)}, f32[4808,128]{1,0:T(8,128)}, f32[8,128]{1,0:T(8,128)}, f32[2,8,256]{2,1,0:T(8,128)}) custom-call(bf16[8,384,768]{2,1,0:T(8,128)(2,1)} %bitcast.91, bf16[768,1280]{1,0:T(8,128)(2,1)} %copy-done.8, f32[1280,768]{1,0:T(8,128)} %convolution_bitcast_fusion.joined_ref, f32[1,768]{1,0:T(1,128)} %broadcast_in_dim.79.bias_ref, ...), custom_call_target="tpu_custom_call" | custom-call | tf_op jit(solution)/shard_map/finish/pallas_call | solution.py:1462
  517.6 0.8 reduce_max.9
  522.5 1.7 copy-done.9
  524.2 1.7 copy-done.11
  525.8 1.7 copy-done.12
  527.5 1.7 copy-done.13
  529.2 17.7 %optimize.1 = (f32[1,614880]{1,0:T(1,128)}, f32[1,614880]{1,0:T(1,128)}, f32[1,614880]{1,0:T(1,128)}, f32[1,614880]{1,0:T(1,128)}, f32[1,615424]{1,0:T(1,128)S(1)}) custom-call(f32[5]{0:T(128)S(1)} %pad_maximum_fusion.2.rates_ref, f32[1,615424]{1,0:T(1,128)S(1)} %bitcast.84, f32[1,614880]{1,0:T(1,128)S(1)} %copy-done.11, f32[1,614880]{1,0:T(1,128)S(1)} %copy-done.12, ...), custom_call_target="tpu_custom_call" | custom-call | tf_op jit(solution)/shard_map/optimize/pallas_call | solution.py:1624
  547.0 1.4 copy-done.10
  548.4 63.8 %share_master.1 = (f32[19216,128]{1,0:T(8,128)}, f32[128,1280]{1,0:T(8,128)}) custom-call(f32[4808,128]{1,0:T(8,128)} %bitcast.85, bf16[8,384,768]{2,1,0:T(8,128)(2,1)} %bitcast.92, bf16[768,1280]{1,0:T(8,128)(2,1)} %copy-done.8, bf16[384,1280]{1,0:T(8,128)(2,1)} %bitcast.80, f32[384,1280]{1,0:T(8,128)} %get-tuple-element.69.middle_ref, f32[1,1280]{1,0:T(1,128)} %copy-done.21), custom_call_target="tpu_custom_call" | custom-call | tf_op jit(solution)/shard_map/share_master/pallas_call | solution.py:1571
  612.2 9.4 %slice.41 = bf16[1,2459520]{1,0:T(2,128)(2,1)} slice(f32[1,2459648]{1,0:T(1,128)} %bitcast.94), slice={[0:1], [0:2459520]} | slice | bytes 9838080 | tf_op jit(solution)/shard_map/slice | solution.py:1795
  621.6 1.4 pad_maximum_fusion
  623.0 0.8 copy-done.27
  624.5 1.2 add_convert_fusion
  (121 shorter events, 7.0 us)
Async XLA Ops:
  0.6 1.4 copy-start
  0.7 8.1 %copy-start.46 = (bf16[160]{0:T(256)(128)(2,1)S(1)}, bf16[160]{0:T(256)(128)(2,1)}, u32[]{:S(2)}) copy-start(bf16[160]{0:T(256)(128)(2,1)} %param.31) | copy-start | bytes 964
  0.7 8.2 %copy-start.47 = (bf16[160]{0:T(256)(128)(2,1)S(1)}, bf16[160]{0:T(256)(128)(2,1)}, u32[]{:S(2)}) copy-start(bf16[160]{0:T(256)(128)(2,1)} %param.34) | copy-start | bytes 964
  0.7 8.4 %copy-start.5 = (bf16[128,3,1280]{2,0,1:T(8,128)(2,1)S(1)}, bf16[128,3,1280]{2,0,1:T(8,128)(2,1)}, u32[]{:S(2)}) copy-start(bf16[128,3,1280]{2,0,1:T(8,128)(2,1)} %param.27) | copy-start | bytes 2949124
  3.2 5.8 copy-start.42
  3.2 5.8 copy-start.43
  3.2 5.9 copy-start.6
  3.2 5.9 copy-start.18
  3.2 5.9 copy-start.19
  7.2 87.0 %copy-start.36 = (s32[3,1024]{1,0:T(4,128)S(1)}, s32[3,1024]{1,0:T(4,128)}, u32[]{:S(2)}) copy-start(s32[3,1024]{1,0:T(4,128)} %param.26) | copy-start | bytes 36868
  7.2 87.0 %copy-start.45 = (s32[3]{0:T(128)S(1)}, s32[3]{0:T(128)}, u32[]{:S(2)}) copy-start(s32[3]{0:T(128)} %param.25) | copy-start | bytes 40
  9.0 85.8 %copy-start.21 = (f32[1,1280]{1,0:T(1,128)}, f32[1,1280]{1,0:T(1,128)S(1)}, u32[]{:S(2)}) copy-start(f32[1,1280]{1,0:T(1,128)S(1)} %reshape.206.gain_ref) | copy-start | bytes 15364
  9.1 85.2 %copy-start.22 = (f32[1,1280]{1,0:T(1,128)}, f32[1,1280]{1,0:T(1,128)S(1)}, u32[]{:S(2)}) copy-start(f32[1,1280]{1,0:T(1,128)S(1)} %reshape.207.shift_ref) | copy-start | bytes 15364
  9.1 1.0 copy-start.20
  90.8 2.2 copy-start.2
  93.0 1.3 copy-start.8
  94.8 67.1 %copy-start.4 = (f32[3,1024,1]{2,1,0:T(8,128)}, f32[3,1024,1]{2,1,0:T(8,128)S(1)}, u32[]{:S(2)}) copy-start(f32[3,1024,1]{2,1,0:T(8,128)S(1)} %copy.38.mask_ref) | copy-start | bytes 36868
  95.6 2.3 copy-start.3
  97.9 0.9 copy-start.17
  161.9 1.2 copy-start.14
  161.9 1.2 copy-start.23
  161.9 1.2 copy-start.24
  161.9 3.3 copy-start.15
  165.2 4.4 copy-start.38
  165.2 4.5 copy-start.7
  174.1 2.1 copy-start.25
  174.1 0.7 copy-start.39
  174.1 0.7 copy-start.40
  179.4 118.5 %copy-start.26 = (f32[384,1280]{1,0:T(8,128)S(1)}, f32[384,1280]{1,0:T(8,128)}, u32[]{:S(2)}) copy-start(f32[384,1280]{1,0:T(8,128)} %copy-done.25) | copy-start | bytes 5898244
  297.9 2.4 copy-start.29
  300.8 1.9 copy-start.16
  302.7 2.5 copy-start.34
  305.5 3.3 copy-start.30
  421.8 11.5 %copy-start.28 = (bf16[8,3,128,768]{3,2,1,0:T(8,128)(2,1)S(1)}, bf16[8,3,128,768]{3,2,1,0:T(8,128)(2,1)}, u32[]{:S(2)}) copy-start(bf16[8,3,128,768]{3,2,1,0:T(8,128)(2,1)} %get-tuple-element.47) | copy-start | bytes 14155780
  436.0 0.6 copy-start.35
  436.6 81.8 %copy-start.37 = (f32[3]{0:T(128)S(1)}, f32[3]{0:T(128)}, u32[]{:S(2)}) copy-start(f32[3]{0:T(128)} %param.47) | copy-start | bytes 40
  522.5 1.7 copy-start.9
  524.2 1.7 copy-start.11
  525.8 1.7 copy-start.12
  527.5 1.7 copy-start.13
  547.0 1.4 copy-start.10
  612.2 9.4 %copy-start.32 = (f32[256,1280]{1,0:T(8,128)S(1)}, f32[256,1280]{1,0:T(8,128)}, u32[]{:S(2)}) copy-start(f32[256,1280]{1,0:T(8,128)} %get-tuple-element.53) | copy-start | bytes 3932164
  612.2 9.4 %copy-start.33 = (f32[128,1280]{1,0:T(8,128)S(1)}, f32[128,1280]{1,0:T(8,128)}, u32[]{:S(2)}) copy-start(f32[128,1280]{1,0:T(8,128)} %get-tuple-element.57) | copy-start | bytes 1966084
  621.6 1.4 copy-start.41
  621.6 2.3 copy-start.27
  621.6 2.8 copy-start.31
  623.0 3.2 copy-start.1
  624.5 1.2 copy-start.44

commit v7 on v6

--- a/solution.py
+++ b/solution.py
@@ -492,10 +492,7 @@
         step = steps.index(name)
         if step > 1:
             across(steps[step - 2]).wait_send()
-        for start in range(0, 2 * half, tile):
-            bufs["pair_out"][step % 2, pl.ds(start, tile)] = produce(
-                groups[name], 1 - c, start
-            ).astype(BF)
+        bufs["pair_out"][step % 2] = produce(groups[name], 1 - c, 0, 2 * half).astype(BF)
         across(name).start()
 
     def crossed(name):
@@ -503,7 +500,7 @@
             across(name).wait_recv()
 
     def share(name, start):
-        total = produce(groups[name], c, start)
+        total = produce(groups[name], c, start, tile)
         if paired:
             total = total + bufs["pair_in"][steps.index(name), pl.ds(start, tile)].astype(F32)
         return total
@@ -602,16 +599,13 @@
     greet(place, line=True, plane=True)
 
     def ready(slot):
-        @pl.loop(0, 3)
-        def _(step):
-            rows = pl.ds(step * 128, 128)
-            product = lax.dot_general(
-                nfull_ref[slot, rows],
-                weight_ref[...],
-                (((1,), (1,)), ((), ())),
-                preferred_element_type=F32,
-            )
-            qkv_ref[slot, rows] = (product + bias_ref[...]).astype(BF)
+        product = lax.dot_general(
+            nfull_ref[slot],
+            weight_ref[...],
+            (((1,), (1,)), ((), ())),
+            preferred_element_type=F32,
+        )
+        qkv_ref[slot] = (product + bias_ref[...]).astype(BF)
 
     drive(
         line_gather(
@@ -813,25 +807,19 @@
         index = len(seen)
         seen.append(slot)
 
-        @pl.loop(0, 3)
-        def _(step):
-            rows = pl.ds(pl.multiple_of(step * 128, 128), 128)
-            rate = activate(slot, rows)
-            if index < 2:
-                rate_ref[index, rows] = rate
-            else:
-                pull_back(slot, rows, rate)
+        rows = pl.ds(0, ROWS)
+        rate = activate(slot, rows)
+        if index < 2:
+            rate_ref[index] = rate
+        else:
+            pull_back(slot, rows, rate)
 
         if index < 2:
             next(down)
 
     def finish_here():
         for index in range(2):
-
-            @pl.loop(0, 3)
-            def _(step):
-                rows = pl.ds(pl.multiple_of(step * 128, 128), 128)
-                pull_back(here[index], rows, rate_ref[index, rows])
+            pull_back(here[index], pl.ds(0, ROWS), rate_ref[index])
 
     down = line_gather(
         place, down_ref, down_all, line_local, line_send, line_recv, False
@@ -840,9 +828,9 @@
         place, normed_ref, normed_all, local, gather_send, gather_recv, ready
     )
 
-    def produce(group, core, start):
+    def produce(group, core, start, rows):
         return jnp.dot(
-            slope_all[group * 2 + core, pl.ds(start, 192)],
+            slope_all[group * 2 + core, pl.ds(start, rows)],
             up_rows(),
             preferred_element_type=F32,
         )
@@ -868,24 +856,18 @@
     next(reduce)
 
     def weight_grads(left_all, right_all, base):
-        for block in range(5):
-            lanes = pl.ds(block * 128, 128)
-
-            @pl.loop(0, 8)
-            def _(slot):
-                product = lax.dot_general(
-                    left_all[slot, :, lanes],
-                    right_all[slot],
-                    (((0,), (0,)), ((), ())),
-                    preferred_element_type=F32,
-                )
-                sum_ref[...] = jnp.where(slot == 0, product, sum_ref[...] + product)
-
-            for part in range(4):
-                unit = block * 128 + part * 32
-                grads_ref[unit // 160, pl.ds(base + unit % 160, 32)] = sum_ref[
-                    pl.ds(part * 32, 32)
-                ].astype(BF)
+        @pl.loop(0, 8)
+        def _(slot):
+            product = lax.dot_general(
+                left_all[slot],
+                right_all[slot],
+                (((0,), (0,)), ((), ())),
+                preferred_element_type=F32,
+            )
+            sum_ref[...] = jnp.where(slot == 0, product, sum_ref[...] + product)
+
+        for level in range(4):
+            grads_ref[level, pl.ds(base, 160)] = sum_ref[pl.ds(level * 160, 160)].astype(BF)
 
     weight_grads(slope_all, normed_all, 0)
     next(reduce)
@@ -916,7 +898,7 @@
             pltpu.VMEM((8, ROWS, 1280), BF),
             pltpu.VMEM((8, ROWS, 640), BF),
             pltpu.VMEM((2, ROWS, 640), F32),
-            pltpu.VMEM((128, 1280), F32),
+            pltpu.VMEM((640, 1280), F32),
             dma(8),
             pltpu.SemaphoreType.DMA(()),
             pltpu.SemaphoreType.DMA(()),
@@ -961,9 +943,9 @@
     arriving = exchange(place, pull_ref, grad_ref, local, send, recv)
     next(arriving)
 
-    def feed_block(group, core, start):
+    def feed_block(group, core, start, rows):
         return jnp.dot(
-            hidden_ref[group * 2 + core, pl.ds(start, 192)],
+            hidden_ref[group * 2 + core, pl.ds(start, rows)],
             weights_ref[...].reshape(640, 1280),
             preferred_element_type=F32,
         )
@@ -994,7 +976,7 @@
 
     out_plane = plane_reduce(
         place,
-        lambda group, core, start: out_grad_ref[group, core, pl.ds(start, 96)].astype(F32),
+        lambda group, core, start, rows: out_grad_ref[group, core, pl.ds(start, rows)].astype(F32),
         96,
         96,
         middle,
@@ -1282,47 +1264,83 @@
                 stage[pl.ds(at + 1, 128, stride=5), :] = second
 
 
-def norm_back(place, frames_ref, middle_ref, gain_ref, grad_ref, offset):
+def norm_back(frames_ref, middle_ref, gain_ref, grad_ref):
     def write(rows, total):
-        rows_in = pl.ds(offset + rows.start, rows.size)
-        value = frames_ref[rows_in].astype(F32)
+        value = frames_ref[rows].astype(F32)
         center = value - jnp.mean(value, axis=-1, keepdims=True)
         spread = jnp.mean(center * center, axis=-1, keepdims=True)
         root = lax.rsqrt(spread + NORM_EPSILON)
         scaled = center * root
         pull = total * gain_ref[...]
         along = jnp.mean(pull * scaled, axis=-1, keepdims=True)
-        grad_ref[rows] = middle_ref[rows_in] + root * (
+        grad_ref[rows] = middle_ref[rows] + root * (
             pull - jnp.mean(pull, axis=-1, keepdims=True) - scaled * along
         )
 
     return write
 
 
-def line_product(place, grad_ref, weight_ref, offset, rows, result, bufs, sems):
+def fetch(first, rows, sems, grad, weight, frames, middle):
+    span = pl.ds(first, rows)
+    pairs = (
+        (grad[0].at[:, span], grad[1]),
+        weight,
+        (frames[0].at[span], frames[1]),
+        (middle[0].at[span], middle[1]),
+    )
+    copies = [
+        pltpu.make_async_copy(source, target, sems.at[index])
+        for index, (source, target) in enumerate(pairs)
+    ]
+    for copy in copies:
+        copy.start()
+    return copies
+
+
+def fetch_scratch(rows):
+    return [
+        pltpu.VMEM((8, rows, 768), BF),
+        pltpu.VMEM((768, 1280), BF),
+        pltpu.VMEM((rows, 1280), BF),
+        pltpu.VMEM((rows, 1280), F32),
+        dma(4),
+    ]
+
+
+def line_product(place, grad_ref, weight_ref, rows, result, bufs, sems):
     def produce(level, core, tile):
         return jnp.dot(
-            grad_ref[level * 2 + core, pl.ds(offset + tile.start, tile.size)],
+            grad_ref[level * 2 + core, tile],
             weight_ref[...],
             preferred_element_type=F32,
         )
 
-    tiles = [pl.ds(start, 128) for start in range(0, rows, 128)]
+    tiles = [pl.ds(0, rows)]
     return line_reduce(place, produce, tiles, result, bufs, sems, True)
 
 
-FIRST_ROWS = 256
+FIRST_ROWS = 128
 
 
 def finish_kernel(
-    split, grad_ref, weight_ref, joined_ref, bias_ref, bias_column_ref, sum_ref, out_ref,
-    up_bias_ref, small_ref, peak_ref, frames_ref, middle_ref, gain_ref, shift_ref,
+    split, grad_in, weight_in, joined_ref, bias_ref, bias_column_ref, sum_ref, out_ref,
+    up_bias_ref, small_ref, peak_ref, frames_in, middle_in, gain_ref, shift_ref,
     input_grad_ref, grads_ref, small_out, peak_out,
+    grad_ref, weight_ref, frames_ref, middle_ref, load,
     stage, packed, sum_rows, column, tiles, small_in, small_all, peak_all, edge,
     local, small_send, small_recv, plane_send, plane_recv, *scratch,
 ):
     place = Place()
     line_bufs, line_sems, bufs, sems = split(scratch)
+    loads = fetch(
+        0,
+        FIRST_ROWS,
+        load,
+        (grad_in, grad_ref),
+        (weight_in, weight_ref),
+        (frames_in, frames_ref),
+        (middle_in, middle_ref),
+    )
     greet(place, mp_all=True, plane=True)
     peers = (place.dpx, place.dpy, place.dpd)
 
@@ -1348,16 +1366,15 @@
         place,
         grad_ref,
         weight_ref,
-        0,
         FIRST_ROWS,
-        norm_back(place, frames_ref, middle_ref, gain_ref, input_grad_ref, 0),
+        norm_back(frames_ref, middle_ref, gain_ref, input_grad_ref),
         line_bufs,
         line_sems,
     )
     for index, group in enumerate(peers):
         tell(index, peak_ref, peak_all, group, lambda copy: copy.start())
-    next(line)
-    next(line)
+    for copy in loads:
+        copy.wait()
 
     for block in range(10):
         lanes = pl.ds(block * 128, 128)
@@ -1384,7 +1401,7 @@
     stage[pl.ds(TABLE["up_bias"][0], 5)] = up_bias_ref[...]
     pack_rows(stage, packed)
 
-    def produce(group, core, start):
+    def produce(group, core, start, rows):
         first = pl.multiple_of(group * GROUP_STEP + start, 16)
         return packed[pl.ds(first, GROUP_ROWS // 2)].astype(F32)
 
@@ -1395,15 +1412,16 @@
     plane = plane_reduce(place, produce, half, half, result, bufs, sems, False)
     next(plane)
     next(plane)
+    next(line)
+    next(line)
     for _ in mixing:
         pass
     small_all[place.dp] = jnp.sum(small_in[...], axis=0)
     for index, group in enumerate(peers):
         tell(3 + index, small_all.at[place.dp], small_all, group, lambda copy: copy.start())
-    next(line)
     next(plane)
     next(line)
-    next(plane)
+    next(line)
     drive(line, plane)
     for index, group in enumerate(peers):
         heard(index, peak_all, group)
@@ -1467,9 +1485,10 @@
             jax.ShapeDtypeStruct((8, 128), F32),
             jax.ShapeDtypeStruct(peaks.shape, F32),
         ),
-        in_specs=[VMEM] * 14,
+        in_specs=[ANY, ANY] + [VMEM] * 8 + [ANY, ANY, VMEM, VMEM],
         out_specs=(VMEM,) * 4,
         scratch_shapes=[
+            *fetch_scratch(FIRST_ROWS),
             pltpu.VMEM((STAGE_ROWS, 128), F32),
             pltpu.VMEM((PACK_ROWS, 128), BF),
             pltpu.VMEM((GROUP_ROWS, 128), F32),
@@ -1495,19 +1514,29 @@
 
 
 def share_master_kernel(
-    split, rows_ref, grad_ref, weight_ref, frames_ref, middle_ref, gain_ref,
-    whole_ref, input_grad_ref, parts, turned, send, recv, *scratch,
+    split, rows_ref, grad_in, weight_in, frames_in, middle_in, gain_ref,
+    whole_out, input_grad_ref,
+    grad_ref, weight_ref, frames_ref, middle_ref, load,
+    whole_ref, parts, turned, store, send, recv, *scratch,
 ):
     place = Place()
     line_bufs, line_sems = split(scratch)
+    loads = fetch(
+        FIRST_ROWS,
+        ROWS - FIRST_ROWS,
+        load,
+        (grad_in, grad_ref),
+        (weight_in, weight_ref),
+        (frames_in, frames_ref),
+        (middle_in, middle_ref),
+    )
     greet(place, line=True, plane=True)
     line = line_product(
         place,
         grad_ref,
         weight_ref,
-        FIRST_ROWS,
         ROWS - FIRST_ROWS,
-        norm_back(place, frames_ref, middle_ref, gain_ref, input_grad_ref, FIRST_ROWS),
+        norm_back(frames_ref, middle_ref, gain_ref, input_grad_ref),
         line_bufs,
         line_sems,
     )
@@ -1540,30 +1569,53 @@
     sends = [hop(0, own, dpx), hop(1, own, dpy)]
     for copy in sends:
         copy.start()
+
+    stores = []
+
+    def keep(index, first, rows):
+        span = pl.ds(pl.multiple_of(first, 16), rows)
+        stores.append(
+            pltpu.make_async_copy(whole_ref.at[span], whole_out.at[span], store.at[index])
+        )
+        stores[-1].start()
+
+    def unpack(group):
+        for start in range(32, GROUP_STEP, 2384):
+            at = pl.multiple_of(group * GROUP_STEP + start, 16)
+            whole_ref[pl.ds(at, 2384)] = parts[group, pl.ds(start, 2384)].astype(F32)
+        keep(len(stores), group * GROUP_STEP + 32, GROUP_STEP - 32)
+
+    for copy in loads:
+        copy.wait()
     next(line)
     next(line)
+    unpack(dp)
     hop(0, parts.at[dpx], dpx).wait_recv()
     sends.append(hop(2, parts.at[dpx, part_a], dpy))
     sends[-1].start()
     hop(1, parts.at[dpy], dpy).wait_recv()
     sends.append(hop(3, parts.at[dpy, part_b], dpx))
     sends[-1].start()
+    unpack(dpx)
+    unpack(dpy)
     next(line)
     next(line)
     hop(2, parts.at[dpd, part_a], dpy).wait_recv()
     hop(3, parts.at[dpd, part_b], dpx).wait_recv()
+    unpack(dpd)
     for group in range(4):
-        base = group * GROUP_STEP
         first = parts[group, pl.ds(0, 32)].astype(F32)
         if group > 0:
             first = first + parts[group - 1, pl.ds(GROUP_STEP, 32)].astype(F32)
-        whole_ref[pl.ds(base, 32)] = first
-        for start in range(32, GROUP_STEP, 1192):
-            whole_ref[pl.ds(base + start, 1192)] = parts[group, pl.ds(start, 1192)].astype(F32)
+        whole_ref[pl.ds(group * GROUP_STEP, 32)] = first
+        keep(4 + group, group * GROUP_STEP, 32)
     whole_ref[pl.ds(4 * GROUP_STEP, 16)] = parts[3, pl.ds(GROUP_STEP, 16)].astype(F32)
+    keep(8, 4 * GROUP_STEP, 16)
     for copy in sends:
         copy.wait_send()
     drive(line)
+    for copy in stores:
+        copy.wait()
 
 
 def share_master(rows, grads, weight, frames, middle, gain):
@@ -1574,11 +1626,14 @@
             jax.ShapeDtypeStruct((PACK_END, 128), F32),
             jax.ShapeDtypeStruct((ROWS - FIRST_ROWS, 1280), F32),
         ),
-        in_specs=[VMEM] * 6,
-        out_specs=(VMEM, VMEM),
+        in_specs=[VMEM, ANY, ANY, ANY, ANY, VMEM],
+        out_specs=(ANY, VMEM),
         scratch_shapes=[
+            *fetch_scratch(ROWS - FIRST_ROWS),
+            pltpu.VMEM((PACK_END, 128), F32),
             pltpu.VMEM((4, GROUP_ROWS, 128), BF),
             pltpu.VMEM((SHARE_ROWS + 40, 128), F32),
+            dma(9),
             dma(4),
             dma(4),
             *shapes,

time: 638 us -> 591 us (0.926); the launches traced: 626 us -> 588 us
  Pallas kernels: 535 us -> 486 us
  local copies, waits for them, and re-layouts: 52.3 us -> 63.3 us
    pallas_call x1, Pallas kernels: 118 us -> 88.1 us  [feed_forward(): pl.pallas_call(functools.partial(feed_forward_kernel, split), out_shape=(...]
    pallas_call x1, Pallas kernels: 81 us -> 68 us  [finish(): pl.pallas_call(functools.partial(finish_kernel, split), out_shape=(jax.Sh...]
    dot_general x2, local copies, waits for them, and re-layouts: 4.42 us -> 15.4 us  [fast_body(): jnp.einsum('schr,shd->crd', attended, out_rows, preferred_element_type=F32)]
where the time goes in v7:
time: 591 us; the launch traced here: 588 us
  Pallas kernels  486 us (82%)
  local copies, waits for them, and re-layouts  63.3 us (11%)
  matrix products  21 us (4%)
  other arithmetic  14 us (2%)
    pallas_call x1, Pallas kernels, attend_back(): pl.pallas_call(functools.partial(attend_back_kernel, split), out_shape=(j...  110 us
    pallas_call x1, Pallas kernels, feed_forward(): pl.pallas_call(functools.partial(feed_forward_kernel, split), out_shape=(...  88.1 us
    pallas_call x1, Pallas kernels, project(): pl.pallas_call(project_kernel, out_shape=(jax.ShapeDtypeStruct((8,) + fra...  78.4 us
    pallas_call x1, Pallas kernels, finish(): pl.pallas_call(functools.partial(finish_kernel, split), out_shape=(jax.Sh...  68 us
    pallas_call x1, Pallas kernels, attend(): pl.pallas_call(attend_kernel, out_shape=(jax.ShapeDtypeStruct((8, 3, 160,...  64 us
    pallas_call x1, Pallas kernels, share_master(): pl.pallas_call(functools.partial(share_master_kernel, split), out_shape=(...  59 us
    unnamed x102, local copies, waits for them, and re-layouts  24 us
    pallas_call x1, Pallas kernels, optimize(): pl.pallas_call(optimize_kernel, grid=(pl.cdiv(SHARE_ENTRIES, STEP_ENTRIES...  17.7 us

profile of v7, /device:TPU:0, one launch (start us, length us, event | category | flops | bytes accessed | tf_op | source)
XLA Modules:
  0.0 588.1 jit_solution(9312304186943629566)
XLA Ops:
  0.7 1.4 copy-done
  2.1 1.1 constant_dynamic-slice_fusion.3
  3.2 2.2 copy.54
  5.4 0.8 dynamic_slice.18
  6.2 1.0 fusion.13.weights_ref
  7.2 0.9 constant_dynamic-slice_fusion.2
  9.1 1.0 copy-done.20
  10.1 78.4 %project.1 = (bf16[8,384,1280]{2,1,0:T(8,128)(2,1)}, bf16[8,384,768]{2,1,0:T(8,128)(2,1)S(1)}, bf16[8,384,1280]{2,1,0:T(8,128)(2,1)}, bf16[768,1280]{1,0:T(8,128)(2,1)S(1)}) custom-call(bf16[384,1280]{1,0:T(8,128)(2,1)S(1)} %bitcast.81, f32[1,1280]{1,0:T(1,128)S(1)} %reshape.206.gain_ref, f32[1,1280]{1,0:T(1,128)S(1)} %reshape.207.shift_ref, ...), custom_call_target="tpu_custom_call" | custom-call | tf_op jit(solution)/shard_map/project/pallas_call | solution.py:619
  88.6 2.2 copy-done.2
  90.8 1.2 copy-done.8
  92.6 0.8 compare_convert_fusion.live_ref
  93.4 2.3 copy-done.3
  95.7 0.9 copy-done.17
  96.6 64.0 %attend.1 = (bf16[8,3,160,128]{3,2,1,0:T(8,128)(2,1)S(1)}, f32[6,1,1024]{2,1,0:T(1,128)S(1)}, f32[2,8,256]{2,1,0:T(8,128)S(1)}, bf16[4,176,1280]{2,1,0:T(8,128)(2,1)S(1)}, bf16[8,192,1280]{2,1,0:T(8,128)(2,1)S(1)}) custom-call(bf16[8,3,128,768]{3,2,1,0:T(8,128)(2,1)S(1)} %bitcast.77, f32[3,1024,1]{2,1,0:T(8,128)S(1)} %copy.38.mask_ref, ...), custom_call_target="tpu_custom_call" | custom-call | tf_op jit(solution)/shard_map/attend/pallas_call | solution.py:708
  160.9 0.9 copy-done.14
  161.9 2.1 copy.40
  163.9 1.7 copy.39
  165.7 13.7 %reshape.222 = bf16[384,160,8]{0,2,1:T(8,128)(2,1)S(1)} reshape(bf16[3,128,160,8]{1,0,3,2:T(4,128)(2,1)} %copy.39) | data formatting | bytes 1966080 | tf_op jit(solution)/shard_map/schr,shd->crd/dot_general | solution.py:1761
  179.4 4.5 fusion.18
  184.6 1.3 add_convert_fusion.1.normed_ref
  185.9 0.7 convert_reduce_fusion.3
  186.7 0.7 reshape.212.bias_ref
  187.3 1.8 constant_dynamic-slice_fusion.1.down_ref
  189.1 88.1 %feed_forward.1 = (f32[384,1280]{1,0:T(8,128)}, bf16[8,384,640]{2,1,0:T(8,128)(2,1)}, bf16[4,336,1280]{2,1,0:T(8,128)(2,1)}, f32[1,640]{1,0:T(1,128)}, bf16[4,160,1280]{2,1,0:T(8,128)(2,1)}) custom-call(bf16[384,1280]{1,0:T(8,128)(2,1)} %add_convert_fusion.1.normed_ref, bf16[8,384,1280]{2,1,0:T(8,128)(2,1)} %get-tuple-element.40.upstream_ref, ...), custom_call_target="tpu_custom_call" | custom-call | tf_op jit(solution)/shard_map/feed_forward/pallas_call | solution.py:885
  277.3 2.3 multiply_reduce_fusion
  280.3 1.7 convert_reduce_fusion.2
  282.2 2.2 bitcast_convert_fusion
  284.6 2.3 pad.25
  287.0 1.0 copy-done.30
  288.0 2.8 fusion.11.pull_ref
  290.8 110.3 %attend_back.1 = (bf16[8,3,128,768]{3,2,1,0:T(8,128)(2,1)}, f32[384,1280]{1,0:T(8,128)}, f32[336,1280]{1,0:T(8,128)}, f32[48,1280]{1,0:T(8,128)}) custom-call(bf16[8,3,128,768]{3,2,1,0:T(8,128)(2,1)} %bitcast.76, f32[3,1024,1]{2,1,0:T(8,128)} %copy-done.4, f32[6,1,1024]{2,1,0:T(1,128)} %copy-done.23, bf16[8,3,160,128]{3,2,1,0:T(8,128)(2,1)} %fusion.11.pull_ref, ...), custom_call_target="tpu_custom_call" | custom-call | tf_op jit(solution)/shard_map/attend_back/pallas_call | solution.py:1083
  401.2 11.5 %convolution_bitcast_fusion.joined_ref = f32[1280,768]{1,0:T(8,128)} fusion(bf16[8,384,1280]{2,1,0:T(8,128)(2,1)} %get-tuple-element.49, bf16[8,384,768]{2,1,0:T(8,128)(2,1)} %bitcast.90), kind=kOutput, calls=%fused_computation.3 | convolution fusion | flops 6039797760 | bytes 16515072 | tf_op jit(solution)/shard_map/prd,pre->de/dot_general | solution.py:1786
  412.7 0.7 convert_reduce_fusion
  413.4 0.9 broadcast_in_dim.86.bias_column_ref
  414.3 0.8 slice.30
  416.0 68.0 %finish.1 = (f32[128,1280]{1,0:T(8,128)}, f32[4808,128]{1,0:T(8,128)}, f32[8,128]{1,0:T(8,128)}, f32[2,8,256]{2,1,0:T(8,128)}) custom-call(bf16[8,384,768]{2,1,0:T(8,128)(2,1)} %bitcast.91, bf16[768,1280]{1,0:T(8,128)(2,1)} %copy-done.8, f32[1280,768]{1,0:T(8,128)} %convolution_bitcast_fusion.joined_ref, f32[1,768]{1,0:T(1,128)} %broadcast_in_dim.79.bias_ref, ...), custom_call_target="tpu_custom_call" | custom-call | tf_op jit(solution)/shard_map/finish/pallas_call | solution.py:1480
  484.0 0.8 reduce_max.9
  488.8 1.7 copy-done.9
  490.5 1.7 copy-done.11
  492.2 1.7 copy-done.12
  493.9 1.7 copy-done.13
  495.6 17.7 %optimize.1 = (f32[1,614880]{1,0:T(1,128)}, f32[1,614880]{1,0:T(1,128)}, f32[1,614880]{1,0:T(1,128)}, f32[1,614880]{1,0:T(1,128)}, f32[1,615424]{1,0:T(1,128)S(1)}) custom-call(f32[5]{0:T(128)S(1)} %pad_maximum_fusion.2.rates_ref, f32[1,615424]{1,0:T(1,128)S(1)} %bitcast.84, f32[1,614880]{1,0:T(1,128)S(1)} %copy-done.11, f32[1,614880]{1,0:T(1,128)S(1)} %copy-done.12, ...), custom_call_target="tpu_custom_call" | custom-call | tf_op jit(solution)/shard_map/optimize/pallas_call | solution.py:1679
  513.4 1.4 copy-done.10
  514.8 59.0 %share_master.1 = (f32[19216,128]{1,0:T(8,128)}, f32[256,1280]{1,0:T(8,128)}) custom-call(f32[4808,128]{1,0:T(8,128)} %bitcast.85, bf16[8,384,768]{2,1,0:T(8,128)(2,1)} %bitcast.92, bf16[768,1280]{1,0:T(8,128)(2,1)} %copy-done.8, bf16[384,1280]{1,0:T(8,128)(2,1)} %bitcast.80, f32[384,1280]{1,0:T(8,128)} %get-tuple-element.69.middle_in, f32[1,1280]{1,0:T(1,128)} %copy-done.21), custom_call_target="tpu_custom_call" | custom-call | tf_op jit(solution)/shard_map/share_master/pallas_call | solution.py:1623
  573.9 9.4 %slice.41 = bf16[1,2459520]{1,0:T(2,128)(2,1)} slice(f32[1,2459648]{1,0:T(1,128)} %bitcast.94), slice={[0:1], [0:2459520]} | slice | bytes 9838080 | tf_op jit(solution)/shard_map/slice | solution.py:1850
  583.3 1.4 pad_maximum_fusion
  584.7 0.8 copy-done.27
  586.1 1.2 add_convert_fusion
  (121 shorter events, 7.0 us)
Async XLA Ops:
  0.6 1.4 copy-start
  0.7 8.1 %copy-start.46 = (bf16[160]{0:T(256)(128)(2,1)S(1)}, bf16[160]{0:T(256)(128)(2,1)}, u32[]{:S(2)}) copy-start(bf16[160]{0:T(256)(128)(2,1)} %param.31) | copy-start | bytes 964
  0.7 8.2 %copy-start.47 = (bf16[160]{0:T(256)(128)(2,1)S(1)}, bf16[160]{0:T(256)(128)(2,1)}, u32[]{:S(2)}) copy-start(bf16[160]{0:T(256)(128)(2,1)} %param.34) | copy-start | bytes 964
  0.7 8.4 %copy-start.5 = (bf16[128,3,1280]{2,0,1:T(8,128)(2,1)S(1)}, bf16[128,3,1280]{2,0,1:T(8,128)(2,1)}, u32[]{:S(2)}) copy-start(bf16[128,3,1280]{2,0,1:T(8,128)(2,1)} %param.27) | copy-start | bytes 2949124
  3.2 5.8 copy-start.42
  3.2 5.8 copy-start.43
  3.2 5.9 %copy-start.6 = (bf16[128,3,1280]{2,0,1:T(8,128)(2,1)S(1)}, bf16[128,3,1280]{2,0,1:T(8,128)(2,1)}, u32[]{:S(2)}) copy-start(bf16[128,3,1280]{2,0,1:T(8,128)(2,1)} %param.24) | copy-start | bytes 2949124
  3.2 5.9 %copy-start.18 = (bf16[1280,160]{0,1:T(8,128)(2,1)S(1)}, bf16[1280,160]{0,1:T(8,128)(2,1)}, u32[]{:S(2)}) copy-start(bf16[1280,160]{0,1:T(8,128)(2,1)} %param.30) | copy-start | bytes 1228804
  3.2 5.9 %copy-start.19 = (bf16[1280,160]{0,1:T(8,128)(2,1)S(1)}, bf16[1280,160]{0,1:T(8,128)(2,1)}, u32[]{:S(2)}) copy-start(bf16[1280,160]{0,1:T(8,128)(2,1)} %param.32) | copy-start | bytes 1228804
  7.2 84.8 %copy-start.36 = (s32[3,1024]{1,0:T(4,128)S(1)}, s32[3,1024]{1,0:T(4,128)}, u32[]{:S(2)}) copy-start(s32[3,1024]{1,0:T(4,128)} %param.26) | copy-start | bytes 36868
  7.2 84.8 %copy-start.45 = (s32[3]{0:T(128)S(1)}, s32[3]{0:T(128)}, u32[]{:S(2)}) copy-start(s32[3]{0:T(128)} %param.25) | copy-start | bytes 40
  9.0 83.6 %copy-start.21 = (f32[1,1280]{1,0:T(1,128)}, f32[1,1280]{1,0:T(1,128)S(1)}, u32[]{:S(2)}) copy-start(f32[1,1280]{1,0:T(1,128)S(1)} %reshape.206.gain_ref) | copy-start | bytes 15364
  9.1 82.9 %copy-start.22 = (f32[1,1280]{1,0:T(1,128)}, f32[1,1280]{1,0:T(1,128)S(1)}, u32[]{:S(2)}) copy-start(f32[1,1280]{1,0:T(1,128)S(1)} %reshape.207.shift_ref) | copy-start | bytes 15364
  9.1 1.0 copy-start.20
  88.6 2.2 copy-start.2
  90.7 1.3 copy-start.8
  92.6 68.0 %copy-start.4 = (f32[3,1024,1]{2,1,0:T(8,128)}, f32[3,1024,1]{2,1,0:T(8,128)S(1)}, u32[]{:S(2)}) copy-start(f32[3,1024,1]{2,1,0:T(8,128)S(1)} %copy.38.mask_ref) | copy-start | bytes 36868
  93.4 2.3 copy-start.3
  95.7 0.9 copy-start.17
  160.6 1.2 copy-start.14
  160.6 1.2 copy-start.23
  160.7 1.2 copy-start.24
  160.7 3.3 copy-start.15
  163.9 15.4 %copy-start.38 = (bf16[1280]{0:T(1024)(128)(2,1)S(1)}, bf16[1280]{0:T(1024)(128)(2,1)}, u32[]{:S(2)}) copy-start(bf16[1280]{0:T(1024)(128)(2,1)} %param.36) | copy-start | bytes 7684
  163.9 15.4 %copy-start.7 = (bf16[128,3,1280]{2,0,1:T(8,128)(2,1)S(1)}, bf16[128,3,1280]{2,0,1:T(8,128)(2,1)}, u32[]{:S(2)}) copy-start(bf16[128,3,1280]{2,0,1:T(8,128)(2,1)} %param.24) | copy-start | bytes 2949124
  183.8 2.1 copy-start.25
  183.8 0.7 copy-start.39
  183.9 0.7 copy-start.40
  189.1 88.1 %copy-start.26 = (f32[384,1280]{1,0:T(8,128)S(1)}, f32[384,1280]{1,0:T(8,128)}, u32[]{:S(2)}) copy-start(f32[384,1280]{1,0:T(8,128)} %copy-done.25) | copy-start | bytes 5898244
  277.3 2.4 copy-start.29
  280.3 1.9 copy-start.16
  282.1 2.2 copy-start.34
  284.6 3.3 copy-start.30
  401.2 11.5 %copy-start.28 = (bf16[8,3,128,768]{3,2,1,0:T(8,128)(2,1)S(1)}, bf16[8,3,128,768]{3,2,1,0:T(8,128)(2,1)}, u32[]{:S(2)}) copy-start(bf16[8,3,128,768]{3,2,1,0:T(8,128)(2,1)} %get-tuple-element.47) | copy-start | bytes 14155780
  415.4 0.6 copy-start.35
  416.0 68.8 %copy-start.37 = (f32[3]{0:T(128)S(1)}, f32[3]{0:T(128)}, u32[]{:S(2)}) copy-start(f32[3]{0:T(128)} %param.47) | copy-start | bytes 40
  488.8 1.7 copy-start.9
  490.5 1.7 copy-start.11
  492.2 1.7 copy-start.12
  493.9 1.7 copy-start.13
  513.4 1.4 copy-start.10
  573.9 9.4 %copy-start.32 = (f32[256,1280]{1,0:T(8,128)S(1)}, f32[256,1280]{1,0:T(8,128)}, u32[]{:S(2)}) copy-start(f32[256,1280]{1,0:T(8,128)} %get-tuple-element.57) | copy-start | bytes 3932164
  573.9 9.4 %copy-start.33 = (f32[128,1280]{1,0:T(8,128)S(1)}, f32[128,1280]{1,0:T(8,128)}, u32[]{:S(2)}) copy-start(f32[128,1280]{1,0:T(8,128)} %get-tuple-element.53) | copy-start | bytes 1966084
  583.3 1.4 copy-start.41
  583.3 2.3 copy-start.27
  583.3 2.8 copy-start.31
  584.7 3.2 copy-start.1
  586.1 1.2 copy-start.44

commit v8 on v7

--- a/solution.py
+++ b/solution.py
@@ -581,10 +581,17 @@
     return scratch, sems
 
 
-def project_kernel(
+OUTER_STARTS = (0, 48, 96, 112)
+
+
+def attention_kernel(
     frames_ref, gain_ref, shift_ref, cot_ref, query_ref, key_ref, value_ref, bias_ref,
-    nfull_ref, qkv_ref, cfull_ref, weight_ref,
-    normed_ref, local, line_send, line_recv, plane_send, plane_recv,
+    mask_ref, live_ref, weights_ref, outer_ref, out_bias_ref, gain_two_ref, shift_two_ref,
+    nfull_ref, qkv_ref, cfull_ref, weight_ref, att_ref, logs_ref, peak_ref, wfull_ref,
+    rows_ref, middle_ref, two_ref,
+    normed_ref, out_ref, vt_ref, outer_all, outer_full,
+    local, first_send, first_recv, cot_send, cot_recv, send, recv, line_send, line_recv,
+    outer_send, outer_recv, plane_send, plane_recv,
 ):
     place = Place()
     weight_ref[...] = jnp.zeros(weight_ref.shape, BF)
@@ -596,7 +603,7 @@
         normed_ref[rows] = layer_norm(
             frames_ref[rows].astype(F32), gain_ref[...], shift_ref[...]
         ).astype(BF)
-    greet(place, line=True, plane=True)
+    greet(place, mp_all=True, plane=True)
 
     def ready(slot):
         product = lax.dot_general(
@@ -605,41 +612,14 @@
             (((1,), (1,)), ((), ())),
             preferred_element_type=F32,
         )
-        qkv_ref[slot] = (product + bias_ref[...]).astype(BF)
+        qkv_ref[slot] = (product + bias_ref[...]).astype(BF).reshape(3, 128, 768)
 
     drive(
         line_gather(
-            place, normed_ref, nfull_ref, local.at[0], line_send, line_recv, True, ready
+            place, normed_ref, nfull_ref, local.at[4], first_send, first_recv, True, ready
         ),
-        plane_gather(place, cot_ref, cfull_ref, local.at[1], plane_send, plane_recv),
-    )
-
-
-def project(frames, gain, shift, cotangent, query, key, value, bias):
-    return pl.pallas_call(
-        project_kernel,
-        out_shape=(
-            jax.ShapeDtypeStruct((8,) + frames.shape, BF),
-            jax.ShapeDtypeStruct((8, ROWS, 768), BF),
-            jax.ShapeDtypeStruct((8,) + cotangent.shape, BF),
-            jax.ShapeDtypeStruct((768, 1280), BF),
-        ),
-        in_specs=[VMEM, VMEM, VMEM, ANY, VMEM, VMEM, VMEM, VMEM],
-        out_specs=(VMEM, VMEM, ANY, VMEM),
-        scratch_shapes=[pltpu.VMEM((ROWS, 1280), BF), dma(2), dma(4, 3), dma(8), dma(9), dma(9)],
-        compiler_params=params(0),
-        name="project",
-    )(frames, gain, shift, cotangent, query, key, value, bias)
-
-
-def attend_kernel(
-    qkv_ref, mask_ref, live_ref, weights_ref, outer_ref,
-    att_ref, logs_ref, peak_ref, wfull_ref, ofull_ref,
-    out_ref, vt_ref, outer_all, local, send, recv, line_send, line_recv,
-    outer_send, outer_recv, plane_send, plane_recv,
-):
-    place = Place()
-    greet(place, mp_all=True, plane=True)
+        plane_gather(place, cot_ref, cfull_ref, local.at[5], cot_send, cot_recv),
+    )
     outer = line_gather(
         place, outer_ref, outer_all, local.at[2], outer_send, outer_recv, False, None, 48
     )
@@ -700,27 +680,60 @@
     next(mixing)
     for _ in outer:
         pass
-    spread = plane_gather(place, outer_all, ofull_ref, local.at[3], plane_send, plane_recv)
-    drive(spread, gather, mixing)
-
-
-def attend(qkv, mask, live, weights, outer):
+    spread = plane_gather(place, outer_all, outer_full, local.at[3], plane_send, plane_recv)
+    drive(spread, mixing)
+    for level in range(LINE):
+        for core in range(2):
+            for group, start in enumerate(OUTER_STARTS):
+                rows_ref[pl.ds((level * 2 + core) * 160 + start, 48)] = outer_full[
+                    group * 2 + core, pl.ds(level * 48, 48)
+                ]
+    for clip in range(3):
+        rows = pl.ds(clip * 128, 128)
+        branch = lax.dot_general(
+            att_ref[:, clip].reshape(1280, 128),
+            rows_ref[...],
+            (((0,), (0,)), ((), ())),
+            preferred_element_type=F32,
+        )
+        middle = frames_ref[rows].astype(F32) + (branch + out_bias_ref[...])
+        middle_ref[rows] = middle
+        two_ref[rows] = layer_norm(middle, gain_two_ref[...], shift_two_ref[...]).astype(BF)
+    drive(gather)
+
+
+def attention(
+    frames, gain, shift, cotangent, query, key, value, bias, mask, live, weights, outer,
+    out_bias, gain_two, shift_two,
+):
     return pl.pallas_call(
-        attend_kernel,
+        attention_kernel,
         out_shape=(
+            jax.ShapeDtypeStruct((8,) + frames.shape, BF),
+            jax.ShapeDtypeStruct((8, 3, 128, 768), BF),
+            jax.ShapeDtypeStruct((8,) + cotangent.shape, BF),
+            jax.ShapeDtypeStruct((768, 1280), BF),
             jax.ShapeDtypeStruct((8, 3, 160, 128), BF),
             jax.ShapeDtypeStruct((6, 1, 1024), F32),
             jax.ShapeDtypeStruct((2, 8, 256), F32),
             jax.ShapeDtypeStruct((4,) + weights.shape, BF),
-            jax.ShapeDtypeStruct((8, 192, 1280), BF),
+            jax.ShapeDtypeStruct((1280, 1280), BF),
+            jax.ShapeDtypeStruct((ROWS, 1280), F32),
+            jax.ShapeDtypeStruct((ROWS, 1280), BF),
         ),
-        in_specs=[VMEM, VMEM, VMEM, ANY, ANY],
-        out_specs=(VMEM, VMEM, VMEM, ANY, ANY),
+        in_specs=[VMEM] * 3 + [ANY] + [VMEM] * 6 + [ANY, ANY] + [VMEM] * 3,
+        out_specs=(VMEM, VMEM, ANY, VMEM, VMEM, VMEM, VMEM, ANY, VMEM, VMEM, VMEM),
         scratch_shapes=[
+            pltpu.VMEM((ROWS, 1280), BF),
             pltpu.VMEM((8, 3, 160, 128), BF),
             pltpu.VMEM((128, 1024), BF),
             pltpu.VMEM((192, 1280), BF),
-            dma(4),
+            pltpu.VMEM((8, 192, 1280), BF),
+            dma(6),
+            dma(4, 3),
+            dma(8),
+            dma(9),
+            dma(9),
             dma(8),
             dma(8),
             dma(4, 3),
@@ -730,9 +743,12 @@
             dma(9),
             dma(9),
         ],
-        compiler_params=params(1),
-        name="attend",
-    )(qkv, mask, live, weights, outer)
+        compiler_params=params(0, 56),
+        name="attention",
+    )(
+        frames, gain, shift, cotangent, query, key, value, bias, mask, live, weights, outer,
+        out_bias, gain_two, shift_two,
+    )
 
 
 def flatten(*pairs):
@@ -1324,8 +1340,8 @@
 
 def finish_kernel(
     split, grad_in, weight_in, joined_ref, bias_ref, bias_column_ref, sum_ref, out_ref,
-    up_bias_ref, small_ref, peak_ref, frames_in, middle_in, gain_ref, shift_ref,
-    input_grad_ref, grads_ref, small_out, peak_out,
+    up_bias_ref, small_ref, peak_ref, frames_in, middle_in, gain_ref, shift_ref, cap_ref,
+    input_grad_ref, grads_ref, small_out, roots_out,
     grad_ref, weight_ref, frames_ref, middle_ref, load,
     stage, packed, sum_rows, column, tiles, small_in, small_all, peak_all, edge,
     local, small_send, small_recv, plane_send, plane_recv, *scratch,
@@ -1429,7 +1445,10 @@
     top = peak_ref[...]
     for group in peers:
         top = jnp.maximum(top, peak_all[group])
-    peak_out[...] = top
+    for head in range(2):
+        peak = jnp.max(jnp.max(top[head], axis=0, keepdims=True), axis=1, keepdims=True)
+        root = jnp.sqrt(cap_ref[...] / jnp.maximum(peak * (1.0 / math.sqrt(HD)), cap_ref[...]))
+        roots_out[head] = jnp.broadcast_to(jnp.where(place.dp == 0, root, 1.0), (8, 128))
     whole = jnp.sum(small_all[...], axis=0)
     lane = lane_of(8)
     row = lax.broadcasted_iota(jnp.int32, (8, 128), 0)
@@ -1472,7 +1491,7 @@
         tell(3 + index, small_all.at[place.dp], small_all, group, lambda copy: copy.wait_send())
 
 
-def finish(grads, weight, joined, bias, sums, out, up_bias, small, peaks, frames, middle, gain, shift):
+def finish(grads, weight, joined, bias, sums, out, up_bias, small, peaks, frames, middle, gain, shift, cap):
     shapes, split = flatten(
         *line_reduce_scratch(FIRST_ROWS, 1280, True),
         *plane_reduce_scratch(GROUP_ROWS // 2, 128, False),
@@ -1483,9 +1502,9 @@
             jax.ShapeDtypeStruct((FIRST_ROWS, 1280), F32),
             jax.ShapeDtypeStruct((SHARE_ROWS, 128), F32),
             jax.ShapeDtypeStruct((8, 128), F32),
-            jax.ShapeDtypeStruct(peaks.shape, F32),
+            jax.ShapeDtypeStruct((2, 8, 128), F32),
         ),
-        in_specs=[ANY, ANY] + [VMEM] * 8 + [ANY, ANY, VMEM, VMEM],
+        in_specs=[ANY, ANY] + [VMEM] * 8 + [ANY, ANY, VMEM, VMEM, VMEM],
         out_specs=(VMEM,) * 4,
         scratch_shapes=[
             *fetch_scratch(FIRST_ROWS),
@@ -1509,7 +1528,7 @@
         name="finish",
     )(
         grads, weight, joined, bias[None], bias[:, None], sums, out, up_bias, small, peaks,
-        frames, middle, gain, shift,
+        frames, middle, gain, shift, cap,
     )
 
 
@@ -1647,7 +1666,7 @@
 
 
 def optimize_kernel(
-    rates_ref, grads_ref, master_ref, first_ref, second_ref,
+    rates_ref, roots_ref, grads_ref, master_ref, first_ref, second_ref,
     owned_out, master_out, first_out, second_out, padded_out,
 ):
     entry = lax.broadcasted_iota(jnp.int32, (1, STEP_ENTRIES), 1)
@@ -1659,7 +1678,7 @@
     block = jnp.floor((entry.astype(F32) + 0.5) * (1.0 / HD))
     odd = block - 2.0 * jnp.floor(block * 0.5) > 0.5
     factor = jnp.where(
-        entry < KEY_END, jnp.where(odd, rates_ref[4], rates_ref[3]), 1.0
+        entry < KEY_END, jnp.where(odd, roots_ref[1, 0:1, 0:1], roots_ref[0, 0:1, 0:1]), 1.0
     )
     master = (master_ref[...] * rates_ref[2] - change) * factor
     owned_out[...] = grads
@@ -1673,18 +1692,22 @@
 SHARE_ENTRIES = 614880
 
 
-def optimize(rates, grads, master, first, second):
+def optimize(rates, roots, grads, master, first, second):
     block = pl.BlockSpec((1, STEP_ENTRIES), lambda step: (0, step))
     share = jax.ShapeDtypeStruct((1, SHARE_ENTRIES), F32)
     return pl.pallas_call(
         optimize_kernel,
         grid=(pl.cdiv(SHARE_ENTRIES, STEP_ENTRIES),),
         out_shape=(share,) * 4 + (jax.ShapeDtypeStruct((1, SHARE_ROWS * 128), F32),),
-        in_specs=[pl.BlockSpec(memory_space=pltpu.SMEM)] + [block] * 4,
+        in_specs=[
+            pl.BlockSpec(memory_space=pltpu.SMEM),
+            pl.BlockSpec((2, 8, 128), lambda step: (0, 0, 0)),
+        ]
+        + [block] * 4,
         out_specs=(block,) * 5,
-        compiler_params=pltpu.CompilerParams(vmem_limit_bytes=32 << 20),
+        compiler_params=pltpu.CompilerParams(vmem_limit_bytes=62 << 20),
         name="optimize",
-    )(rates, grads, master, first, second)
+    )(rates, roots, grads, master, first, second)
 
 
 def fast_body(
@@ -1734,7 +1757,18 @@
         [head_lanes(query_bias), jnp.zeros((256,), F32), head_lanes(value_bias)]
     )[None]
     frame_rows = frames.transpose(1, 0, 2).reshape(ROWS, 1280)
-    normed_full, qkv, upstream_full, joined_weight = project(
+    quarter = group * 160
+    up_share = lax.dynamic_slice_in_dim(up_weight, quarter, 160, 1).T
+    down_share = lax.dynamic_slice_in_dim(down_weight, quarter, 160, 0)
+    bias_share = lax.dynamic_slice_in_dim(up_bias, quarter, 160, 0)
+    bias_rows = jnp.pad(bias_share[None], ((0, 15), (0, 1280 - 160)))
+    message = jnp.concatenate([up_share, bias_rows])
+    outer_start = jnp.minimum(group * 48, 112)
+    outer = lax.dynamic_slice_in_dim(out_weight, outer_start, 48, 0)
+    (
+        normed_full, qkv, upstream_full, joined_weight, attended, logs, peaks, gathered,
+        out_rows, middle, normed_two,
+    ) = attention(
         frame_rows,
         gain_first[None],
         shift_first[None],
@@ -1743,24 +1777,17 @@
         key_weight.T,
         value_weight.T,
         joined_bias,
-    )
-    qkv = qkv.reshape(8, 3, 128, 768)
-
-    quarter = group * 160
-    up_share = lax.dynamic_slice_in_dim(up_weight, quarter, 160, 1).T
-    down_share = lax.dynamic_slice_in_dim(down_weight, quarter, 160, 0)
-    bias_share = lax.dynamic_slice_in_dim(up_bias, quarter, 160, 0)
-    bias_rows = jnp.pad(bias_share[None], ((0, 15), (0, 1280 - 160)))
-    message = jnp.concatenate([up_share, bias_rows])
-    outer = jnp.pad(lax.dynamic_slice_in_dim(out_weight, group * 40, 40, 0), ((0, 8), (0, 0)))
-    attended, logs, peaks, gathered, outer_all = attend(qkv, mask, live, message, outer)
+        mask,
+        live,
+        message,
+        outer,
+        out_bias.astype(F32)[None],
+        gain_second[None],
+        shift_second[None],
+    )
     up_lanes = gathered[:, 160, :160].reshape(1, 640).astype(F32)
-    out_rows = outer_all.reshape(4, 2, 4, 48, 1280)[:, :, :, :40]
-    out_rows = out_rows.transpose(2, 1, 0, 3, 4).reshape(8, 160, 1280)
-
-    branch = jnp.einsum("schr,shd->crd", attended, out_rows, preferred_element_type=F32)
-    middle = inputs + branch.reshape(ROWS, 1280) + out_bias.astype(F32)
-    normed_two = layer_norm(middle, gain_second, shift_second).astype(BF)
+    out_rows = out_rows.reshape(8, 160, 1280)
+
     normed_two_grad, hidden, feed_grads, _, down_all = feed_forward(
         normed_two, upstream_full, gathered, down_share, up_lanes
     )
@@ -1802,7 +1829,7 @@
             jnp.zeros((512,), F32),
         ]
     ).reshape(44, 128)
-    first_grad, grad_rows, small_sum, peak_sum = finish(
+    first_grad, grad_rows, small_sum, roots = finish(
         joined_grad,
         joined_weight,
         joined_weight_grad,
@@ -1816,26 +1843,21 @@
         middle_grad,
         gain_first[None],
         shift_first[None],
+        hyper_rates[2].reshape(1, 1),
     )
     small_total = small_sum.reshape(1024)[:960]
-    head_peak = jnp.max(peak_sum, axis=(1, 2)) / math.sqrt(HD)
     learn_rate = hyper_rates[0]
     weight_decay = hyper_rates[1]
-    logit_cap = hyper_rates[2]
     step_count = adam_step[0].astype(F32)
-    root_factor = jnp.sqrt(logit_cap / jnp.maximum(head_peak, logit_cap))
-    root_factor = jnp.where(group == 0, root_factor, 1.0)
     rates = jnp.stack(
         [
             learn_rate / (1.0 - jnp.power(BETA_FIRST, step_count)),
             1.0 / (1.0 - jnp.power(BETA_SECOND, step_count)),
             1.0 - learn_rate * weight_decay,
-            root_factor[0],
-            root_factor[1],
         ]
     )
     owned_grads, master_new, first_new, second_new, padded = optimize(
-        rates, grad_rows.reshape(1, SHARE_ROWS * 128), master, moment_one, moment_two
+        rates, roots, grad_rows.reshape(1, SHARE_ROWS * 128), master, moment_one, moment_two
     )
     whole, second_grad = share_master(
         padded.reshape(SHARE_ROWS, 128),

time: 591 us -> 599 us (1.014)
  Pallas kernels: 486 us -> 526 us
  local copies, waits for them, and re-layouts: 63.3 us -> 32.1 us
    pallas_call x2 -> x1, Pallas kernels: 142 us -> 166 us  [attention(): pl.pallas_call(attention_kernel, out_shape=(jax.ShapeDtypeStruct((8,) + f...]
    unnamed x102 -> x56, local copies, waits for them, and re-layouts: 24 us -> 6.49 us
    dot_general x2 -> x0, local copies, waits for them, and re-layouts: 15.4 us -> none  [fast_body(): jnp.einsum('schr,shd->crd', attended, out_rows, preferred_element_type=F32)]
    pallas_call x1, Pallas kernels: 88.1 us -> 99.7 us  [feed_forward(): pl.pallas_call(functools.partial(feed_forward_kernel, split), out_shape=(...]
    pallas_call x1, Pallas kernels: 17.7 us -> 24.8 us  [optimize(): pl.pallas_call(optimize_kernel, grid=(pl.cdiv(SHARE_ENTRIES, STEP_ENTRIES...]
where the time goes in v8:
time: 599 us; the launch traced here: 591 us
  Pallas kernels  526 us (88%)
  local copies, waits for them, and re-layouts  32.1 us (5%)
  matrix products  18.4 us (3%)
  other arithmetic  9.91 us (2%)
    pallas_call x1, Pallas kernels, attention(): pl.pallas_call(attention_kernel, out_shape=(jax.ShapeDtypeStruct((8,) + f...  166 us
    pallas_call x1, Pallas kernels, attend_back(): pl.pallas_call(functools.partial(attend_back_kernel, split), out_shape=(j...  110 us
    pallas_call x1, Pallas kernels, feed_forward(): pl.pallas_call(functools.partial(feed_forward_kernel, split), out_shape=(...  99.7 us
    pallas_call x1, Pallas kernels, finish(): pl.pallas_call(functools.partial(finish_kernel, split), out_shape=(jax.Sh...  67.1 us
    pallas_call x1, Pallas kernels, share_master(): pl.pallas_call(functools.partial(share_master_kernel, split), out_shape=(...  58.7 us
    pallas_call x1, Pallas kernels, optimize(): pl.pallas_call(optimize_kernel, grid=(pl.cdiv(SHARE_ENTRIES, STEP_ENTRIES...  24.8 us
    dot_general x1, matrix products, fast_body(): jnp.einsum('prd,pre->de', normed_full, joined_grad, preferred_element_typ...  12.5 us

profile of v8, /device:TPU:0, one launch (start us, length us, event | category | flops | bytes accessed | tf_op | source)
XLA Modules:
  0.0 590.8 jit_solution(11075594388640261488)
XLA Ops:
  0.7 1.4 copy-done
  2.1 0.3 constant_dynamic-slice_fusion.3
  2.4 0.2 copy.47
  2.6 0.8 dynamic_slice.18
  3.4 0.8 fusion.2.weights_ref
  4.2 1.6 constant_dynamic-slice_fusion.2.outer_ref
  6.0 0.6 broadcast_in_dim.76.bias_ref
  6.6 0.6 reshape.193.gain_ref
  7.2 1.7 copy.37.mask_ref
  8.9 0.6 reshape.194.shift_ref
  9.5 0.7 compare_convert_fusion.live_ref
  10.2 0.6 broadcast_in_dim.83.gain_two_ref
  10.8 0.6 reshape.199.out_bias_ref
  11.4 0.6 reshape.200.shift_two_ref
  12.0 166.3 %attention.1 = (bf16[8,384,1280]{2,1,0:T(8,128)(2,1)}, bf16[8,3,128,768]{3,2,1,0:T(8,128)(2,1)}, bf16[8,384,1280]{2,1,0:T(8,128)(2,1)}, bf16[768,1280]{1,0:T(8,1...) custom-call(bf16[384,1280]{1,0:T(8,128)(2,1)} %bitcast.68, ...), custom_call_target="tpu_custom_call" | custom-call | tf_op jit(solution)/shard_map/attention/pallas_call | solution.py:709
  178.2 0.7 convert_reduce_fusion.3
  179.0 0.7 reshape.201.bias_ref
  179.6 1.8 constant_dynamic-slice_fusion.1.down_ref
  181.4 99.7 %feed_forward.1 = (f32[384,1280]{1,0:T(8,128)}, bf16[8,384,640]{2,1,0:T(8,128)(2,1)}, bf16[4,336,1280]{2,1,0:T(8,128)(2,1)}, f32[1,640]{1,0:T(1,128)}, bf16[4,160,1280]{2,1,0:T(8,128)(2,1)}) custom-call(bf16[384,1280]{1,0:T(8,128)(2,1)} %get-tuple-element.41.normed_ref, bf16[8,384,1280]{2,1,0:T(8,128)(2,1)} %get-tuple-element.42.upstream_ref, ...), custom_call_target="tpu_custom_call" | custom-call | tf_op jit(solution)/shard_map/feed_forward/pallas_call | solution.py:901
  281.3 0.3 multiply_reduce_fusion.2
  281.7 1.2 copy-done.6
  282.9 0.7 multiply_reduce_fusion
  283.6 0.6 fusion.5
  284.2 0.6 copy-done.5
  284.8 1.7 convert_reduce_fusion.2
  286.7 3.1 bitcast_convert_fusion
  289.8 0.2 copy.39
  290.0 2.3 pad.20
  292.4 1.0 copy-done.22
  293.4 2.8 fusion.pull_ref
  296.2 109.8 %attend_back.1 = (bf16[8,3,128,768]{3,2,1,0:T(8,128)(2,1)}, f32[384,1280]{1,0:T(8,128)}, f32[336,1280]{1,0:T(8,128)}, f32[48,1280]{1,0:T(8,128)}) custom-call(bf16[8,3,128,768]{3,2,1,0:T(8,128)(2,1)} %get-tuple-element.39.qkv_in, f32[3,1024,1]{2,1,0:T(8,128)} %copy.37.mask_ref, f32[6,1,1024]{2,1,0:T(1,128)} %get-tuple-element.40.logs_ref, ...), custom_call_target="tpu_custom_call" | custom-call | tf_op jit(solution)/shard_map/attend_back/pallas_call | solution.py:1099
  406.0 12.5 %convolution_bitcast_fusion.joined_ref = f32[1280,768]{1,0:T(8,128)} fusion(bf16[8,384,1280]{2,1,0:T(8,128)(2,1)} %get-tuple-element.53, bf16[8,384,768]{2,1,0:T(8,128)(2,1)} %bitcast.62), kind=kOutput, calls=%fused_computation.3 | convolution fusion | flops 6039797760 | bytes 16515072 | tf_op jit(solution)/shard_map/prd,pre->de/dot_general | solution.py:1813
  418.5 0.7 convert_reduce_fusion
  419.2 0.9 broadcast_in_dim.96.bias_column_ref
  420.2 0.8 slice.23
  421.0 0.2 dynamic_update_slice.3
  421.2 0.6 broadcast_in_dim.88.bias_ref
  421.8 0.6 fusion.6
  422.4 67.1 %finish.1 = (f32[128,1280]{1,0:T(8,128)}, f32[4808,128]{1,0:T(8,128)}, f32[8,128]{1,0:T(8,128)}, f32[2,8,128]{2,1,0:T(8,128)}) custom-call(bf16[8,384,768]{2,1,0:T(8,128)(2,1)} %bitcast.63, bf16[768,1280]{1,0:T(8,128)(2,1)} %get-tuple-element.52.weight_in, f32[1280,768]{1,0:T(8,128)} %convolution_bitcast_fusion.joined_ref, ...), custom_call_target="tpu_custom_call" | custom-call | tf_op jit(solution)/shard_map/finish/pallas_call | solution.py:1499
  492.2 0.6 pad_maximum_fusion.2.rates_ref
  492.8 24.8 %optimize.1 = (f32[1,614880]{1,0:T(1,128)}, f32[1,614880]{1,0:T(1,128)}, f32[1,614880]{1,0:T(1,128)}, f32[1,614880]{1,0:T(1,128)}, f32[1,615424]{1,0:T(1,128)}) custom-call(f32[3]{0:T(128)} %pad_maximum_fusion.2.rates_ref, f32[2,8,128]{2,1,0:T(8,128)} %get-tuple-element.58.roots_ref, f32[1,615424]{1,0:T(1,128)} %bitcast.72, f32[1,614880]{1,0:T(1,128)} %master_ref.1, ...), custom_call_target="tpu_custom_call" | custom-call | tf_op jit(solution)/shard_map/optimize/pallas_call | solution.py:1698
  517.6 58.7 %share_master.1 = (f32[19216,128]{1,0:T(8,128)}, f32[256,1280]{1,0:T(8,128)}) custom-call(f32[4808,128]{1,0:T(8,128)} %bitcast.73, bf16[8,384,768]{2,1,0:T(8,128)(2,1)} %bitcast.64, bf16[768,1280]{1,0:T(8,128)(2,1)} %get-tuple-element.52.weight_in, bf16[384,1280]{1,0:T(8,128)(2,1)} %bitcast.70, f32[384,1280]{1,0:T(8,128)} %get-tuple-element.73.middle_in, ...), custom_call_target="tpu_custom_call" | custom-call | tf_op jit(solution)/shard_map/share_master/pallas_call | solution.py:1642
  576.3 9.4 %slice.32 = bf16[1,2459520]{1,0:T(2,128)(2,1)} slice(f32[1,2459648]{1,0:T(1,128)} %bitcast.66), slice={[0:1], [0:2459520]} | slice | bytes 9838080 | tf_op jit(solution)/shard_map/slice | solution.py:1872
  585.7 1.4 pad_maximum_fusion
  587.1 0.8 copy-done.3
  588.0 0.6 copy-done.7
  588.6 1.2 add_convert_fusion
  589.8 0.6 copy.56
  (67 shorter events, 0.9 us)
Async XLA Ops:
  0.6 1.4 copy-start
  0.7 5.1 copy-start.23
  0.7 5.2 copy-start.24
  0.7 5.9 copy-start.16
  0.7 6.5 %copy-start.21 = (s32[3]{0:T(128)S(1)}, s32[3]{0:T(128)}, u32[]{:S(2)}) copy-start(s32[3]{0:T(128)} %param.25) | copy-start | bytes 40
  0.7 6.5 %copy-start.12 = (s32[3,1024]{1,0:T(4,128)S(1)}, s32[3,1024]{1,0:T(4,128)}, u32[]{:S(2)}) copy-start(s32[3,1024]{1,0:T(4,128)} %param.26) | copy-start | bytes 36868
  2.4 6.5 %copy-start.17 = (bf16[1280]{0:T(1024)(128)(2,1)S(1)}, bf16[1280]{0:T(1024)(128)(2,1)}, u32[]{:S(2)}) copy-start(bf16[1280]{0:T(1024)(128)(2,1)} %param.29) | copy-start | bytes 7684
  2.4 7.8 %copy-start.11 = (bf16[1280]{0:T(1024)(128)(2,1)S(1)}, bf16[1280]{0:T(1024)(128)(2,1)}, u32[]{:S(2)}) copy-start(bf16[1280]{0:T(1024)(128)(2,1)} %param.37) | copy-start | bytes 7684
  2.4 8.4 %copy-start.18 = (bf16[1280]{0:T(1024)(128)(2,1)S(1)}, bf16[1280]{0:T(1024)(128)(2,1)}, u32[]{:S(2)}) copy-start(bf16[1280]{0:T(1024)(128)(2,1)} %param.36) | copy-start | bytes 7684
  2.4 9.0 %copy-start.19 = (bf16[1280]{0:T(1024)(128)(2,1)S(1)}, bf16[1280]{0:T(1024)(128)(2,1)}, u32[]{:S(2)}) copy-start(bf16[1280]{0:T(1024)(128)(2,1)} %param.38) | copy-start | bytes 7684
  181.4 99.7 %copy-start.2 = (f32[384,1280]{1,0:T(8,128)S(1)}, f32[384,1280]{1,0:T(8,128)}, u32[]{:S(2)}) copy-start(f32[384,1280]{1,0:T(8,128)} %get-tuple-element.38) | copy-start | bytes 5898244
  281.3 1.5 copy-start.6
  283.6 1.2 copy-start.5
  286.7 3.1 copy-start.10
  290.0 3.3 copy-start.22
  406.0 12.5 %copy-start.4 = (bf16[8,3,128,768]{3,2,1,0:T(8,128)(2,1)S(1)}, bf16[8,3,128,768]{3,2,1,0:T(8,128)(2,1)}, u32[]{:S(2)}) copy-start(bf16[8,3,128,768]{3,2,1,0:T(8,128)(2,1)} %get-tuple-element.51) | copy-start | bytes 14155780
  418.5 3.3 copy-start.14
  421.2 1.2 copy-start.13
  576.3 9.4 %copy-start.8 = (f32[256,1280]{1,0:T(8,128)S(1)}, f32[256,1280]{1,0:T(8,128)}, u32[]{:S(2)}) copy-start(f32[256,1280]{1,0:T(8,128)} %get-tuple-element.61) | copy-start | bytes 3932164
  576.3 9.4 %copy-start.9 = (f32[128,1280]{1,0:T(8,128)S(1)}, f32[128,1280]{1,0:T(8,128)}, u32[]{:S(2)}) copy-start(f32[128,1280]{1,0:T(8,128)} %get-tuple-element.57) | copy-start | bytes 1966084
  585.7 1.4 copy-start.15
  585.7 2.3 copy-start.3
  585.7 2.8 copy-start.7
  587.1 3.2 copy-start.1
  588.6 1.2 copy-start.20

commit v9 on v8

--- a/solution.py
+++ b/solution.py
@@ -581,17 +581,10 @@
     return scratch, sems
 
 
-OUTER_STARTS = (0, 48, 96, 112)
-
-
-def attention_kernel(
+def project_kernel(
     frames_ref, gain_ref, shift_ref, cot_ref, query_ref, key_ref, value_ref, bias_ref,
-    mask_ref, live_ref, weights_ref, outer_ref, out_bias_ref, gain_two_ref, shift_two_ref,
-    nfull_ref, qkv_ref, cfull_ref, weight_ref, att_ref, logs_ref, peak_ref, wfull_ref,
-    rows_ref, middle_ref, two_ref,
-    normed_ref, out_ref, vt_ref, outer_all, outer_full,
-    local, first_send, first_recv, cot_send, cot_recv, send, recv, line_send, line_recv,
-    outer_send, outer_recv, plane_send, plane_recv,
+    nfull_ref, qkv_ref, cfull_ref, weight_ref,
+    normed_ref, local, line_send, line_recv, plane_send, plane_recv,
 ):
     place = Place()
     weight_ref[...] = jnp.zeros(weight_ref.shape, BF)
@@ -603,7 +596,7 @@
         normed_ref[rows] = layer_norm(
             frames_ref[rows].astype(F32), gain_ref[...], shift_ref[...]
         ).astype(BF)
-    greet(place, mp_all=True, plane=True)
+    greet(place, line=True, plane=True)
 
     def ready(slot):
         product = lax.dot_general(
@@ -612,14 +605,45 @@
             (((1,), (1,)), ((), ())),
             preferred_element_type=F32,
         )
-        qkv_ref[slot] = (product + bias_ref[...]).astype(BF).reshape(3, 128, 768)
+        qkv_ref[slot] = (product + bias_ref[...]).astype(BF)
 
     drive(
         line_gather(
-            place, normed_ref, nfull_ref, local.at[4], first_send, first_recv, True, ready
+            place, normed_ref, nfull_ref, local.at[0], line_send, line_recv, True, ready
         ),
-        plane_gather(place, cot_ref, cfull_ref, local.at[5], cot_send, cot_recv),
-    )
+        plane_gather(place, cot_ref, cfull_ref, local.at[1], plane_send, plane_recv),
+    )
+
+
+def project(frames, gain, shift, cotangent, query, key, value, bias):
+    return pl.pallas_call(
+        project_kernel,
+        out_shape=(
+            jax.ShapeDtypeStruct((8,) + frames.shape, BF),
+            jax.ShapeDtypeStruct((8, ROWS, 768), BF),
+            jax.ShapeDtypeStruct((8,) + cotangent.shape, BF),
+            jax.ShapeDtypeStruct((768, 1280), BF),
+        ),
+        in_specs=[VMEM, VMEM, VMEM, ANY, VMEM, VMEM, VMEM, VMEM],
+        out_specs=(VMEM, VMEM, ANY, VMEM),
+        scratch_shapes=[pltpu.VMEM((ROWS, 1280), BF), dma(2), dma(4, 3), dma(8), dma(9), dma(9)],
+        compiler_params=params(0),
+        name="project",
+    )(frames, gain, shift, cotangent, query, key, value, bias)
+
+
+OUTER_STARTS = (0, 48, 96, 112)
+
+
+def attend_kernel(
+    qkv_ref, mask_ref, live_ref, weights_ref, outer_ref, frames_ref, out_bias_ref,
+    gain_two_ref, shift_two_ref,
+    att_ref, logs_ref, peak_ref, wfull_ref, rows_ref, middle_ref, two_ref,
+    out_ref, vt_ref, outer_all, outer_full, local, send, recv, line_send, line_recv,
+    outer_send, outer_recv, plane_send, plane_recv,
+):
+    place = Place()
+    greet(place, mp_all=True, plane=True)
     outer = line_gather(
         place, outer_ref, outer_all, local.at[2], outer_send, outer_recv, False, None, 48
     )
@@ -702,17 +726,10 @@
     drive(gather)
 
 
-def attention(
-    frames, gain, shift, cotangent, query, key, value, bias, mask, live, weights, outer,
-    out_bias, gain_two, shift_two,
-):
+def attend(qkv, mask, live, weights, outer, frames, out_bias, gain_two, shift_two):
     return pl.pallas_call(
-        attention_kernel,
+        attend_kernel,
         out_shape=(
-            jax.ShapeDtypeStruct((8,) + frames.shape, BF),
-            jax.ShapeDtypeStruct((8, 3, 128, 768), BF),
-            jax.ShapeDtypeStruct((8,) + cotangent.shape, BF),
-            jax.ShapeDtypeStruct((768, 1280), BF),
             jax.ShapeDtypeStruct((8, 3, 160, 128), BF),
             jax.ShapeDtypeStruct((6, 1, 1024), F32),
             jax.ShapeDtypeStruct((2, 8, 256), F32),
@@ -721,19 +738,14 @@
             jax.ShapeDtypeStruct((ROWS, 1280), F32),
             jax.ShapeDtypeStruct((ROWS, 1280), BF),
         ),
-        in_specs=[VMEM] * 3 + [ANY] + [VMEM] * 6 + [ANY, ANY] + [VMEM] * 3,
-        out_specs=(VMEM, VMEM, ANY, VMEM, VMEM, VMEM, VMEM, ANY, VMEM, VMEM, VMEM),
+        in_specs=[VMEM, VMEM, VMEM, ANY, ANY, VMEM, VMEM, VMEM, VMEM],
+        out_specs=(VMEM, VMEM, VMEM, ANY, VMEM, VMEM, VMEM),
         scratch_shapes=[
-            pltpu.VMEM((ROWS, 1280), BF),
             pltpu.VMEM((8, 3, 160, 128), BF),
             pltpu.VMEM((128, 1024), BF),
             pltpu.VMEM((192, 1280), BF),
             pltpu.VMEM((8, 192, 1280), BF),
-            dma(6),
-            dma(4, 3),
-            dma(8),
-            dma(9),
-            dma(9),
+            dma(4),
             dma(8),
             dma(8),
             dma(4, 3),
@@ -743,12 +755,9 @@
             dma(9),
             dma(9),
         ],
-        compiler_params=params(0, 56),
-        name="attention",
-    )(
-        frames, gain, shift, cotangent, query, key, value, bias, mask, live, weights, outer,
-        out_bias, gain_two, shift_two,
-    )
+        compiler_params=params(1),
+        name="attend",
+    )(qkv, mask, live, weights, outer, frames, out_bias, gain_two, shift_two)
 
 
 def flatten(*pairs):
@@ -931,11 +940,12 @@
 
 def attend_back_kernel(
     split, qkv_in, mask_ref, logs_ref, pull_ref, hidden_in, weights_ref, feed_grads_in,
-    out_grad_in, dqkv_ref, feed_ref, feed_sum_ref, out_sum_ref,
-    qkv_ref, hidden_ref, feed_grads_ref, out_grad_ref, load,
+    out_grad_in, normed_in, dqkv_ref, feed_ref, feed_sum_ref, out_sum_ref, joined_ref, column_ref,
+    hidden_ref, feed_grads_ref, out_grad_ref, normed_ref, load, normed_load,
     grad_ref, kt_ref, dk_ref, dv_ref, block_ref, middle_ref, local, send, recv, *scratch,
 ):
     place = Place()
+    qkv_ref = dqkv_ref
     (
         line_bufs, line_sems, plane_bufs, plane_sems,
         out_plane_bufs, out_plane_sems, out_line_bufs, out_line_sems,
@@ -1086,10 +1096,43 @@
         def _():
             next(out_plane)
 
+    def bring(slot):
+        return pltpu.make_async_copy(
+            normed_in.at[slot], normed_ref.at[slot % 2], normed_load.at[slot % 2]
+        )
+
+    def weight_grad(slot):
+        bring(slot).wait()
+        if slot < 7:
+            bring(slot + 1).start()
+        grads = dqkv_ref[slot].reshape(ROWS, 768)
+        product = lax.dot_general(
+            normed_ref[slot % 2],
+            grads,
+            (((0,), (0,)), ((), ())),
+            preferred_element_type=F32,
+        )
+        column = jnp.sum(grads.astype(F32), axis=0, keepdims=True)
+        if slot == 0:
+            joined_ref[...] = product
+            column_ref[...] = column
+        else:
+            joined_ref[...] += product
+            column_ref[...] += column
+
+    bring(0).start()
+    next(line)
+    next(out_line)
+    for slot in range(4):
+        weight_grad(slot)
+    next(line)
+    next(out_line)
+    for slot in range(4, 8):
+        weight_grad(slot)
     drive(line, out_line, plane, out_plane)
 
 
-def attend_back(qkv, mask, logs, pull, hidden, weights, feed_grads, out_grad):
+def attend_back(qkv, mask, logs, pull, hidden, weights, feed_grads, out_grad, normed):
     shapes, split = flatten(
         *line_reduce_scratch(336, 1280, False),
         *plane_reduce_scratch(192, 1280),
@@ -1103,12 +1146,16 @@
             jax.ShapeDtypeStruct((ROWS, 1280), F32),
             jax.ShapeDtypeStruct((336, 1280), F32),
             jax.ShapeDtypeStruct((48, 1280), F32),
+            jax.ShapeDtypeStruct((1280, 768), F32),
+            jax.ShapeDtypeStruct((1, 768), F32),
         ),
-        in_specs=[ANY, VMEM, VMEM, ANY, ANY, VMEM, ANY, ANY],
-        out_specs=(VMEM,) * 4,
+        in_specs=[ANY, VMEM, VMEM, ANY, ANY, VMEM, ANY, ANY, ANY],
+        out_specs=(VMEM,) * 6,
         scratch_shapes=[
-            *(pltpu.VMEM(ref.shape, BF) for ref in (qkv, hidden, feed_grads, out_grad)),
+            *(pltpu.VMEM(ref.shape, BF) for ref in (hidden, feed_grads, out_grad)),
+            pltpu.VMEM((2, ROWS, 1280), BF),
             dma(4),
+            dma(2),
             pltpu.VMEM((8, 3, 160, 128), BF),
             pltpu.VMEM((128, 1024), BF),
             pltpu.VMEM((1024, 128), F32),
@@ -1122,7 +1169,7 @@
         ],
         compiler_params=params(2, 62),
         name="attend_back",
-    )(qkv, mask, logs, pull, hidden, weights, feed_grads, out_grad)
+    )(qkv, mask, logs, pull, hidden, weights, feed_grads, out_grad, normed)
 
 
 GROUP_ROWS = 4832
@@ -1765,10 +1812,7 @@
     message = jnp.concatenate([up_share, bias_rows])
     outer_start = jnp.minimum(group * 48, 112)
     outer = lax.dynamic_slice_in_dim(out_weight, outer_start, 48, 0)
-    (
-        normed_full, qkv, upstream_full, joined_weight, attended, logs, peaks, gathered,
-        out_rows, middle, normed_two,
-    ) = attention(
+    normed_full, qkv, upstream_full, joined_weight = project(
         frame_rows,
         gain_first[None],
         shift_first[None],
@@ -1777,10 +1821,15 @@
         key_weight.T,
         value_weight.T,
         joined_bias,
+    )
+    qkv = qkv.reshape(8, 3, 128, 768)
+    attended, logs, peaks, gathered, out_rows, middle, normed_two = attend(
+        qkv,
         mask,
         live,
         message,
         outer,
+        frame_rows,
         out_bias.astype(F32)[None],
         gain_second[None],
         shift_second[None],
@@ -1805,15 +1854,12 @@
         out_grad.astype(BF).reshape(4, 2, 4, 40, 1280), ((0, 0),) * 3 + ((0, 8), (0, 0))
     )
     out_quarters = out_quarters.transpose(2, 1, 0, 3, 4).reshape(4, 2, 192, 1280)
-    joined_grad, feed, feed_sum, out_sum = attend_back(
-        qkv, mask, logs, attended_grad, hidden, down_all, feed_grads, out_quarters
+    joined_grad, feed, feed_sum, out_sum, joined_weight_grad, joined_bias_grad = attend_back(
+        qkv, mask, logs, attended_grad, hidden, down_all, feed_grads, out_quarters, normed_full
     )
     layer_out = (middle + feed + down_bias.astype(F32)).astype(BF)
     joined_grad = joined_grad.reshape(8, ROWS, 768)
-    joined_weight_grad = jnp.einsum(
-        "prd,pre->de", normed_full, joined_grad, preferred_element_type=F32
-    )
-    joined_bias_grad = jnp.sum(joined_grad.astype(F32), axis=(0, 1))
+    joined_bias_grad = joined_bias_grad[0]
 
     level = lax.axis_index("mp") // 2
     up_bias_share = lax.dynamic_slice_in_dim(feed_sum[320], level * 160, 160, 0)

time: 599 us -> 588 us (0.982)
  matrix products: 18.4 us -> 5.1 us
  local copies, waits for them, and re-layouts: 32.1 us -> 43.9 us
  Pallas kernels: 526 us -> 518 us
    unnamed x56 -> x88, local copies, waits for them, and re-layouts: 6.49 us -> 21.6 us
    dot_general x1 -> x0, matrix products: 12.5 us -> none  [fast_body(): jnp.einsum('prd,pre->de', normed_full, joined_grad, preferred_element_typ...]
    pallas_call x1, Pallas kernels: 99.7 us -> 87.8 us  [feed_forward(): pl.pallas_call(functools.partial(feed_forward_kernel, split), out_shape=(...]
    pallas_call x1, Pallas kernels: 110 us -> 116 us  [attend_back(): pl.pallas_call(functools.partial(attend_back_kernel, split), out_shape=(j...]
    pallas_call x1 -> x2, Pallas kernels: 166 us -> 163 us  [the longest x1 84.9 us: attend(): pl.pallas_call(attend_kernel, out_shape=(jax.ShapeDtypeStruct((8, 3, 160,...]
where the time goes in v9:
time: 588 us; the launch traced here: 579 us
  Pallas kernels  518 us (88%)
  local copies, waits for them, and re-layouts  43.9 us (7%)
  other arithmetic  7.81 us (1%)
    pallas_call x1, Pallas kernels, attend_back(): pl.pallas_call(functools.partial(attend_back_kernel, split), out_shape=(j...  116 us
    pallas_call x1, Pallas kernels, feed_forward(): pl.pallas_call(functools.partial(feed_forward_kernel, split), out_shape=(...  87.8 us
    pallas_call x1, Pallas kernels, attend(): pl.pallas_call(attend_kernel, out_shape=(jax.ShapeDtypeStruct((8, 3, 160,...  84.9 us
    pallas_call x1, Pallas kernels, project(): pl.pallas_call(project_kernel, out_shape=(jax.ShapeDtypeStruct((8,) + fra...  78.5 us
    pallas_call x1, Pallas kernels, finish(): pl.pallas_call(functools.partial(finish_kernel, split), out_shape=(jax.Sh...  67.8 us
    pallas_call x1, Pallas kernels, share_master(): pl.pallas_call(functools.partial(share_master_kernel, split), out_shape=(...  58.2 us
    pallas_call x1, Pallas kernels, optimize(): pl.pallas_call(optimize_kernel, grid=(pl.cdiv(SHARE_ENTRIES, STEP_ENTRIES...  24.8 us
    unnamed x88, local copies, waits for them, and re-layouts  21.6 us

profile of v9, /device:TPU:0, one launch (start us, length us, event | category | flops | bytes accessed | tf_op | source)
XLA Modules:
  0.0 579.3 jit_solution(2272006011727104048)
XLA Ops:
  0.7 1.4 copy-done
  2.1 1.1 constant_dynamic-slice_fusion.3
  3.3 1.4 copy.44
  4.6 0.8 dynamic_slice.18
  5.8 1.0 copy-done.13
  6.8 1.0 copy-done.14
  7.8 1.0 copy-done.15
  8.8 78.5 %project.1 = (bf16[8,384,1280]{2,1,0:T(8,128)(2,1)}, bf16[8,384,768]{2,1,0:T(8,128)(2,1)S(1)}, bf16[8,384,1280]{2,1,0:T(8,128)(2,1)}, bf16[768,1280]{1,0:T(8,128)(2,1)S(1)}) custom-call(bf16[384,1280]{1,0:T(8,128)(2,1)S(1)} %bitcast.64, f32[1,1280]{1,0:T(1,128)S(1)} %reshape.197.gain_ref, f32[1,1280]{1,0:T(1,128)S(1)} %reshape.198.shift_ref, ...), custom_call_target="tpu_custom_call" | custom-call | tf_op jit(solution)/shard_map/project/pallas_call | solution.py:619
  87.3 2.2 copy-done.4
  89.4 1.3 copy-done.10
  90.7 0.9 constant_dynamic-slice_fusion.2.outer_ref
  91.7 0.8 select_bitcast_fusion
  92.5 1.7 copy.36.mask_ref
  94.3 1.4 copy-done.7
  95.7 84.9 %attend.1 = (bf16[8,3,160,128]{3,2,1,0:T(8,128)(2,1)S(1)}, f32[6,1,1024]{2,1,0:T(1,128)S(1)}, f32[2,8,256]{2,1,0:T(8,128)S(1)}, bf16[4,176,1280]{2,1,0:T(8,128)(...) custom-call(bf16[8,3,128,768]{3,2,1,0:T(8,128)(2,1)} %bitcast.60, ...), custom_call_target="tpu_custom_call" | custom-call | tf_op jit(solution)/shard_map/attend/pallas_call | solution.py:730
  180.6 0.9 copy-done.12
  181.5 0.6 copy-done.18
  182.2 0.6 copy-done.19
  182.8 1.7 copy-done.20
  184.4 0.9 copy-done.22
  185.4 1.2 copy-done.11
  186.6 0.7 reshape.205.bias_ref
  187.3 1.8 constant_dynamic-slice_fusion.1.down_ref
  189.1 87.8 %feed_forward.1 = (f32[384,1280]{1,0:T(8,128)}, bf16[8,384,640]{2,1,0:T(8,128)(2,1)}, bf16[4,336,1280]{2,1,0:T(8,128)(2,1)}, f32[1,640]{1,0:T(1,128)}, bf16[4,160,1280]{2,1,0:T(8,128)(2,1)}) custom-call(bf16[384,1280]{1,0:T(8,128)(2,1)} %copy-done.12, bf16[8,384,1280]{2,1,0:T(8,128)(2,1)} %get-tuple-element.44.upstream_ref, ...), custom_call_target="tpu_custom_call" | custom-call | tf_op jit(solution)/shard_map/feed_forward/pallas_call | solution.py:910
  277.1 0.3 multiply_reduce_fusion.2
  277.4 1.2 copy-done.24
  278.6 0.7 multiply_reduce_fusion
  279.3 0.6 fusion.5
  280.0 0.6 copy-done.9
  280.5 1.7 convert_reduce_fusion.1
  282.4 2.3 bitcast_convert_fusion
  285.0 2.3 pad.20
  287.3 1.0 copy-done.21
  288.3 2.8 fusion.pull_ref
  291.1 116.4 %attend_back.1 = (bf16[8,3,128,768]{3,2,1,0:T(8,128)(2,1)}, f32[384,1280]{1,0:T(8,128)}, f32[336,1280]{1,0:T(8,128)}, f32[48,1280]{1,0:T(8,128)}, f32[1280,768]{1,0:T(8,128)}, /*index=5*/f32[1,768]{1,0:T(1,128)}) custom-call(bf16[8,3,128,768]{3,2,1,0:T(8,128)(2,1)} %bitcast.61, f32[3,1024,1]{2,1,0:T(8,128)} %copy.36.mask_ref, f32[6,1,1024]{2,1,0:T(1,128)} %copy-done.18, ...), custom_call_target="tpu_custom_call" | custom-call | tf_op jit(solution)/shard_map/attend_back/pallas_call | solution.py:1142
  407.5 1.6 copy.40.bias_column_ref
  409.1 0.8 slice.23
  410.2 0.6 fusion.6
  410.8 67.8 %finish.1 = (f32[128,1280]{1,0:T(8,128)}, f32[4808,128]{1,0:T(8,128)}, f32[8,128]{1,0:T(8,128)}, f32[2,8,128]{2,1,0:T(8,128)}) custom-call(bf16[8,384,768]{2,1,0:T(8,128)(2,1)} %bitcast.71, bf16[768,1280]{1,0:T(8,128)(2,1)} %copy-done.10, f32[1280,768]{1,0:T(8,128)} %get-tuple-element.56.joined_ref, f32[1,768]{1,0:T(1,128)} %get-tuple-element.57.bias_ref, ...), custom_call_target="tpu_custom_call" | custom-call | tf_op jit(solution)/shard_map/finish/pallas_call | solution.py:1546
  481.3 0.6 pad_maximum_fusion.2.rates_ref
  481.9 24.8 %optimize.1 = (f32[1,614880]{1,0:T(1,128)}, f32[1,614880]{1,0:T(1,128)}, f32[1,614880]{1,0:T(1,128)}, f32[1,614880]{1,0:T(1,128)}, f32[1,615424]{1,0:T(1,128)}) custom-call(f32[3]{0:T(128)} %pad_maximum_fusion.2.rates_ref, f32[2,8,128]{2,1,0:T(8,128)} %get-tuple-element.62.roots_ref, f32[1,615424]{1,0:T(1,128)} %bitcast.76, f32[1,614880]{1,0:T(1,128)} %master_ref.1, ...), custom_call_target="tpu_custom_call" | custom-call | tf_op jit(solution)/shard_map/optimize/pallas_call | solution.py:1745
  506.7 58.2 %share_master.1 = (f32[19216,128]{1,0:T(8,128)}, f32[256,1280]{1,0:T(8,128)}) custom-call(f32[4808,128]{1,0:T(8,128)} %bitcast.77, bf16[8,384,768]{2,1,0:T(8,128)(2,1)} %bitcast.72, bf16[768,1280]{1,0:T(8,128)(2,1)} %copy-done.10, bf16[384,1280]{1,0:T(8,128)(2,1)} %bitcast.63, f32[384,1280]{1,0:T(8,128)} %get-tuple-element.77.middle_in, f32[1,1280]{1,0:T(1,128)} %copy-done.16), custom_call_target="tpu_custom_call" | custom-call | tf_op jit(solution)/shard_map/share_master/pallas_call | solution.py:1689
  564.9 9.4 %slice.32 = bf16[1,2459520]{1,0:T(2,128)(2,1)} slice(f32[1,2459648]{1,0:T(1,128)} %bitcast.74), slice={[0:1], [0:2459520]} | slice | bytes 9838080 | tf_op jit(solution)/shard_map/slice | solution.py:1918
  574.3 1.4 pad_maximum_fusion
  575.7 0.8 copy-done.3
  576.5 0.6 copy-done.25
  577.1 1.2 add_convert_fusion
  578.3 0.6 copy.53
  (97 shorter events, 1.4 us)
Async XLA Ops:
  0.6 1.5 copy-start
  0.7 5.1 copy-start.5
  0.7 4.8 copy-start.39
  0.7 4.9 copy-start.40
  0.7 5.0 copy-start.33
  0.7 5.0 copy-start.34
  3.2 2.5 copy-start.8
  5.4 86.2 %copy-start.38 = (s32[3]{0:T(128)S(1)}, s32[3]{0:T(128)}, u32[]{:S(2)}) copy-start(s32[3]{0:T(128)} %param.25) | copy-start | bytes 40
  5.7 88.4 %copy-start.16 = (f32[1,1280]{1,0:T(1,128)}, f32[1,1280]{1,0:T(1,128)S(1)}, u32[]{:S(2)}) copy-start(f32[1,1280]{1,0:T(1,128)S(1)} %reshape.197.gain_ref) | copy-start | bytes 15364
  5.7 88.4 %copy-start.17 = (f32[1,1280]{1,0:T(1,128)}, f32[1,1280]{1,0:T(1,128)S(1)}, u32[]{:S(2)}) copy-start(f32[1,1280]{1,0:T(1,128)S(1)} %reshape.198.shift_ref) | copy-start | bytes 15364
  5.8 1.0 copy-start.13
  6.8 1.0 copy-start.14
  7.8 1.0 copy-start.15
  8.8 85.5 %copy-start.29 = (bf16[1280]{0:T(1024)(128)(2,1)S(1)}, bf16[1280]{0:T(1024)(128)(2,1)}, u32[]{:S(2)}) copy-start(bf16[1280]{0:T(1024)(128)(2,1)} %param.37) | copy-start | bytes 7684
  8.8 85.5 %copy-start.35 = (bf16[1280]{0:T(1024)(128)(2,1)S(1)}, bf16[1280]{0:T(1024)(128)(2,1)}, u32[]{:S(2)}) copy-start(bf16[1280]{0:T(1024)(128)(2,1)} %param.36) | copy-start | bytes 7684
  8.8 85.5 %copy-start.36 = (bf16[1280]{0:T(1024)(128)(2,1)S(1)}, bf16[1280]{0:T(1024)(128)(2,1)}, u32[]{:S(2)}) copy-start(bf16[1280]{0:T(1024)(128)(2,1)} %param.38) | copy-start | bytes 7684
  8.8 85.5 %copy-start.6 = (bf16[128,3,1280]{2,0,1:T(8,128)(2,1)S(1)}, bf16[128,3,1280]{2,0,1:T(8,128)(2,1)}, u32[]{:S(2)}) copy-start(bf16[128,3,1280]{2,0,1:T(8,128)(2,1)} %param.24) | copy-start | bytes 2949124
  87.2 2.2 copy-start.4
  89.4 1.3 copy-start.10
  94.3 1.4 copy-start.7
  180.6 0.9 copy-start.12
  181.5 0.6 copy-start.18
  182.2 0.6 copy-start.19
  182.8 1.7 copy-start.20
  184.4 0.9 copy-start.22
  185.4 1.2 copy-start.11
  185.4 93.9 %copy-start.2 = (f32[384,1280]{1,0:T(8,128)}, f32[384,1280]{1,0:T(8,128)S(1)}, u32[]{:S(2)}) copy-start(f32[384,1280]{1,0:T(8,128)S(1)} %get-tuple-element.41) | copy-start | bytes 5898244
  277.0 1.5 copy-start.24
  279.3 1.2 copy-start.9
  280.5 1.9 copy-start.23
  282.4 2.3 copy-start.28
  285.0 3.3 copy-start.21
  291.1 119.1 %copy-start.31 = (f32[3]{0:T(128)S(1)}, f32[3]{0:T(128)}, u32[]{:S(2)}) copy-start(f32[3]{0:T(128)} %param.47) | copy-start | bytes 40
  410.2 0.6 copy-start.30
  564.9 9.4 %copy-start.26 = (f32[256,1280]{1,0:T(8,128)S(1)}, f32[256,1280]{1,0:T(8,128)}, u32[]{:S(2)}) copy-start(f32[256,1280]{1,0:T(8,128)} %get-tuple-element.65) | copy-start | bytes 3932164
  564.9 9.4 %copy-start.27 = (f32[128,1280]{1,0:T(8,128)S(1)}, f32[128,1280]{1,0:T(8,128)}, u32[]{:S(2)}) copy-start(f32[128,1280]{1,0:T(8,128)} %get-tuple-element.61) | copy-start | bytes 1966084
  574.3 1.4 copy-start.32
  574.3 2.3 copy-start.3
  574.3 2.8 copy-start.25
  575.7 3.2 copy-start.1
  577.1 1.2 copy-start.37

commit v10 on v9

--- a/solution.py
+++ b/solution.py
@@ -712,15 +712,13 @@
                 rows_ref[pl.ds((level * 2 + core) * 160 + start, 48)] = outer_full[
                     group * 2 + core, pl.ds(level * 48, 48)
                 ]
-    for clip in range(3):
-        rows = pl.ds(clip * 128, 128)
-        branch = lax.dot_general(
-            att_ref[:, clip].reshape(1280, 128),
-            rows_ref[...],
-            (((0,), (0,)), ((), ())),
-            preferred_element_type=F32,
-        )
-        middle = frames_ref[rows].astype(F32) + (branch + out_bias_ref[...])
+    mixed = jnp.concatenate([att_ref[:, clip].reshape(1280, 128) for clip in range(3)], axis=1)
+    middle_ref[...] = lax.dot_general(
+        mixed, rows_ref[...], (((0,), (0,)), ((), ())), preferred_element_type=F32
+    )
+    for start in range(0, ROWS, 128):
+        rows = pl.ds(start, 128)
+        middle = frames_ref[rows].astype(F32) + (middle_ref[rows] + out_bias_ref[...])
         middle_ref[rows] = middle
         two_ref[rows] = layer_norm(middle, gain_two_ref[...], shift_two_ref[...]).astype(BF)
     drive(gather)
@@ -1188,6 +1186,8 @@
 )
 PACK_END = 19216
 SHARE_ROWS = 4808
+KEY_END = 409760
+SHARE_ENTRIES = 614880
 
 
 def segment_table():
@@ -1388,7 +1388,7 @@
 def finish_kernel(
     split, grad_in, weight_in, joined_ref, bias_ref, bias_column_ref, sum_ref, out_ref,
     up_bias_ref, small_ref, peak_ref, frames_in, middle_in, gain_ref, shift_ref, cap_ref,
-    input_grad_ref, grads_ref, small_out, roots_out,
+    input_grad_ref, grads_ref, small_out, factor_ref,
     grad_ref, weight_ref, frames_ref, middle_ref, load,
     stage, packed, sum_rows, column, tiles, small_in, small_all, peak_all, edge,
     local, small_send, small_recv, plane_send, plane_recv, *scratch,
@@ -1492,10 +1492,29 @@
     top = peak_ref[...]
     for group in peers:
         top = jnp.maximum(top, peak_all[group])
+    roots = []
     for head in range(2):
         peak = jnp.max(jnp.max(top[head], axis=0, keepdims=True), axis=1, keepdims=True)
-        root = jnp.sqrt(cap_ref[...] / jnp.maximum(peak * (1.0 / math.sqrt(HD)), cap_ref[...]))
-        roots_out[head] = jnp.broadcast_to(jnp.where(place.dp == 0, root, 1.0), (8, 128))
+        roots.append(
+            jnp.sqrt(cap_ref[...] / jnp.maximum(peak * (1.0 / math.sqrt(HD)), cap_ref[...]))
+        )
+    factor_ref[...] = jnp.ones(factor_ref.shape, F32)
+
+    @pl.when(place.dp == 0)
+    def _():
+        full = KEY_END // 128 // 5 * 5
+        for index in range(5):
+            entry = (lane_of(1) + 128 * index).astype(F32)
+            block = jnp.floor((entry + 0.5) * (1.0 / HD))
+            odd = block - 2.0 * jnp.floor(block * 0.5) > 0.5
+            factor = jnp.where(odd, roots[1], roots[0])
+            factor_ref[pl.ds(index, full // 5, stride=5), :] = jnp.broadcast_to(
+                factor, (full // 5, 128)
+            )
+            left = KEY_END - (full + index) * 128
+            if left > 0:
+                factor_ref[pl.ds(full + index, 1)] = jnp.where(lane_of(1) < left, factor, 1.0)
+
     whole = jnp.sum(small_all[...], axis=0)
     lane = lane_of(8)
     row = lax.broadcasted_iota(jnp.int32, (8, 128), 0)
@@ -1549,7 +1568,7 @@
             jax.ShapeDtypeStruct((FIRST_ROWS, 1280), F32),
             jax.ShapeDtypeStruct((SHARE_ROWS, 128), F32),
             jax.ShapeDtypeStruct((8, 128), F32),
-            jax.ShapeDtypeStruct((2, 8, 128), F32),
+            jax.ShapeDtypeStruct((SHARE_ROWS, 128), F32),
         ),
         in_specs=[ANY, ANY] + [VMEM] * 8 + [ANY, ANY, VMEM, VMEM, VMEM],
         out_specs=(VMEM,) * 4,
@@ -1713,48 +1732,35 @@
 
 
 def optimize_kernel(
-    rates_ref, roots_ref, grads_ref, master_ref, first_ref, second_ref,
+    rates_ref, factor_ref, grads_ref, master_ref, first_ref, second_ref,
     owned_out, master_out, first_out, second_out, padded_out,
 ):
     entry = lax.broadcasted_iota(jnp.int32, (1, STEP_ENTRIES), 1)
-    entry = entry + pl.program_id(0) * STEP_ENTRIES
     grads = grads_ref[...]
     first = BETA_FIRST * first_ref[...] + (1.0 - BETA_FIRST) * grads
     second = BETA_SECOND * second_ref[...] + (1.0 - BETA_SECOND) * grads * grads
     change = first * rates_ref[0] / (jnp.sqrt(second * rates_ref[1]) + ADAM_EPSILON)
-    block = jnp.floor((entry.astype(F32) + 0.5) * (1.0 / HD))
-    odd = block - 2.0 * jnp.floor(block * 0.5) > 0.5
-    factor = jnp.where(
-        entry < KEY_END, jnp.where(odd, roots_ref[1, 0:1, 0:1], roots_ref[0, 0:1, 0:1]), 1.0
-    )
-    master = (master_ref[...] * rates_ref[2] - change) * factor
+    master = (master_ref[...] * rates_ref[2] - change) * factor_ref[...]
     owned_out[...] = grads
     master_out[...] = master
     first_out[...] = first
     second_out[...] = second
-    padded_out[...] = jnp.where(entry < SHARE_ENTRIES, master, 0.0)
-
-
-KEY_END = 409760
-SHARE_ENTRIES = 614880
-
-
-def optimize(rates, roots, grads, master, first, second):
+    left = SHARE_ENTRIES - pl.program_id(0) * STEP_ENTRIES
+    padded_out[...] = jnp.where(entry < left, master, 0.0)
+
+
+def optimize(rates, factor, grads, master, first, second):
     block = pl.BlockSpec((1, STEP_ENTRIES), lambda step: (0, step))
     share = jax.ShapeDtypeStruct((1, SHARE_ENTRIES), F32)
     return pl.pallas_call(
         optimize_kernel,
         grid=(pl.cdiv(SHARE_ENTRIES, STEP_ENTRIES),),
         out_shape=(share,) * 4 + (jax.ShapeDtypeStruct((1, SHARE_ROWS * 128), F32),),
-        in_specs=[
-            pl.BlockSpec(memory_space=pltpu.SMEM),
-            pl.BlockSpec((2, 8, 128), lambda step: (0, 0, 0)),
-        ]
-        + [block] * 4,
+        in_specs=[pl.BlockSpec(memory_space=pltpu.SMEM)] + [block] * 5,
         out_specs=(block,) * 5,
         compiler_params=pltpu.CompilerParams(vmem_limit_bytes=62 << 20),
         name="optimize",
-    )(rates, roots, grads, master, first, second)
+    )(rates, factor, grads, master, first, second)
 
 
 def fast_body(
@@ -1875,7 +1881,7 @@
             jnp.zeros((512,), F32),
         ]
     ).reshape(44, 128)
-    first_grad, grad_rows, small_sum, roots = finish(
+    first_grad, grad_rows, small_sum, factor_rows = finish(
         joined_grad,
         joined_weight,
         joined_weight_grad,
@@ -1903,7 +1909,12 @@
         ]
     )
     owned_grads, master_new, first_new, second_new, padded = optimize(
-        rates, roots, grad_rows.reshape(1, SHARE_ROWS * 128), master, moment_one, moment_two
+        rates,
+        factor_rows.reshape(1, SHARE_ROWS * 128),
+        grad_rows.reshape(1, SHARE_ROWS * 128),
+        master,
+        moment_one,
+        moment_two,
     )
     whole, second_grad = share_master(
         padded.reshape(SHARE_ROWS, 128),

time: 588 us -> 577 us (0.981)
  Pallas kernels: 518 us -> 508 us
    pallas_call x1, Pallas kernels: 24.8 us -> 13.4 us  [optimize(): pl.pallas_call(optimize_kernel, grid=(pl.cdiv(SHARE_ENTRIES, STEP_ENTRIES...]
where the time goes in v10:
time: 577 us; the launch traced here: 569 us
  Pallas kernels  508 us (88%)
  local copies, waits for them, and re-layouts  43.9 us (8%)
  other arithmetic  7.81 us (1%)
    pallas_call x1, Pallas kernels, attend_back(): pl.pallas_call(functools.partial(attend_back_kernel, split), out_shape=(j...  116 us
    pallas_call x1, Pallas kernels, feed_forward(): pl.pallas_call(functools.partial(feed_forward_kernel, split), out_shape=(...  87.8 us
    pallas_call x1, Pallas kernels, attend(): pl.pallas_call(attend_kernel, out_shape=(jax.ShapeDtypeStruct((8, 3, 160,...  84.8 us
    pallas_call x1, Pallas kernels, project(): pl.pallas_call(project_kernel, out_shape=(jax.ShapeDtypeStruct((8,) + fra...  78.5 us
    pallas_call x1, Pallas kernels, finish(): pl.pallas_call(functools.partial(finish_kernel, split), out_shape=(jax.Sh...  68.8 us
    pallas_call x1, Pallas kernels, share_master(): pl.pallas_call(functools.partial(share_master_kernel, split), out_shape=(...  58.1 us
    unnamed x88, local copies, waits for them, and re-layouts  21.6 us
    pallas_call x1, Pallas kernels, optimize(): pl.pallas_call(optimize_kernel, grid=(pl.cdiv(SHARE_ENTRIES, STEP_ENTRIES...  13.4 us

profile of v10, /device:TPU:0, one launch (start us, length us, event | category | flops | bytes accessed | tf_op | source)
XLA Modules:
  0.0 568.6 jit_solution(1218959937831349960)
XLA Ops:
  0.7 1.4 copy-done
  2.1 1.1 constant_dynamic-slice_fusion.3
  3.3 1.4 copy.44
  4.6 0.8 dynamic_slice.18
  5.8 1.0 copy-done.13
  6.8 1.0 copy-done.14
  7.8 1.0 copy-done.15
  8.8 78.5 %project.1 = (bf16[8,384,1280]{2,1,0:T(8,128)(2,1)}, bf16[8,384,768]{2,1,0:T(8,128)(2,1)S(1)}, bf16[8,384,1280]{2,1,0:T(8,128)(2,1)}, bf16[768,1280]{1,0:T(8,128)(2,1)S(1)}) custom-call(bf16[384,1280]{1,0:T(8,128)(2,1)S(1)} %bitcast.65, f32[1,1280]{1,0:T(1,128)S(1)} %reshape.201.gain_ref, f32[1,1280]{1,0:T(1,128)S(1)} %reshape.202.shift_ref, ...), custom_call_target="tpu_custom_call" | custom-call | tf_op jit(solution)/shard_map/project/pallas_call | solution.py:619
  87.3 2.2 copy-done.4
  89.4 1.3 copy-done.10
  90.7 0.9 constant_dynamic-slice_fusion.2.outer_ref
  91.7 0.8 select_bitcast_fusion
  92.5 1.7 copy.36.mask_ref
  94.3 1.4 copy-done.7
  95.7 84.8 %attend.1 = (bf16[8,3,160,128]{3,2,1,0:T(8,128)(2,1)S(1)}, f32[6,1,1024]{2,1,0:T(1,128)S(1)}, f32[2,8,256]{2,1,0:T(8,128)S(1)}, bf16[4,176,1280]{2,1,0:T(8,128)(...) custom-call(bf16[8,3,128,768]{3,2,1,0:T(8,128)(2,1)} %bitcast.61, ...), custom_call_target="tpu_custom_call" | custom-call | tf_op jit(solution)/shard_map/attend/pallas_call | solution.py:728
  180.5 0.9 copy-done.12
  181.5 0.6 copy-done.18
  182.1 0.6 copy-done.19
  182.7 1.7 copy-done.20
  184.4 0.9 copy-done.22
  185.3 1.2 copy-done.11
  186.5 0.7 reshape.209.bias_ref
  187.2 1.8 constant_dynamic-slice_fusion.1.down_ref
  189.0 87.8 %feed_forward.1 = (f32[384,1280]{1,0:T(8,128)}, bf16[8,384,640]{2,1,0:T(8,128)(2,1)}, bf16[4,336,1280]{2,1,0:T(8,128)(2,1)}, f32[1,640]{1,0:T(1,128)}, bf16[4,160,1280]{2,1,0:T(8,128)(2,1)}) custom-call(bf16[384,1280]{1,0:T(8,128)(2,1)} %copy-done.12, bf16[8,384,1280]{2,1,0:T(8,128)(2,1)} %get-tuple-element.44.upstream_ref, ...), custom_call_target="tpu_custom_call" | custom-call | tf_op jit(solution)/shard_map/feed_forward/pallas_call | solution.py:908
  277.0 0.3 multiply_reduce_fusion.2
  277.4 1.2 copy-done.24
  278.6 0.7 multiply_reduce_fusion
  279.3 0.6 fusion.5
  279.9 0.6 copy-done.9
  280.5 1.7 convert_reduce_fusion.1
  282.4 2.4 bitcast_convert_fusion
  285.1 2.3 pad.20
  287.5 1.0 copy-done.21
  288.5 2.8 fusion.pull_ref
  291.3 116.1 %attend_back.1 = (bf16[8,3,128,768]{3,2,1,0:T(8,128)(2,1)}, f32[384,1280]{1,0:T(8,128)}, f32[336,1280]{1,0:T(8,128)}, f32[48,1280]{1,0:T(8,128)}, f32[1280,768]{1,0:T(8,128)}, /*index=5*/f32[1,768]{1,0:T(1,128)}) custom-call(bf16[8,3,128,768]{3,2,1,0:T(8,128)(2,1)} %bitcast.62, f32[3,1024,1]{2,1,0:T(8,128)} %copy.36.mask_ref, f32[6,1,1024]{2,1,0:T(1,128)} %copy-done.18, ...), custom_call_target="tpu_custom_call" | custom-call | tf_op jit(solution)/shard_map/attend_back/pallas_call | solution.py:1140
  407.4 1.6 copy.40.bias_column_ref
  409.0 0.8 slice.23
  410.1 0.6 fusion.6
  410.7 68.8 %finish.1 = (f32[128,1280]{1,0:T(8,128)}, f32[4808,128]{1,0:T(8,128)}, f32[8,128]{1,0:T(8,128)}, f32[4808,128]{1,0:T(8,128)}) custom-call(bf16[8,384,768]{2,1,0:T(8,128)(2,1)} %bitcast.72, bf16[768,1280]{1,0:T(8,128)(2,1)} %copy-done.10, f32[1280,768]{1,0:T(8,128)} %get-tuple-element.56.joined_ref, f32[1,768]{1,0:T(1,128)} %get-tuple-element.57.bias_ref, ...), custom_call_target="tpu_custom_call" | custom-call | tf_op jit(solution)/shard_map/finish/pallas_call | solution.py:1565
  482.2 0.6 pad_maximum_fusion.2.rates_ref
  482.8 13.4 %optimize.1 = (f32[1,614880]{1,0:T(1,128)}, f32[1,614880]{1,0:T(1,128)}, f32[1,614880]{1,0:T(1,128)}, f32[1,614880]{1,0:T(1,128)}, f32[1,615424]{1,0:T(1,128)}) custom-call(f32[3]{0:T(128)} %pad_maximum_fusion.2.rates_ref, f32[1,615424]{1,0:T(1,128)} %bitcast.78, f32[1,615424]{1,0:T(1,128)} %bitcast.77, f32[1,614880]{1,0:T(1,128)} %master_ref.1, ...), custom_call_target="tpu_custom_call" | custom-call | tf_op jit(solution)/shard_map/optimize/pallas_call | solution.py:1755
  496.2 58.1 %share_master.1 = (f32[19216,128]{1,0:T(8,128)}, f32[256,1280]{1,0:T(8,128)}) custom-call(f32[4808,128]{1,0:T(8,128)} %bitcast.79, bf16[8,384,768]{2,1,0:T(8,128)(2,1)} %bitcast.73, bf16[768,1280]{1,0:T(8,128)(2,1)} %copy-done.10, bf16[384,1280]{1,0:T(8,128)(2,1)} %bitcast.64, f32[384,1280]{1,0:T(8,128)} %get-tuple-element.77.middle_in, f32[1,1280]{1,0:T(1,128)} %copy-done.16), custom_call_target="tpu_custom_call" | custom-call | tf_op jit(solution)/shard_map/share_master/pallas_call | solution.py:1708
  554.4 9.4 %slice.32 = bf16[1,2459520]{1,0:T(2,128)(2,1)} slice(f32[1,2459648]{1,0:T(1,128)} %bitcast.75), slice={[0:1], [0:2459520]} | slice | bytes 9838080 | tf_op jit(solution)/shard_map/slice | solution.py:1929
  563.8 1.4 pad_maximum_fusion
  565.2 0.8 copy-done.3
  566.0 0.6 copy-done.25
  566.6 1.2 add_convert_fusion
  567.8 0.6 copy.53
  (97 shorter events, 1.4 us)
Async XLA Ops:
  0.6 1.5 copy-start
  0.7 5.1 copy-start.5
  0.7 4.8 copy-start.39
  0.7 4.9 copy-start.40
  0.7 5.0 copy-start.33
  0.7 5.0 copy-start.34
  3.2 2.5 copy-start.8
  5.4 86.2 %copy-start.38 = (s32[3]{0:T(128)S(1)}, s32[3]{0:T(128)}, u32[]{:S(2)}) copy-start(s32[3]{0:T(128)} %param.25) | copy-start | bytes 40
  5.7 88.4 %copy-start.16 = (f32[1,1280]{1,0:T(1,128)}, f32[1,1280]{1,0:T(1,128)S(1)}, u32[]{:S(2)}) copy-start(f32[1,1280]{1,0:T(1,128)S(1)} %reshape.201.gain_ref) | copy-start | bytes 15364
  5.7 88.4 %copy-start.17 = (f32[1,1280]{1,0:T(1,128)}, f32[1,1280]{1,0:T(1,128)S(1)}, u32[]{:S(2)}) copy-start(f32[1,1280]{1,0:T(1,128)S(1)} %reshape.202.shift_ref) | copy-start | bytes 15364
  5.8 1.0 copy-start.13
  6.8 1.0 copy-start.14
  7.8 1.0 copy-start.15
  8.8 85.5 %copy-start.29 = (bf16[1280]{0:T(1024)(128)(2,1)S(1)}, bf16[1280]{0:T(1024)(128)(2,1)}, u32[]{:S(2)}) copy-start(bf16[1280]{0:T(1024)(128)(2,1)} %param.37) | copy-start | bytes 7684
  8.8 85.5 %copy-start.35 = (bf16[1280]{0:T(1024)(128)(2,1)S(1)}, bf16[1280]{0:T(1024)(128)(2,1)}, u32[]{:S(2)}) copy-start(bf16[1280]{0:T(1024)(128)(2,1)} %param.36) | copy-start | bytes 7684
  8.8 85.5 %copy-start.36 = (bf16[1280]{0:T(1024)(128)(2,1)S(1)}, bf16[1280]{0:T(1024)(128)(2,1)}, u32[]{:S(2)}) copy-start(bf16[1280]{0:T(1024)(128)(2,1)} %param.38) | copy-start | bytes 7684
  8.8 85.5 %copy-start.6 = (bf16[128,3,1280]{2,0,1:T(8,128)(2,1)S(1)}, bf16[128,3,1280]{2,0,1:T(8,128)(2,1)}, u32[]{:S(2)}) copy-start(bf16[128,3,1280]{2,0,1:T(8,128)(2,1)} %param.24) | copy-start | bytes 2949124
  87.2 2.2 copy-start.4
  89.4 1.3 copy-start.10
  94.3 1.4 copy-start.7
  180.5 0.9 copy-start.12
  181.5 0.6 copy-start.18
  182.1 0.6 copy-start.19
  182.7 1.7 copy-start.20
  184.4 0.9 copy-start.22
  185.3 1.2 copy-start.11
  185.3 94.0 %copy-start.2 = (f32[384,1280]{1,0:T(8,128)}, f32[384,1280]{1,0:T(8,128)S(1)}, u32[]{:S(2)}) copy-start(f32[384,1280]{1,0:T(8,128)S(1)} %get-tuple-element.41) | copy-start | bytes 5898244
  277.0 1.5 copy-start.24
  279.3 1.2 copy-start.9
  280.5 1.9 copy-start.23
  282.4 2.5 copy-start.28
  285.1 3.3 copy-start.21
  291.3 118.8 %copy-start.31 = (f32[3]{0:T(128)S(1)}, f32[3]{0:T(128)}, u32[]{:S(2)}) copy-start(f32[3]{0:T(128)} %param.47) | copy-start | bytes 40
  410.1 0.6 copy-start.30
  554.3 9.4 %copy-start.26 = (f32[256,1280]{1,0:T(8,128)S(1)}, f32[256,1280]{1,0:T(8,128)}, u32[]{:S(2)}) copy-start(f32[256,1280]{1,0:T(8,128)} %get-tuple-element.65) | copy-start | bytes 3932164
  554.4 9.4 %copy-start.27 = (f32[128,1280]{1,0:T(8,128)S(1)}, f32[128,1280]{1,0:T(8,128)}, u32[]{:S(2)}) copy-start(f32[128,1280]{1,0:T(8,128)} %get-tuple-element.61) | copy-start | bytes 1966084
  563.7 1.4 copy-start.32
  563.8 2.3 copy-start.3
  563.8 2.8 copy-start.25
  565.2 3.2 copy-start.1
  566.6 1.2 copy-start.37

commit v11 on v10

--- a/solution.py
+++ b/solution.py
@@ -705,7 +705,7 @@
     for _ in outer:
         pass
     spread = plane_gather(place, outer_all, outer_full, local.at[3], plane_send, plane_recv)
-    drive(spread, mixing)
+    drive(spread, gather, mixing)
     for level in range(LINE):
         for core in range(2):
             for group, start in enumerate(OUTER_STARTS):
@@ -721,7 +721,6 @@
         middle = frames_ref[rows].astype(F32) + (middle_ref[rows] + out_bias_ref[...])
         middle_ref[rows] = middle
         two_ref[rows] = layer_norm(middle, gain_two_ref[...], shift_two_ref[...]).astype(BF)
-    drive(gather)
 
 
 def attend(qkv, mask, live, weights, outer, frames, out_bias, gain_two, shift_two):

time: 577 us -> 564 us (0.977)
  Pallas kernels: 508 us -> 494 us
    pallas_call x1, Pallas kernels: 84.8 us -> 68.4 us  [attend(): pl.pallas_call(attend_kernel, out_shape=(jax.ShapeDtypeStruct((8, 3, 160,...]
where the time goes in v11:
time: 564 us; the launch traced here: 555 us
  Pallas kernels  494 us (88%)
  local copies, waits for them, and re-layouts  43.9 us (8%)
  other arithmetic  7.81 us (1%)
    pallas_call x1, Pallas kernels, attend_back(): pl.pallas_call(functools.partial(attend_back_kernel, split), out_shape=(j...  117 us
    pallas_call x1, Pallas kernels, feed_forward(): pl.pallas_call(functools.partial(feed_forward_kernel, split), out_shape=(...  87.8 us
    pallas_call x1, Pallas kernels, project(): pl.pallas_call(project_kernel, out_shape=(jax.ShapeDtypeStruct((8,) + fra...  78.5 us
    pallas_call x1, Pallas kernels, finish(): pl.pallas_call(functools.partial(finish_kernel, split), out_shape=(jax.Sh...  69.7 us
    pallas_call x1, Pallas kernels, attend(): pl.pallas_call(attend_kernel, out_shape=(jax.ShapeDtypeStruct((8, 3, 160,...  68.4 us
    pallas_call x1, Pallas kernels, share_master(): pl.pallas_call(functools.partial(share_master_kernel, split), out_shape=(...  58.8 us
    unnamed x88, local copies, waits for them, and re-layouts  21.6 us
    pallas_call x1, Pallas kernels, optimize(): pl.pallas_call(optimize_kernel, grid=(pl.cdiv(SHARE_ENTRIES, STEP_ENTRIES...  13.4 us

profile of v11, /device:TPU:0, one launch (start us, length us, event | category | flops | bytes accessed | tf_op | source)
XLA Modules:
  0.0 554.9 jit_solution(14753208873606567539)
XLA Ops:
  0.7 1.4 copy-done
  2.1 1.1 constant_dynamic-slice_fusion.3
  3.3 1.4 copy.44
  4.6 0.8 dynamic_slice.18
  5.8 1.0 copy-done.13
  6.8 1.0 copy-done.14
  7.8 1.0 copy-done.15
  8.8 78.5 %project.1 = (bf16[8,384,1280]{2,1,0:T(8,128)(2,1)}, bf16[8,384,768]{2,1,0:T(8,128)(2,1)S(1)}, bf16[8,384,1280]{2,1,0:T(8,128)(2,1)}, bf16[768,1280]{1,0:T(8,128)(2,1)S(1)}) custom-call(bf16[384,1280]{1,0:T(8,128)(2,1)S(1)} %bitcast.65, f32[1,1280]{1,0:T(1,128)S(1)} %reshape.201.gain_ref, f32[1,1280]{1,0:T(1,128)S(1)} %reshape.202.shift_ref, ...), custom_call_target="tpu_custom_call" | custom-call | tf_op jit(solution)/shard_map/project/pallas_call | solution.py:619
  87.3 2.2 copy-done.4
  89.4 1.3 copy-done.10
  90.7 0.9 constant_dynamic-slice_fusion.2.outer_ref
  91.7 0.8 select_bitcast_fusion
  92.5 1.7 copy.36.mask_ref
  94.3 1.4 copy-done.7
  95.7 68.4 %attend.1 = (bf16[8,3,160,128]{3,2,1,0:T(8,128)(2,1)S(1)}, f32[6,1,1024]{2,1,0:T(1,128)S(1)}, f32[2,8,256]{2,1,0:T(8,128)S(1)}, bf16[4,176,1280]{2,1,0:T(8,128)(...) custom-call(bf16[8,3,128,768]{3,2,1,0:T(8,128)(2,1)} %bitcast.61, ...), custom_call_target="tpu_custom_call" | custom-call | tf_op jit(solution)/shard_map/attend/pallas_call | solution.py:727
  164.2 0.9 copy-done.12
  165.1 0.6 copy-done.18
  165.7 0.6 copy-done.19
  166.3 1.7 copy-done.20
  168.0 0.9 copy-done.22
  168.9 1.2 copy-done.11
  170.2 0.7 reshape.209.bias_ref
  170.8 1.8 constant_dynamic-slice_fusion.1.down_ref
  172.6 87.8 %feed_forward.1 = (f32[384,1280]{1,0:T(8,128)}, bf16[8,384,640]{2,1,0:T(8,128)(2,1)}, bf16[4,336,1280]{2,1,0:T(8,128)(2,1)}, f32[1,640]{1,0:T(1,128)}, bf16[4,160,1280]{2,1,0:T(8,128)(2,1)}) custom-call(bf16[384,1280]{1,0:T(8,128)(2,1)} %copy-done.12, bf16[8,384,1280]{2,1,0:T(8,128)(2,1)} %get-tuple-element.44.upstream_ref, ...), custom_call_target="tpu_custom_call" | custom-call | tf_op jit(solution)/shard_map/feed_forward/pallas_call | solution.py:907
  260.6 0.3 multiply_reduce_fusion.2
  260.9 1.2 copy-done.24
  262.1 0.7 multiply_reduce_fusion
  262.9 0.6 fusion.5
  263.5 0.6 copy-done.9
  264.1 1.7 convert_reduce_fusion.1
  266.0 2.5 bitcast_convert_fusion
  268.7 2.3 pad.20
  271.0 1.0 copy-done.21
  272.0 2.8 fusion.pull_ref
  274.9 117.2 %attend_back.1 = (bf16[8,3,128,768]{3,2,1,0:T(8,128)(2,1)}, f32[384,1280]{1,0:T(8,128)}, f32[336,1280]{1,0:T(8,128)}, f32[48,1280]{1,0:T(8,128)}, f32[1280,768]{1,0:T(8,128)}, /*index=5*/f32[1,768]{1,0:T(1,128)}) custom-call(bf16[8,3,128,768]{3,2,1,0:T(8,128)(2,1)} %bitcast.62, f32[3,1024,1]{2,1,0:T(8,128)} %copy.36.mask_ref, f32[6,1,1024]{2,1,0:T(1,128)} %copy-done.18, ...), custom_call_target="tpu_custom_call" | custom-call | tf_op jit(solution)/shard_map/attend_back/pallas_call | solution.py:1139
  392.1 1.6 copy.40.bias_column_ref
  393.7 0.8 slice.23
  394.8 0.6 fusion.6
  395.4 69.7 %finish.1 = (f32[128,1280]{1,0:T(8,128)}, f32[4808,128]{1,0:T(8,128)}, f32[8,128]{1,0:T(8,128)}, f32[4808,128]{1,0:T(8,128)}) custom-call(bf16[8,384,768]{2,1,0:T(8,128)(2,1)} %bitcast.72, bf16[768,1280]{1,0:T(8,128)(2,1)} %copy-done.10, f32[1280,768]{1,0:T(8,128)} %get-tuple-element.56.joined_ref, f32[1,768]{1,0:T(1,128)} %get-tuple-element.57.bias_ref, ...), custom_call_target="tpu_custom_call" | custom-call | tf_op jit(solution)/shard_map/finish/pallas_call | solution.py:1564
  467.8 0.6 pad_maximum_fusion.2.rates_ref
  468.4 13.4 %optimize.1 = (f32[1,614880]{1,0:T(1,128)}, f32[1,614880]{1,0:T(1,128)}, f32[1,614880]{1,0:T(1,128)}, f32[1,614880]{1,0:T(1,128)}, f32[1,615424]{1,0:T(1,128)}) custom-call(f32[3]{0:T(128)} %pad_maximum_fusion.2.rates_ref, f32[1,615424]{1,0:T(1,128)} %bitcast.78, f32[1,615424]{1,0:T(1,128)} %bitcast.77, f32[1,614880]{1,0:T(1,128)} %master_ref.1, ...), custom_call_target="tpu_custom_call" | custom-call | tf_op jit(solution)/shard_map/optimize/pallas_call | solution.py:1754
  481.8 58.8 %share_master.1 = (f32[19216,128]{1,0:T(8,128)}, f32[256,1280]{1,0:T(8,128)}) custom-call(f32[4808,128]{1,0:T(8,128)} %bitcast.79, bf16[8,384,768]{2,1,0:T(8,128)(2,1)} %bitcast.73, bf16[768,1280]{1,0:T(8,128)(2,1)} %copy-done.10, bf16[384,1280]{1,0:T(8,128)(2,1)} %bitcast.64, f32[384,1280]{1,0:T(8,128)} %get-tuple-element.77.middle_in, f32[1,1280]{1,0:T(1,128)} %copy-done.16), custom_call_target="tpu_custom_call" | custom-call | tf_op jit(solution)/shard_map/share_master/pallas_call | solution.py:1707
  540.7 9.4 %slice.32 = bf16[1,2459520]{1,0:T(2,128)(2,1)} slice(f32[1,2459648]{1,0:T(1,128)} %bitcast.75), slice={[0:1], [0:2459520]} | slice | bytes 9838080 | tf_op jit(solution)/shard_map/slice | solution.py:1928
  550.1 1.4 pad_maximum_fusion
  551.5 0.8 copy-done.3
  552.3 0.6 copy-done.25
  552.9 1.2 add_convert_fusion
  554.1 0.6 copy.53
  (97 shorter events, 1.4 us)
Async XLA Ops:
  0.6 1.5 copy-start
  0.7 5.1 copy-start.5
  0.7 4.8 copy-start.39
  0.7 4.9 copy-start.40
  0.7 5.0 copy-start.33
  0.7 5.0 copy-start.34
  3.2 2.5 copy-start.8
  5.4 86.2 %copy-start.38 = (s32[3]{0:T(128)S(1)}, s32[3]{0:T(128)}, u32[]{:S(2)}) copy-start(s32[3]{0:T(128)} %param.25) | copy-start | bytes 40
  5.7 88.4 %copy-start.16 = (f32[1,1280]{1,0:T(1,128)}, f32[1,1280]{1,0:T(1,128)S(1)}, u32[]{:S(2)}) copy-start(f32[1,1280]{1,0:T(1,128)S(1)} %reshape.201.gain_ref) | copy-start | bytes 15364
  5.7 88.4 %copy-start.17 = (f32[1,1280]{1,0:T(1,128)}, f32[1,1280]{1,0:T(1,128)S(1)}, u32[]{:S(2)}) copy-start(f32[1,1280]{1,0:T(1,128)S(1)} %reshape.202.shift_ref) | copy-start | bytes 15364
  5.8 1.0 copy-start.13
  6.8 1.0 copy-start.14
  7.8 1.0 copy-start.15
  8.8 85.5 %copy-start.29 = (bf16[1280]{0:T(1024)(128)(2,1)S(1)}, bf16[1280]{0:T(1024)(128)(2,1)}, u32[]{:S(2)}) copy-start(bf16[1280]{0:T(1024)(128)(2,1)} %param.37) | copy-start | bytes 7684
  8.8 85.5 %copy-start.35 = (bf16[1280]{0:T(1024)(128)(2,1)S(1)}, bf16[1280]{0:T(1024)(128)(2,1)}, u32[]{:S(2)}) copy-start(bf16[1280]{0:T(1024)(128)(2,1)} %param.36) | copy-start | bytes 7684
  8.8 85.5 %copy-start.36 = (bf16[1280]{0:T(1024)(128)(2,1)S(1)}, bf16[1280]{0:T(1024)(128)(2,1)}, u32[]{:S(2)}) copy-start(bf16[1280]{0:T(1024)(128)(2,1)} %param.38) | copy-start | bytes 7684
  8.8 85.5 %copy-start.6 = (bf16[128,3,1280]{2,0,1:T(8,128)(2,1)S(1)}, bf16[128,3,1280]{2,0,1:T(8,128)(2,1)}, u32[]{:S(2)}) copy-start(bf16[128,3,1280]{2,0,1:T(8,128)(2,1)} %param.24) | copy-start | bytes 2949124
  87.2 2.2 copy-start.4
  89.4 1.3 copy-start.10
  94.3 1.4 copy-start.7
  164.2 0.9 copy-start.12
  165.1 0.6 copy-start.18
  165.7 0.6 copy-start.19
  166.3 1.7 copy-start.20
  168.0 0.9 copy-start.22
  168.9 1.2 copy-start.11
  168.9 93.9 %copy-start.2 = (f32[384,1280]{1,0:T(8,128)}, f32[384,1280]{1,0:T(8,128)S(1)}, u32[]{:S(2)}) copy-start(f32[384,1280]{1,0:T(8,128)S(1)} %get-tuple-element.41) | copy-start | bytes 5898244
  260.6 1.5 copy-start.24
  262.9 1.2 copy-start.9
  264.1 1.9 copy-start.23
  265.9 2.5 copy-start.28
  268.7 3.3 copy-start.21
  274.9 119.9 %copy-start.31 = (f32[3]{0:T(128)S(1)}, f32[3]{0:T(128)}, u32[]{:S(2)}) copy-start(f32[3]{0:T(128)} %param.47) | copy-start | bytes 40
  394.8 0.6 copy-start.30
  540.6 9.4 %copy-start.26 = (f32[256,1280]{1,0:T(8,128)S(1)}, f32[256,1280]{1,0:T(8,128)}, u32[]{:S(2)}) copy-start(f32[256,1280]{1,0:T(8,128)} %get-tuple-element.65) | copy-start | bytes 3932164
  540.7 9.4 %copy-start.27 = (f32[128,1280]{1,0:T(8,128)S(1)}, f32[128,1280]{1,0:T(8,128)}, u32[]{:S(2)}) copy-start(f32[128,1280]{1,0:T(8,128)} %get-tuple-element.61) | copy-start | bytes 1966084
  550.0 1.4 copy-start.32
  550.1 2.3 copy-start.3
  550.1 2.8 copy-start.25
  551.5 3.2 copy-start.1
  552.9 1.2 copy-start.37
